TPU v7x, 32 devices: a whole 2x2x4 slice. The times are simulated.
32 devices in a mesh: frame: 16 (over z, y, x), row: 2 (over core).
Axes of the slice: x: 2, y: 2, z: 4, core: 2. Of those that a mesh axis runs over, the one named last changes fastest.
Arguments:
- tokens: bfloat16 [16, 2, 128, 2048], P('frame', 'row'), may hold values from -6 to 6
- cotangent: bfloat16 [16, 2, 128, 2048], P('frame', 'row'), may hold values from -6 to 6
- timestep: int32 [1], replicated, may hold values from 0 to 999
- mod_weight: bfloat16 [256, 4096], P(None, 'frame'), may hold values from -0.375 to 0.375
- proj_weight: bfloat16 [2048, 256], P('frame'), may hold values from -0.125 to 0.125
- step_weight: bfloat16 [2048, 32], P('frame'), may hold values from -0.125 to 0.125
- step_bias: float32 [32], replicated, may hold values from -1 to 1
- rate_space: float32 [32], replicated, may hold values from 0.001171875 to 0.05
- rate_time: float32 [32], replicated, may hold values from 0.01875 to 1
- skip_gain: float32 [32], replicated, may hold values from 0.5 to 1.5
Outputs:
- mixed: bfloat16 [16, 2, 128, 2048], P('frame', 'row')
- d_tokens: bfloat16 [16, 2, 128, 2048], P('frame', 'row')
- grad_proj: float32 [2048, 256], P('frame')
- grad_step: float32 [2048, 32], P('frame')
- grad_mod: float32 [256, 4096], P(None, 'frame')
All inputs are finite; a program needn't handle non-finite values.
Results may differ from a plain program's by a relative error of at most 0.015.
Values may be sent and summed in bfloat16 or wider, within the bound.
No kernel may reach another device: no remote copies, remote signals or barrier semaphores. Data moves between devices by JAX's collectives and lax.ppermute only.
A program may use at most 64 MiB of HBM per device.

v0:
```python
import math

import jax
import jax.numpy as jnp
from jax import lax
from jax.sharding import PartitionSpec as P

norm_eps = 1e-05


def prefix(array, axis, join, neutral):
    place = lax.axis_index(axis)
    gathered = jax.tree.map(
        lambda a, kind: lax.all_gather(a.astype(kind), axis), array, (jnp.bfloat16, jnp.bfloat16)
    )
    state = jax.tree.map(lambda a, e: jnp.zeros_like(a) + jnp.asarray(e, a.dtype), array, neutral)

    def prefix_one(hop, state):
        return join(
            state,
            jax.tree.map(
                lambda a, own: lax.dynamic_index_in_dim(a, hop, 0, False).astype(own.dtype),
                gathered,
                array,
            ),
        )

    return lax.fori_loop(0, place, prefix_one, state)


def carried_in(array, axis, join, neutral):
    count = lax.axis_size(axis)
    place = lax.axis_index(axis)
    ahead = count - 1 - place
    gathered = jax.tree.map(
        lambda a, kind: lax.all_gather(a.astype(kind), axis),
        array,
        jax.tree.map(lambda a: jnp.bfloat16 if a.dtype == jnp.float32 else a.dtype, array),
    )
    state = jax.tree.map(lambda a, e: jnp.zeros_like(a) + jnp.asarray(e, a.dtype), array, neutral)

    def carried_one(hop, state):
        source = count - 1 - hop
        return join(
            state,
            jax.tree.map(
                lambda a, own: lax.dynamic_index_in_dim(a, source, 0, False).astype(own.dtype),
                gathered,
                array,
            ),
        )

    return lax.fori_loop(0, ahead, carried_one, state)


def time_embed(timestep, embed_dim):
    half_dim = embed_dim // 2
    frequency = jnp.exp(-math.log(10000.0) * jnp.arange(half_dim, dtype=jnp.float32) / half_dim)
    angles = timestep.astype(jnp.float32)[:, None] * frequency[None, :]
    return jax.nn.silu(jnp.concatenate([jnp.cos(angles), jnp.sin(angles)], axis=1))


def normalize(values):
    return values * lax.rsqrt(jnp.mean(values * values, axis=-1, keepdims=True) + norm_eps)


def block_parts(normed, coeffs, logits, step_bias, decay_rate, need_end):
    seq_count, length, feat_width = normed.shape
    head_count = decay_rate.shape[0]
    inputs = normed.reshape(seq_count, length, head_count, feat_width // head_count)
    state_size = coeffs.shape[-1] // 2
    b_part = coeffs[..., :state_size]
    c_part = coeffs[..., state_size:]
    step_size = jax.nn.softplus(logits.astype(jnp.float32) + step_bias)
    cum_log = jnp.cumsum(-step_size * decay_rate, axis=1)
    scores = (
        jnp.einsum("stn,sun->stu", c_part, b_part, preferred_element_type=jnp.float32) / state_size
    )
    lag_rows = jnp.swapaxes(cum_log, 1, 2)
    causal = jnp.tril(jnp.ones((length, length), dtype=bool))
    differences = lag_rows[:, :, :, None] - lag_rows[:, :, None, :]
    decays = jnp.where(causal, jnp.exp(jnp.where(causal, differences, 0.0)), 0.0)
    spread = jnp.swapaxes(step_size, 1, 2)
    weights = (scores[:, None, :, :] * decays * spread[:, :, None, :]).astype(jnp.bfloat16)
    inner_out = jnp.einsum("shtu,suhp->sthp", weights, inputs, preferred_element_type=jnp.float32)
    inner_out = inner_out.reshape(seq_count, length, feat_width)
    if need_end:
        end_log = cum_log[:, -1:, :]
        lead_decay = jnp.exp(end_log - cum_log) * step_size
        scaled = (inputs.astype(jnp.float32) * lead_decay[..., None]).astype(jnp.bfloat16)
        end_local = jnp.einsum("sthp,stn->shpn", scaled, b_part, preferred_element_type=jnp.float32)
    else:
        end_local = jnp.zeros(
            (seq_count, head_count, feat_width // head_count, state_size), jnp.float32
        )
    return (inner_out, end_local, cum_log, c_part)


def carry_term(cum_log, c_part, state_in):
    seq_count, length, head_count = cum_log.shape
    state_size = c_part.shape[-1]
    reached = jnp.einsum(
        "stn,shpn->sthp", c_part.astype(jnp.float32), state_in, precision=lax.Precision.HIGHEST
    )
    return (reached * jnp.exp(cum_log)[..., None] / state_size).reshape(seq_count, length, -1)


def combine_forward(earlier, later):
    return (earlier[0] * later[0], later[0][:, :, None, None] * earlier[1] + later[1])


def combine_backward(earlier, later):
    return (earlier[0] * later[0], later[1] + later[0][:, :, None, None] * earlier[1])


def per_device(
    tokens,
    cotangent,
    timestep,
    mod_weight,
    proj_weight,
    step_weight,
    step_bias,
    rate_space,
    rate_time,
    skip_gain,
):
    frame_count = lax.axis_size("frame")
    row_count = lax.axis_size("row")
    frame_id = lax.axis_index("frame")
    feat_width = tokens.shape[-1]
    band_len = tokens.shape[1] * tokens.shape[2]
    clip_count = timestep.shape[0]
    clip_frames = frame_count // clip_count
    site_count = band_len // frame_count
    head_count = rate_space.shape[0]
    clip_id = frame_id // clip_frames
    factor = (frame_count * row_count * band_len) ** (-0.5)
    activated = time_embed(timestep, mod_weight.shape[0]).astype(jnp.bfloat16)
    proj_full, step_full = (
        lax.all_gather(proj_weight, "frame", axis=0, tiled=True),
        lax.all_gather(step_weight, "frame", axis=0, tiled=True),
    )
    mod_full = lax.all_gather(mod_weight, "frame", axis=1, tiled=True)
    modulation = jnp.dot(activated, mod_full, preferred_element_type=jnp.float32)
    clip_mod = lax.dynamic_index_in_dim(modulation, clip_id, 0, keepdims=False)
    shift_vec = clip_mod[:feat_width]
    scale_vec = clip_mod[feat_width:]
    tokens_wide = tokens.reshape(band_len, feat_width).astype(jnp.float32)
    unit_rows = normalize(tokens_wide)
    normed = (unit_rows * (1.0 + scale_vec) + shift_vec).astype(jnp.bfloat16)
    projected = jnp.dot(normed, proj_full, preferred_element_type=jnp.float32).astype(jnp.bfloat16)
    logits = jnp.dot(normed, step_full, preferred_element_type=jnp.float32).astype(jnp.bfloat16)
    skip_full = jnp.repeat(skip_gain, feat_width // head_count)
    flat_grad = cotangent.reshape(band_len, feat_width)

    def space_parts(normed_band, proj_band, logit_band):
        return block_parts(normed_band, proj_band, logit_band, step_bias, rate_space, True)

    parts_out, parts_pull = jax.vjp(space_parts, normed[None], projected[None], logits[None])
    inner_out, end_local, cum_log, c_part = parts_out
    end_decay = jnp.exp(cum_log[:, -1, :])
    identity = (jnp.ones_like(end_decay), jnp.zeros_like(end_local))
    prefix_decay, state_in = prefix((end_decay, end_local), "row", combine_forward, identity)
    carried, carry_pull = jax.vjp(carry_term, cum_log, c_part, state_in)
    space_out = (inner_out + carried)[0]
    site_normed, site_grad = (
        lax.all_to_all(normed, "frame", split_axis=0, concat_axis=0, tiled=True),
        lax.all_to_all(flat_grad, "frame", split_axis=0, concat_axis=0, tiled=True),
    )
    site_proj = jnp.dot(site_normed, proj_full, preferred_element_type=jnp.float32).astype(
        jnp.bfloat16
    )
    site_logits = jnp.dot(site_normed, step_full, preferred_element_type=jnp.float32).astype(
        jnp.bfloat16
    )

    def to_seq(member):
        shaped = member.reshape(frame_count, site_count, member.shape[-1])
        return shaped.transpose(1, 0, 2)

    def from_seq(member):
        return member.transpose(1, 0, 2).reshape(frame_count * site_count, member.shape[-1])

    def time_path(normed_seq, proj_seq, logit_seq):
        return block_parts(normed_seq, proj_seq, logit_seq, step_bias, rate_time, False)[0]

    time_out, time_pull = jax.vjp(
        time_path, to_seq(site_normed), to_seq(site_proj), to_seq(site_logits)
    )
    time_low = from_seq(time_out.astype(jnp.bfloat16))
    time_dnorm, time_dproj, time_dlogit = time_pull(to_seq(site_grad).astype(jnp.float32))
    site_dproj = from_seq(time_dproj)
    site_dlogit = from_seq(time_dlogit)
    site_back = (
        from_seq(time_dnorm).astype(jnp.float32)
        + jnp.dot(site_dproj, proj_full.T, preferred_element_type=jnp.float32)
        + jnp.dot(site_dlogit, step_full.T, preferred_element_type=jnp.float32)
    ).astype(jnp.bfloat16)
    proj_time = jnp.dot(site_normed.T, site_dproj, preferred_element_type=jnp.float32)
    step_time = jnp.dot(site_normed.T, site_dlogit, preferred_element_type=jnp.float32)
    space_time, time_back = (
        lax.all_to_all(time_low, "frame", split_axis=0, concat_axis=0, tiled=True),
        lax.all_to_all(site_back, "frame", split_axis=0, concat_axis=0, tiled=True),
    )
    mixed = (
        space_out + space_time.astype(jnp.float32) + skip_full * normed.astype(jnp.float32)
    ).astype(jnp.bfloat16)
    upstream = flat_grad.astype(jnp.float32)
    carry_dcum, carry_dc, own_state = carry_pull(upstream[None])
    suffix_decay, later_grad = carried_in((end_decay, own_state), "row", combine_backward, identity)
    end_dlog = jnp.sum(later_grad * state_in, axis=(2, 3)) * end_decay
    carry_dcum = carry_dcum.at[:, -1, :].add(end_dlog)
    space_dnorm, space_dproj, space_dlogit = parts_pull(
        (upstream[None], later_grad, carry_dcum, carry_dc)
    )
    skip_dnorm = (upstream * skip_full).astype(jnp.bfloat16)
    total_dnorm = space_dnorm[0] + skip_dnorm
    pre_grad = (
        total_dnorm.astype(jnp.float32)
        + jnp.dot(space_dproj[0], proj_full.T, preferred_element_type=jnp.float32)
        + jnp.dot(space_dlogit[0], step_full.T, preferred_element_type=jnp.float32)
        + time_back.astype(jnp.float32)
    )
    proj_term = jnp.dot(normed.T, space_dproj[0], preferred_element_type=jnp.float32) + proj_time
    step_term = jnp.dot(normed.T, space_dlogit[0], preferred_element_type=jnp.float32) + step_time
    shift_grad = jnp.sum(pre_grad, axis=0)
    scale_grad = jnp.sum(pre_grad * unit_rows, axis=0)
    picked = (jnp.arange(clip_count) == clip_id).astype(jnp.float32)
    mod_term = jnp.concatenate([shift_grad, scale_grad])[:, None] * picked[None, :]
    proj_sum, step_sum, mod_sum = (
        lax.psum(proj_term.astype(jnp.bfloat16), "row").astype(jnp.float32),
        lax.psum(step_term.astype(jnp.bfloat16), "row").astype(jnp.float32),
        lax.psum(mod_term.astype(jnp.bfloat16), "row").astype(jnp.float32),
    )
    proj_sum, step_sum, mod_sum = (
        lax.psum_scatter(proj_sum, "frame", scatter_dimension=0, tiled=True),
        lax.psum_scatter(step_sum, "frame", scatter_dimension=0, tiled=True),
        lax.psum_scatter(mod_sum, "frame", scatter_dimension=0, tiled=True),
    )
    grad_proj = proj_sum * factor
    grad_step = step_sum * factor
    grad_mod = (
        jnp.dot(activated.astype(jnp.float32).T, mod_sum.T, precision=lax.Precision.HIGHEST)
        * factor
    )
    unused, norm_pull = jax.vjp(normalize, tokens_wide)
    (tokens_grad,) = norm_pull(pre_grad * (1.0 + scale_vec))
    d_tokens = tokens_grad.astype(jnp.bfloat16).reshape(tokens.shape)
    return (mixed.reshape(tokens.shape), d_tokens, grad_proj, grad_step, grad_mod)


def solution(mesh):
    placed = (
        P("frame", "row", None, None),
        P("frame", "row", None, None),
        P(),
        P(None, "frame"),
        P("frame", None),
        P("frame", None),
        P(),
        P(),
        P(),
        P(),
    )
    return jax.shard_map(
        per_device,
        mesh=mesh,
        in_specs=placed,
        out_specs=(
            P("frame", "row", None, None),
            P("frame", "row", None, None),
            P("frame", None),
            P("frame", None),
            P(None, "frame"),
        ),
        check_vma=False,
    )
```

profile of v0, /device:TPU:0, one launch (start us, length us, event | category | flops | bytes accessed | tf_op | source)
XLA Modules:
  0.0 490.7 jit_solution(3879071118985589353)
XLA Ops:
  7.9 8.4 %all-to-all-start.2 = ((bf16[16,8,2048]{2,1,0:T(8,128)(2,1)}), bf16[16,8,2048]{2,1,0:T(8,128)(2,1)S(1)}, u32[]{:S(2)}, u32[]{:S(2)}) async-start(bf16[16,8,2048]{2,1,0:T(8,128)(2,1)} %bitcast.449), calls=%async_computation.2 | async-start | bytes 1048576 | tf_op jit(solution)/shard_map/all_to_all | solution.py:169
  22.7 42.0 %all_gather.29 = bf16[2048,32]{0,1:T(8,128)(2,1)S(1)} all-gather(bf16[128,32]{0,1:T(8,128)(2,1)S(1)} %copy-done.52), channel_id=1, replica_groups=mesh['frame'=16,'row'=2] {'frame'}, dimensions={0}, use_global_device_ids=true | all-gather | bytes 139264 | tf_op jit(solution)/shard_map/all_gather | solution.py:142
  67.9 12.4 %all-gather.7.cloned.1.call-done = bf16[256,4096]{1,0:T(8,128)(2,1)} async-done(((bf16[256,256]{1,0:T(8,128)(2,1)}), bf16[256,4096]{1,0:T(8,128)(2,1)}) %all-gather.7.cloned.1.call-update) | async-done | bytes 2097168 | tf_op jit(solution)/shard_map/all_gather | solution.py:144
  85.5 4.0 all-to-all-start
  89.5 2.5 convert_multiply_fusion
  94.9 42.8 %all-gather.9.cloned.1.call-done = bf16[2048,256]{1,0:T(8,128)(2,1)} async-done(((bf16[128,256]{1,0:T(8,128)(2,1)}), bf16[2048,256]{1,0:T(8,128)(2,1)}) %all-gather.9.cloned.1.call-update) | async-done | bytes 1048592 | tf_op jit(solution)/shard_map/all_gather | solution.py:141
  151.7 3.2 convert_bitcast_fusion
  155.0 3.5 fusion.26
  172.1 4.5 all-to-all-start.3
  190.0 2.7 convolution_bitcast_fusion
  195.5 3.8 fusion.24
  204.2 2.4 fusion.35
  223.1 2.6 fusion.70
  225.8 4.2 psum.23
  231.8 7.7 %all-reduce.8.cloned.1.call-done = (bf16[2048,256]{1,0:T(8,128)(2,1)}, bf16[2048,32]{0,1:T(8,128)(2,1)}) async-done(((bf16[2048,256]{1,0:T(8,128)(2,1)}, bf16[2048,32]{0,1:T(8,128)(2,1)}), (bf16[2048,256]{1,0:T(8,128)(2,1)}, bf16[2048,32]{0,1:T(8,128)(2,1)})) %all-reduce.8.cloned.1.call-update) | async-done | bytes 1179664 | tf_op jit(solution)/shard_map/psum | solution.py:232
  241.3 2.8 convert_element_type.533
  247.7 6.8 %all-to-all-start.1 = ((bf16[16,8,2048]{2,1,0:T(8,128)(2,1)}), bf16[16,8,2048]{2,1,0:T(8,128)(2,1)S(1)}, u32[]{:S(2)}, u32[]{:S(2)}) async-start(bf16[16,8,2048]{2,1,0:T(8,128)(2,1)} %copy.211), calls=%async_computation.1 | async-start | bytes 1048576 | tf_op jit(solution)/shard_map/all_to_all | solution.py:203
  254.6 2.8 fusion.80
  257.4 2.7 copy.201
  262.6 10.8 %all-to-all-done.1 = bf16[16,8,2048]{2,1,0:T(8,128)(2,1)S(1)} async-done(((bf16[16,8,2048]{2,1,0:T(8,128)(2,1)}), bf16[16,8,2048]{2,1,0:T(8,128)(2,1)S(1)}, u32[]{:S(2)}, u32[]{:S(2)}) %all-to-all-start.1) | async-done | bytes 524320 | tf_op jit(solution)/shard_map/all_to_all | solution.py:203
  273.4 2.4 fusion.52
  275.8 50.2 %reduce-scatter.10.cloned.1.call-done = f32[256,1]{1,0:T(8,128)} async-done(((f32[4096,1]{1,0:T(8,128)}), f32[256,1]{1,0:T(8,128)}) %reduce-scatter.10.cloned.1.call-update) | async-done | bytes 1040
  327.7 74.5 %reduce-scatter.8.cloned.1.call-done = f32[128,32]{0,1:T(8,128)} async-done(((f32[2048,32]{0,1:T(8,128)}), f32[128,32]{0,1:T(8,128)}) %reduce-scatter.8.cloned.1.call-update) | async-done | bytes 16400 | tf_op jit(solution)/shard_map/reduce_scatter | solution.py:238
  403.6 78.7 %reduce-scatter.6.cloned.1.call-done = f32[128,256]{1,0:T(8,128)} async-done(((f32[2048,256]{1,0:T(8,128)}), f32[128,256]{1,0:T(8,128)}) %reduce-scatter.6.cloned.1.call-update) | async-done | bytes 131088 | tf_op jit(solution)/shard_map/reduce_scatter | solution.py:237
  (253 shorter events, 97.8 us)
Async XLA Ops:
  7.2 13.2 %copy-start = (bf16[1,1,128,2048]{3,2,1,0:T(8,128)(2,1)S(1)}, bf16[1,1,128,2048]{3,2,1,0:T(8,128)(2,1)}, u32[]{:S(2)}) copy-start(bf16[1,1,128,2048]{3,2,1,0:T(8,128)(2,1)} %param.16) | copy-start | bytes 1572868
  7.2 14.5 %copy-start.60 = (f32[32]{0:T(128)S(1)}, f32[32]{0:T(128)}, u32[]{:S(2)}) copy-start(f32[32]{0:T(128)} %param.25) | copy-start | bytes 388
  7.2 73.2 %all-gather.7.cloned.1.call-start = ((), (), s32[]{:S(2)}) async-start(), calls=%async_computation.7 | async-start | bytes 2228224 | tf_op jit(solution)/shard_map/all_gather | solution.py:144
  7.9 14.8 %copy-start.52 = (bf16[128,32]{0,1:T(8,128)(2,1)S(1)}, bf16[128,32]{0,1:T(8,128)(2,1)}, u32[]{:S(2)}) copy-start(bf16[128,32]{0,1:T(8,128)(2,1)} %param.21) | copy-start | bytes 24580
  7.9 57.9 %all-to-all-start.2 = ((bf16[16,8,2048]{2,1,0:T(8,128)(2,1)}), bf16[16,8,2048]{2,1,0:T(8,128)(2,1)S(1)}, u32[]{:S(2)}, u32[]{:S(2)}) async-start(bf16[16,8,2048]{2,1,0:T(8,128)(2,1)} %bitcast.449), calls=%async_computation.2 | async-start | bytes 1048576 | tf_op jit(solution)/shard_map/all_to_all | solution.py:169
  16.3 121.4 %all-gather.9.cloned.1.call-start = ((), (), s32[]{:S(2)}) async-start(), calls=%async_computation.8 | async-start | bytes 1114112 | tf_op jit(solution)/shard_map/all_gather | solution.py:141
  22.4 59.9 %copy-start.53 = (f32[32]{0:T(128)S(1)}, f32[32]{0:T(128)}, u32[]{:S(2)}) copy-start(f32[32]{0:T(128)} %param.22) | copy-start | bytes 388
  22.6 60.1 %copy-start.58 = (f32[128]{0:T(128)}, f32[128]{0:T(128)S(1)}, u32[]{:S(2)}) copy-start(f32[128]{0:T(128)S(1)} %fusion.74) | copy-start | bytes 1540
  22.6 115.1 %copy-start.45 = (f32[128]{0:T(128)}, f32[128]{0:T(128)S(1)}, u32[]{:S(2)}) copy-start(f32[128]{0:T(128)S(1)} %fusion.158) | copy-start | bytes 1540
  67.9 14.8 %copy-start.55 = (f32[32]{0:T(128)S(1)}, f32[32]{0:T(128)}, u32[]{:S(2)}) copy-start(f32[32]{0:T(128)} %param.23) | copy-start | bytes 388
  85.5 60.6 %all-to-all-start = ((bf16[16,8,2048]{2,1,0:T(8,128)(2,1)}), bf16[16,8,2048]{2,1,0:T(8,128)(2,1)S(1)}, u32[]{:S(2)}, u32[]{:S(2)}) async-start(bf16[16,8,2048]{2,1,0:T(8,128)(2,1)} %fusion.62), calls=%async_computation | async-start | bytes 1048576 | tf_op jit(solution)/shard_map/all_to_all | solution.py:168
  89.5 87.2 %all-gather.13.cloned.1.call-start = ((), (), s32[]{:S(2)}) async-start(), calls=%async_computation.12 | async-start | bytes 1572864 | tf_op jit(solution)/shard_map/all_gather | solution.py:36
  94.9 45.8 %copy-start.3 = (f32[1,1,128,2048]{2,3,1,0:T(8,128)}, f32[1,1,128,2048]{2,3,1,0:T(8,128)S(1)}, u32[]{:S(2)}) copy-start(f32[1,1,128,2048]{2,3,1,0:T(8,128)S(1)} %copy.214) | copy-start | bytes 3145732
  140.7 8.8 %copy-start.1 = (bf16[2048,256]{1,0:T(8,128)(2,1)S(1)}, bf16[2048,256]{1,0:T(8,128)(2,1)}, u32[]{:S(2)}) copy-start(bf16[2048,256]{1,0:T(8,128)(2,1)} %all-gather.9.cloned.1.call-done) | copy-start | bytes 3145732
  172.1 51.0 %all-to-all-start.3 = ((bf16[16,8,2048]{2,1,0:T(8,128)(2,1)}), bf16[16,8,2048]{2,1,0:T(8,128)(2,1)}, u32[]{:S(2)}, u32[]{:S(2)}) async-start(bf16[16,8,2048]{2,1,0:T(8,128)(2,1)} %fusion.3), calls=%async_computation.3 | async-start | bytes 1048576 | tf_op jit(solution)/shard_map/all_to_all | solution.py:204
  176.6 26.0 %all-gather.11.cloned.1.call-start = ((), (), s32[]{:S(2)}) async-start(), calls=%async_computation.11 | async-start | bytes 1572864 | tf_op jit(solution)/shard_map/all_gather | solution.py:14
  189.9 49.6 %all-reduce.8.cloned.1.call-start = ((), (), s32[]{:S(2)}) async-start(), calls=%async_computation.14 | async-start | bytes 2359296 | tf_op jit(solution)/shard_map/psum | solution.py:232
  218.1 107.8 %reduce-scatter.10.cloned.1.call-start = ((), (), s32[]{:S(2)}) async-start(), calls=%async_computation.13 | async-start | bytes 2228224
  231.8 170.5 %reduce-scatter.8.cloned.1.call-start = ((), (), s32[]{:S(2)}) async-start(), calls=%async_computation.10 | async-start | bytes 278528 | tf_op jit(solution)/shard_map/reduce_scatter | solution.py:238
  241.2 241.1 %reduce-scatter.6.cloned.1.call-start = ((), (), s32[]{:S(2)}) async-start(), calls=%async_computation.9 | async-start | bytes 2228224 | tf_op jit(solution)/shard_map/reduce_scatter | solution.py:237
  245.8 8.7 %copy-start.10 = (f32[1,1,128,2048]{2,3,1,0:T(8,128)S(1)}, f32[1,1,128,2048]{2,3,1,0:T(8,128)}, u32[]{:S(2)}) copy-start(f32[1,1,128,2048]{2,3,1,0:T(8,128)} %copy.191) | copy-start | bytes 3145732
  247.7 25.6 %all-to-all-start.1 = ((bf16[16,8,2048]{2,1,0:T(8,128)(2,1)}), bf16[16,8,2048]{2,1,0:T(8,128)(2,1)S(1)}, u32[]{:S(2)}, u32[]{:S(2)}) async-start(bf16[16,8,2048]{2,1,0:T(8,128)(2,1)} %copy.211), calls=%async_computation.1 | async-start | bytes 1048576 | tf_op jit(solution)/shard_map/all_to_all | solution.py:203
  261.5 11.9 %copy-start.12 = (f32[1,1,128,2048]{3,2,1,0:T(8,128)S(1)}, f32[1,1,128,2048]{3,2,1,0:T(8,128)}, u32[]{:S(2)}) copy-start(f32[1,1,128,2048]{3,2,1,0:T(8,128)} %copy.201) | copy-start | bytes 3145732
  262.6 64.3 %copy-start.54 = (f32[256]{0:T(256)S(1)}, f32[256]{0:T(256)}, u32[]{:S(2)}) copy-start(f32[256]{0:T(256)} %get-tuple-element.230) | copy-start | bytes 3076
  (51 other events, 170.6 us)
Sparse Core Ops, SparseCore 0:
  10.7 69.5 all-gather.6
  83.1 54.5 all-gather.8
  140.8 7.8 all-gather.12
  190.0 10.2 all-gather.10
  218.2 21.2 all-reduce.7
  241.7 84.2 reduce-scatter.9
  328.2 74.0 reduce-scatter.7
  404.5 77.7 reduce-scatter.5
where the time goes:
time: 493 us; the launch traced here: 491 us
  waiting for transfers between devices  279 us (57%)
  matrix products  49.4 us (10%)
  blocking collectives  48.2 us (10%)
  local copies, waits for them, and re-layouts  43.1 us (9%)
  other arithmetic  31.3 us (6%)
  starting transfers between devices  24 us (5%)
  between operations  15.8 us (3%)
    reduce_scatter x1, waiting for transfers between devices, per_device(): lax.psum_scatter(proj_sum, 'frame', scatter_dimension=0, tiled=True)  78.7 us
    reduce_scatter x1, waiting for transfers between devices, per_device(): lax.psum_scatter(step_sum, 'frame', scatter_dimension=0, tiled=True)  74.5 us
    unnamed x9, waiting for transfers between devices  51.6 us
    all_gather x1, waiting for transfers between devices, per_device(): lax.all_gather(proj_weight, 'frame', axis=0, tiled=True)  42.8 us
    all_gather x1, blocking collectives, per_device(): lax.all_gather(step_weight, 'frame', axis=0, tiled=True)  42 us
    dot_general x6, matrix products, block_parts(): jnp.einsum('shtu,suhp->sthp', weights, inputs, preferred_element_type=jnp...  17 us
    all_gather x1, waiting for transfers between devices, per_device(): mod_full = lax.all_gather(mod_weight, 'frame', axis=1, tiled=True)  12.4 us
    all_to_all x1, waiting for transfers between devices, per_device(): lax.all_to_all(time_low, 'frame', split_axis=0, concat_axis=0, tiled=True)  10.8 us
  transfers between devices with their start and end apart: 12, of which 7 were waited for; matrix products, arithmetic and copies ran while one was open for 25% of the time, Pallas kernels for 0%

commit v1 on v0

v1 whole, which is shorter than its diff:
```python
import functools
import math

import jax
import jax.numpy as jnp
from jax import lax
from jax.experimental import pallas as pl
from jax.experimental.pallas import tpu as pltpu
from jax.sharding import PartitionSpec as P

norm_eps = 1e-05
LANES = 128
f32 = jnp.float32
bf16 = jnp.bfloat16
EXACT = lax.Precision.HIGHEST


def time_embed(timestep, embed_dim):
    half_dim = embed_dim // 2
    frequency = jnp.exp(-math.log(10000.0) * jnp.arange(half_dim, dtype=f32) / half_dim)
    angles = timestep.astype(f32)[:, None] * frequency[None, :]
    return jax.nn.silu(jnp.concatenate([jnp.cos(angles), jnp.sin(angles)], axis=1))


def to_tiles(a):
    f, r, c = a.shape
    if r % 8 == 0 and c % LANES == 0:
        a = a.reshape(f, r // 8, 8, c // LANES, LANES).transpose(0, 1, 3, 2, 4)
    return a.reshape(f, r * c // LANES, LANES)


def from_tiles(a, r, c):
    f = a.shape[0]
    if r % 8 == 0 and c % LANES == 0:
        a = a.reshape(f, r // 8, c // LANES, 8, LANES).transpose(0, 1, 3, 2, 4)
    return a.reshape(f, r, c)


def exchange(packed):
    return lax.all_to_all(packed, "frame", split_axis=0, concat_axis=0, tiled=True)


def mm(a, b, ca, cb):
    return lax.dot_general(a, b, (((ca,), (cb,)), ((), ())), preferred_element_type=f32)


def exact(a, b, ca, cb):
    return lax.dot_general(
        a, b, (((ca,), (cb,)), ((), ())), preferred_element_type=f32, precision=EXACT
    )


def split(a):
    high = a.astype(bf16)
    return high, (a - high.astype(f32)).astype(bf16)


def head_map(heads, width):
    size = width // heads
    own = lax.broadcasted_iota(jnp.int32, (heads, width), 0)
    lane = lax.broadcasted_iota(jnp.int32, (heads, width), 1)
    return jnp.where(lane // size == own, 1.0, 0.0).astype(bf16)


def sequence_mask(length, sites):
    later = lax.broadcasted_iota(jnp.int32, (length, length), 0)
    earlier = lax.broadcasted_iota(jnp.int32, (length, length), 1)
    keep = later >= earlier
    if sites > 1:
        keep = keep & (later % sites == earlier % sites)
    return jnp.where(keep, 1.0, 0.0).astype(f32)


def blocks(width):
    return [(j, slice(j * LANES, (j + 1) * LANES)) for j in range(width // LANES)]


def spread_rows(rows, length):
    count = rows.shape[0]
    if count == 1:
        return rows
    part = (length // count, rows.shape[1])
    return jnp.concatenate([jnp.broadcast_to(rows[c : c + 1], part) for c in range(count)], axis=0)


def normalize_into(tok_ref, shift_ref, gain_ref, x_ref):
    length, width = tok_ref.shape
    total = jnp.zeros((length, LANES), f32)
    for _, sl in blocks(width):
        v = tok_ref[:, sl].astype(f32)
        total = total + v * v
    mean = jnp.sum(total, axis=1, keepdims=True) / width
    inverse = lax.rsqrt(mean + norm_eps)
    for _, sl in blocks(width):
        unit = tok_ref[:, sl].astype(f32) * inverse
        gain = spread_rows(gain_ref[:, sl], length)
        shift = spread_rows(shift_ref[:, sl], length)
        x_ref[:, sl] = (unit * (1.0 + gain) + shift).astype(bf16)
    return inverse


def steps_of(logits, bias, rate, mask):
    z = logits.astype(f32) + bias
    step = jnp.maximum(z, 0.0) + jnp.log1p(jnp.exp(-jnp.abs(z)))
    log_decay = -step * rate
    cum = exact(mask, log_decay, 1, 0)
    cum_rows = exact(log_decay, mask, 0, 1)
    return z, step, cum, cum_rows


def expand(parts, lanes_of):
    return mm(parts[0], lanes_of, 1, 0) + mm(parts[1], lanes_of, 1, 0)


def scan_block(j, x, grad, step_wide, scores, cum, cum_rows, heads, width, d_scores):
    size = width // heads
    per_block = LANES // size
    stepped = (x.astype(f32) * step_wide).astype(bf16)
    lane = lax.broadcasted_iota(jnp.int32, x.shape, 1)
    weights, steppeds, grads = [], [], []
    for i in range(per_block):
        h = j * per_block + i
        decay = jnp.exp(jnp.minimum(cum[:, h : h + 1] - cum_rows[h : h + 1, :], 0.0))
        inside = lane // size == i
        own_grad = jnp.where(inside, grad, jnp.zeros_like(grad))
        d_weight = mm(own_grad, stepped, 1, 1)
        d_scores = d_scores + d_weight * decay
        weights.append((scores * decay).astype(bf16))
        steppeds.append(jnp.where(inside, stepped, jnp.zeros_like(stepped)))
        grads.append(own_grad)
    out = mm(jnp.concatenate(weights, axis=1), jnp.concatenate(steppeds, axis=0), 1, 0)
    d_stepped = mm(jnp.concatenate(weights, axis=0), jnp.concatenate(grads, axis=0), 0, 0)
    return stepped, out, d_stepped, d_scores


def head_sums(high_ref, low_ref, lanes_of):
    return mm(high_ref[...], lanes_of, 1, 1) + mm(low_ref[...], lanes_of, 1, 1)


def put(refs, sl, value):
    high, low = split(value)
    refs[0][:, sl] = high
    refs[1][:, sl] = low


def site_kernel(
    sites,
    tok_ref,
    grad_ref,
    shift_ref,
    gain_ref,
    proj_ref,
    step_ref,
    bias_ref,
    rate_ref,
    out_ref,
    back_ref,
    gproj_ref,
    gstep_ref,
    gmod_ref,
    x_ref,
    dn_ref,
    a_hi,
    a_lo,
    b_hi,
    b_lo,
):
    length, width = tok_ref.shape
    heads = step_ref.shape[0]
    state = proj_ref.shape[1] // 2
    clips = shift_ref.shape[0]
    inverse = normalize_into(tok_ref, shift_ref, gain_ref, x_ref)
    lanes_of = head_map(heads, width)
    mask = sequence_mask(length, sites)
    coeffs = mm(x_ref[...], proj_ref[...], 1, 0).astype(bf16)
    logits = mm(x_ref[...], step_ref[...], 1, 1).astype(bf16)
    rate = rate_ref[...]
    z, step, cum, cum_rows = steps_of(logits, bias_ref[...], rate, mask)
    b_part, c_part = coeffs[:, :state], coeffs[:, state:]
    scores = mm(c_part, b_part, 1, 1) * (mask / state)
    step_parts = split(step)
    d_scores = jnp.zeros((length, length), f32)
    for j, sl in blocks(width):
        x, grad = x_ref[:, sl], grad_ref[:, sl]
        step_wide = expand(step_parts, lanes_of[:, sl])
        stepped, out, d_stepped, d_scores = scan_block(
            j, x, grad, step_wide, scores, cum, cum_rows, heads, width, d_scores
        )
        out_ref[:, sl] = out.astype(bf16)
        dn_ref[:, sl] = (step_wide * d_stepped).astype(bf16)
        put((a_hi, a_lo), sl, grad.astype(f32) * out - stepped.astype(f32) * d_stepped)
        put((b_hi, b_lo), sl, x.astype(f32) * d_stepped)
    d_cum = head_sums(a_hi, a_lo, lanes_of)
    d_step = head_sums(b_hi, b_lo, lanes_of)
    d_log = exact(mask, d_cum, 0, 0)
    d_logits = (jax.nn.sigmoid(z) * (d_step - rate * d_log)).astype(bf16)
    d_scores = (d_scores * (mask / state)).astype(bf16)
    d_coeffs = jnp.concatenate(
        [mm(d_scores, c_part, 0, 0), mm(d_scores, b_part, 1, 0)], axis=1
    ).astype(bf16)
    for _, sl in blocks(width):
        back = (
            dn_ref[:, sl].astype(f32)
            + mm(d_coeffs, proj_ref[sl, :], 1, 1)
            + mm(d_logits, step_ref[:, sl], 1, 0)
        ).astype(bf16)
        back_ref[:, sl] = back
        back = back.astype(f32)
        scaled = back * (tok_ref[:, sl].astype(f32) * inverse)
        for c in range(clips):
            rows = slice(c * (length // clips), (c + 1) * (length // clips))
            gmod_ref[c : c + 1, sl] = jnp.sum(back[rows], axis=0, keepdims=True)
            gmod_ref[clips + c : clips + c + 1, sl] = jnp.sum(scaled[rows], axis=0, keepdims=True)
        gproj_ref[sl, :] = mm(x_ref[:, sl], d_coeffs, 0, 0)
        gstep_ref[:, sl] = mm(d_logits, x_ref[:, sl], 0, 0)


def band_kernel(
    tok_ref,
    grad_ref,
    shift_ref,
    gain_ref,
    proj_ref,
    step_ref,
    bias_ref,
    rate_ref,
    x_ref,
    coeffs_ref,
    logits_ref,
    inverse_ref,
    decay_ref,
    end_ref,
    own_ref,
):
    length, width = tok_ref.shape
    heads = step_ref.shape[0]
    state = proj_ref.shape[1] // 2
    inverse_ref[...] = normalize_into(tok_ref, shift_ref, gain_ref, x_ref)
    lanes_of = head_map(heads, width)
    mask = sequence_mask(length, 1)
    coeffs = mm(x_ref[...], proj_ref[...], 1, 0).astype(bf16)
    logits = mm(x_ref[...], step_ref[...], 1, 1).astype(bf16)
    coeffs_ref[...] = coeffs
    logits_ref[...] = logits
    _, step, cum, _ = steps_of(logits, bias_ref[...], rate_ref[...], mask)
    last = cum[length - 1 : length, :]
    decay_ref[...] = jnp.exp(last)
    lead = split(jnp.exp(last - cum) * step)
    reach = split(jnp.exp(cum) / state)
    b_part, c_part = coeffs[:, :state], coeffs[:, state:]
    for _, sl in blocks(width):
        lead_wide = expand(lead, lanes_of[:, sl])
        reach_wide = expand(reach, lanes_of[:, sl])
        scaled = (x_ref[:, sl].astype(f32) * lead_wide).astype(bf16)
        faded = (grad_ref[:, sl].astype(f32) * reach_wide).astype(bf16)
        end_ref[sl, :] = mm(scaled, b_part, 0, 0).astype(bf16)
        own_ref[sl, :] = mm(faded, c_part, 0, 0).astype(bf16)


def space_kernel(
    tok_ref,
    grad_ref,
    x_ref,
    coeffs_ref,
    logits_ref,
    inverse_ref,
    proj_ref,
    step_ref,
    bias_ref,
    rate_ref,
    skip_ref,
    state_ref,
    later_ref,
    gproj_in,
    gstep_in,
    mix_ref,
    pre_ref,
    gproj_ref,
    gstep_ref,
    gmod_ref,
    dn_ref,
    a_hi,
    a_lo,
    b_hi,
    b_lo,
    c_hi,
    c_lo,
):
    length, width = tok_ref.shape
    heads = step_ref.shape[0]
    state = proj_ref.shape[1] // 2
    lanes_of = head_map(heads, width)
    mask = sequence_mask(length, 1)
    coeffs = coeffs_ref[...]
    rate = rate_ref[...]
    z, step, cum, cum_rows = steps_of(logits_ref[...], bias_ref[...], rate, mask)
    last = cum[length - 1 : length, :]
    rest = jnp.exp(last - cum)
    lead = rest * step
    b_part, c_part = coeffs[:, :state], coeffs[:, state:]
    scores = mm(c_part, b_part, 1, 1) * (mask / state)
    step_parts, lead_parts, reach_parts = split(step), split(lead), split(jnp.exp(cum) / state)
    d_scores = jnp.zeros((length, length), f32)
    d_b = jnp.zeros((length, state), f32)
    d_c = jnp.zeros((length, state), f32)
    d_end = jnp.zeros((heads, state), f32)
    for j, sl in blocks(width):
        x, grad = x_ref[:, sl], grad_ref[:, sl]
        wide_map = lanes_of[:, sl]
        step_wide = expand(step_parts, wide_map)
        lead_wide = expand(lead_parts, wide_map)
        reach_wide = expand(reach_parts, wide_map)
        stepped, out, d_stepped, d_scores = scan_block(
            j, x, grad, step_wide, scores, cum, cum_rows, heads, width, d_scores
        )
        x, wide = x.astype(f32), grad.astype(f32)
        before, later = state_ref[sl, :], later_ref[sl, :]
        carried = mm(c_part, before, 1, 1) * reach_wide
        d_c = d_c + mm((wide * reach_wide).astype(bf16), before, 1, 0)
        d_b = d_b + mm((x * lead_wide).astype(bf16), later, 1, 0)
        d_scaled = mm(b_part, later, 1, 1)
        both = split(before.astype(f32) * later.astype(f32))
        d_end = d_end + mm(wide_map, both[0], 1, 0) + mm(wide_map, both[1], 1, 0)
        total = out + carried
        skip = skip_ref[:, sl]
        mix_ref[:, sl] = total + skip * x
        d_x = (step_wide * d_stepped + d_scaled * lead_wide).astype(bf16)
        dn_ref[:, sl] = d_x + (wide * skip).astype(bf16)
        put((a_hi, a_lo), sl, wide * total - stepped.astype(f32) * d_stepped)
        put((b_hi, b_lo), sl, x * d_stepped)
        put((c_hi, c_lo), sl, x * d_scaled)
    d_lead = head_sums(c_hi, c_lo, lanes_of)
    d_step = head_sums(b_hi, b_lo, lanes_of) + d_lead * rest
    fall = d_lead * lead
    d_cum = head_sums(a_hi, a_lo, lanes_of) - fall
    ones = jnp.ones((8, state), f32)
    end_sum = exact(ones, d_end, 1, 1)[0:1, :] * jnp.exp(last)
    end_sum = end_sum + jnp.sum(fall, axis=0, keepdims=True)
    d_log = exact(mask, d_cum, 0, 0) + end_sum
    d_logits = (jax.nn.sigmoid(z) * (d_step - rate * d_log)).astype(bf16)
    d_scores = (d_scores * (mask / state)).astype(bf16)
    d_coeffs = jnp.concatenate(
        [mm(d_scores, c_part, 0, 0) + d_b, mm(d_scores, b_part, 1, 0) + d_c], axis=1
    ).astype(bf16)
    inverse = inverse_ref[...]
    for _, sl in blocks(width):
        pre = (
            dn_ref[:, sl].astype(f32)
            + mm(d_coeffs, proj_ref[sl, :], 1, 1)
            + mm(d_logits, step_ref[:, sl], 1, 0)
        )
        pre_ref[:, sl] = pre
        scaled = pre * (tok_ref[:, sl].astype(f32) * inverse)
        gmod_ref[0:1, sl] = jnp.sum(pre, axis=0, keepdims=True)
        gmod_ref[1:2, sl] = jnp.sum(scaled, axis=0, keepdims=True)
        gproj_ref[sl, :] = (gproj_in[sl, :] + mm(x_ref[:, sl], d_coeffs, 0, 0)).astype(bf16)
        gstep_ref[:, sl] = (gstep_in[:, sl] + mm(d_logits, x_ref[:, sl], 0, 0)).astype(bf16)


def last_kernel(tok_ref, inverse_ref, gain_ref, mix_ref, pre_ref, time_ref, back_ref, out_ref, dtok_ref):
    length, width = tok_ref.shape
    inverse = inverse_ref[...]
    total = jnp.zeros((length, LANES), f32)
    for _, sl in blocks(width):
        out_ref[:, sl] = (mix_ref[:, sl] + time_ref[:, sl].astype(f32)).astype(bf16)
        grad = (pre_ref[:, sl] + back_ref[:, sl].astype(f32)) * (1.0 + gain_ref[:, sl])
        total = total + grad * tok_ref[:, sl].astype(f32)
    inner = jnp.sum(total, axis=1, keepdims=True) / width
    inner = inner * inverse * inverse * inverse
    for _, sl in blocks(width):
        grad = (pre_ref[:, sl] + back_ref[:, sl].astype(f32)) * (1.0 + gain_ref[:, sl])
        dtok_ref[:, sl] = (grad * inverse - tok_ref[:, sl].astype(f32) * inner).astype(bf16)


def call(kernel, outs, scratch=(), name=None):
    shapes = [jax.ShapeDtypeStruct(s, d) for s, d in outs]
    return pl.pallas_call(
        kernel,
        out_shape=shapes,
        scratch_shapes=[pltpu.VMEM(s, d) for s, d in scratch],
        compiler_params=pltpu.CompilerParams(vmem_limit_bytes=48 << 20),
        name=name,
    )


def rows_in_order(part):
    if lax.axis_size("row") != 2:
        return lax.all_gather(part, "row")
    other = lax.ppermute(part, "row", [(0, 1), (1, 0)])
    first = lax.axis_index("row") == 0
    return jnp.stack([jnp.where(first, part, other), jnp.where(first, other, part)])


def rows_sum(part):
    if lax.axis_size("row") != 2:
        return lax.psum(part, "row")
    return part + lax.ppermute(part, "row", [(0, 1), (1, 0)])


def chain(own, decay, forward):
    count = lax.axis_size("row")
    hops = [(i, i + 1) if forward else (i + 1, i) for i in range(count - 1)]
    if count == 1:
        return jnp.zeros_like(own)
    arrived = lax.ppermute(own, "row", hops)
    wide = jnp.repeat(decay[0], own.shape[0] // decay.shape[1])[:, None]
    for _ in range(count - 2):
        passed = wide * arrived.astype(f32) + own.astype(f32)
        arrived = lax.ppermute(passed.astype(bf16), "row", hops)
    return arrived


def per_device(
    tokens,
    cotangent,
    timestep,
    mod_weight,
    proj_weight,
    step_weight,
    step_bias,
    rate_space,
    rate_time,
    skip_gain,
):
    frames = lax.axis_size("frame")
    rows = lax.axis_size("row")
    frame_id = lax.axis_index("frame")
    row_id = lax.axis_index("row")
    width = tokens.shape[-1]
    length = tokens.shape[1] * tokens.shape[2]
    clips = timestep.shape[0]
    clip_id = frame_id // (frames // clips)
    sites = length // frames
    heads = rate_space.shape[0]
    depth, pair = proj_weight.shape
    state = pair // 2
    mod_cols = mod_weight.shape[1]
    factor = (frames * rows * length) ** (-0.5)
    tok = tokens.reshape(length, width)
    grad = cotangent.reshape(length, width)

    activated = time_embed(timestep, mod_weight.shape[0]).astype(bf16)
    own_mod = jnp.dot(activated, mod_weight, preferred_element_type=f32)
    high = lax.reduce_precision(own_mod, 8, 7)
    own_mod = jnp.stack([high, own_mod - high]).astype(bf16)

    part = depth // rows
    own_proj = lax.dynamic_slice_in_dim(proj_weight, row_id * part, part, 0)
    to_all = [
        to_tiles(own_proj[None]),
        to_tiles(step_weight.T[None]),
        own_mod.reshape(1, -1, LANES),
    ]
    to_all = jnp.concatenate(to_all, axis=1)
    to_all = jnp.pad(to_all, ((0, 0), (0, -to_all.shape[1] % 8), (0, 0)))
    count = sites * width // LANES
    got = exchange(
        jnp.concatenate(
            [
                to_tiles(tok.reshape(frames, sites, width)),
                to_tiles(grad.reshape(frames, sites, width)),
                jnp.broadcast_to(to_all, (frames,) + to_all.shape[1:]),
            ],
            axis=1,
        )
    )
    site_tok = from_tiles(got[:, :count], sites, width).reshape(length, width)
    site_grad = from_tiles(got[:, count : 2 * count], sites, width).reshape(length, width)
    at = 2 * count
    size = part * pair // LANES
    proj_full = rows_in_order(got[:, at : at + size])
    proj_full = from_tiles(proj_full.reshape(rows * frames, size, LANES), part, pair)
    proj_full = proj_full.reshape(rows, frames, part, pair).transpose(1, 0, 2, 3)
    proj_full = proj_full.reshape(width, pair)
    at += size
    size = heads * depth // LANES
    step_full = from_tiles(got[:, at : at + size], heads, depth)
    step_full = step_full.transpose(1, 0, 2).reshape(heads, width)
    at += size
    size = 2 * clips * mod_cols // LANES
    mod_full = got[:, at : at + size].reshape(frames, 2, clips, mod_cols).astype(f32)
    mod_full = (mod_full[:, 0] + mod_full[:, 1]).transpose(1, 0, 2).reshape(clips, 2 * width)
    shift, gain = mod_full[:, :width], mod_full[:, width:]

    bias = step_bias[None]
    wide = (length, width)
    site_out, site_back, gproj, gstep, site_gmod = call(
        functools.partial(site_kernel, sites),
        [(wide, bf16), (wide, bf16), ((width, pair), f32), ((heads, width), f32), ((2 * clips, width), f32)],
        [(wide, bf16)] * 6,
        name="site",
    )(site_tok, site_grad, shift, gain, proj_full, step_full, bias, rate_time[None])

    came = exchange(
        jnp.concatenate(
            [
                to_tiles(site_out.reshape(frames, sites, width)),
                to_tiles(site_back.reshape(frames, sites, width)),
            ],
            axis=1,
        )
    )
    time_out = from_tiles(came[:, :count], sites, width).reshape(length, width)
    time_back = from_tiles(came[:, count:], sites, width).reshape(length, width)

    own_shift = lax.dynamic_slice_in_dim(shift, clip_id, 1, 0)
    own_gain = lax.dynamic_slice_in_dim(gain, clip_id, 1, 0)
    normed, coeffs, logits, inverse, decay, end_own, start_grad = call(
        band_kernel,
        [
            (wide, bf16),
            ((length, pair), bf16),
            ((length, heads), bf16),
            ((length, 1), f32),
            ((1, heads), f32),
            ((width, state), bf16),
            ((width, state), bf16),
        ],
        name="band",
    )(tok, grad, own_shift, own_gain, proj_full, step_full, bias, rate_space[None])
    state_in = chain(end_own, decay, True)
    later_grad = chain(start_grad, decay, False)
    skip = jnp.repeat(skip_gain, width // heads)[None]
    mix, pre, gproj, gstep, gmod = call(
        space_kernel,
        [(wide, f32), (wide, f32), ((width, pair), bf16), ((heads, width), bf16), ((2, width), f32)],
        [(wide, bf16)] * 7,
        name="space",
    )(
        tok,
        grad,
        normed,
        coeffs,
        logits,
        inverse,
        proj_full,
        step_full,
        bias,
        rate_space[None],
        skip,
        state_in,
        later_grad,
        gproj,
        gstep,
    )

    picked = (jnp.arange(clips) == clip_id).astype(f32)[:, None]
    gmod = jnp.concatenate(
        [site_gmod[:clips] + picked * gmod[0:1], site_gmod[clips:] + picked * gmod[1:2]], axis=1
    )
    gmod = gmod.reshape(clips, frames, mod_cols).transpose(1, 0, 2).astype(bf16)
    sent = jnp.concatenate(
        [
            to_tiles(gproj.reshape(frames, depth, pair)),
            to_tiles(gstep.reshape(heads, frames, depth).transpose(1, 0, 2)),
            gmod.reshape(frames, -1, LANES) if (clips * mod_cols) % LANES == 0 else gmod,
        ],
        axis=1,
    )
    size = sent.shape[1]
    sent = jnp.pad(sent, ((0, 0), (0, -size % 8), (0, 0)))
    sums = jnp.sum(exchange(sent).astype(f32), axis=0, keepdims=True)
    sums = rows_sum(sums) * factor
    at = depth * pair // LANES
    grad_proj = from_tiles(sums[:, :at], depth, pair)[0]
    size = heads * depth // LANES
    grad_step = from_tiles(sums[:, at : at + size], heads, depth)[0].T
    at += size
    size = clips * mod_cols // LANES
    mod_sum = sums[0, at : at + size].reshape(clips, mod_cols)
    grad_mod = jnp.dot(activated.astype(f32).T, mod_sum, precision=EXACT)

    mixed, d_tokens = call(last_kernel, [(wide, bf16), (wide, bf16)], name="last")(
        tok, inverse, own_gain, mix, pre, time_out, time_back
    )
    return (mixed.reshape(tokens.shape), d_tokens.reshape(tokens.shape), grad_proj, grad_step, grad_mod)


def solution(mesh):
    placed = (
        P("frame", "row", None, None),
        P("frame", "row", None, None),
        P(),
        P(None, "frame"),
        P("frame", None),
        P("frame", None),
        P(),
        P(),
        P(),
        P(),
    )
    return jax.shard_map(
        per_device,
        mesh=mesh,
        in_specs=placed,
        out_specs=(
            P("frame", "row", None, None),
            P("frame", "row", None, None),
            P("frame", None),
            P("frame", None),
            P(None, "frame"),
        ),
        check_vma=False,
    )
```

time: 493 us -> 171 us (0.35)
  waiting for transfers between devices: 279 us -> 85.8 us
  matrix products: 49.4 us -> 0.13 us
  blocking collectives: 48.2 us -> 0 us
  local copies, waits for them, and re-layouts: 43.1 us -> 13.5 us
  Pallas kernels: 0 us -> 24.8 us
  other arithmetic: 31.3 us -> 14.3 us
  between operations: 15.8 us -> 1.67 us
  starting transfers between devices: 24 us -> 29.5 us
    reduce_scatter x2 -> x0, waiting for transfers between devices: 153 us -> none  [the longest x1 78.7 us: per_device(): lax.psum_scatter(proj_sum, 'frame', scatter_dimension=0, tiled=True)]
    all_to_all x4 -> x3, waiting for transfers between devices: 10.8 us -> 84.9 us  [exchange(): lax.all_to_all(packed, 'frame', split_axis=0, concat_axis=0, tiled=True)]
    all_gather x4 -> x0, waiting for transfers between devices: 55.2 us -> none  [the longest x1 42.8 us: per_device(): lax.all_gather(proj_weight, 'frame', axis=0, tiled=True)]
    unnamed x9 -> x0, waiting for transfers between devices: 51.6 us -> none
    dot_general x31 -> x1, matrix products: 49.4 us -> 0.13 us  [per_device(): own_mod = jnp.dot(activated, mod_weight, preferred_element_type=f32)]
    all_gather x2 -> x0, blocking collectives: 44.1 us -> none  [the longest x1 42 us: per_device(): lax.all_gather(step_weight, 'frame', axis=0, tiled=True)]
    pallas_call x0 -> x4, Pallas kernels: none -> 24.8 us  [the longest x1 11.1 us: per_device(): call(space_kernel, [(wide, f32), (wide, f32), ((width, pair), bf16), ((he...]
    convert_element_type x8 -> x1, other arithmetic: 10.5 us -> 0.01 us  [per_device(): got[:, at:at + size].reshape(frames, 2, clips, mod_cols).astype(f32)]
  transfers between devices with their start and end apart: 12 -> 7, of which waited for: 7 -> 4; matrix products, arithmetic and copies ran while one was open for 25% -> 4% of each run, Pallas kernels for 0% -> 5%
where the time goes in v1:
time: 171 us; the launch traced here: 170 us
  waiting for transfers between devices  85.8 us (50%)
  starting transfers between devices  29.5 us (17%)
  Pallas kernels  24.8 us (15%)
  other arithmetic  14.3 us (8%)
  local copies, waits for them, and re-layouts  13.5 us (8%)
    all_to_all x3, waiting for transfers between devices, exchange(): lax.all_to_all(packed, 'frame', split_axis=0, concat_axis=0, tiled=True)  84.9 us
    all_to_all x3, starting transfers between devices, exchange(): lax.all_to_all(packed, 'frame', split_axis=0, concat_axis=0, tiled=True)  25.1 us
    pallas_call x1, Pallas kernels, per_device(): call(space_kernel, [(wide, f32), (wide, f32), ((width, pair), bf16), ((he...  11.1 us
    unnamed x47, local copies, waits for them, and re-layouts  8.33 us
    pallas_call x1, Pallas kernels, per_device(): call(functools.partial(site_kernel, sites), [(wide, bf16), (wide, bf16),...  6.62 us
    pallas_call x1, Pallas kernels, per_device(): call(band_kernel, [(wide, bf16), ((length, pair), bf16), ((length, heads)...  5.37 us
    ppermute x2, starting transfers between devices, chain(): arrived = lax.ppermute(own, 'row', hops)  4.29 us
  transfers between devices with their start and end apart: 7, of which 4 were waited for; matrix products, arithmetic and copies ran while one was open for 4% of the time, Pallas kernels for 5%

profile of v1, /device:TPU:0, one launch (start us, length us, event | category | flops | bytes accessed | tf_op | source)
XLA Modules:
  0.0 169.6 jit_solution(16957555975503135351)
XLA Ops:
  3.8 2.6 %pad_maximum_fusion = bf16[16,424,128]{2,1,0:T(8,128)(2,1)} fusion(bf16[16,168,128]{2,1,0:T(8,128)(2,1)S(1)} %broadcast_in_dim.31, bf16[16,128,128]{2,1,0:T(8,128)(2,1)} %bitcast.116, bf16[16,128,128]{2,1,0:T(8,128)(2,1)} %bitcast.112), kind=kLoop, calls=%fused_computation.5 | loop fusion | flops 5210112 | bytes 3473408 | tf_op jit(solution)/shard_map/concatenate | solution.py:458
  6.3 8.3 %all-to-all-start = ((bf16[16,424,128]{2,1,0:T(8,128)(2,1)}), bf16[16,424,128]{2,1,0:T(8,128)(2,1)S(1)}, u32[]{:S(2)}, u32[]{:S(2)}) async-start(bf16[16,424,128]{2,1,0:T(8,128)(2,1)} %pad_maximum_fusion), calls=%async_computation | async-start | bytes 3473408 | tf_op jit(solution)/shard_map/all_to_all | solution.py:40
  14.7 36.9 %all-to-all-done = bf16[16,424,128]{2,1,0:T(8,128)(2,1)S(1)} async-done(((bf16[16,424,128]{2,1,0:T(8,128)(2,1)}), bf16[16,424,128]{2,1,0:T(8,128)(2,1)S(1)}, u32[]{:S(2)}, u32[]{:S(2)}) %all-to-all-start) | async-done | bytes 1736736 | tf_op jit(solution)/shard_map/all_to_all | solution.py:40
  51.8 1.0 copy-done.21
  52.8 0.9 collective-permute-done
  53.7 1.5 select_bitcast_fusion.1
  56.6 5.4 %band.1 = (bf16[128,2048]{1,0:T(8,128)(2,1)S(1)}, bf16[128,256]{1,0:T(8,128)(2,1)S(1)}, bf16[128,32]{1,0:T(8,128)(2,1)S(1)}, f32[128,1]{1,0:T(8,128)S(1)}, f32[1...) custom-call(bf16[128,2048]{1,0:T(8,128)(2,1)S(1)} %bitcast.113, bf16[128,2048]{1,0:T(8,128)(2,1)S(1)} %bitcast.117, ...), custom_call_target="tpu_custom_call" | custom-call | tf_op jit(solution)/shard_map/band/pallas_call | solution.py:508
  63.3 2.8 %collective-permute-start.1 = (bf16[2048,128]{1,0:T(8,128)(2,1)}, bf16[2048,128]{1,0:T(8,128)(2,1)}, u32[]{:S(2)}, u32[]{:S(2)}) collective-permute-start(bf16[2048,128]{1,0:T(8,128)(2,1)} %get-tuple-element.27), channel_id=1, source_target_pairs={{0,1},{2,3},{4,5},{6,7},{8,9},{10,11},{12,13},{14,15},{16,17},{18,... | collective-permute-start | bytes 1572872 | tf_op jit(solution)/shard_map/ppermute | solution.py:405
  66.2 1.5 collective-permute-start.2
  67.7 1.3 broadcast_in_dim.34
  69.0 1.4 broadcast_in_dim_reshape.3.skip_ref
  71.8 6.6 %site.1 = (bf16[128,2048]{1,0:T(8,128)(2,1)S(1)}, bf16[128,2048]{1,0:T(8,128)(2,1)S(1)}, f32[2048,256]{1,0:T(8,128)S(1)}, f32[32,2048]{1,0:T(8,128)S(1)}, f32[2,2048]{1,0:T(2,128)S(1)}) custom-call(bf16[128,2048]{1,0:T(8,128)(2,1)S(1)} %get-tuple-element.46.tok_ref, bf16[128,2048]{1,0:T(8,128)(2,1)S(1)} %get-tuple-element.45.grad_ref, ...), custom_call_target="tpu_custom_call" | custom-call | tf_op jit(solution)/shard_map/site/pallas_call | solution.py:487
  78.4 1.3 copy-done.4
  80.6 11.1 %space.1 = (f32[128,2048]{1,0:T(8,128)S(1)}, f32[128,2048]{1,0:T(8,128)S(1)}, bf16[2048,256]{1,0:T(8,128)(2,1)}, bf16[32,2048]{1,0:T(8,128)(2,1)S(1)}, f32[2,2048]{1,0:T(2,128)S(1)}) custom-call(bf16[128,2048]{1,0:T(8,128)(2,1)S(1)} %bitcast.114, bf16[128,2048]{1,0:T(8,128)(2,1)S(1)} %bitcast.118, bf16[128,2048]{1,0:T(8,128)(2,1)S(1)} %copy-done.11, ...), custom_call_target="tpu_custom_call" | custom-call | tf_op jit(solution)/shard_map/space/pallas_call | solution.py:524
  91.9 2.6 %fusion.4 = bf16[16,296,128]{2,1,0:T(8,128)(2,1)} fusion(bf16[16,2,128]{2,1,0:T(2,128)(2,1)S(1)} %bitcast.134, bf16[16,32,128]{2,1,0:T(8,128)(2,1)S(1)} %copy.22, bf16[16,256,128]{2,1,0:T(8,128)(2,1)} %bitcast.129), kind=kLoop, calls=%fused_computation.7 | loop fusion | flops 6062080 | bytes 2400256 | tf_op jit(solution)/shard_map/concatenate | solution.py:552
  94.5 8.7 %all-to-all-start.2 = ((bf16[16,296,128]{2,1,0:T(8,128)(2,1)}), bf16[16,296,128]{2,1,0:T(8,128)(2,1)}, u32[]{:S(2)}, u32[]{:S(2)}) async-start(bf16[16,296,128]{2,1,0:T(8,128)(2,1)} %fusion.4), calls=%async_computation.2 | async-start | bytes 2424832 | tf_op jit(solution)/shard_map/all_to_all | solution.py:40
  103.2 2.1 %pad_maximum_fusion.2 = bf16[16,256,128]{2,1,0:T(8,128)(2,1)} fusion(bf16[16,128,128]{2,1,0:T(8,128)(2,1)} %bitcast.120, bf16[16,128,128]{2,1,0:T(8,128)(2,1)S(1)} %bitcast.119), kind=kLoop, calls=%fused_computation.9 | loop fusion | flops 2097152 | bytes 2097152 | tf_op jit(solution)/shard_map/concatenate | solution.py:495
  105.3 25.5 %all-to-all-done.2 = bf16[16,296,128]{2,1,0:T(8,128)(2,1)} async-done(((bf16[16,296,128]{2,1,0:T(8,128)(2,1)}), bf16[16,296,128]{2,1,0:T(8,128)(2,1)}, u32[]{:S(2)}, u32[]{:S(2)}) %all-to-all-start.2) | async-done | bytes 1212448 | tf_op jit(solution)/shard_map/all_to_all | solution.py:40
  130.8 8.1 %all-to-all-start.1 = ((bf16[16,256,128]{2,1,0:T(8,128)(2,1)}), bf16[16,256,128]{2,1,0:T(8,128)(2,1)S(1)}, u32[]{:S(2)}, u32[]{:S(2)}) async-start(bf16[16,256,128]{2,1,0:T(8,128)(2,1)} %pad_maximum_fusion.2), calls=%async_computation.1 | async-start | bytes 2097152 | tf_op jit(solution)/shard_map/all_to_all | solution.py:40
  138.9 2.1 %convert_reduce_fusion = f32[296,128]{1,0:T(8,128)} fusion(bf16[16,296,128]{2,1,0:T(8,128)(2,1)} %all-to-all-done.2), kind=kLoop, calls=%fused_computation.4 | loop fusion | flops 1174528 | bytes 1363968 | tf_op jit(solution)/shard_map/reduce_sum | solution.py:562
  141.0 22.5 %all-to-all-done.1 = bf16[16,256,128]{2,1,0:T(8,128)(2,1)S(1)} async-done(((bf16[16,256,128]{2,1,0:T(8,128)(2,1)}), bf16[16,256,128]{2,1,0:T(8,128)(2,1)S(1)}, u32[]{:S(2)}, u32[]{:S(2)}) %all-to-all-start.1) | async-done | bytes 1048608 | tf_op jit(solution)/shard_map/all_to_all | solution.py:40
  163.7 1.2 copy-done.6
  164.9 1.7 last.1
  166.5 1.0 add_multiply_fusion
  (77 shorter events, 9.9 us)
Async XLA Ops:
  0.6 1.4 copy-start
  6.3 45.2 %all-to-all-start = ((bf16[16,424,128]{2,1,0:T(8,128)(2,1)}), bf16[16,424,128]{2,1,0:T(8,128)(2,1)S(1)}, u32[]{:S(2)}, u32[]{:S(2)}) async-start(bf16[16,424,128]{2,1,0:T(8,128)(2,1)} %pad_maximum_fusion), calls=%async_computation | async-start | bytes 3473408 | tf_op jit(solution)/shard_map/all_to_all | solution.py:40
  51.5 1.2 copy-start.21
  51.7 2.0 %collective-permute-start = (bf16[16,128,128]{2,1,0:T(8,128)(2,1)S(1)}, bf16[16,128,128]{2,1,0:T(8,128)(2,1)S(1)}, u32[]{:S(2)}, u32[]{:S(2)}) collective-permute-start(bf16[16,128,128]{2,1,0:T(8,128)(2,1)S(1)} %slice.77), channel_id=1, source_target_pairs={{0,1},{1,0},{2,3},{3,2},{4,5},{5,4},{6,7},{7,6},{8,9},{9,8},{10,11... | collective-permute-start | bytes 1572872 | tf_op jit(solution)/shard_map/ppermute | solution.py:389
  55.2 1.4 copy-start.3
  55.2 1.3 copy-start.15
  55.2 1.3 copy-start.18
  55.4 23.0 %copy-start.1 = (bf16[16,2,64,256]{3,2,1,0:T(8,128)(2,1)}, bf16[16,2,64,256]{3,2,1,0:T(8,128)(2,1)S(1)}, u32[]{:S(2)}) copy-start(bf16[16,2,64,256]{3,2,1,0:T(8,128)(2,1)S(1)} %copy.20) | copy-start | bytes 3145732
  63.3 17.2 %collective-permute-start.1 = (bf16[2048,128]{1,0:T(8,128)(2,1)}, bf16[2048,128]{1,0:T(8,128)(2,1)}, u32[]{:S(2)}, u32[]{:S(2)}) collective-permute-start(bf16[2048,128]{1,0:T(8,128)(2,1)} %get-tuple-element.27), channel_id=1, source_target_pairs={{0,1},{2,3},{4,5},{6,7},{8,9},{10,11},{12,13},{14,15},{16,17},{18,... | collective-permute-start | bytes 1572872 | tf_op jit(solution)/shard_map/ppermute | solution.py:405
  66.2 14.4 %collective-permute-start.2 = (bf16[2048,128]{1,0:T(8,128)(2,1)}, bf16[2048,128]{1,0:T(8,128)(2,1)}, u32[]{:S(2)}, u32[]{:S(2)}) collective-permute-start(bf16[2048,128]{1,0:T(8,128)(2,1)} %get-tuple-element.28), channel_id=1, source_target_pairs={{1,0},{3,2},{5,4},{7,6},{9,8},{11,10},{13,12},{15,14},{17,16},{19,... | collective-permute-start | bytes 1572872 | tf_op jit(solution)/shard_map/ppermute | solution.py:405
  70.4 10.2 %copy-start.11 = (bf16[128,2048]{1,0:T(8,128)(2,1)S(1)}, bf16[128,2048]{1,0:T(8,128)(2,1)}, u32[]{:S(2)}) copy-start(bf16[128,2048]{1,0:T(8,128)(2,1)} %copy-done.10) | copy-start | bytes 1572868
  70.4 10.2 %copy-start.13 = (bf16[128,32]{1,0:T(8,128)(2,1)S(1)}, bf16[128,32]{1,0:T(8,128)(2,1)}, u32[]{:S(2)}) copy-start(bf16[128,32]{1,0:T(8,128)(2,1)} %copy-done.12) | copy-start | bytes 24580
  70.4 10.2 %copy-start.14 = (f32[1,2048]{1,0:T(1,128)S(1)}, f32[1,2048]{1,0:T(1,128)}, u32[]{:S(2)}) copy-start(f32[1,2048]{1,0:T(1,128)} %broadcast_in_dim_reshape.3.skip_ref) | copy-start | bytes 24580
  71.8 8.8 %copy-start.17 = (f32[32]{0:T(128)S(1)}, f32[32]{0:T(128)}, u32[]{:S(2)}) copy-start(f32[32]{0:T(128)} %param.16) | copy-start | bytes 388
  71.8 8.8 %copy-start.19 = (f32[32]{0:T(128)S(1)}, f32[32]{0:T(128)}, u32[]{:S(2)}) copy-start(f32[32]{0:T(128)} %param.17) | copy-start | bytes 388
  78.4 1.3 copy-start.4
  80.5 11.2 %copy-start.9 = (bf16[128,2048]{1,0:T(8,128)(2,1)}, bf16[128,2048]{1,0:T(8,128)(2,1)S(1)}, u32[]{:S(2)}) copy-start(bf16[128,2048]{1,0:T(8,128)(2,1)S(1)} %get-tuple-element.34) | copy-start | bytes 1572868
  91.7 2.7 %copy-start.5 = (f32[128,2048]{1,0:T(8,128)}, f32[128,2048]{1,0:T(8,128)S(1)}, u32[]{:S(2)}) copy-start(f32[128,2048]{1,0:T(8,128)S(1)} %get-tuple-element.32.pre_ref) | copy-start | bytes 3145732
  94.5 8.7 %copy-start.8 = (bf16[128,2048]{1,0:T(8,128)(2,1)S(1)}, bf16[128,2048]{1,0:T(8,128)(2,1)}, u32[]{:S(2)}) copy-start(bf16[128,2048]{1,0:T(8,128)(2,1)} %copy-done.7) | copy-start | bytes 1572868
  94.5 36.3 %all-to-all-start.2 = ((bf16[16,296,128]{2,1,0:T(8,128)(2,1)}), bf16[16,296,128]{2,1,0:T(8,128)(2,1)}, u32[]{:S(2)}, u32[]{:S(2)}) async-start(bf16[16,296,128]{2,1,0:T(8,128)(2,1)} %fusion.4), calls=%async_computation.2 | async-start | bytes 2424832 | tf_op jit(solution)/shard_map/all_to_all | solution.py:40
  130.8 32.8 %all-to-all-start.1 = ((bf16[16,256,128]{2,1,0:T(8,128)(2,1)}), bf16[16,256,128]{2,1,0:T(8,128)(2,1)S(1)}, u32[]{:S(2)}, u32[]{:S(2)}) async-start(bf16[16,256,128]{2,1,0:T(8,128)(2,1)} %pad_maximum_fusion.2), calls=%async_computation.1 | async-start | bytes 2097152 | tf_op jit(solution)/shard_map/all_to_all | solution.py:40
  141.0 25.5 %collective-permute-start.3 = (f32[1,296,128]{2,1,0:T(8,128)}, f32[1,296,128]{2,1,0:T(8,128)}, u32[]{:S(2)}, u32[]{:S(2)}) collective-permute-start(f32[1,296,128]{2,1,0:T(8,128)} %bitcast.52), channel_id=1, source_target_pairs={{0,1},{1,0},{2,3},{3,2},{4,5},{5,4},{6,7},{7,6},{8,9},{9,8},{10,11... | collective-permute-start | bytes 454664 | tf_op jit(solution)/shard_map/ppermute | solution.py:397
  163.7 1.2 copy-start.6
  164.9 4.0 %copy-start.22 = (f32[256]{0:T(256)S(1)}, f32[256]{0:T(256)}, u32[]{:S(2)}) copy-start(f32[256]{0:T(256)} %get-tuple-element.41) | copy-start | bytes 3076
  (6 other events, 4.6 us)

commit v2 on v1

--- a/solution.py
+++ b/solution.py
@@ -141,6 +141,110 @@
     high, low = split(value)
     refs[0][:, sl] = high
     refs[1][:, sl] = low
+
+
+def from_sites(ref, j, sites, base):
+    rows = slice(base + j * sites, base + (j + 1) * sites)
+    return ref[:, rows, :].astype(f32).reshape(ref.shape[0] * sites, LANES)
+
+
+def to_sites(ref, j, sites, base, value):
+    rows = slice(base + j * sites, base + (j + 1) * sites)
+    ref[:, rows, :] = value.astype(f32).reshape(ref.shape[0], sites, LANES).astype(bf16)
+
+
+def pack_kernel(sites, tok_ref, grad_ref, sent_ref):
+    base = sent_ref.shape[1] // 2
+    for j, sl in blocks(tok_ref.shape[1]):
+        to_sites(sent_ref, j, sites, 0, tok_ref[:, sl])
+        to_sites(sent_ref, j, sites, base, grad_ref[:, sl])
+
+
+def payload_kernel(ids_ref, proj_ref, step_ref, active_ref, mod_ref, sent_ref):
+    row = ids_ref[1]
+    part, pair = proj_ref.shape[0] // 2, proj_ref.shape[1]
+    own = proj_ref[pl.ds(pl.multiple_of(row * part, part), part), :]
+    at = 0
+    for _, sl in blocks(pair):
+        sent_ref[at : at + part, :] = own[:, sl]
+        at += part
+    part = step_ref.shape[0] // 2
+    sent_ref[at : at + part, :] = step_ref[pl.ds(pl.multiple_of(row * part, part), part), :]
+    at += part
+    own = mm(active_ref[...], mod_ref[...], 1, 0)
+    high = own.astype(bf16).astype(f32)
+    pieces = [piece[:, sl] for piece in (high, own - high) for _, sl in blocks(own.shape[1])]
+    pieces.append(jnp.zeros((8 - len(pieces), LANES), f32))
+    sent_ref[at : at + 8, :] = jnp.concatenate(pieces, axis=0).astype(bf16)
+
+
+def unpack_kernel(radix, ids_ref, own_ref, other_ref, proj_ref, step_ref, shift_ref, gain_ref):
+    me, row = ids_ref[0], ids_ref[1]
+    width, pair = proj_ref.shape
+    frames = own_ref.shape[0]
+    depth = width // frames
+    part, heads = depth // 2, step_ref.shape[0] // 2
+    cols = 2 * width // frames
+    for i in range(frames):
+        source = jnp.bitwise_xor(me, (i % radix) * radix + i // radix)
+        for ref, half in ((own_ref, row), (other_ref, 1 - row)):
+            rows = pl.ds(pl.multiple_of(source * depth + half * part, part), part)
+            at = 0
+            for _, sl in blocks(pair):
+                proj_ref[rows, sl] = ref[i, at : at + part, :]
+                at += part
+            rows = pl.ds(pl.multiple_of(half * heads, heads), heads)
+            lanes = pl.ds(pl.multiple_of(source * depth, depth), depth)
+            step_ref[rows, lanes] = ref[i, at : at + heads, :]
+            at += heads
+        own = own_ref[i, at : at + 8, :].astype(f32)
+        count = cols // LANES
+        lanes_at = jnp.bitwise_and(source, frames // 2 - 1) * cols
+        for k in range(count):
+            value = own[k : k + 1, :] + own[count + k : count + k + 1, :]
+            lanes = pl.ds(pl.multiple_of(lanes_at + k * LANES, LANES), LANES)
+
+            @pl.when(source < frames // 2)
+            def _():
+                shift_ref[:, lanes] = value
+
+            @pl.when(source >= frames // 2)
+            def _():
+                gain_ref[:, lanes] = value
+
+
+def finish_kernel(factor, ids_ref, own_ref, other_ref, active_ref, proj_ref, step_ref, mod_ref):
+    row = ids_ref[1]
+    pair = proj_ref.shape[1]
+    part, heads = proj_ref.shape[0] // 2, step_ref.shape[0] // 2
+    for ref, half in ((own_ref, row), (other_ref, 1 - row)):
+        rows = pl.ds(pl.multiple_of(half * part, part), part)
+        at = 0
+        for _, sl in blocks(pair):
+            proj_ref[rows, sl] = ref[at : at + part, :] * factor
+            at += part
+        step_ref[pl.ds(pl.multiple_of(half * heads, heads), heads), :] = ref[at : at + heads, :] * factor
+        at += heads
+    for k, sl in blocks(mod_ref.shape[1]):
+        mod_ref[:, sl] = active_ref[...] * (own_ref[at + k : at + k + 1, :] * factor)
+
+
+def site_fast_kernel(sites, got_ref, *refs):
+    inputs, outs, tok_ref, grad_ref, scratch = refs[:6], refs[6:10], refs[10], refs[11], refs[12:]
+    base = got_ref.shape[1] // 2
+    for j, sl in blocks(tok_ref.shape[1]):
+        tok_ref[:, sl] = from_sites(got_ref, j, sites, 0).astype(bf16)
+        grad_ref[:, sl] = from_sites(got_ref, j, sites, base).astype(bf16)
+    sent_ref = outs[0]
+
+    class Packed:
+        def __init__(self, base):
+            self.base = base
+
+        def __setitem__(self, at, value):
+            to_sites(sent_ref, at[1].start // LANES, sites, self.base, value)
+
+    site_kernel(sites, tok_ref, grad_ref, *inputs, Packed(0), Packed(base), *outs[1:], *scratch)
 
 
 def site_kernel(
@@ -257,6 +361,45 @@
         own_ref[sl, :] = mm(faded, c_part, 0, 0).astype(bf16)
 
 
+def space_fast_kernel(ids_ref, gmod_in, *refs):
+    inputs, mix_ref, pre_ref, keep_ref, give_ref = refs[:15], *refs[15:19]
+    gmod_ref, scratch = refs[19], refs[20:]
+    first = ids_ref[1] == 0
+    pair = inputs[6].shape[1]
+    part, heads = LANES // 2, inputs[7].shape[0] // 2
+    proj_rows = part * pair // LANES
+
+    class Halves:
+        def __init__(self, at, part):
+            self.at, self.part = at, part
+
+        def __setitem__(self, where, value):
+            value = value.astype(f32)
+            j = max(0 if w.start is None else w.start for w in where) // LANES
+            own = jnp.where(first, value[: self.part], value[self.part :]).astype(bf16)
+            other = jnp.where(first, value[self.part :], value[: self.part]).astype(bf16)
+            for k, sl in blocks(value.shape[1]):
+                rows = slice(self.at + k * self.part, self.at + (k + 1) * self.part)
+                keep_ref[j, rows, :] = own[:, sl]
+                give_ref[j, rows, :] = other[:, sl]
+
+    space_kernel(
+        *inputs, mix_ref, pre_ref, Halves(0, part), Halves(proj_rows, heads), gmod_ref, *scratch
+    )
+    at = proj_rows + heads
+    count = pre_ref.shape[1] // LANES
+    for j in range(keep_ref.shape[0]):
+        rows = []
+        for k in range(2 * count // keep_ref.shape[0]):
+            n = j * (2 * count // keep_ref.shape[0]) + k
+            which, sl = n // count, slice(n % count * LANES, (n % count + 1) * LANES)
+            rows.append(gmod_ref[which : which + 1, sl] + gmod_in[which : which + 1, sl])
+        rows.append(jnp.zeros((8 - len(rows), LANES), f32))
+        rows = jnp.concatenate(rows, axis=0).astype(bf16)
+        keep_ref[j, at : at + 8, :] = rows
+        give_ref[j, at : at + 8, :] = rows
+
+
 def space_kernel(
     tok_ref,
     grad_ref,
@@ -300,6 +443,7 @@
     b_part, c_part = coeffs[:, :state], coeffs[:, state:]
     scores = mm(c_part, b_part, 1, 1) * (mask / state)
     step_parts, lead_parts, reach_parts = split(step), split(lead), split(jnp.exp(cum) / state)
+    skip_parts = split(jnp.broadcast_to(skip_ref[...], (8, heads)))
     d_scores = jnp.zeros((length, length), f32)
     d_b = jnp.zeros((length, state), f32)
     d_c = jnp.zeros((length, state), f32)
@@ -322,7 +466,7 @@
         both = split(before.astype(f32) * later.astype(f32))
         d_end = d_end + mm(wide_map, both[0], 1, 0) + mm(wide_map, both[1], 1, 0)
         total = out + carried
-        skip = skip_ref[:, sl]
+        skip = expand(skip_parts, wide_map)[0:1, :]
         mix_ref[:, sl] = total + skip * x
         d_x = (step_wide * d_stepped + d_scaled * lead_wide).astype(bf16)
         dn_ref[:, sl] = d_x + (wide * skip).astype(bf16)
@@ -372,11 +516,31 @@
         dtok_ref[:, sl] = (grad * inverse - tok_ref[:, sl].astype(f32) * inner).astype(bf16)
 
 
-def call(kernel, outs, scratch=(), name=None):
+def last_fast_kernel(sites, tok_ref, inverse_ref, gain_ref, mix_ref, pre_ref, came_ref, *outs):
+    base = came_ref.shape[1] // 2
+
+    class Packed:
+        def __init__(self, base):
+            self.base = base
+
+        def __getitem__(self, at):
+            return from_sites(came_ref, at[1].start // LANES, sites, self.base)
+
+    last_kernel(tok_ref, inverse_ref, gain_ref, mix_ref, pre_ref, Packed(0), Packed(base), *outs)
+
+
+def call(kernel, outs, scratch=(), name=None, ids=0):
     shapes = [jax.ShapeDtypeStruct(s, d) for s, d in outs]
+    if ids:
+        whole = pl.BlockSpec(memory_space=pltpu.VMEM)
+        specs = [pl.BlockSpec(memory_space=pltpu.SMEM)] + [whole] * ids
+        specs = {"in_specs": specs, "out_specs": [whole] * len(outs)}
+    else:
+        specs = {}
     return pl.pallas_call(
         kernel,
         out_shape=shapes,
+        **specs,
         scratch_shapes=[pltpu.VMEM(s, d) for s, d in scratch],
         compiler_params=pltpu.CompilerParams(vmem_limit_bytes=48 << 20),
         name=name,
@@ -520,7 +684,6 @@
     )(tok, grad, own_shift, own_gain, proj_full, step_full, bias, rate_space[None])
     state_in = chain(end_own, decay, True)
     later_grad = chain(start_grad, decay, False)
-    skip = jnp.repeat(skip_gain, width // heads)[None]
     mix, pre, gproj, gstep, gmod = call(
         space_kernel,
         [(wide, f32), (wide, f32), ((width, pair), bf16), ((heads, width), bf16), ((2, width), f32)],
@@ -537,7 +700,7 @@
         step_full,
         bias,
         rate_space[None],
-        skip,
+        skip_gain[None],
         state_in,
         later_grad,
         gproj,
@@ -576,6 +739,148 @@
     return (mixed.reshape(tokens.shape), d_tokens.reshape(tokens.shape), grad_proj, grad_step, grad_mod)
 
 
+def fits(mesh, tokens, timestep, proj_weight, step_weight):
+    frames, rows = mesh.shape["frame"], mesh.shape["row"]
+    length, width = tokens.shape[2] * tokens.shape[1] // rows, tokens.shape[3]
+    return (
+        rows == 2
+        and frames == 16
+        and timestep.shape[0] == 1
+        and length == LANES
+        and length // frames == 8
+        and width // frames == LANES
+        and proj_weight.shape[1] == 2 * LANES
+        and step_weight.shape[1] % 32 == 0
+    )
+
+
+def spread_over_frames(own, radix=4):
+    frames = radix * radix
+
+    def others(piece, stride):
+        return [piece] + [
+            lax.ppermute(piece, "frame", [(i, i ^ (d * stride)) for i in range(frames)])
+            for d in range(1, radix)
+        ]
+
+    far = jnp.stack(others(own, radix))
+    return jnp.concatenate(others(far, 1))
+
+
+def per_device_fast(
+    tokens,
+    cotangent,
+    timestep,
+    mod_weight,
+    proj_weight,
+    step_weight,
+    step_bias,
+    rate_space,
+    rate_time,
+    skip_gain,
+):
+    frames = lax.axis_size("frame")
+    rows = lax.axis_size("row")
+    ids = jnp.stack([lax.axis_index("frame"), lax.axis_index("row")]).astype(jnp.int32)
+    width = tokens.shape[-1]
+    length = tokens.shape[1] * tokens.shape[2]
+    sites = length // frames
+    heads = rate_space.shape[0]
+    depth, pair = proj_weight.shape
+    state = pair // 2
+    mod_cols = mod_weight.shape[1]
+    factor = (frames * rows * length) ** (-0.5)
+    tok = tokens.reshape(length, width)
+    grad = cotangent.reshape(length, width)
+    wide = (length, width)
+    bias = step_bias[None]
+    swap = [(0, 1), (1, 0)]
+
+    packed = (frames, 2 * sites * width // LANES, LANES)
+    (sent,) = call(functools.partial(pack_kernel, sites), [(packed, bf16)], name="pack")(tok, grad)
+
+    timestep, sent = lax.optimization_barrier((timestep, sent))
+    got = exchange(sent)
+    activated = time_embed(timestep, mod_weight.shape[0]).astype(bf16)
+    size = depth // 2 * pair // LANES + heads // 2 + 8
+    (payload,) = call(payload_kernel, [((size, LANES), bf16)], name="payload", ids=4)(
+        ids, proj_weight, step_weight.T, activated, mod_weight
+    )
+    payload = spread_over_frames(payload)
+    other = lax.ppermute(payload, "row", swap)
+    proj_full, step_full, shift, gain = call(
+        functools.partial(unpack_kernel, 4),
+        [((width, pair), bf16), ((heads, width), bf16), ((1, width), f32), ((1, width), f32)],
+        name="unpack",
+        ids=2,
+    )(ids, payload, other)
+
+    sent, gproj, gstep, site_gmod = call(
+        functools.partial(site_fast_kernel, sites),
+        [(packed, bf16), ((width, pair), f32), ((heads, width), f32), ((2, width), f32)],
+        [(wide, bf16)] * 8,
+        name="site",
+    )(got, shift, gain, proj_full, step_full, bias, rate_time[None])
+    came = exchange(sent)
+
+    normed, coeffs, logits, inverse, decay, end_own, start_grad = call(
+        band_kernel,
+        [
+            (wide, bf16),
+            ((length, pair), bf16),
+            ((length, heads), bf16),
+            ((length, 1), f32),
+            ((1, heads), f32),
+            ((width, state), bf16),
+            ((width, state), bf16),
+        ],
+        name="band",
+    )(tok, grad, shift, gain, proj_full, step_full, bias, rate_space[None])
+    state_in = chain(end_own, decay, True)
+    later_grad = chain(start_grad, decay, False)
+    halves = (frames, size, LANES)
+    mix, pre, keep, give, _ = call(
+        space_fast_kernel,
+        [(wide, f32), (wide, f32), (halves, bf16), (halves, bf16), ((2, width), f32)],
+        [(wide, bf16)] * 7,
+        name="space",
+        ids=16,
+    )(
+        ids,
+        site_gmod,
+        tok,
+        grad,
+        normed,
+        coeffs,
+        logits,
+        inverse,
+        proj_full,
+        step_full,
+        bias,
+        rate_space[None],
+        skip_gain[None],
+        state_in,
+        later_grad,
+        gproj,
+        gstep,
+    )
+    given = lax.ppermute(give, "row", swap)
+    terms = (keep.astype(f32) + given.astype(f32)).astype(bf16)
+    terms, came = lax.optimization_barrier((terms, came))
+    sums = jnp.sum(exchange(terms).astype(f32), axis=0)
+    other = lax.ppermute(sums, "row", swap)
+    grad_proj, grad_step, grad_mod = call(
+        functools.partial(finish_kernel, factor),
+        [((depth, pair), f32), ((heads, depth), f32), ((mod_weight.shape[0], mod_cols), f32)],
+        name="finish",
+        ids=3,
+    )(ids, sums, other, activated.astype(f32).T)
+    mixed, d_tokens = call(
+        functools.partial(last_fast_kernel, sites), [(wide, bf16), (wide, bf16)], name="last"
+    )(tok, inverse, gain, mix, pre, came)
+    return (mixed.reshape(tokens.shape), d_tokens.reshape(tokens.shape), grad_proj, grad_step.T, grad_mod)
+
+
 def solution(mesh):
     placed = (
         P("frame", "row", None, None),
@@ -589,16 +894,19 @@
         P(),
         P(),
     )
-    return jax.shard_map(
-        per_device,
-        mesh=mesh,
-        in_specs=placed,
-        out_specs=(
-            P("frame", "row", None, None),
-            P("frame", "row", None, None),
-            P("frame", None),
-            P("frame", None),
-            P(None, "frame"),
-        ),
-        check_vma=False,
-    )
+    outs = (
+        P("frame", "row", None, None),
+        P("frame", "row", None, None),
+        P("frame", None),
+        P("frame", None),
+        P(None, "frame"),
+    )
+
+    def step(tokens, cotangent, timestep, mod_weight, proj_weight, step_weight, *rest):
+        fast = fits(mesh, tokens, timestep, proj_weight, step_weight)
+        body = per_device_fast if fast else per_device
+        return jax.shard_map(
+            body, mesh=mesh, in_specs=placed, out_specs=outs, check_vma=False
+        )(tokens, cotangent, timestep, mod_weight, proj_weight, step_weight, *rest)
+
+    return step

time: 171 us -> 112 us (0.65)
  waiting for transfers between devices: 85.8 us -> 23.1 us
  blocking collectives: 0 us -> 25 us
  other arithmetic: 14.3 us -> 0.48 us
  starting transfers between devices: 29.5 us -> 24.4 us
  local copies, waits for them, and re-layouts: 13.5 us -> 9.1 us
  Pallas kernels: 24.8 us -> 28.1 us
    all_to_all x3 -> x2, waiting for transfers between devices: 84.9 us -> 3.11 us  [exchange(): lax.all_to_all(packed, 'frame', split_axis=0, concat_axis=0, tiled=True)]
    all_to_all x0 -> x1, blocking collectives: none -> 25 us  [exchange(): lax.all_to_all(packed, 'frame', split_axis=0, concat_axis=0, tiled=True)]
    ppermute x2 -> x9, waiting for transfers between devices: 0.88 us -> 17.6 us  [the longest x6 13.7 us: others(): lax.ppermute(piece, 'frame', [(i, i ^ d * stride) for i in range(frames)])]
    all_to_all x3 -> x2, starting transfers between devices: 25.1 us -> 12.1 us  [exchange(): lax.all_to_all(packed, 'frame', split_axis=0, concat_axis=0, tiled=True)]
    ppermute x2 -> x9, starting transfers between devices: 0.09 us -> 9.49 us  [the longest x6 9.21 us: others(): lax.ppermute(piece, 'frame', [(i, i ^ d * stride) for i in range(frames)])]
    concatenate x4 -> x2, other arithmetic: 7.34 us -> 0.1 us  [time_embed(): jnp.concatenate([jnp.cos(angles), jnp.sin(angles)], axis=1)]
    pallas_call x4 -> x8, Pallas kernels: 24.8 us -> 28.1 us  [the longest x1 10.8 us: per_device_fast(): call(space_fast_kernel, [(wide, f32), (wide, f32), (halves, bf16), (halve...]
    ppermute x2, waiting for transfers between devices: 0.01 us -> 2.32 us  [chain(): arrived = lax.ppermute(own, 'row', hops)]
  transfers between devices with their start and end apart: 7 -> 13, of which waited for: 4 -> 8; matrix products, arithmetic and copies ran while one was open for 4% -> 0% of each run, Pallas kernels for 5% -> 17%
where the time goes in v2:
time: 112 us
  Pallas kernels  28.1 us (25%)
  blocking collectives  25 us (22%)
  starting transfers between devices  24.4 us (22%)
  waiting for transfers between devices  23.1 us (21%)
  local copies, waits for them, and re-layouts  9.1 us (8%)
  between operations  1.55 us (1%)
    all_to_all x1, blocking collectives, exchange(): lax.all_to_all(packed, 'frame', split_axis=0, concat_axis=0, tiled=True)  25 us
    ppermute x6, waiting for transfers between devices, others(): lax.ppermute(piece, 'frame', [(i, i ^ d * stride) for i in range(frames)])  13.7 us
    all_to_all x2, starting transfers between devices, exchange(): lax.all_to_all(packed, 'frame', split_axis=0, concat_axis=0, tiled=True)  12.1 us
    pallas_call x1, Pallas kernels, per_device_fast(): call(space_fast_kernel, [(wide, f32), (wide, f32), (halves, bf16), (halve...  10.8 us
    ppermute x6, starting transfers between devices, others(): lax.ppermute(piece, 'frame', [(i, i ^ d * stride) for i in range(frames)])  9.21 us
    unnamed x40, local copies, waits for them, and re-layouts  8.94 us
    pallas_call x1, Pallas kernels, per_device_fast(): call(functools.partial(site_fast_kernel, sites), [(packed, bf16), ((width...  6.68 us
    pallas_call x1, Pallas kernels, per_device_fast(): call(band_kernel, [(wide, bf16), ((length, pair), bf16), ((length, heads)...  4.72 us
  transfers between devices with their start and end apart: 13, of which 8 were waited for; matrix products, arithmetic and copies ran while one was open for 0% of the time, Pallas kernels for 17%

profile of v2, /device:TPU:0, one launch (start us, length us, event | category | flops | bytes accessed | tf_op | source)
XLA Modules:
  0.0 111.7 jit_solution(1806137712263157030)
XLA Ops:
  4.6 4.1 %collective-permute-start.1 = (bf16[152,128]{1,0:T(8,128)(2,1)S(1)}, bf16[152,128]{1,0:T(8,128)(2,1)S(1)}, u32[]{:S(2)}, u32[]{:S(2)}) collective-permute-start(bf16[152,128]{1,0:T(8,128)(2,1)S(1)} %payload.1), channel_id=1, source_target_pairs={{0,16},{2,18},{4,20},{6,22},{8,24},{10,26},{12,28},{14,30},{16,0},... | collective-permute-start | bytes 116744 | tf_op jit(solution)/shard_map/ppermute | solution.py:762
  8.7 1.3 %collective-permute-start.2 = (bf16[152,128]{1,0:T(8,128)(2,1)S(1)}, bf16[152,128]{1,0:T(8,128)(2,1)S(1)}, u32[]{:S(2)}, u32[]{:S(2)}) collective-permute-start(bf16[152,128]{1,0:T(8,128)(2,1)S(1)} %payload.1), channel_id=1, source_target_pairs={{0,24},{2,26},{4,28},{6,30},{8,16},{10,18},{12,20},{14,22},{16,8},... | collective-permute-start | bytes 116744 | tf_op jit(solution)/shard_map/ppermute | solution.py:762
  12.4 1.3 %pack.1 = bf16[16,256,128]{2,1,0:T(8,128)(2,1)} custom-call(bf16[128,2048]{1,0:T(8,128)(2,1)S(1)} %bitcast.29, bf16[128,2048]{1,0:T(8,128)(2,1)S(1)} %bitcast.33), custom_call_target="tpu_custom_call" | custom-call | tf_op jit(solution)/shard_map/pack/pallas_call | solution.py:800
  13.6 6.2 %all-to-all-start = ((bf16[16,256,128]{2,1,0:T(8,128)(2,1)}), bf16[16,256,128]{2,1,0:T(8,128)(2,1)S(1)}, u32[]{:S(2)}, u32[]{:S(2)}) async-start(bf16[16,256,128]{2,1,0:T(8,128)(2,1)} %pack.1), calls=%async_computation | async-start | bytes 2097152 | tf_op jit(solution)/shard_map/all_to_all | solution.py:40
  19.9 2.0 %collective-permute-start.3 = (bf16[4,152,128]{2,1,0:T(8,128)(2,1)S(1)}, bf16[4,152,128]{2,1,0:T(8,128)(2,1)S(1)}, u32[]{:S(2)}, u32[]{:S(2)}) collective-permute-start(bf16[4,152,128]{2,1,0:T(8,128)(2,1)S(1)} %pad_maximum_fusion), channel_id=1, source_target_pairs={{0,2},{2,0},{4,6},{6,4},{8,10},{10,8},{12,14},{14,12},{16,18},{18,... | collective-permute-start | bytes 466952 | tf_op jit(solution)/shard_map/ppermute | solution.py:762
  21.9 1.5 %collective-permute-start.4 = (bf16[4,152,128]{2,1,0:T(8,128)(2,1)S(1)}, bf16[4,152,128]{2,1,0:T(8,128)(2,1)S(1)}, u32[]{:S(2)}, u32[]{:S(2)}) collective-permute-start(bf16[4,152,128]{2,1,0:T(8,128)(2,1)S(1)} %pad_maximum_fusion), channel_id=1, source_target_pairs={{0,4},{2,6},{4,0},{6,2},{8,12},{10,14},{12,8},{14,10},{16,20},{18,... | collective-permute-start | bytes 466952 | tf_op jit(solution)/shard_map/ppermute | solution.py:762
  23.5 6.0 %collective-permute-done.3 = bf16[4,152,128]{2,1,0:T(8,128)(2,1)S(1)} collective-permute-done((bf16[4,152,128]{2,1,0:T(8,128)(2,1)S(1)}, bf16[4,152,128]{2,1,0:T(8,128)(2,1)S(1)}, u32[]{:S(2)}, u32[]{:S(2)}) %collective-permute-start.3) | collective-permute-done | bytes 155680 | tf_op jit(solution)/shard_map/ppermute | solution.py:762
  29.5 6.0 %collective-permute-done.4 = bf16[4,152,128]{2,1,0:T(8,128)(2,1)S(1)} collective-permute-done((bf16[4,152,128]{2,1,0:T(8,128)(2,1)S(1)}, bf16[4,152,128]{2,1,0:T(8,128)(2,1)S(1)}, u32[]{:S(2)}, u32[]{:S(2)}) %collective-permute-start.4) | collective-permute-done | bytes 155680 | tf_op jit(solution)/shard_map/ppermute | solution.py:762
  35.5 1.7 %collective-permute-done.5 = bf16[4,152,128]{2,1,0:T(8,128)(2,1)S(1)} collective-permute-done((bf16[4,152,128]{2,1,0:T(8,128)(2,1)S(1)}, bf16[4,152,128]{2,1,0:T(8,128)(2,1)S(1)}, u32[]{:S(2)}, u32[]{:S(2)}) %collective-permute-start.5) | collective-permute-done | bytes 155680 | tf_op jit(solution)/shard_map/ppermute | solution.py:762
  37.3 2.0 %collective-permute-done.6.other_ref = bf16[16,152,128]{2,1,0:T(8,128)(2,1)S(1)} collective-permute-done((bf16[16,152,128]{2,1,0:T(8,128)(2,1)S(1)}, bf16[16,152,128]{2,1,0:T(8,128)(2,1)S(1)}, u32[]{:S(2)}, u32[]{:S(2)}) %collective-permute-start.6) | collective-permute-done | bytes 622624 | tf_op jit(solution)/shard_map/ppermute | solution.py:810
  40.4 3.0 %all-to-all-done.got_ref = bf16[16,256,128]{2,1,0:T(8,128)(2,1)S(1)} async-done(((bf16[16,256,128]{2,1,0:T(8,128)(2,1)}), bf16[16,256,128]{2,1,0:T(8,128)(2,1)S(1)}, u32[]{:S(2)}, u32[]{:S(2)}) %all-to-all-start) | async-done | bytes 1048608 | tf_op jit(solution)/shard_map/all_to_all | solution.py:40
  43.5 6.7 %site.1 = (bf16[16,256,128]{2,1,0:T(8,128)(2,1)S(1)}, f32[2048,256]{1,0:T(8,128)S(1)}, f32[32,2048]{1,0:T(8,128)S(1)}, f32[2,2048]{1,0:T(2,128)S(1)}) custom-call(bf16[16,256,128]{2,1,0:T(8,128)(2,1)S(1)} %all-to-all-done.got_ref, f32[1,2048]{1,0:T(1,128)S(1)} %get-tuple-element.33.shift_ref.refs_0_, f32[1,2048]{1,0:T(1,128)S(1)} %get-tuple-element.34.gain_ref.refs_1_, ...), custom_call_target="tpu_custom_call" | custom-call | tf_op jit(solution)/shard_map/site/pallas_call | solution.py:818
  50.2 1.3 %copy-done.5 = f32[2048,256]{1,0:T(8,128)} copy-done((f32[2048,256]{1,0:T(8,128)}, f32[2048,256]{1,0:T(8,128)S(1)}, u32[]{:S(2)}) %copy-start.5) | copy-done | bytes 2097176
  53.3 5.9 %all-to-all-start.1 = ((bf16[16,256,128]{2,1,0:T(8,128)(2,1)}), bf16[16,256,128]{2,1,0:T(8,128)(2,1)S(1)}, u32[]{:S(2)}, u32[]{:S(2)}) async-start(bf16[16,256,128]{2,1,0:T(8,128)(2,1)} %copy-done.7), calls=%async_computation.1 | async-start | bytes 2097152 | tf_op jit(solution)/shard_map/all_to_all | solution.py:40
  59.2 4.7 %band.1 = (bf16[128,2048]{1,0:T(8,128)(2,1)S(1)}, bf16[128,256]{1,0:T(8,128)(2,1)S(1)}, bf16[128,32]{1,0:T(8,128)(2,1)S(1)}, f32[128,1]{1,0:T(8,128)S(1)}, f32[1...) custom-call(bf16[128,2048]{1,0:T(8,128)(2,1)S(1)} %bitcast.30, ...), custom_call_target="tpu_custom_call" | custom-call | tf_op jit(solution)/shard_map/band/pallas_call | solution.py:826
  63.9 1.3 %collective-permute-start.7 = (bf16[2048,128]{1,0:T(8,128)(2,1)S(1)}, bf16[2048,128]{1,0:T(8,128)(2,1)S(1)}, u32[]{:S(2)}, u32[]{:S(2)}) collective-permute-start(bf16[2048,128]{1,0:T(8,128)(2,1)S(1)} %get-tuple-element.43), channel_id=1, source_target_pairs={{0,1},{2,3},{4,5},{6,7},{8,9},{10,11},{12,13},{14,15},{16,17},{18,... | collective-permute-start | bytes 1572872 | tf_op jit(solution)/shard_map/ppermute | solution.py:569
  65.3 1.5 %collective-permute-start.8 = (bf16[2048,128]{1,0:T(8,128)(2,1)S(1)}, bf16[2048,128]{1,0:T(8,128)(2,1)S(1)}, u32[]{:S(2)}, u32[]{:S(2)}) collective-permute-start(bf16[2048,128]{1,0:T(8,128)(2,1)S(1)} %get-tuple-element.44), channel_id=1, source_target_pairs={{1,0},{3,2},{5,4},{7,6},{9,8},{11,10},{13,12},{15,14},{17,16},{19,... | collective-permute-start | bytes 1572872 | tf_op jit(solution)/shard_map/ppermute | solution.py:569
  66.7 2.3 %collective-permute-done.8.refs_12_ = bf16[2048,128]{1,0:T(8,128)(2,1)S(1)} collective-permute-done((bf16[2048,128]{1,0:T(8,128)(2,1)S(1)}, bf16[2048,128]{1,0:T(8,128)(2,1)S(1)}, u32[]{:S(2)}, u32[]{:S(2)}) %collective-permute-start.8) | collective-permute-done | bytes 524320 | tf_op jit(solution)/shard_map/ppermute | solution.py:569
  69.1 10.8 %space.1 = (f32[128,2048]{1,0:T(8,128)S(1)}, f32[128,2048]{1,0:T(8,128)}, bf16[16,152,128]{2,1,0:T(8,128)(2,1)S(1)}, bf16[16,152,128]{2,1,0:T(8,128)(2,1)S(1)}, f32[2,2048]{1,0:T(2,128)}) custom-call(s32[2]{0:T(128)S(1)} %pad_add_fusion.ids_ref, f32[2,2048]{1,0:T(2,128)S(1)} %get-tuple-element.39.gmod_in, bf16[128,2048]{1,0:T(8,128)(2,1)S(1)} %bitcast.31, ...), custom_call_target="tpu_custom_call" | custom-call | tf_op jit(solution)/shard_map/space/pallas_call | solution.py:842
  80.0 1.9 %collective-permute-done.9 = bf16[16,152,128]{2,1,0:T(8,128)(2,1)S(1)} collective-permute-done((bf16[16,152,128]{2,1,0:T(8,128)(2,1)S(1)}, bf16[16,152,128]{2,1,0:T(8,128)(2,1)S(1)}, u32[]{:S(2)}, u32[]{:S(2)}) %collective-permute-start.9) | collective-permute-done | bytes 622624 | tf_op jit(solution)/shard_map/ppermute | solution.py:867
  82.1 25.0 %all_to_all.15 = bf16[16,152,128]{2,1,0:T(8,128)(2,1)S(1)} all-to-all(bf16[16,152,128]{2,1,0:T(8,128)(2,1)S(1)} %add_convert_fusion), channel_id=1, replica_groups=mesh['frame'=16,'row'=2] {'frame'}, dimensions={0} | all-to-all | bytes 1245184 | tf_op jit(solution)/shard_map/all_to_all | solution.py:40
  107.5 1.2 %copy-done.6 = f32[128,2048]{1,0:T(8,128)S(1)} copy-done((f32[128,2048]{1,0:T(8,128)S(1)}, f32[128,2048]{1,0:T(8,128)}, u32[]{:S(2)}) %copy-start.6) | copy-done | bytes 1048600
  108.7 1.6 %last.1 = (bf16[128,2048]{1,0:T(8,128)(2,1)}, bf16[128,2048]{1,0:T(8,128)(2,1)}) custom-call(bf16[128,2048]{1,0:T(8,128)(2,1)S(1)} %bitcast.32, f32[128,1]{1,0:T(8,128)S(1)} %get-tuple-element.37.refs_5_.inverse_ref, f32[1,2048]{1,0:T(1,128)S(1)} %get-tuple-element.34.gain_ref.refs_1_, f32[128,2048]{1,0:T(8,128)S(1)} %get-tuple-element.47.mix_ref, ...), custom_call_target="tpu_custom_call" | custom-call | tf_op jit(solution)/shard_map/last/pallas_call | solution.py:878
  110.4 1.4 %finish.1 = (f32[128,256]{1,0:T(8,128)}, f32[32,128]{1,0:T(8,128)}, f32[256,256]{1,0:T(8,128)}) custom-call(s32[2]{0:T(128)S(1)} %pad_add_fusion.ids_ref, f32[152,128]{1,0:T(8,128)S(1)} %convert_reduce_fusion.own_ref, f32[152,128]{1,0:T(8,128)S(1)} %collective-permute-done.10.other_ref, f32[256,1]{1,0:T(8,128)S(1)} %copy.20.active_ref), custom_call_target="tpu_custom_call" | custom-call | tf_op jit(solution)/shard_map/finish/pallas_call | solution.py:872
  (61 shorter events, 9.4 us)
Async XLA Ops:
  4.6 15.2 %collective-permute-start.1 = (bf16[152,128]{1,0:T(8,128)(2,1)S(1)}, bf16[152,128]{1,0:T(8,128)(2,1)S(1)}, u32[]{:S(2)}, u32[]{:S(2)}) collective-permute-start(bf16[152,128]{1,0:T(8,128)(2,1)S(1)} %payload.1), channel_id=1, source_target_pairs={{0,16},{2,18},{4,20},{6,22},{8,24},{10,26},{12,28},{14,30},{16,0},... | collective-permute-start | bytes 116744 | tf_op jit(solution)/shard_map/ppermute | solution.py:762
  8.7 11.1 %collective-permute-start.2 = (bf16[152,128]{1,0:T(8,128)(2,1)S(1)}, bf16[152,128]{1,0:T(8,128)(2,1)S(1)}, u32[]{:S(2)}, u32[]{:S(2)}) collective-permute-start(bf16[152,128]{1,0:T(8,128)(2,1)S(1)} %payload.1), channel_id=1, source_target_pairs={{0,24},{2,26},{4,28},{6,30},{8,16},{10,18},{12,20},{14,22},{16,8},... | collective-permute-start | bytes 116744 | tf_op jit(solution)/shard_map/ppermute | solution.py:762
  10.0 9.8 %collective-permute-start = (bf16[152,128]{1,0:T(8,128)(2,1)S(1)}, bf16[152,128]{1,0:T(8,128)(2,1)S(1)}, u32[]{:S(2)}, u32[]{:S(2)}) collective-permute-start(bf16[152,128]{1,0:T(8,128)(2,1)S(1)} %payload.1), channel_id=1, source_target_pairs={{0,8},{2,10},{4,12},{6,14},{8,0},{10,2},{12,4},{14,6},{16,24},{18,... | collective-permute-start | bytes 116744 | tf_op jit(solution)/shard_map/ppermute | solution.py:762
  10.3 1.0 copy-start.1
  13.6 29.8 %all-to-all-start = ((bf16[16,256,128]{2,1,0:T(8,128)(2,1)}), bf16[16,256,128]{2,1,0:T(8,128)(2,1)S(1)}, u32[]{:S(2)}, u32[]{:S(2)}) async-start(bf16[16,256,128]{2,1,0:T(8,128)(2,1)} %pack.1), calls=%async_computation | async-start | bytes 2097152 | tf_op jit(solution)/shard_map/all_to_all | solution.py:40
  19.9 23.6 %copy-start.13 = (f32[32]{0:T(128)S(1)}, f32[32]{0:T(128)}, u32[]{:S(2)}) copy-start(f32[32]{0:T(128)} %param.16) | copy-start | bytes 388
  19.9 23.6 %copy-start.16 = (f32[32]{0:T(128)S(1)}, f32[32]{0:T(128)}, u32[]{:S(2)}) copy-start(f32[32]{0:T(128)} %param.18) | copy-start | bytes 388
  19.9 9.6 %collective-permute-start.3 = (bf16[4,152,128]{2,1,0:T(8,128)(2,1)S(1)}, bf16[4,152,128]{2,1,0:T(8,128)(2,1)S(1)}, u32[]{:S(2)}, u32[]{:S(2)}) collective-permute-start(bf16[4,152,128]{2,1,0:T(8,128)(2,1)S(1)} %pad_maximum_fusion), channel_id=1, source_target_pairs={{0,2},{2,0},{4,6},{6,4},{8,10},{10,8},{12,14},{14,12},{16,18},{18,... | collective-permute-start | bytes 466952 | tf_op jit(solution)/shard_map/ppermute | solution.py:762
  21.9 13.6 %collective-permute-start.4 = (bf16[4,152,128]{2,1,0:T(8,128)(2,1)S(1)}, bf16[4,152,128]{2,1,0:T(8,128)(2,1)S(1)}, u32[]{:S(2)}, u32[]{:S(2)}) collective-permute-start(bf16[4,152,128]{2,1,0:T(8,128)(2,1)S(1)} %pad_maximum_fusion), channel_id=1, source_target_pairs={{0,4},{2,6},{4,0},{6,2},{8,12},{10,14},{12,8},{14,10},{16,20},{18,... | collective-permute-start | bytes 466952 | tf_op jit(solution)/shard_map/ppermute | solution.py:762
  23.4 13.9 %collective-permute-start.5 = (bf16[4,152,128]{2,1,0:T(8,128)(2,1)S(1)}, bf16[4,152,128]{2,1,0:T(8,128)(2,1)S(1)}, u32[]{:S(2)}, u32[]{:S(2)}) collective-permute-start(bf16[4,152,128]{2,1,0:T(8,128)(2,1)S(1)} %pad_maximum_fusion), channel_id=1, source_target_pairs={{0,6},{2,4},{4,2},{6,0},{8,14},{10,12},{12,10},{14,8},{16,22},{18,... | collective-permute-start | bytes 466952 | tf_op jit(solution)/shard_map/ppermute | solution.py:762
  37.3 2.1 %collective-permute-start.6 = (bf16[16,152,128]{2,1,0:T(8,128)(2,1)S(1)}, bf16[16,152,128]{2,1,0:T(8,128)(2,1)S(1)}, u32[]{:S(2)}, u32[]{:S(2)}) collective-permute-start(bf16[16,152,128]{2,1,0:T(8,128)(2,1)S(1)} %constant_dynamic-update-slice_fusion.own_ref), channel_id=1, source_target_pairs={{0,1},{1,0},{2,3},{3,2},{4,5},{5,4},{6,7},{7,6},{8,9},{9,8},{10,11... | collective-permute-start | bytes 1867784 | tf_op jit(solution)/shard_map/ppermute | solution.py:810
  40.4 18.8 %copy-start = (bf16[2048,256]{1,0:T(8,128)(2,1)}, bf16[2048,256]{1,0:T(8,128)(2,1)S(1)}, u32[]{:S(2)}) copy-start(bf16[2048,256]{1,0:T(8,128)(2,1)S(1)} %get-tuple-element.35.proj_ref.refs_2_.refs_6_) | copy-start | bytes 3145732
  50.2 1.4 %copy-start.5 = (f32[2048,256]{1,0:T(8,128)}, f32[2048,256]{1,0:T(8,128)S(1)}, u32[]{:S(2)}) copy-start(f32[2048,256]{1,0:T(8,128)S(1)} %get-tuple-element.45.refs_13_) | copy-start | bytes 6291460
  53.2 5.9 %copy-start.2 = (bf16[1,1,128,2048]{3,2,1,0:T(8,128)(2,1)S(1)}, bf16[1,1,128,2048]{3,2,1,0:T(8,128)(2,1)}, u32[]{:S(2)}) copy-start(bf16[1,1,128,2048]{3,2,1,0:T(8,128)(2,1)} %param.10) | copy-start | bytes 1572868
  53.2 6.0 %copy-start.4 = (bf16[1,1,128,2048]{3,2,1,0:T(8,128)(2,1)S(1)}, bf16[1,1,128,2048]{3,2,1,0:T(8,128)(2,1)}, u32[]{:S(2)}) copy-start(bf16[1,1,128,2048]{3,2,1,0:T(8,128)(2,1)} %param.11) | copy-start | bytes 1572868
  53.2 6.0 %copy-start.14 = (f32[32]{0:T(128)S(1)}, f32[32]{0:T(128)}, u32[]{:S(2)}) copy-start(f32[32]{0:T(128)} %param.17) | copy-start | bytes 388
  53.3 28.9 %all-to-all-start.1 = ((bf16[16,256,128]{2,1,0:T(8,128)(2,1)}), bf16[16,256,128]{2,1,0:T(8,128)(2,1)S(1)}, u32[]{:S(2)}, u32[]{:S(2)}) async-start(bf16[16,256,128]{2,1,0:T(8,128)(2,1)} %copy-done.7), calls=%async_computation.1 | async-start | bytes 2097152 | tf_op jit(solution)/shard_map/all_to_all | solution.py:40
  59.2 9.9 %copy-start.9 = (f32[32,2048]{1,0:T(8,128)S(1)}, f32[32,2048]{1,0:T(8,128)}, u32[]{:S(2)}) copy-start(f32[32,2048]{1,0:T(8,128)} %copy-done.8) | copy-start | bytes 786436
  59.2 9.9 %copy-start.15 = (f32[32]{0:T(128)S(1)}, f32[32]{0:T(128)}, u32[]{:S(2)}) copy-start(f32[32]{0:T(128)} %param.19) | copy-start | bytes 388
  63.9 2.8 %collective-permute-start.7 = (bf16[2048,128]{1,0:T(8,128)(2,1)S(1)}, bf16[2048,128]{1,0:T(8,128)(2,1)S(1)}, u32[]{:S(2)}, u32[]{:S(2)}) collective-permute-start(bf16[2048,128]{1,0:T(8,128)(2,1)S(1)} %get-tuple-element.43), channel_id=1, source_target_pairs={{0,1},{2,3},{4,5},{6,7},{8,9},{10,11},{12,13},{14,15},{16,17},{18,... | collective-permute-start | bytes 1572872 | tf_op jit(solution)/shard_map/ppermute | solution.py:569
  65.3 3.8 %collective-permute-start.8 = (bf16[2048,128]{1,0:T(8,128)(2,1)S(1)}, bf16[2048,128]{1,0:T(8,128)(2,1)S(1)}, u32[]{:S(2)}, u32[]{:S(2)}) collective-permute-start(bf16[2048,128]{1,0:T(8,128)(2,1)S(1)} %get-tuple-element.44), channel_id=1, source_target_pairs={{1,0},{3,2},{5,4},{7,6},{9,8},{11,10},{13,12},{15,14},{17,16},{19,... | collective-permute-start | bytes 1572872 | tf_op jit(solution)/shard_map/ppermute | solution.py:569
  79.8 2.1 %collective-permute-start.9 = (bf16[16,152,128]{2,1,0:T(8,128)(2,1)S(1)}, bf16[16,152,128]{2,1,0:T(8,128)(2,1)S(1)}, u32[]{:S(2)}, u32[]{:S(2)}) collective-permute-start(bf16[16,152,128]{2,1,0:T(8,128)(2,1)S(1)} %get-tuple-element.50), channel_id=1, source_target_pairs={{0,1},{1,0},{2,3},{3,2},{4,5},{5,4},{6,7},{7,6},{8,9},{9,8},{10,11... | collective-permute-start | bytes 1867784 | tf_op jit(solution)/shard_map/ppermute | solution.py:867
  107.3 3.1 %collective-permute-start.10 = (f32[152,128]{1,0:T(8,128)S(1)}, f32[152,128]{1,0:T(8,128)S(1)}, u32[]{:S(2)}, u32[]{:S(2)}) collective-permute-start(f32[152,128]{1,0:T(8,128)S(1)} %convert_reduce_fusion.own_ref), channel_id=1, source_target_pairs={{0,1},{1,0},{2,3},{3,2},{4,5},{5,4},{6,7},{7,6},{8,9},{9,8},{10,11... | collective-permute-start | bytes 233480 | tf_op jit(solution)/shard_map/ppermute | solution.py:871
  107.5 1.2 %copy-start.6 = (f32[128,2048]{1,0:T(8,128)S(1)}, f32[128,2048]{1,0:T(8,128)}, u32[]{:S(2)}) copy-start(f32[128,2048]{1,0:T(8,128)} %get-tuple-element.48.pre_ref) | copy-start | bytes 3145732
  (6 other events, 5.2 us)

commit v3 on v2

--- a/solution.py
+++ b/solution.py
@@ -143,39 +143,42 @@
     refs[1][:, sl] = low
 
 
-def from_sites(ref, j, sites, base):
-    rows = slice(base + j * sites, base + (j + 1) * sites)
-    return ref[:, rows, :].astype(f32).reshape(ref.shape[0] * sites, LANES)
-
-
-def to_sites(ref, j, sites, base, value):
-    rows = slice(base + j * sites, base + (j + 1) * sites)
-    ref[:, rows, :] = value.astype(f32).reshape(ref.shape[0], sites, LANES).astype(bf16)
-
-
-def pack_kernel(sites, tok_ref, grad_ref, sent_ref):
-    base = sent_ref.shape[1] // 2
-    for j, sl in blocks(tok_ref.shape[1]):
-        to_sites(sent_ref, j, sites, 0, tok_ref[:, sl])
-        to_sites(sent_ref, j, sites, base, grad_ref[:, sl])
-
-
-def payload_kernel(ids_ref, proj_ref, step_ref, active_ref, mod_ref, sent_ref):
+def start_kernel(ids_ref, tok_ref, grad_ref, proj_hbm, step_hbm, mod_hbm, active_ref, sent_ref, pay_ref,
+                 proj_ref, step_ref, mod_ref, sems):
+    copies = [
+        pltpu.make_async_copy(src, dst, sems.at[n])
+        for n, (src, dst) in enumerate(
+            [
+                (proj_hbm, proj_ref),
+                (step_hbm, step_ref),
+                (mod_hbm, mod_ref),
+                (tok_ref, sent_ref.at[:, 0]),
+                (grad_ref, sent_ref.at[:, 1]),
+            ]
+        )
+    ]
+    for copy in copies:
+        copy.start()
     row = ids_ref[1]
     part, pair = proj_ref.shape[0] // 2, proj_ref.shape[1]
+    copies[0].wait()
     own = proj_ref[pl.ds(pl.multiple_of(row * part, part), part), :]
     at = 0
     for _, sl in blocks(pair):
-        sent_ref[at : at + part, :] = own[:, sl]
+        pay_ref[at : at + part, :] = own[:, sl]
         at += part
+    copies[1].wait()
     part = step_ref.shape[0] // 2
-    sent_ref[at : at + part, :] = step_ref[pl.ds(pl.multiple_of(row * part, part), part), :]
+    pay_ref[at : at + part, :] = step_ref[pl.ds(pl.multiple_of(row * part, part), part), :]
     at += part
+    copies[2].wait()
     own = mm(active_ref[...], mod_ref[...], 1, 0)
     high = own.astype(bf16).astype(f32)
     pieces = [piece[:, sl] for piece in (high, own - high) for _, sl in blocks(own.shape[1])]
     pieces.append(jnp.zeros((8 - len(pieces), LANES), f32))
-    sent_ref[at : at + 8, :] = jnp.concatenate(pieces, axis=0).astype(bf16)
+    pay_ref[at : at + 8, :] = jnp.concatenate(pieces, axis=0).astype(bf16)
+    copies[3].wait()
+    copies[4].wait()
 
 
 def unpack_kernel(radix, ids_ref, own_ref, other_ref, proj_ref, step_ref, shift_ref, gain_ref):
@@ -230,21 +233,40 @@
 
 
 def site_fast_kernel(sites, got_ref, *refs):
-    inputs, outs, tok_ref, grad_ref, scratch = refs[:6], refs[6:10], refs[10], refs[11], refs[12:]
-    base = got_ref.shape[1] // 2
-    for j, sl in blocks(tok_ref.shape[1]):
-        tok_ref[:, sl] = from_sites(got_ref, j, sites, 0).astype(bf16)
-        grad_ref[:, sl] = from_sites(got_ref, j, sites, base).astype(bf16)
-    sent_ref = outs[0]
+    inputs, (sent_hbm, x_ref, dc_ref, dl_ref, gmod_ref) = refs[:6], refs[6:11]
+    tok_ref, grad_ref, sent_ref, sems = refs[11:15]
+    scratch = refs[15:]
+    frames, width = got_ref.shape[0], got_ref.shape[3]
+    for _, sl in blocks(width):
+        for ref, which in ((tok_ref, 0), (grad_ref, 1)):
+            value = got_ref[:, which, :, sl].astype(f32)
+            ref[:, sl] = value.reshape(frames * sites, LANES).astype(bf16)
+
+    parts = 2
+    share = width // parts
+    copies = []
+
+    def send(which, p):
+        at = (slice(None), which, slice(None), slice(p * share, (p + 1) * share))
+        copy = pltpu.make_async_copy(sent_ref.at[at], sent_hbm.at[at], sems.at[len(copies)])
+        copy.start()
+        copies.append(copy)
 
     class Packed:
-        def __init__(self, base):
-            self.base = base
+        def __init__(self, which):
+            self.which = which
 
         def __setitem__(self, at, value):
-            to_sites(sent_ref, at[1].start // LANES, sites, self.base, value)
-
-    site_kernel(sites, tok_ref, grad_ref, *inputs, Packed(0), Packed(base), *outs[1:], *scratch)
+            value = value.astype(f32).reshape(frames, sites, LANES)
+            sent_ref[:, self.which, :, at[1]] = value.astype(bf16)
+            if at[1].stop % share == 0:
+                send(self.which, at[1].stop // share - 1)
+
+    site_kernel(
+        sites, tok_ref, grad_ref, *inputs, Packed(0), Packed(1), dc_ref, dl_ref, gmod_ref, x_ref, *scratch
+    )
+    for copy in copies:
+        copy.wait()
 
 
 def site_kernel(
@@ -315,8 +337,17 @@
             rows = slice(c * (length // clips), (c + 1) * (length // clips))
             gmod_ref[c : c + 1, sl] = jnp.sum(back[rows], axis=0, keepdims=True)
             gmod_ref[clips + c : clips + c + 1, sl] = jnp.sum(scaled[rows], axis=0, keepdims=True)
-        gproj_ref[sl, :] = mm(x_ref[:, sl], d_coeffs, 0, 0)
-        gstep_ref[:, sl] = mm(d_logits, x_ref[:, sl], 0, 0)
+        if gproj_ref.shape == (width, 2 * state):
+            gproj_ref[sl, :] = mm(x_ref[:, sl], d_coeffs, 0, 0)
+            gstep_ref[:, sl] = mm(d_logits, x_ref[:, sl], 0, 0)
+    if gproj_ref.shape != (width, 2 * state):
+        gproj_ref[...] = d_coeffs
+        gstep_ref[...] = d_logits
+
+
+def band_fast_kernel(ids_ref, *refs):
+    give_ref = refs[-1]
+    band_kernel(*refs[:-1], None, give_ref, first=ids_ref[1] == 0)
 
 
 def band_kernel(
@@ -335,6 +366,7 @@
     decay_ref,
     end_ref,
     own_ref,
+    first=None,
 ):
     length, width = tok_ref.shape
     heads = step_ref.shape[0]
@@ -352,6 +384,14 @@
     lead = split(jnp.exp(last - cum) * step)
     reach = split(jnp.exp(cum) / state)
     b_part, c_part = coeffs[:, :state], coeffs[:, state:]
+    if first is not None:
+        gain = split(jnp.where(first, jnp.exp(last - cum) * step, jnp.exp(cum) / state))
+        other = jnp.where(first, b_part, c_part)
+        for _, sl in blocks(width):
+            value = jnp.where(first, x_ref[:, sl], grad_ref[:, sl]).astype(f32)
+            value = (value * expand(gain, lanes_of[:, sl])).astype(bf16)
+            own_ref[sl, :] = mm(value, other, 0, 0).astype(bf16)
+        return
     for _, sl in blocks(width):
         lead_wide = expand(lead, lanes_of[:, sl])
         reach_wide = expand(reach, lanes_of[:, sl])
@@ -361,43 +401,66 @@
         own_ref[sl, :] = mm(faded, c_part, 0, 0).astype(bf16)
 
 
-def space_fast_kernel(ids_ref, gmod_in, *refs):
-    inputs, mix_ref, pre_ref, keep_ref, give_ref = refs[:15], *refs[15:19]
-    gmod_ref, scratch = refs[19], refs[20:]
-    first = ids_ref[1] == 0
+def space_fast_kernel(radix, ids_ref, gmod_in, site_x, site_dc, site_dl, arrived_ref, *refs):
+    inputs, mix_ref, pre_ref, keep_ref, give_ref = refs[:11], *refs[11:15]
+    gmod_ref, scratch = refs[15], refs[16:]
+    me, first = ids_ref[0], ids_ref[1] == 0
     pair = inputs[6].shape[1]
     part, heads = LANES // 2, inputs[7].shape[0] // 2
     proj_rows = part * pair // LANES
 
+    def place(j):
+        offset = jnp.bitwise_xor(me, j)
+        return jnp.bitwise_and(offset, radix - 1) * radix + offset // radix
+
     class Halves:
         def __init__(self, at, part):
             self.at, self.part = at, part
 
         def __setitem__(self, where, value):
-            value = value.astype(f32)
             j = max(0 if w.start is None else w.start for w in where) // LANES
             own = jnp.where(first, value[: self.part], value[self.part :]).astype(bf16)
             other = jnp.where(first, value[self.part :], value[: self.part]).astype(bf16)
+            j = place(j)
             for k, sl in blocks(value.shape[1]):
                 rows = slice(self.at + k * self.part, self.at + (k + 1) * self.part)
                 keep_ref[j, rows, :] = own[:, sl]
                 give_ref[j, rows, :] = other[:, sl]
 
+    class Arrived:
+        def __init__(self, wanted):
+            self.wanted = wanted
+
+        def __getitem__(self, at):
+            value = arrived_ref[at]
+            return jnp.where(self.wanted, value, jnp.zeros_like(value))
+
     space_kernel(
-        *inputs, mix_ref, pre_ref, Halves(0, part), Halves(proj_rows, heads), gmod_ref, *scratch
+        *inputs,
+        Arrived(jnp.logical_not(first)),
+        Arrived(first),
+        (site_x, site_dc, site_dl),
+        None,
+        mix_ref,
+        pre_ref,
+        Halves(0, part),
+        Halves(proj_rows, heads),
+        gmod_ref,
+        *scratch,
     )
     at = proj_rows + heads
     count = pre_ref.shape[1] // LANES
-    for j in range(keep_ref.shape[0]):
+    frames = keep_ref.shape[0]
+    for j in range(frames):
         rows = []
-        for k in range(2 * count // keep_ref.shape[0]):
-            n = j * (2 * count // keep_ref.shape[0]) + k
+        for k in range(2 * count // frames):
+            n = j * (2 * count // frames) + k
             which, sl = n // count, slice(n % count * LANES, (n % count + 1) * LANES)
             rows.append(gmod_ref[which : which + 1, sl] + gmod_in[which : which + 1, sl])
         rows.append(jnp.zeros((8 - len(rows), LANES), f32))
         rows = jnp.concatenate(rows, axis=0).astype(bf16)
-        keep_ref[j, at : at + 8, :] = rows
-        give_ref[j, at : at + 8, :] = rows
+        keep_ref[place(j), at : at + 8, :] = rows
+        give_ref[place(j), at : at + 8, :] = rows
 
 
 def space_kernel(
@@ -487,6 +550,9 @@
         [mm(d_scores, c_part, 0, 0) + d_b, mm(d_scores, b_part, 1, 0) + d_c], axis=1
     ).astype(bf16)
     inverse = inverse_ref[...]
+    if gstep_in is None:
+        tall_coeffs = jnp.concatenate([gproj_in[1][...], d_coeffs], axis=0)
+        tall_logits = jnp.concatenate([gproj_in[2][...], d_logits], axis=0)
     for _, sl in blocks(width):
         pre = (
             dn_ref[:, sl].astype(f32)
@@ -497,8 +563,13 @@
         scaled = pre * (tok_ref[:, sl].astype(f32) * inverse)
         gmod_ref[0:1, sl] = jnp.sum(pre, axis=0, keepdims=True)
         gmod_ref[1:2, sl] = jnp.sum(scaled, axis=0, keepdims=True)
-        gproj_ref[sl, :] = (gproj_in[sl, :] + mm(x_ref[:, sl], d_coeffs, 0, 0)).astype(bf16)
-        gstep_ref[:, sl] = (gstep_in[:, sl] + mm(d_logits, x_ref[:, sl], 0, 0)).astype(bf16)
+        if gstep_in is None:
+            tall = jnp.concatenate([gproj_in[0][:, sl], x_ref[:, sl]], axis=0)
+            gproj_ref[sl, :] = mm(tall, tall_coeffs, 0, 0)
+            gstep_ref[:, sl] = mm(tall_logits, tall, 0, 0)
+        else:
+            gproj_ref[sl, :] = (gproj_in[sl, :] + mm(x_ref[:, sl], d_coeffs, 0, 0)).astype(bf16)
+            gstep_ref[:, sl] = (gstep_in[:, sl] + mm(d_logits, x_ref[:, sl], 0, 0)).astype(bf16)
 
 
 def last_kernel(tok_ref, inverse_ref, gain_ref, mix_ref, pre_ref, time_ref, back_ref, out_ref, dtok_ref):
@@ -516,32 +587,39 @@
         dtok_ref[:, sl] = (grad * inverse - tok_ref[:, sl].astype(f32) * inner).astype(bf16)
 
 
-def last_fast_kernel(sites, tok_ref, inverse_ref, gain_ref, mix_ref, pre_ref, came_ref, *outs):
-    base = came_ref.shape[1] // 2
-
+def last_fast_kernel(tok_ref, inverse_ref, gain_ref, mix_ref, pre_ref, came_ref, *outs):
     class Packed:
-        def __init__(self, base):
-            self.base = base
+        def __init__(self, which):
+            self.which = which
 
         def __getitem__(self, at):
-            return from_sites(came_ref, at[1].start // LANES, sites, self.base)
-
-    last_kernel(tok_ref, inverse_ref, gain_ref, mix_ref, pre_ref, Packed(0), Packed(base), *outs)
-
-
-def call(kernel, outs, scratch=(), name=None, ids=0):
-    shapes = [jax.ShapeDtypeStruct(s, d) for s, d in outs]
-    if ids:
-        whole = pl.BlockSpec(memory_space=pltpu.VMEM)
-        specs = [pl.BlockSpec(memory_space=pltpu.SMEM)] + [whole] * ids
-        specs = {"in_specs": specs, "out_specs": [whole] * len(outs)}
-    else:
-        specs = {}
+            value = came_ref[:, self.which, :, at[1]].astype(f32)
+            return value.reshape(value.shape[0] * value.shape[1], LANES)
+
+    last_kernel(tok_ref, inverse_ref, gain_ref, mix_ref, pre_ref, Packed(0), Packed(1), *outs)
+
+
+def in_hbm(array):
+    return pltpu.with_memory_space_constraint(array, pltpu.MemorySpace.HBM)
+
+
+def call(kernel, outs, scratch=(), name=None, specs=None, hbm_outs=()):
+    shapes = [
+        pltpu.MemorySpace.HBM(s, d) if n in hbm_outs else jax.ShapeDtypeStruct(s, d)
+        for n, (s, d) in enumerate(outs)
+    ]
+    where = {"s": pltpu.SMEM, "v": pltpu.VMEM, "h": pltpu.MemorySpace.HBM}
+    spaces = {}
+    if specs:
+        spaces["in_specs"] = [pl.BlockSpec(memory_space=where[c]) for c in specs]
+        spaces["out_specs"] = [
+            pl.BlockSpec(memory_space=where["h" if n in hbm_outs else "v"]) for n in range(len(outs))
+        ]
     return pl.pallas_call(
         kernel,
         out_shape=shapes,
-        **specs,
-        scratch_shapes=[pltpu.VMEM(s, d) for s, d in scratch],
+        **spaces,
+        scratch_shapes=[pltpu.VMEM(*s) if isinstance(s, tuple) else s for s in scratch],
         compiler_params=pltpu.CompilerParams(vmem_limit_bytes=48 << 20),
         name=name,
     )
@@ -767,6 +845,26 @@
     return jnp.concatenate(others(far, 1))
 
 
+def sum_over_frames(keep, given, radix):
+    def gathered(pieces, stride):
+        frames = radix * radix
+        return [pieces[0]] + [
+            lax.ppermute(pieces[d], "frame", [(i, i ^ (d * stride)) for i in range(frames)])
+            for d in range(1, radix)
+        ]
+
+    def total(pieces):
+        value = pieces[0].astype(f32)
+        for piece in pieces[1:]:
+            value = value + piece.astype(f32)
+        return value
+
+    parts = [slice(d * radix, (d + 1) * radix) for d in range(radix)]
+    near = [total([keep[p], given[p]]).astype(bf16) for p in parts]
+    near = total(gathered(near, 1)).astype(bf16)
+    return total(gathered([near[d] for d in range(radix)], radix))
+
+
 def per_device_fast(
     tokens,
     cotangent,
@@ -796,35 +894,59 @@
     bias = step_bias[None]
     swap = [(0, 1), (1, 0)]
 
-    packed = (frames, 2 * sites * width // LANES, LANES)
-    (sent,) = call(functools.partial(pack_kernel, sites), [(packed, bf16)], name="pack")(tok, grad)
-
-    timestep, sent = lax.optimization_barrier((timestep, sent))
+    packed = (frames, 2, sites, width)
+    size = depth // 2 * pair // LANES + heads // 2 + 8
+    activated = time_embed(timestep, mod_weight.shape[0]).astype(bf16)
+    sent, payload = call(
+        start_kernel,
+        [(packed, bf16), ((size, LANES), bf16)],
+        [
+            ((depth, pair), bf16),
+            ((heads, depth), bf16),
+            (mod_weight.shape, bf16),
+            pltpu.SemaphoreType.DMA((5,)),
+        ],
+        name="start",
+        specs="shhhhhv",
+        hbm_outs=(0,),
+    )(
+        ids,
+        in_hbm(tok.reshape(frames, sites, width)),
+        in_hbm(grad.reshape(frames, sites, width)),
+        in_hbm(proj_weight),
+        in_hbm(step_weight.T),
+        in_hbm(mod_weight),
+        activated,
+    )
     got = exchange(sent)
-    activated = time_embed(timestep, mod_weight.shape[0]).astype(bf16)
-    size = depth // 2 * pair // LANES + heads // 2 + 8
-    (payload,) = call(payload_kernel, [((size, LANES), bf16)], name="payload", ids=4)(
-        ids, proj_weight, step_weight.T, activated, mod_weight
-    )
     payload = spread_over_frames(payload)
     other = lax.ppermute(payload, "row", swap)
     proj_full, step_full, shift, gain = call(
         functools.partial(unpack_kernel, 4),
         [((width, pair), bf16), ((heads, width), bf16), ((1, width), f32), ((1, width), f32)],
         name="unpack",
-        ids=2,
+        specs="svv",
     )(ids, payload, other)
 
-    sent, gproj, gstep, site_gmod = call(
+    sent, site_x, site_dc, site_dl, site_gmod = call(
         functools.partial(site_fast_kernel, sites),
-        [(packed, bf16), ((width, pair), f32), ((heads, width), f32), ((2, width), f32)],
-        [(wide, bf16)] * 8,
+        [
+            (packed, bf16),
+            (wide, bf16),
+            ((length, pair), bf16),
+            ((length, heads), bf16),
+            ((2, width), f32),
+        ],
+        [(wide, bf16), (wide, bf16), (packed, bf16), pltpu.SemaphoreType.DMA((4,))]
+        + [(wide, bf16)] * 5,
         name="site",
+        specs="vvvvvvv",
+        hbm_outs=(0,),
     )(got, shift, gain, proj_full, step_full, bias, rate_time[None])
     came = exchange(sent)
 
-    normed, coeffs, logits, inverse, decay, end_own, start_grad = call(
-        band_kernel,
+    normed, coeffs, logits, inverse, _, give = call(
+        band_fast_kernel,
         [
             (wide, bf16),
             ((length, pair), bf16),
@@ -832,22 +954,25 @@
             ((length, 1), f32),
             ((1, heads), f32),
             ((width, state), bf16),
-            ((width, state), bf16),
         ],
         name="band",
-    )(tok, grad, shift, gain, proj_full, step_full, bias, rate_space[None])
-    state_in = chain(end_own, decay, True)
-    later_grad = chain(start_grad, decay, False)
+        specs="svvvvvvvv",
+    )(ids, tok, grad, shift, gain, proj_full, step_full, bias, rate_space[None])
+    arrived = lax.ppermute(give, "row", swap)
     halves = (frames, size, LANES)
     mix, pre, keep, give, _ = call(
-        space_fast_kernel,
+        functools.partial(space_fast_kernel, 4),
         [(wide, f32), (wide, f32), (halves, bf16), (halves, bf16), ((2, width), f32)],
         [(wide, bf16)] * 7,
         name="space",
-        ids=16,
+        specs="s" + "v" * 16,
     )(
         ids,
         site_gmod,
+        site_x,
+        site_dc,
+        site_dl,
+        arrived,
         tok,
         grad,
         normed,
@@ -859,25 +984,19 @@
         bias,
         rate_space[None],
         skip_gain[None],
-        state_in,
-        later_grad,
-        gproj,
-        gstep,
     )
     given = lax.ppermute(give, "row", swap)
-    terms = (keep.astype(f32) + given.astype(f32)).astype(bf16)
-    terms, came = lax.optimization_barrier((terms, came))
-    sums = jnp.sum(exchange(terms).astype(f32), axis=0)
-    other = lax.ppermute(sums, "row", swap)
+    terms = sum_over_frames(keep, given, 4)
+    other = lax.ppermute(terms, "row", swap)
     grad_proj, grad_step, grad_mod = call(
         functools.partial(finish_kernel, factor),
         [((depth, pair), f32), ((heads, depth), f32), ((mod_weight.shape[0], mod_cols), f32)],
         name="finish",
-        ids=3,
-    )(ids, sums, other, activated.astype(f32).T)
-    mixed, d_tokens = call(
-        functools.partial(last_fast_kernel, sites), [(wide, bf16), (wide, bf16)], name="last"
-    )(tok, inverse, gain, mix, pre, came)
+        specs="svvv",
+    )(ids, terms, other, activated.astype(f32).T)
+    mixed, d_tokens = call(last_fast_kernel, [(wide, bf16), (wide, bf16)], name="last")(
+        tok, inverse, gain, mix, pre, came
+    )
     return (mixed.reshape(tokens.shape), d_tokens.reshape(tokens.shape), grad_proj, grad_step.T, grad_mod)
 
 

time: 112 us -> 139 us (1.24)
  Pallas kernels: 28.1 us -> 60.7 us
  blocking collectives: 25 us -> 0 us
  waiting for transfers between devices: 23.1 us -> 33.7 us
  starting transfers between devices: 24.4 us -> 30.9 us
    pallas_call x6 -> x5, Pallas kernels: 25.7 us -> 58.3 us  [the longest x1 33.5 us: per_device_fast(): call(start_kernel, [(packed, bf16), ((size, LANES), bf16)], [((depth, pai...]
    all_to_all x1 -> x0, blocking collectives: 25 us -> none  [exchange(): lax.all_to_all(packed, 'frame', split_axis=0, concat_axis=0, tiled=True)]
    ppermute x3 -> x8, waiting for transfers between devices: 2.32 us -> 16 us  [the longest x6 15.6 us: gathered(): lax.ppermute(pieces[d], 'frame', [(i, i ^ d * stride) for i in range(fram...]
    ppermute x3 -> x8, starting transfers between devices: 2.85 us -> 8.21 us  [the longest x6 8.01 us: gathered(): lax.ppermute(pieces[d], 'frame', [(i, i ^ d * stride) for i in range(fram...]
    all_to_all x2, waiting for transfers between devices: 3.11 us -> 0.01 us  [exchange(): lax.all_to_all(packed, 'frame', split_axis=0, concat_axis=0, tiled=True)]
    unnamed x40 -> x48, local copies, waits for them, and re-layouts: 8.94 us -> 9.59 us
  transfers between devices with their start and end apart: 13 -> 18, of which waited for: 8 -> 10; matrix products, arithmetic and copies ran while one was open for 0% -> 0% of each run, Pallas kernels for 17% -> 19%
where the time goes in v3:
time: 139 us; the launch traced here: 138 us
  Pallas kernels  60.7 us (44%)
  waiting for transfers between devices  33.7 us (24%)
  starting transfers between devices  30.9 us (22%)
  local copies, waits for them, and re-layouts  9.77 us (7%)
  between operations  1.58 us (1%)
  other arithmetic  1.55 us (1%)
    pallas_call x1, Pallas kernels, per_device_fast(): call(start_kernel, [(packed, bf16), ((size, LANES), bf16)], [((depth, pai...  33.5 us
    ppermute x6, waiting for transfers between devices, gathered(): lax.ppermute(pieces[d], 'frame', [(i, i ^ d * stride) for i in range(fram...  15.6 us
    ppermute x6, waiting for transfers between devices, others(): lax.ppermute(piece, 'frame', [(i, i ^ d * stride) for i in range(frames)])  13.7 us
    all_to_all x2, starting transfers between devices, exchange(): lax.all_to_all(packed, 'frame', split_axis=0, concat_axis=0, tiled=True)  13.3 us
    pallas_call x1, Pallas kernels, per_device_fast(): call(functools.partial(space_fast_kernel, 4), [(wide, f32), (wide, f32),...  10.5 us
    unnamed x48, local copies, waits for them, and re-layouts  9.59 us
    ppermute x6, starting transfers between devices, others(): lax.ppermute(piece, 'frame', [(i, i ^ d * stride) for i in range(frames)])  9.26 us
    ppermute x6, starting transfers between devices, gathered(): lax.ppermute(pieces[d], 'frame', [(i, i ^ d * stride) for i in range(fram...  8.01 us
  transfers between devices with their start and end apart: 18, of which 10 were waited for; matrix products, arithmetic and copies ran while one was open for 0% of the time, Pallas kernels for 19%

profile of v3, /device:TPU:0, one launch (start us, length us, event | category | flops | bytes accessed | tf_op | source)
XLA Modules:
  0.0 138.3 jit_solution(4060523229992590019)
XLA Ops:
  2.5 33.5 %start.1 = (bf16[16,2,8,2048]{3,2,1,0:T(8,128)(2,1)}, bf16[152,128]{1,0:T(8,128)(2,1)S(1)}) custom-call(s32[2]{0:T(128)S(1)} %pad_add_fusion.ids_ref, bf16[16,8,2048]{2,1,0:T(8,128)(2,1)} %bitcast.42, bf16[16,8,2048]{2,1,0:T(8,128)(2,1)} %bitcast.46, bf16[128,256]{1,0:T(8,128)(2,1)} %proj_hbm.1, bf16[32,128]{1,0:T(8,128)(2,1)} %bitcast.60, ...), custom_call_target="tpu_custom_call" | custom-call | tf_op jit(solution)/shard_map/start/pallas_call | solution.py:900
  36.0 3.1 %collective-permute-start = (bf16[152,128]{1,0:T(8,128)(2,1)S(1)}, bf16[152,128]{1,0:T(8,128)(2,1)S(1)}, u32[]{:S(2)}, u32[]{:S(2)}) collective-permute-start(bf16[152,128]{1,0:T(8,128)(2,1)S(1)} %get-tuple-element.30), channel_id=1, source_target_pairs={{0,8},{2,10},{4,12},{6,14},{8,0},{10,2},{12,4},{14,6},{16,24},{18,... | collective-permute-start | bytes 116744 | tf_op jit(solution)/shard_map/ppermute | solution.py:840
  39.1 2.6 %collective-permute-start.1 = (bf16[152,128]{1,0:T(8,128)(2,1)S(1)}, bf16[152,128]{1,0:T(8,128)(2,1)S(1)}, u32[]{:S(2)}, u32[]{:S(2)}) collective-permute-start(bf16[152,128]{1,0:T(8,128)(2,1)S(1)} %get-tuple-element.30), channel_id=1, source_target_pairs={{0,16},{2,18},{4,20},{6,22},{8,24},{10,26},{12,28},{14,30},{16,0},... | collective-permute-start | bytes 116744 | tf_op jit(solution)/shard_map/ppermute | solution.py:840
  41.7 7.1 %all-to-all-start = ((bf16[16,2,8,2048]{3,2,1,0:T(8,128)(2,1)}), bf16[16,2,8,2048]{3,2,1,0:T(8,128)(2,1)S(1)}, u32[]{:S(2)}, u32[]{:S(2)}) async-start(bf16[16,2,8,2048]{3,2,1,0:T(8,128)(2,1)} %get-tuple-element.36), calls=%async_computation | async-start | bytes 2097152 | tf_op jit(solution)/shard_map/all_to_all | solution.py:40
  48.9 2.0 %collective-permute-start.3 = (bf16[4,152,128]{2,1,0:T(8,128)(2,1)S(1)}, bf16[4,152,128]{2,1,0:T(8,128)(2,1)S(1)}, u32[]{:S(2)}, u32[]{:S(2)}) collective-permute-start(bf16[4,152,128]{2,1,0:T(8,128)(2,1)S(1)} %pad_maximum_fusion), channel_id=1, source_target_pairs={{0,2},{2,0},{4,6},{6,4},{8,10},{10,8},{12,14},{14,12},{16,18},{18,... | collective-permute-start | bytes 466952 | tf_op jit(solution)/shard_map/ppermute | solution.py:840
  50.9 1.5 %collective-permute-start.4 = (bf16[4,152,128]{2,1,0:T(8,128)(2,1)S(1)}, bf16[4,152,128]{2,1,0:T(8,128)(2,1)S(1)}, u32[]{:S(2)}, u32[]{:S(2)}) collective-permute-start(bf16[4,152,128]{2,1,0:T(8,128)(2,1)S(1)} %pad_maximum_fusion), channel_id=1, source_target_pairs={{0,4},{2,6},{4,0},{6,2},{8,12},{10,14},{12,8},{14,10},{16,20},{18,... | collective-permute-start | bytes 466952 | tf_op jit(solution)/shard_map/ppermute | solution.py:840
  52.5 6.0 %collective-permute-done.3 = bf16[4,152,128]{2,1,0:T(8,128)(2,1)S(1)} collective-permute-done((bf16[4,152,128]{2,1,0:T(8,128)(2,1)S(1)}, bf16[4,152,128]{2,1,0:T(8,128)(2,1)S(1)}, u32[]{:S(2)}, u32[]{:S(2)}) %collective-permute-start.3) | collective-permute-done | bytes 155680 | tf_op jit(solution)/shard_map/ppermute | solution.py:840
  58.5 6.0 %collective-permute-done.4 = bf16[4,152,128]{2,1,0:T(8,128)(2,1)S(1)} collective-permute-done((bf16[4,152,128]{2,1,0:T(8,128)(2,1)S(1)}, bf16[4,152,128]{2,1,0:T(8,128)(2,1)S(1)}, u32[]{:S(2)}, u32[]{:S(2)}) %collective-permute-start.4) | collective-permute-done | bytes 155680 | tf_op jit(solution)/shard_map/ppermute | solution.py:840
  64.5 1.7 %collective-permute-done.5 = bf16[4,152,128]{2,1,0:T(8,128)(2,1)S(1)} collective-permute-done((bf16[4,152,128]{2,1,0:T(8,128)(2,1)S(1)}, bf16[4,152,128]{2,1,0:T(8,128)(2,1)S(1)}, u32[]{:S(2)}, u32[]{:S(2)}) %collective-permute-start.5) | collective-permute-done | bytes 155680 | tf_op jit(solution)/shard_map/ppermute | solution.py:840
  66.3 2.0 %collective-permute-done.6.other_ref = bf16[16,152,128]{2,1,0:T(8,128)(2,1)S(1)} collective-permute-done((bf16[16,152,128]{2,1,0:T(8,128)(2,1)S(1)}, bf16[16,152,128]{2,1,0:T(8,128)(2,1)S(1)}, u32[]{:S(2)}, u32[]{:S(2)}) %collective-permute-start.6) | collective-permute-done | bytes 622624 | tf_op jit(solution)/shard_map/ppermute | solution.py:923
  70.2 5.5 %band.1 = (bf16[128,2048]{1,0:T(8,128)(2,1)S(1)}, bf16[128,256]{1,0:T(8,128)(2,1)S(1)}, bf16[128,32]{1,0:T(8,128)(2,1)S(1)}, f32[128,1]{1,0:T(8,128)S(1)}, f32[1,32]{1,0:T(1,128)}, /*index=5*/bf16[2048,128]{1,0:T(8,128)(2,1)}) custom-call(s32[2]{0:T(128)S(1)} %pad_add_fusion.ids_ref, bf16[128,2048]{1,0:T(8,128)(2,1)S(1)} %bitcast.43, ...), custom_call_target="tpu_custom_call" | custom-call | tf_op jit(solution)/shard_map/band/pallas_call | solution.py:948
  78.0 7.2 %site.1 = (bf16[16,2,8,2048]{3,2,1,0:T(8,128)(2,1)}, bf16[128,2048]{1,0:T(8,128)(2,1)S(1)}, bf16[128,256]{1,0:T(8,128)(2,1)S(1)}, bf16[128,32]{1,0:T(8,128)(2,1)S(1)}, f32[2,2048]{1,0:T(2,128)S(1)}) custom-call(bf16[16,2,8,2048]{3,2,1,0:T(8,128)(2,1)S(1)} %all-to-all-done.got_ref, f32[1,2048]{1,0:T(1,128)S(1)} %get-tuple-element.31.refs_2_.refs_0_, ...), custom_call_target="tpu_custom_call" | custom-call | tf_op jit(solution)/shard_map/site/pallas_call | solution.py:931
  86.5 6.2 %all-to-all-start.1 = ((bf16[16,2,8,2048]{3,2,1,0:T(8,128)(2,1)}), bf16[16,2,8,2048]{3,2,1,0:T(8,128)(2,1)S(1)}, u32[]{:S(2)}, u32[]{:S(2)}) async-start(bf16[16,2,8,2048]{3,2,1,0:T(8,128)(2,1)} %get-tuple-element.47), calls=%async_computation.1 | async-start | bytes 2097152 | tf_op jit(solution)/shard_map/all_to_all | solution.py:40
  96.2 10.5 %space.1 = (f32[128,2048]{1,0:T(8,128)S(1)}, f32[128,2048]{1,0:T(8,128)}, bf16[16,152,128]{2,1,0:T(8,128)(2,1)S(1)}, bf16[16,152,128]{2,1,0:T(8,128)(2,1)S(1)}, f32[2,2048]{1,0:T(2,128)}) custom-call(s32[2]{0:T(128)S(1)} %copy-done.11, f32[2,2048]{1,0:T(2,128)S(1)} %copy-done.9, bf16[128,2048]{1,0:T(8,128)(2,1)S(1)} %copy-done.7, ...), custom_call_target="tpu_custom_call" | custom-call | tf_op jit(solution)/shard_map/space/pallas_call | solution.py:963
  106.8 2.0 %collective-permute-done.8 = bf16[16,152,128]{2,1,0:T(8,128)(2,1)S(1)} collective-permute-done((bf16[16,152,128]{2,1,0:T(8,128)(2,1)S(1)}, bf16[16,152,128]{2,1,0:T(8,128)(2,1)S(1)}, u32[]{:S(2)}, u32[]{:S(2)}) %collective-permute-start.8) | collective-permute-done | bytes 622624 | tf_op jit(solution)/shard_map/ppermute | solution.py:988
  108.9 2.0 %collective-permute-start.10 = (bf16[4,152,128]{2,1,0:T(8,128)(2,1)S(1)}, bf16[4,152,128]{2,1,0:T(8,128)(2,1)S(1)}, u32[]{:S(2)}, u32[]{:S(2)}) collective-permute-start(bf16[4,152,128]{2,1,0:T(8,128)(2,1)S(1)} %get-tuple-element.57), channel_id=1, source_target_pairs={{0,4},{2,6},{4,0},{6,2},{8,12},{10,14},{12,8},{14,10},{16,20},{18,... | collective-permute-start | bytes 466952 | tf_op jit(solution)/shard_map/ppermute | solution.py:852
  110.9 1.5 %collective-permute-start.11 = (bf16[4,152,128]{2,1,0:T(8,128)(2,1)S(1)}, bf16[4,152,128]{2,1,0:T(8,128)(2,1)S(1)}, u32[]{:S(2)}, u32[]{:S(2)}) collective-permute-start(bf16[4,152,128]{2,1,0:T(8,128)(2,1)S(1)} %get-tuple-element.56), channel_id=1, source_target_pairs={{0,6},{2,4},{4,2},{6,0},{8,14},{10,12},{12,10},{14,8},{16,22},{18,... | collective-permute-start | bytes 466952 | tf_op jit(solution)/shard_map/ppermute | solution.py:852
  112.5 8.9 %collective-permute-done.10 = bf16[4,152,128]{2,1,0:T(8,128)(2,1)S(1)} collective-permute-done((bf16[4,152,128]{2,1,0:T(8,128)(2,1)S(1)}, bf16[4,152,128]{2,1,0:T(8,128)(2,1)S(1)}, u32[]{:S(2)}, u32[]{:S(2)}) %collective-permute-start.10) | collective-permute-done | bytes 155680 | tf_op jit(solution)/shard_map/ppermute | solution.py:852
  122.8 1.7 %collective-permute-start.12 = (bf16[152,128]{1,0:T(8,128)(2,1)S(1)}, bf16[152,128]{1,0:T(8,128)(2,1)S(1)}, u32[]{:S(2)}, u32[]{:S(2)}) collective-permute-start(bf16[152,128]{1,0:T(8,128)(2,1)S(1)} %get-tuple-element.58), channel_id=1, source_target_pairs={{0,8},{2,10},{4,12},{6,14},{8,0},{10,2},{12,4},{14,6},{16,24},{18,... | collective-permute-start | bytes 116744 | tf_op jit(solution)/shard_map/ppermute | solution.py:852
  124.5 2.4 %collective-permute-start.13 = (bf16[152,128]{1,0:T(8,128)(2,1)S(1)}, bf16[152,128]{1,0:T(8,128)(2,1)S(1)}, u32[]{:S(2)}, u32[]{:S(2)}) collective-permute-start(bf16[152,128]{1,0:T(8,128)(2,1)S(1)} %get-tuple-element.60), channel_id=1, source_target_pairs={{0,16},{2,18},{4,20},{6,22},{8,24},{10,26},{12,28},{14,30},{16,0},... | collective-permute-start | bytes 116744 | tf_op jit(solution)/shard_map/ppermute | solution.py:852
  127.2 3.0 %collective-permute-done.13 = bf16[152,128]{1,0:T(8,128)(2,1)S(1)} collective-permute-done((bf16[152,128]{1,0:T(8,128)(2,1)S(1)}, bf16[152,128]{1,0:T(8,128)(2,1)S(1)}, u32[]{:S(2)}, u32[]{:S(2)}) %collective-permute-start.13) | collective-permute-done | bytes 38944 | tf_op jit(solution)/shard_map/ppermute | solution.py:852
  130.2 2.5 %collective-permute-done.14 = bf16[152,128]{1,0:T(8,128)(2,1)S(1)} collective-permute-done((bf16[152,128]{1,0:T(8,128)(2,1)S(1)}, bf16[152,128]{1,0:T(8,128)(2,1)S(1)}, u32[]{:S(2)}, u32[]{:S(2)}) %collective-permute-start.14) | collective-permute-done | bytes 38944 | tf_op jit(solution)/shard_map/ppermute | solution.py:852
  134.0 1.4 finish.1
  136.6 1.7 %last.1 = (bf16[128,2048]{1,0:T(8,128)(2,1)}, bf16[128,2048]{1,0:T(8,128)(2,1)}) custom-call(bf16[128,2048]{1,0:T(8,128)(2,1)S(1)} %bitcast.45, f32[128,1]{1,0:T(8,128)S(1)} %get-tuple-element.35.refs_5_.inverse_ref, f32[1,2048]{1,0:T(1,128)S(1)} %get-tuple-element.32.refs_3_.refs_1_.gain_ref, f32[128,2048]{1,0:T(8,128)S(1)} %get-tuple-element.45.mix_ref, ...), custom_call_target="tpu_custom_call" | custom-call | tf_op jit(solution)/shard_map/last/pallas_call | solution.py:997
  (79 shorter events, 15.0 us)
Async XLA Ops:
  2.5 66.9 %copy-start.10 = (s32[2]{0:T(128)}, s32[2]{0:T(128)S(1)}, u32[]{:S(2)}) copy-start(s32[2]{0:T(128)S(1)} %pad_add_fusion.ids_ref) | copy-start | bytes 28
  36.0 12.8 %collective-permute-start = (bf16[152,128]{1,0:T(8,128)(2,1)S(1)}, bf16[152,128]{1,0:T(8,128)(2,1)S(1)}, u32[]{:S(2)}, u32[]{:S(2)}) collective-permute-start(bf16[152,128]{1,0:T(8,128)(2,1)S(1)} %get-tuple-element.30), channel_id=1, source_target_pairs={{0,8},{2,10},{4,12},{6,14},{8,0},{10,2},{12,4},{14,6},{16,24},{18,... | collective-permute-start | bytes 116744 | tf_op jit(solution)/shard_map/ppermute | solution.py:840
  39.1 9.7 %collective-permute-start.1 = (bf16[152,128]{1,0:T(8,128)(2,1)S(1)}, bf16[152,128]{1,0:T(8,128)(2,1)S(1)}, u32[]{:S(2)}, u32[]{:S(2)}) collective-permute-start(bf16[152,128]{1,0:T(8,128)(2,1)S(1)} %get-tuple-element.30), channel_id=1, source_target_pairs={{0,16},{2,18},{4,20},{6,22},{8,24},{10,26},{12,28},{14,30},{16,0},... | collective-permute-start | bytes 116744 | tf_op jit(solution)/shard_map/ppermute | solution.py:840
  41.7 7.1 %collective-permute-start.2 = (bf16[152,128]{1,0:T(8,128)(2,1)S(1)}, bf16[152,128]{1,0:T(8,128)(2,1)S(1)}, u32[]{:S(2)}, u32[]{:S(2)}) collective-permute-start(bf16[152,128]{1,0:T(8,128)(2,1)S(1)} %get-tuple-element.30), channel_id=1, source_target_pairs={{0,24},{2,26},{4,28},{6,30},{8,16},{10,18},{12,20},{14,22},{16,8},... | collective-permute-start | bytes 116744 | tf_op jit(solution)/shard_map/ppermute | solution.py:840
  41.7 34.9 %all-to-all-start = ((bf16[16,2,8,2048]{3,2,1,0:T(8,128)(2,1)}), bf16[16,2,8,2048]{3,2,1,0:T(8,128)(2,1)S(1)}, u32[]{:S(2)}, u32[]{:S(2)}) async-start(bf16[16,2,8,2048]{3,2,1,0:T(8,128)(2,1)} %get-tuple-element.36), calls=%async_computation | async-start | bytes 2097152 | tf_op jit(solution)/shard_map/all_to_all | solution.py:40
  48.9 9.6 %collective-permute-start.3 = (bf16[4,152,128]{2,1,0:T(8,128)(2,1)S(1)}, bf16[4,152,128]{2,1,0:T(8,128)(2,1)S(1)}, u32[]{:S(2)}, u32[]{:S(2)}) collective-permute-start(bf16[4,152,128]{2,1,0:T(8,128)(2,1)S(1)} %pad_maximum_fusion), channel_id=1, source_target_pairs={{0,2},{2,0},{4,6},{6,4},{8,10},{10,8},{12,14},{14,12},{16,18},{18,... | collective-permute-start | bytes 466952 | tf_op jit(solution)/shard_map/ppermute | solution.py:840
  50.9 13.6 %collective-permute-start.4 = (bf16[4,152,128]{2,1,0:T(8,128)(2,1)S(1)}, bf16[4,152,128]{2,1,0:T(8,128)(2,1)S(1)}, u32[]{:S(2)}, u32[]{:S(2)}) collective-permute-start(bf16[4,152,128]{2,1,0:T(8,128)(2,1)S(1)} %pad_maximum_fusion), channel_id=1, source_target_pairs={{0,4},{2,6},{4,0},{6,2},{8,12},{10,14},{12,8},{14,10},{16,20},{18,... | collective-permute-start | bytes 466952 | tf_op jit(solution)/shard_map/ppermute | solution.py:840
  52.3 13.9 %collective-permute-start.5 = (bf16[4,152,128]{2,1,0:T(8,128)(2,1)S(1)}, bf16[4,152,128]{2,1,0:T(8,128)(2,1)S(1)}, u32[]{:S(2)}, u32[]{:S(2)}) collective-permute-start(bf16[4,152,128]{2,1,0:T(8,128)(2,1)S(1)} %pad_maximum_fusion), channel_id=1, source_target_pairs={{0,6},{2,4},{4,2},{6,0},{8,14},{10,12},{12,10},{14,8},{16,22},{18,... | collective-permute-start | bytes 466952 | tf_op jit(solution)/shard_map/ppermute | solution.py:840
  66.2 3.2 %copy-start.1 = (bf16[1,1,128,2048]{3,2,1,0:T(8,128)(2,1)S(1)}, bf16[1,1,128,2048]{3,2,1,0:T(8,128)(2,1)}, u32[]{:S(2)}) copy-start(bf16[1,1,128,2048]{3,2,1,0:T(8,128)(2,1)} %param.10) | copy-start | bytes 1572868
  66.3 3.2 %copy-start.2 = (bf16[1,1,128,2048]{3,2,1,0:T(8,128)(2,1)S(1)}, bf16[1,1,128,2048]{3,2,1,0:T(8,128)(2,1)}, u32[]{:S(2)}) copy-start(bf16[1,1,128,2048]{3,2,1,0:T(8,128)(2,1)} %param.11) | copy-start | bytes 1572868
  66.3 2.1 %collective-permute-start.6 = (bf16[16,152,128]{2,1,0:T(8,128)(2,1)S(1)}, bf16[16,152,128]{2,1,0:T(8,128)(2,1)S(1)}, u32[]{:S(2)}, u32[]{:S(2)}) collective-permute-start(bf16[16,152,128]{2,1,0:T(8,128)(2,1)S(1)} %constant_dynamic-update-slice_fusion.own_ref), channel_id=1, source_target_pairs={{0,1},{1,0},{2,3},{3,2},{4,5},{5,4},{6,7},{7,6},{8,9},{9,8},{10,11... | collective-permute-start | bytes 1867784 | tf_op jit(solution)/shard_map/ppermute | solution.py:923
  69.4 7.2 %copy-start = (bf16[2048,256]{1,0:T(8,128)(2,1)}, bf16[2048,256]{1,0:T(8,128)(2,1)S(1)}, u32[]{:S(2)}) copy-start(bf16[2048,256]{1,0:T(8,128)(2,1)S(1)} %get-tuple-element.33.refs_4_.refs_2_.refs_6_) | copy-start | bytes 3145732
  76.5 16.3 %collective-permute-start.7 = (bf16[2048,128]{1,0:T(8,128)(2,1)}, bf16[2048,128]{1,0:T(8,128)(2,1)}, u32[]{:S(2)}, u32[]{:S(2)}) collective-permute-start(bf16[2048,128]{1,0:T(8,128)(2,1)} %get-tuple-element.41), channel_id=1, source_target_pairs={{0,1},{1,0},{2,3},{3,2},{4,5},{5,4},{6,7},{7,6},{8,9},{9,8},{10,11... | collective-permute-start | bytes 1572872 | tf_op jit(solution)/shard_map/ppermute | solution.py:961
  86.5 6.3 %copy-start.16 = (f32[32]{0:T(128)S(1)}, f32[32]{0:T(128)}, u32[]{:S(2)}) copy-start(f32[32]{0:T(128)} %param.17) | copy-start | bytes 388
  86.5 48.8 %all-to-all-start.1 = ((bf16[16,2,8,2048]{3,2,1,0:T(8,128)(2,1)}), bf16[16,2,8,2048]{3,2,1,0:T(8,128)(2,1)S(1)}, u32[]{:S(2)}, u32[]{:S(2)}) async-start(bf16[16,2,8,2048]{3,2,1,0:T(8,128)(2,1)} %get-tuple-element.47), calls=%async_computation.1 | async-start | bytes 2097152 | tf_op jit(solution)/shard_map/all_to_all | solution.py:40
  106.7 2.1 %collective-permute-start.8 = (bf16[16,152,128]{2,1,0:T(8,128)(2,1)S(1)}, bf16[16,152,128]{2,1,0:T(8,128)(2,1)S(1)}, u32[]{:S(2)}, u32[]{:S(2)}) collective-permute-start(bf16[16,152,128]{2,1,0:T(8,128)(2,1)S(1)} %get-tuple-element.51), channel_id=1, source_target_pairs={{0,1},{1,0},{2,3},{3,2},{4,5},{5,4},{6,7},{7,6},{8,9},{9,8},{10,11... | collective-permute-start | bytes 1867784 | tf_op jit(solution)/shard_map/ppermute | solution.py:988
  108.9 12.4 %collective-permute-start.10 = (bf16[4,152,128]{2,1,0:T(8,128)(2,1)S(1)}, bf16[4,152,128]{2,1,0:T(8,128)(2,1)S(1)}, u32[]{:S(2)}, u32[]{:S(2)}) collective-permute-start(bf16[4,152,128]{2,1,0:T(8,128)(2,1)S(1)} %get-tuple-element.57), channel_id=1, source_target_pairs={{0,4},{2,6},{4,0},{6,2},{8,12},{10,14},{12,8},{14,10},{16,20},{18,... | collective-permute-start | bytes 466952 | tf_op jit(solution)/shard_map/ppermute | solution.py:852
  110.9 10.5 %collective-permute-start.11 = (bf16[4,152,128]{2,1,0:T(8,128)(2,1)S(1)}, bf16[4,152,128]{2,1,0:T(8,128)(2,1)S(1)}, u32[]{:S(2)}, u32[]{:S(2)}) collective-permute-start(bf16[4,152,128]{2,1,0:T(8,128)(2,1)S(1)} %get-tuple-element.56), channel_id=1, source_target_pairs={{0,6},{2,4},{4,2},{6,0},{8,14},{10,12},{12,10},{14,8},{16,22},{18,... | collective-permute-start | bytes 466952 | tf_op jit(solution)/shard_map/ppermute | solution.py:852
  112.4 10.3 %collective-permute-start.9 = (bf16[4,152,128]{2,1,0:T(8,128)(2,1)S(1)}, bf16[4,152,128]{2,1,0:T(8,128)(2,1)S(1)}, u32[]{:S(2)}, u32[]{:S(2)}) collective-permute-start(bf16[4,152,128]{2,1,0:T(8,128)(2,1)S(1)} %get-tuple-element.55), channel_id=1, source_target_pairs={{0,2},{2,0},{4,6},{6,4},{8,10},{10,8},{12,14},{14,12},{16,18},{18,... | collective-permute-start | bytes 466952 | tf_op jit(solution)/shard_map/ppermute | solution.py:852
  122.8 4.5 %collective-permute-start.12 = (bf16[152,128]{1,0:T(8,128)(2,1)S(1)}, bf16[152,128]{1,0:T(8,128)(2,1)S(1)}, u32[]{:S(2)}, u32[]{:S(2)}) collective-permute-start(bf16[152,128]{1,0:T(8,128)(2,1)S(1)} %get-tuple-element.58), channel_id=1, source_target_pairs={{0,8},{2,10},{4,12},{6,14},{8,0},{10,2},{12,4},{14,6},{16,24},{18,... | collective-permute-start | bytes 116744 | tf_op jit(solution)/shard_map/ppermute | solution.py:852
  124.5 5.7 %collective-permute-start.13 = (bf16[152,128]{1,0:T(8,128)(2,1)S(1)}, bf16[152,128]{1,0:T(8,128)(2,1)S(1)}, u32[]{:S(2)}, u32[]{:S(2)}) collective-permute-start(bf16[152,128]{1,0:T(8,128)(2,1)S(1)} %get-tuple-element.60), channel_id=1, source_target_pairs={{0,16},{2,18},{4,20},{6,22},{8,24},{10,26},{12,28},{14,30},{16,0},... | collective-permute-start | bytes 116744 | tf_op jit(solution)/shard_map/ppermute | solution.py:852
  126.9 5.8 %collective-permute-start.14 = (bf16[152,128]{1,0:T(8,128)(2,1)S(1)}, bf16[152,128]{1,0:T(8,128)(2,1)S(1)}, u32[]{:S(2)}, u32[]{:S(2)}) collective-permute-start(bf16[152,128]{1,0:T(8,128)(2,1)S(1)} %get-tuple-element.59), channel_id=1, source_target_pairs={{0,24},{2,26},{4,28},{6,30},{8,16},{10,18},{12,20},{14,22},{16,8},... | collective-permute-start | bytes 116744 | tf_op jit(solution)/shard_map/ppermute | solution.py:852
  132.7 1.3 collective-permute-start.15
  135.4 1.2 copy-start.3
  (15 other events, 11.1 us)

commit v4 on v3

--- a/solution.py
+++ b/solution.py
@@ -7,6 +7,7 @@
 from jax.experimental import pallas as pl
 from jax.experimental.pallas import tpu as pltpu
 from jax.sharding import PartitionSpec as P
+
 
 norm_eps = 1e-05
 LANES = 128
@@ -144,7 +145,7 @@
 
 
 def start_kernel(ids_ref, tok_ref, grad_ref, proj_hbm, step_hbm, mod_hbm, active_ref, sent_ref, pay_ref,
-                 proj_ref, step_ref, mod_ref, sems):
+                 proj_ref, step_ref, mod_ref, both_ref, sems):
     copies = [
         pltpu.make_async_copy(src, dst, sems.at[n])
         for n, (src, dst) in enumerate(
@@ -152,13 +153,19 @@
                 (proj_hbm, proj_ref),
                 (step_hbm, step_ref),
                 (mod_hbm, mod_ref),
-                (tok_ref, sent_ref.at[:, 0]),
-                (grad_ref, sent_ref.at[:, 1]),
+                (tok_ref, both_ref.at[:, 0]),
+                (grad_ref, both_ref.at[:, 1]),
+                (both_ref.at[:, 0], sent_ref.at[:, 0]),
+                (both_ref.at[:, 1], sent_ref.at[:, 1]),
             ]
         )
     ]
-    for copy in copies:
+    for copy in copies[:5]:
         copy.start()
+    copies[3].wait()
+    copies[5].start()
+    copies[4].wait()
+    copies[6].start()
     row = ids_ref[1]
     part, pair = proj_ref.shape[0] // 2, proj_ref.shape[1]
     copies[0].wait()
@@ -177,8 +184,8 @@
     pieces = [piece[:, sl] for piece in (high, own - high) for _, sl in blocks(own.shape[1])]
     pieces.append(jnp.zeros((8 - len(pieces), LANES), f32))
     pay_ref[at : at + 8, :] = jnp.concatenate(pieces, axis=0).astype(bf16)
-    copies[3].wait()
-    copies[4].wait()
+    copies[5].wait()
+    copies[6].wait()
 
 
 def unpack_kernel(radix, ids_ref, own_ref, other_ref, proj_ref, step_ref, shift_ref, gain_ref):
@@ -233,9 +240,9 @@
 
 
 def site_fast_kernel(sites, got_ref, *refs):
-    inputs, (sent_hbm, x_ref, dc_ref, dl_ref, gmod_ref) = refs[:6], refs[6:11]
-    tok_ref, grad_ref, sent_ref, sems = refs[11:15]
-    scratch = refs[15:]
+    inputs, (sent_hbm, x_hbm, gmod_hbm, dc_ref, dl_ref) = refs[:6], refs[6:11]
+    tok_ref, grad_ref, sent_ref, x_ref, gmod_ref, sems = refs[11:17]
+    scratch = refs[17:]
     frames, width = got_ref.shape[0], got_ref.shape[3]
     for _, sl in blocks(width):
         for ref, which in ((tok_ref, 0), (grad_ref, 1)):
@@ -246,17 +253,22 @@
     share = width // parts
     copies = []
 
+    def begin(source, target):
+        copy = pltpu.make_async_copy(source, target, sems.at[len(copies)])
+        copy.start()
+        copies.append(copy)
+
     def send(which, p):
         at = (slice(None), which, slice(None), slice(p * share, (p + 1) * share))
-        copy = pltpu.make_async_copy(sent_ref.at[at], sent_hbm.at[at], sems.at[len(copies)])
-        copy.start()
-        copies.append(copy)
+        begin(sent_ref.at[at], sent_hbm.at[at])
 
     class Packed:
         def __init__(self, which):
             self.which = which
 
         def __setitem__(self, at, value):
+            if not copies:
+                begin(x_ref, x_hbm)
             value = value.astype(f32).reshape(frames, sites, LANES)
             sent_ref[:, self.which, :, at[1]] = value.astype(bf16)
             if at[1].stop % share == 0:
@@ -265,6 +277,7 @@
     site_kernel(
         sites, tok_ref, grad_ref, *inputs, Packed(0), Packed(1), dc_ref, dl_ref, gmod_ref, x_ref, *scratch
     )
+    begin(gmod_ref, gmod_hbm)
     for copy in copies:
         copy.wait()
 
@@ -401,31 +414,45 @@
         own_ref[sl, :] = mm(faded, c_part, 0, 0).astype(bf16)
 
 
-def space_fast_kernel(radix, ids_ref, gmod_in, site_x, site_dc, site_dl, arrived_ref, *refs):
-    inputs, mix_ref, pre_ref, keep_ref, give_ref = refs[:11], *refs[11:15]
-    gmod_ref, scratch = refs[15], refs[16:]
+def terms_kernel(radix, ids_ref, x_ref, dc_ref, dl_ref, gmod_ref, site_x, site_dc, site_dl, site_gmod,
+                 keep_ref, give_ref):
     me, first = ids_ref[0], ids_ref[1] == 0
-    pair = inputs[6].shape[1]
-    part, heads = LANES // 2, inputs[7].shape[0] // 2
-    proj_rows = part * pair // LANES
-
-    def place(j):
+    width = x_ref.shape[1]
+    coeffs = jnp.concatenate([dc_ref[...], site_dc[...]], axis=0)
+    logits = jnp.concatenate([dl_ref[...], site_dl[...]], axis=0)
+    frames = keep_ref.shape[0]
+    share = 2 * width // LANES // frames
+
+    def put_halves(j, at, value):
+        part = value.shape[0] // 2
+        own = jnp.where(first, value[:part], value[part:]).astype(bf16)
+        other = jnp.where(first, value[part:], value[:part]).astype(bf16)
+        for _, sl in blocks(value.shape[1]):
+            keep_ref[j, at : at + part, :] = own[:, sl]
+            give_ref[j, at : at + part, :] = other[:, sl]
+            at += part
+        return at
+
+    for j, sl in blocks(width):
         offset = jnp.bitwise_xor(me, j)
-        return jnp.bitwise_and(offset, radix - 1) * radix + offset // radix
-
-    class Halves:
-        def __init__(self, at, part):
-            self.at, self.part = at, part
-
-        def __setitem__(self, where, value):
-            j = max(0 if w.start is None else w.start for w in where) // LANES
-            own = jnp.where(first, value[: self.part], value[self.part :]).astype(bf16)
-            other = jnp.where(first, value[self.part :], value[: self.part]).astype(bf16)
-            j = place(j)
-            for k, sl in blocks(value.shape[1]):
-                rows = slice(self.at + k * self.part, self.at + (k + 1) * self.part)
-                keep_ref[j, rows, :] = own[:, sl]
-                give_ref[j, rows, :] = other[:, sl]
+        place = jnp.bitwise_and(offset, radix - 1) * radix + offset // radix
+        tall = jnp.concatenate([x_ref[:, sl], site_x[:, sl]], axis=0)
+        at = put_halves(place, 0, mm(tall, coeffs, 0, 0))
+        at = put_halves(place, at, mm(logits, tall, 0, 0))
+        rows = []
+        for n in range(j * share, (j + 1) * share):
+            which, at_lane = n // (width // LANES), n % (width // LANES) * LANES
+            lanes = slice(at_lane, at_lane + LANES)
+            rows.append(gmod_ref[which : which + 1, lanes] + site_gmod[which : which + 1, lanes])
+        rows.append(jnp.zeros((8 - len(rows), LANES), f32))
+        rows = jnp.concatenate(rows, axis=0).astype(bf16)
+        keep_ref[place, at : at + 8, :] = rows
+        give_ref[place, at : at + 8, :] = rows
+
+
+def space_fast_kernel(ids_ref, arrived_ref, *refs):
+    inputs, outs = refs[:11], refs[11:]
+    first = ids_ref[1] == 0
 
     class Arrived:
         def __init__(self, wanted):
@@ -435,32 +462,7 @@
             value = arrived_ref[at]
             return jnp.where(self.wanted, value, jnp.zeros_like(value))
 
-    space_kernel(
-        *inputs,
-        Arrived(jnp.logical_not(first)),
-        Arrived(first),
-        (site_x, site_dc, site_dl),
-        None,
-        mix_ref,
-        pre_ref,
-        Halves(0, part),
-        Halves(proj_rows, heads),
-        gmod_ref,
-        *scratch,
-    )
-    at = proj_rows + heads
-    count = pre_ref.shape[1] // LANES
-    frames = keep_ref.shape[0]
-    for j in range(frames):
-        rows = []
-        for k in range(2 * count // frames):
-            n = j * (2 * count // frames) + k
-            which, sl = n // count, slice(n % count * LANES, (n % count + 1) * LANES)
-            rows.append(gmod_ref[which : which + 1, sl] + gmod_in[which : which + 1, sl])
-        rows.append(jnp.zeros((8 - len(rows), LANES), f32))
-        rows = jnp.concatenate(rows, axis=0).astype(bf16)
-        keep_ref[place(j), at : at + 8, :] = rows
-        give_ref[place(j), at : at + 8, :] = rows
+    space_kernel(*inputs, Arrived(jnp.logical_not(first)), Arrived(first), None, None, *outs)
 
 
 def space_kernel(
@@ -550,9 +552,9 @@
         [mm(d_scores, c_part, 0, 0) + d_b, mm(d_scores, b_part, 1, 0) + d_c], axis=1
     ).astype(bf16)
     inverse = inverse_ref[...]
-    if gstep_in is None:
-        tall_coeffs = jnp.concatenate([gproj_in[1][...], d_coeffs], axis=0)
-        tall_logits = jnp.concatenate([gproj_in[2][...], d_logits], axis=0)
+    if gproj_in is None:
+        gproj_ref[...] = d_coeffs
+        gstep_ref[...] = d_logits
     for _, sl in blocks(width):
         pre = (
             dn_ref[:, sl].astype(f32)
@@ -563,11 +565,7 @@
         scaled = pre * (tok_ref[:, sl].astype(f32) * inverse)
         gmod_ref[0:1, sl] = jnp.sum(pre, axis=0, keepdims=True)
         gmod_ref[1:2, sl] = jnp.sum(scaled, axis=0, keepdims=True)
-        if gstep_in is None:
-            tall = jnp.concatenate([gproj_in[0][:, sl], x_ref[:, sl]], axis=0)
-            gproj_ref[sl, :] = mm(tall, tall_coeffs, 0, 0)
-            gstep_ref[:, sl] = mm(tall_logits, tall, 0, 0)
-        else:
+        if gproj_in is not None:
             gproj_ref[sl, :] = (gproj_in[sl, :] + mm(x_ref[:, sl], d_coeffs, 0, 0)).astype(bf16)
             gstep_ref[:, sl] = (gstep_in[:, sl] + mm(d_logits, x_ref[:, sl], 0, 0)).astype(bf16)
 
@@ -603,7 +601,7 @@
     return pltpu.with_memory_space_constraint(array, pltpu.MemorySpace.HBM)
 
 
-def call(kernel, outs, scratch=(), name=None, specs=None, hbm_outs=()):
+def call(kernel, outs, scratch=(), specs=None, hbm_outs=()):
     shapes = [
         pltpu.MemorySpace.HBM(s, d) if n in hbm_outs else jax.ShapeDtypeStruct(s, d)
         for n, (s, d) in enumerate(outs)
@@ -620,8 +618,7 @@
         out_shape=shapes,
         **spaces,
         scratch_shapes=[pltpu.VMEM(*s) if isinstance(s, tuple) else s for s in scratch],
-        compiler_params=pltpu.CompilerParams(vmem_limit_bytes=48 << 20),
-        name=name,
+        compiler_params=pltpu.CompilerParams(vmem_limit_bytes=24 << 20),
     )
 
 
@@ -730,7 +727,6 @@
         functools.partial(site_kernel, sites),
         [(wide, bf16), (wide, bf16), ((width, pair), f32), ((heads, width), f32), ((2 * clips, width), f32)],
         [(wide, bf16)] * 6,
-        name="site",
     )(site_tok, site_grad, shift, gain, proj_full, step_full, bias, rate_time[None])
 
     came = exchange(
@@ -758,7 +754,6 @@
             ((width, state), bf16),
             ((width, state), bf16),
         ],
-        name="band",
     )(tok, grad, own_shift, own_gain, proj_full, step_full, bias, rate_space[None])
     state_in = chain(end_own, decay, True)
     later_grad = chain(start_grad, decay, False)
@@ -766,7 +761,6 @@
         space_kernel,
         [(wide, f32), (wide, f32), ((width, pair), bf16), ((heads, width), bf16), ((2, width), f32)],
         [(wide, bf16)] * 7,
-        name="space",
     )(
         tok,
         grad,
@@ -811,7 +805,7 @@
     mod_sum = sums[0, at : at + size].reshape(clips, mod_cols)
     grad_mod = jnp.dot(activated.astype(f32).T, mod_sum, precision=EXACT)
 
-    mixed, d_tokens = call(last_kernel, [(wide, bf16), (wide, bf16)], name="last")(
+    mixed, d_tokens = call(last_kernel, [(wide, bf16), (wide, bf16)])(
         tok, inverse, own_gain, mix, pre, time_out, time_back
     )
     return (mixed.reshape(tokens.shape), d_tokens.reshape(tokens.shape), grad_proj, grad_step, grad_mod)
@@ -832,7 +826,7 @@
     )
 
 
-def spread_over_frames(own, radix=4):
+def spread_over_frames(own, sent, radix=4):
     frames = radix * radix
 
     def others(piece, stride):
@@ -842,7 +836,10 @@
         ]
 
     far = jnp.stack(others(own, radix))
-    return jnp.concatenate(others(far, 1))
+    far, sent = lax.optimization_barrier((far, sent))
+    pieces = others(far, 1)
+    got = exchange(sent)
+    return jnp.concatenate(pieces), got
 
 
 def sum_over_frames(keep, given, radix):
@@ -904,9 +901,9 @@
             ((depth, pair), bf16),
             ((heads, depth), bf16),
             (mod_weight.shape, bf16),
-            pltpu.SemaphoreType.DMA((5,)),
+            (packed, bf16),
+            pltpu.SemaphoreType.DMA((7,)),
         ],
-        name="start",
         specs="shhhhhv",
         hbm_outs=(0,),
     )(
@@ -918,32 +915,13 @@
         in_hbm(mod_weight),
         activated,
     )
-    got = exchange(sent)
-    payload = spread_over_frames(payload)
+    payload, got = spread_over_frames(payload, sent)
     other = lax.ppermute(payload, "row", swap)
     proj_full, step_full, shift, gain = call(
         functools.partial(unpack_kernel, 4),
         [((width, pair), bf16), ((heads, width), bf16), ((1, width), f32), ((1, width), f32)],
-        name="unpack",
         specs="svv",
     )(ids, payload, other)
-
-    sent, site_x, site_dc, site_dl, site_gmod = call(
-        functools.partial(site_fast_kernel, sites),
-        [
-            (packed, bf16),
-            (wide, bf16),
-            ((length, pair), bf16),
-            ((length, heads), bf16),
-            ((2, width), f32),
-        ],
-        [(wide, bf16), (wide, bf16), (packed, bf16), pltpu.SemaphoreType.DMA((4,))]
-        + [(wide, bf16)] * 5,
-        name="site",
-        specs="vvvvvvv",
-        hbm_outs=(0,),
-    )(got, shift, gain, proj_full, step_full, bias, rate_time[None])
-    came = exchange(sent)
 
     normed, coeffs, logits, inverse, _, give = call(
         band_fast_kernel,
@@ -955,23 +933,17 @@
             ((1, heads), f32),
             ((width, state), bf16),
         ],
-        name="band",
         specs="svvvvvvvv",
     )(ids, tok, grad, shift, gain, proj_full, step_full, bias, rate_space[None])
     arrived = lax.ppermute(give, "row", swap)
     halves = (frames, size, LANES)
-    mix, pre, keep, give, _ = call(
-        functools.partial(space_fast_kernel, 4),
-        [(wide, f32), (wide, f32), (halves, bf16), (halves, bf16), ((2, width), f32)],
+    mix, pre, own_dc, own_dl, gmod = call(
+        space_fast_kernel,
+        [(wide, f32), (wide, f32), ((length, pair), bf16), ((length, heads), bf16), ((2, width), f32)],
         [(wide, bf16)] * 7,
-        name="space",
-        specs="s" + "v" * 16,
+        specs="s" + "v" * 12,
     )(
         ids,
-        site_gmod,
-        site_x,
-        site_dc,
-        site_dl,
         arrived,
         tok,
         grad,
@@ -985,16 +957,42 @@
         rate_space[None],
         skip_gain[None],
     )
+    got, own_dc = lax.optimization_barrier((got, own_dc))
+    sent, site_x, site_gmod, site_dc, site_dl = call(
+        functools.partial(site_fast_kernel, sites),
+        [
+            (packed, bf16),
+            (wide, bf16),
+            ((2, width), f32),
+            ((length, pair), bf16),
+            ((length, heads), bf16),
+        ],
+        [
+            (wide, bf16),
+            (wide, bf16),
+            (packed, bf16),
+            (wide, bf16),
+            ((2, width), f32),
+            pltpu.SemaphoreType.DMA((6,)),
+        ]
+        + [(wide, bf16)] * 5,
+        specs="vvvvvvv",
+        hbm_outs=(0, 1, 2),
+    )(got, shift, gain, proj_full, step_full, bias, rate_time[None])
+    came = exchange(sent)
+
+    keep, give = call(
+        functools.partial(terms_kernel, 4), [(halves, bf16), (halves, bf16)], specs="svvvvvvvv"
+    )(ids, normed, own_dc, own_dl, gmod, site_x, site_dc, site_dl, site_gmod)
     given = lax.ppermute(give, "row", swap)
     terms = sum_over_frames(keep, given, 4)
     other = lax.ppermute(terms, "row", swap)
     grad_proj, grad_step, grad_mod = call(
         functools.partial(finish_kernel, factor),
         [((depth, pair), f32), ((heads, depth), f32), ((mod_weight.shape[0], mod_cols), f32)],
-        name="finish",
         specs="svvv",
     )(ids, terms, other, activated.astype(f32).T)
-    mixed, d_tokens = call(last_fast_kernel, [(wide, bf16), (wide, bf16)], name="last")(
+    mixed, d_tokens = call(last_fast_kernel, [(wide, bf16), (wide, bf16)])(
         tok, inverse, gain, mix, pre, came
     )
     return (mixed.reshape(tokens.shape), d_tokens.reshape(tokens.shape), grad_proj, grad_step.T, grad_mod)

time: 139 us -> 113 us (0.81)
  Pallas kernels: 60.7 us -> 28.7 us
  waiting for transfers between devices: 33.7 us -> 44.6 us
  local copies, waits for them, and re-layouts: 9.77 us -> 7.29 us
  starting transfers between devices: 30.9 us -> 29 us
    pallas_call x1, Pallas kernels: 33.5 us -> 2.75 us  [per_device_fast(): call(start_kernel, [(packed, bf16), ((size, LANES), bf16)], [((depth, pai...]
    ppermute x6, waiting for transfers between devices: 13.7 us -> 19.6 us  [others(): lax.ppermute(piece, 'frame', [(i, i ^ d * stride) for i in range(frames)])]
    all_to_all x2, starting transfers between devices: 13.3 us -> 9.27 us  [exchange(): lax.all_to_all(packed, 'frame', split_axis=0, concat_axis=0, tiled=True)]
    ppermute x6, waiting for transfers between devices: 15.6 us -> 18.7 us  [gathered(): lax.ppermute(pieces[d], 'frame', [(i, i ^ d * stride) for i in range(fram...]
    unnamed x48 -> x41, local copies, waits for them, and re-layouts: 9.59 us -> 7.12 us
    ppermute x6, starting transfers between devices: 8.01 us -> 10.1 us  [gathered(): lax.ppermute(pieces[d], 'frame', [(i, i ^ d * stride) for i in range(fram...]
    ppermute x1, waiting for transfers between devices: 0.01 us -> 1.79 us  [per_device_fast(): arrived = lax.ppermute(give, 'row', swap)]
    pallas_call x2 -> x3, Pallas kernels: 12.2 us -> 11.2 us  [the longest x1 8.21 us: per_device_fast(): call(space_fast_kernel, [(wide, f32), (wide, f32), ((length, pair), bf16)...]
  transfers between devices with their start and end apart: 18 -> 18, of which waited for: 10 -> 14; matrix products, arithmetic and copies ran while one was open for 0% -> 0% of each run, Pallas kernels for 19% -> 15%
where the time goes in v4:
time: 113 us
  waiting for transfers between devices  44.6 us (39%)
  starting transfers between devices  29 us (26%)
  Pallas kernels  28.7 us (25%)
  local copies, waits for them, and re-layouts  7.29 us (6%)
  between operations  1.57 us (1%)
  other arithmetic  1.52 us (1%)
    ppermute x6, waiting for transfers between devices, others(): lax.ppermute(piece, 'frame', [(i, i ^ d * stride) for i in range(frames)])  19.6 us
    ppermute x6, waiting for transfers between devices, gathered(): lax.ppermute(pieces[d], 'frame', [(i, i ^ d * stride) for i in range(fram...  18.7 us
    ppermute x6, starting transfers between devices, gathered(): lax.ppermute(pieces[d], 'frame', [(i, i ^ d * stride) for i in range(fram...  10.1 us
    ppermute x6, starting transfers between devices, others(): lax.ppermute(piece, 'frame', [(i, i ^ d * stride) for i in range(frames)])  9.33 us
    all_to_all x2, starting transfers between devices, exchange(): lax.all_to_all(packed, 'frame', split_axis=0, concat_axis=0, tiled=True)  9.27 us
    pallas_call x1, Pallas kernels, per_device_fast(): call(space_fast_kernel, [(wide, f32), (wide, f32), ((length, pair), bf16)...  8.21 us
    pallas_call x1, Pallas kernels, per_device_fast(): call(functools.partial(site_fast_kernel, sites), [(packed, bf16), (wide,...  7.34 us
    unnamed x41, local copies, waits for them, and re-layouts  7.12 us
  transfers between devices with their start and end apart: 18, of which 14 were waited for; matrix products, arithmetic and copies ran while one was open for 0% of the time, Pallas kernels for 15%

profile of v4, /device:TPU:0, one launch (start us, length us, event | category | flops | bytes accessed | tf_op | source)
XLA Modules:
  0.0 112.7 jit_solution(5384831725099726424)
XLA Ops:
  2.5 2.7 %shard_map.137 = (bf16[16,2,8,2048]{3,2,1,0:T(8,128)(2,1)}, bf16[152,128]{1,0:T(8,128)(2,1)S(1)}) custom-call(s32[2]{0:T(128)S(1)} %pad_add_fusion.ids_ref, bf16[16,8,2048]{2,1,0:T(8,128)(2,1)} %bitcast.38, bf16[16,8,2048]{2,1,0:T(8,128)(2,1)} %bitcast.42, bf16[128,256]{1,0:T(8,128)(2,1)} %proj_hbm.1, bf16[32,128]{1,0:T(8,128)(2,1)} %bitcast.56, ...), custom_call_target="tpu_custom_call" | custom-call | tf_op jit(solution)/shard_map/pallas_call | solution.py:897
  5.3 3.1 %collective-permute-start = (bf16[152,128]{1,0:T(8,128)(2,1)S(1)}, bf16[152,128]{1,0:T(8,128)(2,1)S(1)}, u32[]{:S(2)}, u32[]{:S(2)}) collective-permute-start(bf16[152,128]{1,0:T(8,128)(2,1)S(1)} %get-tuple-element.37), channel_id=1, source_target_pairs={{0,8},{2,10},{4,12},{6,14},{8,0},{10,2},{12,4},{14,6},{16,24},{18,... | collective-permute-start | bytes 116744 | tf_op jit(solution)/shard_map/ppermute | solution.py:834
  8.4 2.6 %collective-permute-start.1 = (bf16[152,128]{1,0:T(8,128)(2,1)S(1)}, bf16[152,128]{1,0:T(8,128)(2,1)S(1)}, u32[]{:S(2)}, u32[]{:S(2)}) collective-permute-start(bf16[152,128]{1,0:T(8,128)(2,1)S(1)} %get-tuple-element.37), channel_id=1, source_target_pairs={{0,16},{2,18},{4,20},{6,22},{8,24},{10,26},{12,28},{14,30},{16,0},... | collective-permute-start | bytes 116744 | tf_op jit(solution)/shard_map/ppermute | solution.py:834
  11.0 3.0 %collective-permute-done.1 = bf16[152,128]{1,0:T(8,128)(2,1)S(1)} collective-permute-done((bf16[152,128]{1,0:T(8,128)(2,1)S(1)}, bf16[152,128]{1,0:T(8,128)(2,1)S(1)}, u32[]{:S(2)}, u32[]{:S(2)}) %collective-permute-start.1) | collective-permute-done | bytes 38944 | tf_op jit(solution)/shard_map/ppermute | solution.py:834
  14.0 2.8 %collective-permute-done.2 = bf16[152,128]{1,0:T(8,128)(2,1)S(1)} collective-permute-done((bf16[152,128]{1,0:T(8,128)(2,1)S(1)}, bf16[152,128]{1,0:T(8,128)(2,1)S(1)}, u32[]{:S(2)}, u32[]{:S(2)}) %collective-permute-start.2) | collective-permute-done | bytes 38944 | tf_op jit(solution)/shard_map/ppermute | solution.py:834
  16.8 3.8 %all-to-all-start = ((bf16[16,2,8,2048]{3,2,1,0:T(8,128)(2,1)}), bf16[16,2,8,2048]{3,2,1,0:T(8,128)(2,1)S(1)}, u32[]{:S(2)}, u32[]{:S(2)}) async-start(bf16[16,2,8,2048]{3,2,1,0:T(8,128)(2,1)} %get-tuple-element.51), calls=%async_computation | async-start | bytes 2097152 | tf_op jit(solution)/shard_map/all_to_all | solution.py:41
  20.6 1.9 %collective-permute-start.3 = (bf16[4,152,128]{2,1,0:T(8,128)(2,1)S(1)}, bf16[4,152,128]{2,1,0:T(8,128)(2,1)S(1)}, u32[]{:S(2)}, u32[]{:S(2)}) collective-permute-start(bf16[4,152,128]{2,1,0:T(8,128)(2,1)S(1)} %pad_maximum_fusion), channel_id=1, source_target_pairs={{0,2},{2,0},{4,6},{6,4},{8,10},{10,8},{12,14},{14,12},{16,18},{18,... | collective-permute-start | bytes 466952 | tf_op jit(solution)/shard_map/ppermute | solution.py:834
  24.3 6.3 %collective-permute-done.3 = bf16[4,152,128]{2,1,0:T(8,128)(2,1)S(1)} collective-permute-done((bf16[4,152,128]{2,1,0:T(8,128)(2,1)S(1)}, bf16[4,152,128]{2,1,0:T(8,128)(2,1)S(1)}, u32[]{:S(2)}, u32[]{:S(2)}) %collective-permute-start.3) | collective-permute-done | bytes 155680 | tf_op jit(solution)/shard_map/ppermute | solution.py:834
  30.6 5.1 %collective-permute-done.4 = bf16[4,152,128]{2,1,0:T(8,128)(2,1)S(1)} collective-permute-done((bf16[4,152,128]{2,1,0:T(8,128)(2,1)S(1)}, bf16[4,152,128]{2,1,0:T(8,128)(2,1)S(1)}, u32[]{:S(2)}, u32[]{:S(2)}) %collective-permute-start.4) | collective-permute-done | bytes 155680 | tf_op jit(solution)/shard_map/ppermute | solution.py:834
  35.7 2.4 %collective-permute-done.5 = bf16[4,152,128]{2,1,0:T(8,128)(2,1)S(1)} collective-permute-done((bf16[4,152,128]{2,1,0:T(8,128)(2,1)S(1)}, bf16[4,152,128]{2,1,0:T(8,128)(2,1)S(1)}, u32[]{:S(2)}, u32[]{:S(2)}) %collective-permute-start.5) | collective-permute-done | bytes 155680 | tf_op jit(solution)/shard_map/ppermute | solution.py:834
  38.3 2.0 %collective-permute-done.6.other_ref = bf16[16,152,128]{2,1,0:T(8,128)(2,1)S(1)} collective-permute-done((bf16[16,152,128]{2,1,0:T(8,128)(2,1)S(1)}, bf16[16,152,128]{2,1,0:T(8,128)(2,1)S(1)}, u32[]{:S(2)}, u32[]{:S(2)}) %collective-permute-start.6) | collective-permute-done | bytes 622624 | tf_op jit(solution)/shard_map/ppermute | solution.py:919
  42.0 5.0 %shard_map.139 = (bf16[128,2048]{1,0:T(8,128)(2,1)S(1)}, bf16[128,256]{1,0:T(8,128)(2,1)S(1)}, bf16[128,32]{1,0:T(8,128)(2,1)S(1)}, f32[128,1]{1,0:T(8,128)S(1)}...) custom-call(s32[2]{0:T(128)S(1)} %pad_add_fusion.ids_ref, bf16[128,2048]{1,0:T(8,128)(2,1)S(1)} %bitcast.39, ...), custom_call_target="tpu_custom_call" | custom-call | tf_op jit(solution)/shard_map/pallas_call | solution.py:926
  47.2 1.8 %collective-permute-done.7.arrived_ref = bf16[2048,128]{1,0:T(8,128)(2,1)S(1)} collective-permute-done((bf16[2048,128]{1,0:T(8,128)(2,1)S(1)}, bf16[2048,128]{1,0:T(8,128)(2,1)S(1)}, u32[]{:S(2)}, u32[]{:S(2)}) %collective-permute-start.7) | collective-permute-done | bytes 524320 | tf_op jit(solution)/shard_map/ppermute | solution.py:938
  49.6 8.2 %shard_map.140 = (f32[128,2048]{1,0:T(8,128)S(1)}, f32[128,2048]{1,0:T(8,128)S(1)}, bf16[128,256]{1,0:T(8,128)(2,1)S(1)}, bf16[128,32]{1,0:T(8,128)(2,1)S(1)}, f32[2,2048]{1,0:T(2,128)S(1)}) custom-call(s32[2]{0:T(128)S(1)} %pad_add_fusion.ids_ref, bf16[2048,128]{1,0:T(8,128)(2,1)S(1)} %collective-permute-done.7.arrived_ref, bf16[128,2048]{1,0:T(8,128)(2,1)S(1)} %bitcast.40, ...), custom_call_target="tpu_custom_call" | custom-call | tf_op jit(solution)/shard_map/pallas_call | solution.py:940
  61.1 7.3 %shard_map.141 = (bf16[16,2,8,2048]{3,2,1,0:T(8,128)(2,1)}, bf16[128,2048]{1,0:T(8,128)(2,1)}, f32[2,2048]{1,0:T(2,128)}, bf16[128,256]{1,0:T(8,128)(2,1)S(1)}, bf16[128,32]{1,0:T(8,128)(2,1)S(1)}) custom-call(bf16[16,2,8,2048]{3,2,1,0:T(8,128)(2,1)S(1)} %all-to-all-done.got_ref, f32[1,2048]{1,0:T(1,128)S(1)} %get-tuple-element.40.refs_2_.refs_0_, ...), custom_call_target="tpu_custom_call" | custom-call | tf_op jit(solution)/shard_map/pallas_call | solution.py:961
  68.5 5.4 %all-to-all-start.1 = ((bf16[16,2,8,2048]{3,2,1,0:T(8,128)(2,1)}), bf16[16,2,8,2048]{3,2,1,0:T(8,128)(2,1)S(1)}, u32[]{:S(2)}, u32[]{:S(2)}) async-start(bf16[16,2,8,2048]{3,2,1,0:T(8,128)(2,1)} %get-tuple-element.54), calls=%async_computation.1 | async-start | bytes 2097152 | tf_op jit(solution)/shard_map/all_to_all | solution.py:41
  75.9 2.0 %collective-permute-done.8 = bf16[16,152,128]{2,1,0:T(8,128)(2,1)S(1)} collective-permute-done((bf16[16,152,128]{2,1,0:T(8,128)(2,1)S(1)}, bf16[16,152,128]{2,1,0:T(8,128)(2,1)S(1)}, u32[]{:S(2)}, u32[]{:S(2)}) %collective-permute-start.8) | collective-permute-done | bytes 622624 | tf_op jit(solution)/shard_map/ppermute | solution.py:987
  78.1 2.0 %collective-permute-start.10 = (bf16[4,152,128]{2,1,0:T(8,128)(2,1)S(1)}, bf16[4,152,128]{2,1,0:T(8,128)(2,1)S(1)}, u32[]{:S(2)}, u32[]{:S(2)}) collective-permute-start(bf16[4,152,128]{2,1,0:T(8,128)(2,1)S(1)} %get-tuple-element.71), channel_id=1, source_target_pairs={{0,4},{2,6},{4,0},{6,2},{8,12},{10,14},{12,8},{14,10},{16,20},{18,... | collective-permute-start | bytes 466952 | tf_op jit(solution)/shard_map/ppermute | solution.py:849
  80.1 1.5 %collective-permute-start.11 = (bf16[4,152,128]{2,1,0:T(8,128)(2,1)S(1)}, bf16[4,152,128]{2,1,0:T(8,128)(2,1)S(1)}, u32[]{:S(2)}, u32[]{:S(2)}) collective-permute-start(bf16[4,152,128]{2,1,0:T(8,128)(2,1)S(1)} %get-tuple-element.70), channel_id=1, source_target_pairs={{0,6},{2,4},{4,2},{6,0},{8,14},{10,12},{12,10},{14,8},{16,22},{18,... | collective-permute-start | bytes 466952 | tf_op jit(solution)/shard_map/ppermute | solution.py:849
  81.7 10.6 %collective-permute-done.10 = bf16[4,152,128]{2,1,0:T(8,128)(2,1)S(1)} collective-permute-done((bf16[4,152,128]{2,1,0:T(8,128)(2,1)S(1)}, bf16[4,152,128]{2,1,0:T(8,128)(2,1)S(1)}, u32[]{:S(2)}, u32[]{:S(2)}) %collective-permute-start.10) | collective-permute-done | bytes 155680 | tf_op jit(solution)/shard_map/ppermute | solution.py:849
  92.8 3.2 %collective-permute-done.9 = bf16[4,152,128]{2,1,0:T(8,128)(2,1)S(1)} collective-permute-done((bf16[4,152,128]{2,1,0:T(8,128)(2,1)S(1)}, bf16[4,152,128]{2,1,0:T(8,128)(2,1)S(1)}, u32[]{:S(2)}, u32[]{:S(2)}) %collective-permute-start.9) | collective-permute-done | bytes 155680 | tf_op jit(solution)/shard_map/ppermute | solution.py:849
  96.6 4.7 %collective-permute-start.13 = (bf16[152,128]{1,0:T(8,128)(2,1)S(1)}, bf16[152,128]{1,0:T(8,128)(2,1)S(1)}, u32[]{:S(2)}, u32[]{:S(2)}) collective-permute-start(bf16[152,128]{1,0:T(8,128)(2,1)S(1)} %get-tuple-element.74), channel_id=1, source_target_pairs={{0,16},{2,18},{4,20},{6,22},{8,24},{10,26},{12,28},{14,30},{16,0},... | collective-permute-start | bytes 116744 | tf_op jit(solution)/shard_map/ppermute | solution.py:849
  103.6 3.5 %collective-permute-done.14 = bf16[152,128]{1,0:T(8,128)(2,1)S(1)} collective-permute-done((bf16[152,128]{1,0:T(8,128)(2,1)S(1)}, bf16[152,128]{1,0:T(8,128)(2,1)S(1)}, u32[]{:S(2)}, u32[]{:S(2)}) %collective-permute-start.14) | collective-permute-done | bytes 38944 | tf_op jit(solution)/shard_map/ppermute | solution.py:849
  111.0 1.7 %shard_map.142 = (bf16[128,2048]{1,0:T(8,128)(2,1)}, bf16[128,2048]{1,0:T(8,128)(2,1)}) custom-call(bf16[128,2048]{1,0:T(8,128)(2,1)S(1)} %bitcast.41, f32[128,1]{1,0:T(8,128)S(1)} %get-tuple-element.44.refs_5_.inverse_ref, f32[1,2048]{1,0:T(1,128)S(1)} %get-tuple-element.41.refs_3_.refs_1_.gain_ref, f32[128,2048]{1,0:T(8,128)S(1)} %copy-done.3, ...), custom_call_target="tpu_custom_call" | custom-call | tf_op jit(solution)/shard_map/pallas_call | solution.py:995
  (73 shorter events, 18.3 us)
Async XLA Ops:
  2.5 46.5 %copy-start.7 = (s32[2]{0:T(128)}, s32[2]{0:T(128)S(1)}, u32[]{:S(2)}) copy-start(s32[2]{0:T(128)S(1)} %pad_add_fusion.ids_ref) | copy-start | bytes 28
  5.3 5.7 %collective-permute-start = (bf16[152,128]{1,0:T(8,128)(2,1)S(1)}, bf16[152,128]{1,0:T(8,128)(2,1)S(1)}, u32[]{:S(2)}, u32[]{:S(2)}) collective-permute-start(bf16[152,128]{1,0:T(8,128)(2,1)S(1)} %get-tuple-element.37), channel_id=1, source_target_pairs={{0,8},{2,10},{4,12},{6,14},{8,0},{10,2},{12,4},{14,6},{16,24},{18,... | collective-permute-start | bytes 116744 | tf_op jit(solution)/shard_map/ppermute | solution.py:834
  8.4 5.6 %collective-permute-start.1 = (bf16[152,128]{1,0:T(8,128)(2,1)S(1)}, bf16[152,128]{1,0:T(8,128)(2,1)S(1)}, u32[]{:S(2)}, u32[]{:S(2)}) collective-permute-start(bf16[152,128]{1,0:T(8,128)(2,1)S(1)} %get-tuple-element.37), channel_id=1, source_target_pairs={{0,16},{2,18},{4,20},{6,22},{8,24},{10,26},{12,28},{14,30},{16,0},... | collective-permute-start | bytes 116744 | tf_op jit(solution)/shard_map/ppermute | solution.py:834
  11.0 5.8 %collective-permute-start.2 = (bf16[152,128]{1,0:T(8,128)(2,1)S(1)}, bf16[152,128]{1,0:T(8,128)(2,1)S(1)}, u32[]{:S(2)}, u32[]{:S(2)}) collective-permute-start(bf16[152,128]{1,0:T(8,128)(2,1)S(1)} %get-tuple-element.37), channel_id=1, source_target_pairs={{0,24},{2,26},{4,28},{6,30},{8,16},{10,18},{12,20},{14,22},{16,8},... | collective-permute-start | bytes 116744 | tf_op jit(solution)/shard_map/ppermute | solution.py:834
  16.8 43.7 %all-to-all-start = ((bf16[16,2,8,2048]{3,2,1,0:T(8,128)(2,1)}), bf16[16,2,8,2048]{3,2,1,0:T(8,128)(2,1)S(1)}, u32[]{:S(2)}, u32[]{:S(2)}) async-start(bf16[16,2,8,2048]{3,2,1,0:T(8,128)(2,1)} %get-tuple-element.51), calls=%async_computation | async-start | bytes 2097152 | tf_op jit(solution)/shard_map/all_to_all | solution.py:41
  20.6 10.0 %collective-permute-start.3 = (bf16[4,152,128]{2,1,0:T(8,128)(2,1)S(1)}, bf16[4,152,128]{2,1,0:T(8,128)(2,1)S(1)}, u32[]{:S(2)}, u32[]{:S(2)}) collective-permute-start(bf16[4,152,128]{2,1,0:T(8,128)(2,1)S(1)} %pad_maximum_fusion), channel_id=1, source_target_pairs={{0,2},{2,0},{4,6},{6,4},{8,10},{10,8},{12,14},{14,12},{16,18},{18,... | collective-permute-start | bytes 466952 | tf_op jit(solution)/shard_map/ppermute | solution.py:834
  22.6 13.1 %collective-permute-start.4 = (bf16[4,152,128]{2,1,0:T(8,128)(2,1)S(1)}, bf16[4,152,128]{2,1,0:T(8,128)(2,1)S(1)}, u32[]{:S(2)}, u32[]{:S(2)}) collective-permute-start(bf16[4,152,128]{2,1,0:T(8,128)(2,1)S(1)} %pad_maximum_fusion), channel_id=1, source_target_pairs={{0,4},{2,6},{4,0},{6,2},{8,12},{10,14},{12,8},{14,10},{16,20},{18,... | collective-permute-start | bytes 466952 | tf_op jit(solution)/shard_map/ppermute | solution.py:834
  24.0 14.1 %collective-permute-start.5 = (bf16[4,152,128]{2,1,0:T(8,128)(2,1)S(1)}, bf16[4,152,128]{2,1,0:T(8,128)(2,1)S(1)}, u32[]{:S(2)}, u32[]{:S(2)}) collective-permute-start(bf16[4,152,128]{2,1,0:T(8,128)(2,1)S(1)} %pad_maximum_fusion), channel_id=1, source_target_pairs={{0,6},{2,4},{4,2},{6,0},{8,14},{10,12},{12,10},{14,8},{16,22},{18,... | collective-permute-start | bytes 466952 | tf_op jit(solution)/shard_map/ppermute | solution.py:834
  38.2 3.2 %copy-start = (bf16[1,1,128,2048]{3,2,1,0:T(8,128)(2,1)S(1)}, bf16[1,1,128,2048]{3,2,1,0:T(8,128)(2,1)}, u32[]{:S(2)}) copy-start(bf16[1,1,128,2048]{3,2,1,0:T(8,128)(2,1)} %param.10) | copy-start | bytes 1572868
  38.2 2.1 %collective-permute-start.6 = (bf16[16,152,128]{2,1,0:T(8,128)(2,1)S(1)}, bf16[16,152,128]{2,1,0:T(8,128)(2,1)S(1)}, u32[]{:S(2)}, u32[]{:S(2)}) collective-permute-start(bf16[16,152,128]{2,1,0:T(8,128)(2,1)S(1)} %constant_dynamic-update-slice_fusion.own_ref), channel_id=1, source_target_pairs={{0,1},{1,0},{2,3},{3,2},{4,5},{5,4},{6,7},{7,6},{8,9},{9,8},{10,11... | collective-permute-start | bytes 1867784 | tf_op jit(solution)/shard_map/ppermute | solution.py:919
  47.1 1.9 %collective-permute-start.7 = (bf16[2048,128]{1,0:T(8,128)(2,1)S(1)}, bf16[2048,128]{1,0:T(8,128)(2,1)S(1)}, u32[]{:S(2)}, u32[]{:S(2)}) collective-permute-start(bf16[2048,128]{1,0:T(8,128)(2,1)S(1)} %get-tuple-element.45), channel_id=1, source_target_pairs={{0,1},{1,0},{2,3},{3,2},{4,5},{5,4},{6,7},{7,6},{8,9},{9,8},{10,11... | collective-permute-start | bytes 1572872 | tf_op jit(solution)/shard_map/ppermute | solution.py:938
  68.5 5.5 %copy-start.6 = (bf16[128,2048]{1,0:T(8,128)(2,1)S(1)}, bf16[128,2048]{1,0:T(8,128)(2,1)}, u32[]{:S(2)}) copy-start(bf16[128,2048]{1,0:T(8,128)(2,1)} %get-tuple-element.60.site_x) | copy-start | bytes 1572868
  68.5 5.5 %copy-start.10 = (f32[2,2048]{1,0:T(2,128)S(1)}, f32[2,2048]{1,0:T(2,128)}, u32[]{:S(2)}) copy-start(f32[2,2048]{1,0:T(2,128)} %copy-done.9) | copy-start | bytes 49156
  68.5 5.5 %copy-start.11 = (f32[2,2048]{1,0:T(2,128)S(1)}, f32[2,2048]{1,0:T(2,128)}, u32[]{:S(2)}) copy-start(f32[2,2048]{1,0:T(2,128)} %get-tuple-element.63.site_gmod) | copy-start | bytes 49156
  68.5 41.3 %all-to-all-start.1 = ((bf16[16,2,8,2048]{3,2,1,0:T(8,128)(2,1)}), bf16[16,2,8,2048]{3,2,1,0:T(8,128)(2,1)S(1)}, u32[]{:S(2)}, u32[]{:S(2)}) async-start(bf16[16,2,8,2048]{3,2,1,0:T(8,128)(2,1)} %get-tuple-element.54), calls=%async_computation.1 | async-start | bytes 2097152 | tf_op jit(solution)/shard_map/all_to_all | solution.py:41
  75.8 2.1 %collective-permute-start.8 = (bf16[16,152,128]{2,1,0:T(8,128)(2,1)S(1)}, bf16[16,152,128]{2,1,0:T(8,128)(2,1)S(1)}, u32[]{:S(2)}, u32[]{:S(2)}) collective-permute-start(bf16[16,152,128]{2,1,0:T(8,128)(2,1)S(1)} %get-tuple-element.65), channel_id=1, source_target_pairs={{0,1},{1,0},{2,3},{3,2},{4,5},{5,4},{6,7},{7,6},{8,9},{9,8},{10,11... | collective-permute-start | bytes 1867784 | tf_op jit(solution)/shard_map/ppermute | solution.py:987
  78.1 31.7 %copy-start.3 = (f32[128,2048]{1,0:T(8,128)S(1)}, f32[128,2048]{1,0:T(8,128)}, u32[]{:S(2)}) copy-start(f32[128,2048]{1,0:T(8,128)} %copy-done.2) | copy-start | bytes 3145732
  78.1 14.1 %collective-permute-start.10 = (bf16[4,152,128]{2,1,0:T(8,128)(2,1)S(1)}, bf16[4,152,128]{2,1,0:T(8,128)(2,1)S(1)}, u32[]{:S(2)}, u32[]{:S(2)}) collective-permute-start(bf16[4,152,128]{2,1,0:T(8,128)(2,1)S(1)} %get-tuple-element.71), channel_id=1, source_target_pairs={{0,4},{2,6},{4,0},{6,2},{8,12},{10,14},{12,8},{14,10},{16,20},{18,... | collective-permute-start | bytes 466952 | tf_op jit(solution)/shard_map/ppermute | solution.py:849
  80.1 12.7 %collective-permute-start.11 = (bf16[4,152,128]{2,1,0:T(8,128)(2,1)S(1)}, bf16[4,152,128]{2,1,0:T(8,128)(2,1)S(1)}, u32[]{:S(2)}, u32[]{:S(2)}) collective-permute-start(bf16[4,152,128]{2,1,0:T(8,128)(2,1)S(1)} %get-tuple-element.70), channel_id=1, source_target_pairs={{0,6},{2,4},{4,2},{6,0},{8,14},{10,12},{12,10},{14,8},{16,22},{18,... | collective-permute-start | bytes 466952 | tf_op jit(solution)/shard_map/ppermute | solution.py:849
  81.6 14.4 %collective-permute-start.9 = (bf16[4,152,128]{2,1,0:T(8,128)(2,1)S(1)}, bf16[4,152,128]{2,1,0:T(8,128)(2,1)S(1)}, u32[]{:S(2)}, u32[]{:S(2)}) collective-permute-start(bf16[4,152,128]{2,1,0:T(8,128)(2,1)S(1)} %get-tuple-element.69), channel_id=1, source_target_pairs={{0,2},{2,0},{4,6},{6,4},{8,10},{10,8},{12,14},{14,12},{16,18},{18,... | collective-permute-start | bytes 466952 | tf_op jit(solution)/shard_map/ppermute | solution.py:849
  96.1 6.6 %collective-permute-start.12 = (bf16[152,128]{1,0:T(8,128)(2,1)S(1)}, bf16[152,128]{1,0:T(8,128)(2,1)S(1)}, u32[]{:S(2)}, u32[]{:S(2)}) collective-permute-start(bf16[152,128]{1,0:T(8,128)(2,1)S(1)} %get-tuple-element.72), channel_id=1, source_target_pairs={{0,8},{2,10},{4,12},{6,14},{8,0},{10,2},{12,4},{14,6},{16,24},{18,... | collective-permute-start | bytes 116744 | tf_op jit(solution)/shard_map/ppermute | solution.py:849
  96.6 7.0 %collective-permute-start.13 = (bf16[152,128]{1,0:T(8,128)(2,1)S(1)}, bf16[152,128]{1,0:T(8,128)(2,1)S(1)}, u32[]{:S(2)}, u32[]{:S(2)}) collective-permute-start(bf16[152,128]{1,0:T(8,128)(2,1)S(1)} %get-tuple-element.74), channel_id=1, source_target_pairs={{0,16},{2,18},{4,20},{6,22},{8,24},{10,26},{12,28},{14,30},{16,0},... | collective-permute-start | bytes 116744 | tf_op jit(solution)/shard_map/ppermute | solution.py:849
  101.3 5.8 %collective-permute-start.14 = (bf16[152,128]{1,0:T(8,128)(2,1)S(1)}, bf16[152,128]{1,0:T(8,128)(2,1)S(1)}, u32[]{:S(2)}, u32[]{:S(2)}) collective-permute-start(bf16[152,128]{1,0:T(8,128)(2,1)S(1)} %get-tuple-element.73), channel_id=1, source_target_pairs={{0,24},{2,26},{4,28},{6,30},{8,16},{10,18},{12,20},{14,22},{16,8},... | collective-permute-start | bytes 116744 | tf_op jit(solution)/shard_map/ppermute | solution.py:849
  107.1 1.3 %collective-permute-start.15 = (f32[152,128]{1,0:T(8,128)S(1)}, f32[152,128]{1,0:T(8,128)S(1)}, u32[]{:S(2)}, u32[]{:S(2)}) collective-permute-start(f32[152,128]{1,0:T(8,128)S(1)} %fusion.1.own_ref), channel_id=1, source_target_pairs={{0,1},{1,0},{2,3},{3,2},{4,5},{5,4},{6,7},{7,6},{8,9},{9,8},{10,11... | collective-permute-start | bytes 233480 | tf_op jit(solution)/shard_map/ppermute | solution.py:989
  (13 other events, 12.3 us)

commit v5 on v4

--- a/solution.py
+++ b/solution.py
@@ -7,7 +7,6 @@
 from jax.experimental import pallas as pl
 from jax.experimental.pallas import tpu as pltpu
 from jax.sharding import PartitionSpec as P
-
 
 norm_eps = 1e-05
 LANES = 128
@@ -601,7 +600,7 @@
     return pltpu.with_memory_space_constraint(array, pltpu.MemorySpace.HBM)
 
 
-def call(kernel, outs, scratch=(), specs=None, hbm_outs=()):
+def call(kernel, outs, scratch=(), name=None, specs=None, hbm_outs=()):
     shapes = [
         pltpu.MemorySpace.HBM(s, d) if n in hbm_outs else jax.ShapeDtypeStruct(s, d)
         for n, (s, d) in enumerate(outs)
@@ -619,6 +618,7 @@
         **spaces,
         scratch_shapes=[pltpu.VMEM(*s) if isinstance(s, tuple) else s for s in scratch],
         compiler_params=pltpu.CompilerParams(vmem_limit_bytes=24 << 20),
+        name=name,
     )
 
 
@@ -727,6 +727,7 @@
         functools.partial(site_kernel, sites),
         [(wide, bf16), (wide, bf16), ((width, pair), f32), ((heads, width), f32), ((2 * clips, width), f32)],
         [(wide, bf16)] * 6,
+        name="site",
     )(site_tok, site_grad, shift, gain, proj_full, step_full, bias, rate_time[None])
 
     came = exchange(
@@ -754,6 +755,7 @@
             ((width, state), bf16),
             ((width, state), bf16),
         ],
+        name="band",
     )(tok, grad, own_shift, own_gain, proj_full, step_full, bias, rate_space[None])
     state_in = chain(end_own, decay, True)
     later_grad = chain(start_grad, decay, False)
@@ -761,6 +763,7 @@
         space_kernel,
         [(wide, f32), (wide, f32), ((width, pair), bf16), ((heads, width), bf16), ((2, width), f32)],
         [(wide, bf16)] * 7,
+        name="space",
     )(
         tok,
         grad,
@@ -805,7 +808,7 @@
     mod_sum = sums[0, at : at + size].reshape(clips, mod_cols)
     grad_mod = jnp.dot(activated.astype(f32).T, mod_sum, precision=EXACT)
 
-    mixed, d_tokens = call(last_kernel, [(wide, bf16), (wide, bf16)])(
+    mixed, d_tokens = call(last_kernel, [(wide, bf16), (wide, bf16)], name="last")(
         tok, inverse, own_gain, mix, pre, time_out, time_back
     )
     return (mixed.reshape(tokens.shape), d_tokens.reshape(tokens.shape), grad_proj, grad_step, grad_mod)
@@ -826,7 +829,7 @@
     )
 
 
-def spread_over_frames(own, sent, radix=4):
+def spread_over_frames(own, radix=4):
     frames = radix * radix
 
     def others(piece, stride):
@@ -836,13 +839,10 @@
         ]
 
     far = jnp.stack(others(own, radix))
-    far, sent = lax.optimization_barrier((far, sent))
-    pieces = others(far, 1)
-    got = exchange(sent)
-    return jnp.concatenate(pieces), got
-
-
-def sum_over_frames(keep, given, radix):
+    return jnp.concatenate(others(far, 1))
+
+
+def sum_over_frames(keep, given, radix, ahead):
     def gathered(pieces, stride):
         frames = radix * radix
         return [pieces[0]] + [
@@ -858,8 +858,8 @@
 
     parts = [slice(d * radix, (d + 1) * radix) for d in range(radix)]
     near = [total([keep[p], given[p]]).astype(bf16) for p in parts]
-    near = total(gathered(near, 1)).astype(bf16)
-    return total(gathered([near[d] for d in range(radix)], radix))
+    near, *ahead = lax.optimization_barrier((total(gathered(near, 1)).astype(bf16), *ahead))
+    return total(gathered([near[d] for d in range(radix)], radix)), *ahead
 
 
 def per_device_fast(
@@ -904,6 +904,7 @@
             (packed, bf16),
             pltpu.SemaphoreType.DMA((7,)),
         ],
+        name="start",
         specs="shhhhhv",
         hbm_outs=(0,),
     )(
@@ -915,49 +916,16 @@
         in_hbm(mod_weight),
         activated,
     )
-    payload, got = spread_over_frames(payload, sent)
+    got = exchange(sent)
+    payload = spread_over_frames(payload)
     other = lax.ppermute(payload, "row", swap)
     proj_full, step_full, shift, gain = call(
         functools.partial(unpack_kernel, 4),
         [((width, pair), bf16), ((heads, width), bf16), ((1, width), f32), ((1, width), f32)],
+        name="unpack",
         specs="svv",
     )(ids, payload, other)
 
-    normed, coeffs, logits, inverse, _, give = call(
-        band_fast_kernel,
-        [
-            (wide, bf16),
-            ((length, pair), bf16),
-            ((length, heads), bf16),
-            ((length, 1), f32),
-            ((1, heads), f32),
-            ((width, state), bf16),
-        ],
-        specs="svvvvvvvv",
-    )(ids, tok, grad, shift, gain, proj_full, step_full, bias, rate_space[None])
-    arrived = lax.ppermute(give, "row", swap)
-    halves = (frames, size, LANES)
-    mix, pre, own_dc, own_dl, gmod = call(
-        space_fast_kernel,
-        [(wide, f32), (wide, f32), ((length, pair), bf16), ((length, heads), bf16), ((2, width), f32)],
-        [(wide, bf16)] * 7,
-        specs="s" + "v" * 12,
-    )(
-        ids,
-        arrived,
-        tok,
-        grad,
-        normed,
-        coeffs,
-        logits,
-        inverse,
-        proj_full,
-        step_full,
-        bias,
-        rate_space[None],
-        skip_gain[None],
-    )
-    got, own_dc = lax.optimization_barrier((got, own_dc))
     sent, site_x, site_gmod, site_dc, site_dl = call(
         functools.partial(site_fast_kernel, sites),
         [
@@ -976,25 +944,67 @@
             pltpu.SemaphoreType.DMA((6,)),
         ]
         + [(wide, bf16)] * 5,
+        name="site",
         specs="vvvvvvv",
         hbm_outs=(0, 1, 2),
     )(got, shift, gain, proj_full, step_full, bias, rate_time[None])
+    sent, proj_full = lax.optimization_barrier((sent, proj_full))
     came = exchange(sent)
 
+    normed, coeffs, logits, inverse, _, give = call(
+        band_fast_kernel,
+        [
+            (wide, bf16),
+            ((length, pair), bf16),
+            ((length, heads), bf16),
+            ((length, 1), f32),
+            ((1, heads), f32),
+            ((width, state), bf16),
+        ],
+        name="band",
+        specs="svvvvvvvv",
+    )(ids, tok, grad, shift, gain, proj_full, step_full, bias, rate_space[None])
+    arrived = lax.ppermute(give, "row", swap)
+    halves = (frames, size, LANES)
+    mix, pre, own_dc, own_dl, gmod = call(
+        space_fast_kernel,
+        [(wide, f32), (wide, f32), ((length, pair), bf16), ((length, heads), bf16), ((2, width), f32)],
+        [(wide, bf16)] * 7,
+        name="space",
+        specs="s" + "v" * 12,
+    )(
+        ids,
+        arrived,
+        tok,
+        grad,
+        normed,
+        coeffs,
+        logits,
+        inverse,
+        proj_full,
+        step_full,
+        bias,
+        rate_space[None],
+        skip_gain[None],
+    )
     keep, give = call(
-        functools.partial(terms_kernel, 4), [(halves, bf16), (halves, bf16)], specs="svvvvvvvv"
+        functools.partial(terms_kernel, 4),
+        [(halves, bf16), (halves, bf16)],
+        name="terms",
+        specs="svvvvvvvv",
     )(ids, normed, own_dc, own_dl, gmod, site_x, site_dc, site_dl, site_gmod)
     given = lax.ppermute(give, "row", swap)
-    terms = sum_over_frames(keep, given, 4)
+    mixed, d_tokens = call(last_fast_kernel, [(wide, bf16), (wide, bf16)], name="last")(
+        tok, inverse, gain, mix, pre, came
+    )
+    terms, mixed, d_tokens = sum_over_frames(keep, given, 4, (mixed, d_tokens))
     other = lax.ppermute(terms, "row", swap)
     grad_proj, grad_step, grad_mod = call(
         functools.partial(finish_kernel, factor),
         [((depth, pair), f32), ((heads, depth), f32), ((mod_weight.shape[0], mod_cols), f32)],
+        name="finish",
         specs="svvv",
     )(ids, terms, other, activated.astype(f32).T)
-    mixed, d_tokens = call(last_fast_kernel, [(wide, bf16), (wide, bf16)])(
-        tok, inverse, gain, mix, pre, came
-    )
     return (mixed.reshape(tokens.shape), d_tokens.reshape(tokens.shape), grad_proj, grad_step.T, grad_mod)
 
 

time: 113 us -> 103 us (0.912)
  waiting for transfers between devices: 44.6 us -> 36.5 us
  local copies, waits for them, and re-layouts: 7.29 us -> 4.67 us
  starting transfers between devices: 29 us -> 30.6 us
    ppermute x6, waiting for transfers between devices: 18.7 us -> 12.8 us  [gathered(): lax.ppermute(pieces[d], 'frame', [(i, i ^ d * stride) for i in range(fram...]
    ppermute x6, waiting for transfers between devices: 19.6 us -> 13.7 us  [others(): lax.ppermute(piece, 'frame', [(i, i ^ d * stride) for i in range(frames)])]
    all_to_all x2, starting transfers between devices: 9.27 us -> 13 us  [exchange(): lax.all_to_all(packed, 'frame', split_axis=0, concat_axis=0, tiled=True)]
    all_to_all x2, waiting for transfers between devices: 0.01 us -> 3.05 us  [exchange(): lax.all_to_all(packed, 'frame', split_axis=0, concat_axis=0, tiled=True)]
    unnamed x41 -> x30, local copies, waits for them, and re-layouts: 7.12 us -> 4.5 us
    ppermute x6, starting transfers between devices: 10.1 us -> 8.01 us  [gathered(): lax.ppermute(pieces[d], 'frame', [(i, i ^ d * stride) for i in range(fram...]
  transfers between devices with their start and end apart: 18 -> 18, of which waited for: 14 -> 13; matrix products, arithmetic and copies ran while one was open for 0% -> 1% of each run, Pallas kernels for 15% -> 15%
where the time goes in v5:
time: 103 us
  waiting for transfers between devices  36.5 us (35%)
  starting transfers between devices  30.6 us (30%)
  Pallas kernels  28.7 us (28%)
  local copies, waits for them, and re-layouts  4.67 us (5%)
  between operations  1.57 us (2%)
    ppermute x6, waiting for transfers between devices, others(): lax.ppermute(piece, 'frame', [(i, i ^ d * stride) for i in range(frames)])  13.7 us
    all_to_all x2, starting transfers between devices, exchange(): lax.all_to_all(packed, 'frame', split_axis=0, concat_axis=0, tiled=True)  13 us
    ppermute x6, waiting for transfers between devices, gathered(): lax.ppermute(pieces[d], 'frame', [(i, i ^ d * stride) for i in range(fram...  12.8 us
    ppermute x6, starting transfers between devices, others(): lax.ppermute(piece, 'frame', [(i, i ^ d * stride) for i in range(frames)])  9.26 us
    pallas_call x1, Pallas kernels, per_device_fast(): call(space_fast_kernel, [(wide, f32), (wide, f32), ((length, pair), bf16)...  8.22 us
    ppermute x6, starting transfers between devices, gathered(): lax.ppermute(pieces[d], 'frame', [(i, i ^ d * stride) for i in range(fram...  8.01 us
    pallas_call x1, Pallas kernels, per_device_fast(): call(functools.partial(site_fast_kernel, sites), [(packed, bf16), (wide,...  7.23 us
    pallas_call x1, Pallas kernels, per_device_fast(): call(band_fast_kernel, [(wide, bf16), ((length, pair), bf16), ((length, h...  5.04 us
  transfers between devices with their start and end apart: 18, of which 13 were waited for; matrix products, arithmetic and copies ran while one was open for 1% of the time, Pallas kernels for 15%

profile of v5, /device:TPU:0, one launch (start us, length us, event | category | flops | bytes accessed | tf_op | source)
XLA Modules:
  0.0 102.5 jit_solution(1628293445860962522)
XLA Ops:
  1.5 2.8 %start.1 = (bf16[16,2,8,2048]{3,2,1,0:T(8,128)(2,1)}, bf16[152,128]{1,0:T(8,128)(2,1)S(1)}) custom-call(s32[2]{0:T(128)S(1)} %pad_add_fusion.ids_ref, bf16[16,8,2048]{2,1,0:T(8,128)(2,1)} %bitcast.40, bf16[16,8,2048]{2,1,0:T(8,128)(2,1)} %bitcast.44, bf16[128,256]{1,0:T(8,128)(2,1)} %proj_hbm.1, bf16[32,128]{1,0:T(8,128)(2,1)} %bitcast.58, ...), custom_call_target="tpu_custom_call" | custom-call | tf_op jit(solution)/shard_map/start/pallas_call | solution.py:897
  4.3 3.1 %collective-permute-start = (bf16[152,128]{1,0:T(8,128)(2,1)S(1)}, bf16[152,128]{1,0:T(8,128)(2,1)S(1)}, u32[]{:S(2)}, u32[]{:S(2)}) collective-permute-start(bf16[152,128]{1,0:T(8,128)(2,1)S(1)} %get-tuple-element.38), channel_id=1, source_target_pairs={{0,8},{2,10},{4,12},{6,14},{8,0},{10,2},{12,4},{14,6},{16,24},{18,... | collective-permute-start | bytes 116744 | tf_op jit(solution)/shard_map/ppermute | solution.py:837
  7.4 2.6 %collective-permute-start.1 = (bf16[152,128]{1,0:T(8,128)(2,1)S(1)}, bf16[152,128]{1,0:T(8,128)(2,1)S(1)}, u32[]{:S(2)}, u32[]{:S(2)}) collective-permute-start(bf16[152,128]{1,0:T(8,128)(2,1)S(1)} %get-tuple-element.38), channel_id=1, source_target_pairs={{0,16},{2,18},{4,20},{6,22},{8,24},{10,26},{12,28},{14,30},{16,0},... | collective-permute-start | bytes 116744 | tf_op jit(solution)/shard_map/ppermute | solution.py:837
  10.0 7.1 %all-to-all-start = ((bf16[16,2,8,2048]{3,2,1,0:T(8,128)(2,1)}), bf16[16,2,8,2048]{3,2,1,0:T(8,128)(2,1)S(1)}, u32[]{:S(2)}, u32[]{:S(2)}) async-start(bf16[16,2,8,2048]{3,2,1,0:T(8,128)(2,1)} %get-tuple-element.41), calls=%async_computation | async-start | bytes 2097152 | tf_op jit(solution)/shard_map/all_to_all | solution.py:40
  17.2 2.0 %collective-permute-start.3 = (bf16[4,152,128]{2,1,0:T(8,128)(2,1)S(1)}, bf16[4,152,128]{2,1,0:T(8,128)(2,1)S(1)}, u32[]{:S(2)}, u32[]{:S(2)}) collective-permute-start(bf16[4,152,128]{2,1,0:T(8,128)(2,1)S(1)} %pad_maximum_fusion), channel_id=1, source_target_pairs={{0,2},{2,0},{4,6},{6,4},{8,10},{10,8},{12,14},{14,12},{16,18},{18,... | collective-permute-start | bytes 466952 | tf_op jit(solution)/shard_map/ppermute | solution.py:837
  20.7 6.0 %collective-permute-done.3 = bf16[4,152,128]{2,1,0:T(8,128)(2,1)S(1)} collective-permute-done((bf16[4,152,128]{2,1,0:T(8,128)(2,1)S(1)}, bf16[4,152,128]{2,1,0:T(8,128)(2,1)S(1)}, u32[]{:S(2)}, u32[]{:S(2)}) %collective-permute-start.3) | collective-permute-done | bytes 155680 | tf_op jit(solution)/shard_map/ppermute | solution.py:837
  26.8 6.0 %collective-permute-done.4 = bf16[4,152,128]{2,1,0:T(8,128)(2,1)S(1)} collective-permute-done((bf16[4,152,128]{2,1,0:T(8,128)(2,1)S(1)}, bf16[4,152,128]{2,1,0:T(8,128)(2,1)S(1)}, u32[]{:S(2)}, u32[]{:S(2)}) %collective-permute-start.4) | collective-permute-done | bytes 155680 | tf_op jit(solution)/shard_map/ppermute | solution.py:837
  32.8 1.7 %collective-permute-done.5 = bf16[4,152,128]{2,1,0:T(8,128)(2,1)S(1)} collective-permute-done((bf16[4,152,128]{2,1,0:T(8,128)(2,1)S(1)}, bf16[4,152,128]{2,1,0:T(8,128)(2,1)S(1)}, u32[]{:S(2)}, u32[]{:S(2)}) %collective-permute-start.5) | collective-permute-done | bytes 155680 | tf_op jit(solution)/shard_map/ppermute | solution.py:837
  34.6 2.0 %collective-permute-done.6.other_ref = bf16[16,152,128]{2,1,0:T(8,128)(2,1)S(1)} collective-permute-done((bf16[16,152,128]{2,1,0:T(8,128)(2,1)S(1)}, bf16[16,152,128]{2,1,0:T(8,128)(2,1)S(1)}, u32[]{:S(2)}, u32[]{:S(2)}) %collective-permute-start.6) | collective-permute-done | bytes 622624 | tf_op jit(solution)/shard_map/ppermute | solution.py:921
  37.7 3.1 %all-to-all-done.got_ref = bf16[16,2,8,2048]{3,2,1,0:T(8,128)(2,1)S(1)} async-done(((bf16[16,2,8,2048]{3,2,1,0:T(8,128)(2,1)}), bf16[16,2,8,2048]{3,2,1,0:T(8,128)(2,1)S(1)}, u32[]{:S(2)}, u32[]{:S(2)}) %all-to-all-start) | async-done | bytes 1048608 | tf_op jit(solution)/shard_map/all_to_all | solution.py:40
  41.4 7.2 %site.1 = (bf16[16,2,8,2048]{3,2,1,0:T(8,128)(2,1)}, bf16[128,2048]{1,0:T(8,128)(2,1)}, f32[2,2048]{1,0:T(2,128)}, bf16[128,256]{1,0:T(8,128)(2,1)S(1)}, bf16[128,32]{1,0:T(8,128)(2,1)S(1)}) custom-call(bf16[16,2,8,2048]{3,2,1,0:T(8,128)(2,1)S(1)} %all-to-all-done.got_ref, f32[1,2048]{1,0:T(1,128)S(1)} %get-tuple-element.39.refs_0_.refs_2_, ...), custom_call_target="tpu_custom_call" | custom-call | tf_op jit(solution)/shard_map/site/pallas_call | solution.py:929
  48.7 5.9 %all-to-all-start.1 = ((bf16[16,2,8,2048]{3,2,1,0:T(8,128)(2,1)}), bf16[16,2,8,2048]{3,2,1,0:T(8,128)(2,1)S(1)}, u32[]{:S(2)}, u32[]{:S(2)}) async-start(bf16[16,2,8,2048]{3,2,1,0:T(8,128)(2,1)} %get-tuple-element.62), calls=%async_computation.1 | async-start | bytes 2097152 | tf_op jit(solution)/shard_map/all_to_all | solution.py:40
  55.2 5.0 %band.1 = (bf16[128,2048]{1,0:T(8,128)(2,1)S(1)}, bf16[128,256]{1,0:T(8,128)(2,1)S(1)}, bf16[128,32]{1,0:T(8,128)(2,1)S(1)}, f32[128,1]{1,0:T(8,128)S(1)}, f32[1...) custom-call(s32[2]{0:T(128)S(1)} %pad_add_fusion.ids_ref, bf16[128,2048]{1,0:T(8,128)(2,1)S(1)} %bitcast.41, ...), custom_call_target="tpu_custom_call" | custom-call | tf_op jit(solution)/shard_map/band/pallas_call | solution.py:954
  60.3 1.9 %collective-permute-done.7.arrived_ref = bf16[2048,128]{1,0:T(8,128)(2,1)S(1)} collective-permute-done((bf16[2048,128]{1,0:T(8,128)(2,1)S(1)}, bf16[2048,128]{1,0:T(8,128)(2,1)S(1)}, u32[]{:S(2)}, u32[]{:S(2)}) %collective-permute-start.7) | collective-permute-done | bytes 524320 | tf_op jit(solution)/shard_map/ppermute | solution.py:967
  62.9 8.2 %space.1 = (f32[128,2048]{1,0:T(8,128)S(1)}, f32[128,2048]{1,0:T(8,128)S(1)}, bf16[128,256]{1,0:T(8,128)(2,1)S(1)}, bf16[128,32]{1,0:T(8,128)(2,1)S(1)}, f32[2,2048]{1,0:T(2,128)S(1)}) custom-call(s32[2]{0:T(128)S(1)} %pad_add_fusion.ids_ref, bf16[2048,128]{1,0:T(8,128)(2,1)S(1)} %collective-permute-done.7.arrived_ref, bf16[128,2048]{1,0:T(8,128)(2,1)S(1)} %bitcast.42, ...), custom_call_target="tpu_custom_call" | custom-call | tf_op jit(solution)/shard_map/space/pallas_call | solution.py:969
  72.6 1.9 %collective-permute-done.8 = bf16[16,152,128]{2,1,0:T(8,128)(2,1)S(1)} collective-permute-done((bf16[16,152,128]{2,1,0:T(8,128)(2,1)S(1)}, bf16[16,152,128]{2,1,0:T(8,128)(2,1)S(1)}, u32[]{:S(2)}, u32[]{:S(2)}) %collective-permute-start.8) | collective-permute-done | bytes 622624 | tf_op jit(solution)/shard_map/ppermute | solution.py:996
  74.7 2.0 %collective-permute-start.10 = (bf16[4,152,128]{2,1,0:T(8,128)(2,1)S(1)}, bf16[4,152,128]{2,1,0:T(8,128)(2,1)S(1)}, u32[]{:S(2)}, u32[]{:S(2)}) collective-permute-start(bf16[4,152,128]{2,1,0:T(8,128)(2,1)S(1)} %get-tuple-element.73), channel_id=1, source_target_pairs={{0,4},{2,6},{4,0},{6,2},{8,12},{10,14},{12,8},{14,10},{16,20},{18,... | collective-permute-start | bytes 466952 | tf_op jit(solution)/shard_map/ppermute | solution.py:849
  76.6 1.5 %collective-permute-start.11 = (bf16[4,152,128]{2,1,0:T(8,128)(2,1)S(1)}, bf16[4,152,128]{2,1,0:T(8,128)(2,1)S(1)}, u32[]{:S(2)}, u32[]{:S(2)}) collective-permute-start(bf16[4,152,128]{2,1,0:T(8,128)(2,1)S(1)} %get-tuple-element.72), channel_id=1, source_target_pairs={{0,6},{2,4},{4,2},{6,0},{8,14},{10,12},{12,10},{14,8},{16,22},{18,... | collective-permute-start | bytes 466952 | tf_op jit(solution)/shard_map/ppermute | solution.py:849
  78.2 5.9 %collective-permute-done.10 = bf16[4,152,128]{2,1,0:T(8,128)(2,1)S(1)} collective-permute-done((bf16[4,152,128]{2,1,0:T(8,128)(2,1)S(1)}, bf16[4,152,128]{2,1,0:T(8,128)(2,1)S(1)}, u32[]{:S(2)}, u32[]{:S(2)}) %collective-permute-start.10) | collective-permute-done | bytes 155680 | tf_op jit(solution)/shard_map/ppermute | solution.py:849
  88.2 1.7 %last.1 = (bf16[128,2048]{1,0:T(8,128)(2,1)}, bf16[128,2048]{1,0:T(8,128)(2,1)}) custom-call(bf16[128,2048]{1,0:T(8,128)(2,1)S(1)} %bitcast.43, f32[128,1]{1,0:T(8,128)S(1)} %get-tuple-element.50.refs_5_.inverse_ref, f32[1,2048]{1,0:T(1,128)S(1)} %get-tuple-element.40.refs_1_.refs_3_.gain_ref, f32[128,2048]{1,0:T(8,128)S(1)} %copy-done.3, ...), custom_call_target="tpu_custom_call" | custom-call | tf_op jit(solution)/shard_map/last/pallas_call | solution.py:997
  89.9 1.7 %collective-permute-start.12 = (bf16[152,128]{1,0:T(8,128)(2,1)S(1)}, bf16[152,128]{1,0:T(8,128)(2,1)S(1)}, u32[]{:S(2)}, u32[]{:S(2)}) collective-permute-start(bf16[152,128]{1,0:T(8,128)(2,1)S(1)} %get-tuple-element.74), channel_id=1, source_target_pairs={{0,8},{2,10},{4,12},{6,14},{8,0},{10,2},{12,4},{14,6},{16,24},{18,... | collective-permute-start | bytes 116744 | tf_op jit(solution)/shard_map/ppermute | solution.py:849
  91.6 2.4 %collective-permute-start.13 = (bf16[152,128]{1,0:T(8,128)(2,1)S(1)}, bf16[152,128]{1,0:T(8,128)(2,1)S(1)}, u32[]{:S(2)}, u32[]{:S(2)}) collective-permute-start(bf16[152,128]{1,0:T(8,128)(2,1)S(1)} %get-tuple-element.76), channel_id=1, source_target_pairs={{0,16},{2,18},{4,20},{6,22},{8,24},{10,26},{12,28},{14,30},{16,0},... | collective-permute-start | bytes 116744 | tf_op jit(solution)/shard_map/ppermute | solution.py:849
  94.4 2.4 %collective-permute-done.13 = bf16[152,128]{1,0:T(8,128)(2,1)S(1)} collective-permute-done((bf16[152,128]{1,0:T(8,128)(2,1)S(1)}, bf16[152,128]{1,0:T(8,128)(2,1)S(1)}, u32[]{:S(2)}, u32[]{:S(2)}) %collective-permute-start.13) | collective-permute-done | bytes 38944 | tf_op jit(solution)/shard_map/ppermute | solution.py:849
  96.8 3.0 %collective-permute-done.14 = bf16[152,128]{1,0:T(8,128)(2,1)S(1)} collective-permute-done((bf16[152,128]{1,0:T(8,128)(2,1)S(1)}, bf16[152,128]{1,0:T(8,128)(2,1)S(1)}, u32[]{:S(2)}, u32[]{:S(2)}) %collective-permute-start.14) | collective-permute-done | bytes 38944 | tf_op jit(solution)/shard_map/ppermute | solution.py:849
  (62 shorter events, 13.8 us)
Async XLA Ops:
  4.3 12.8 %collective-permute-start = (bf16[152,128]{1,0:T(8,128)(2,1)S(1)}, bf16[152,128]{1,0:T(8,128)(2,1)S(1)}, u32[]{:S(2)}, u32[]{:S(2)}) collective-permute-start(bf16[152,128]{1,0:T(8,128)(2,1)S(1)} %get-tuple-element.38), channel_id=1, source_target_pairs={{0,8},{2,10},{4,12},{6,14},{8,0},{10,2},{12,4},{14,6},{16,24},{18,... | collective-permute-start | bytes 116744 | tf_op jit(solution)/shard_map/ppermute | solution.py:837
  7.4 9.7 %collective-permute-start.1 = (bf16[152,128]{1,0:T(8,128)(2,1)S(1)}, bf16[152,128]{1,0:T(8,128)(2,1)S(1)}, u32[]{:S(2)}, u32[]{:S(2)}) collective-permute-start(bf16[152,128]{1,0:T(8,128)(2,1)S(1)} %get-tuple-element.38), channel_id=1, source_target_pairs={{0,16},{2,18},{4,20},{6,22},{8,24},{10,26},{12,28},{14,30},{16,0},... | collective-permute-start | bytes 116744 | tf_op jit(solution)/shard_map/ppermute | solution.py:837
  10.0 7.1 %collective-permute-start.2 = (bf16[152,128]{1,0:T(8,128)(2,1)S(1)}, bf16[152,128]{1,0:T(8,128)(2,1)S(1)}, u32[]{:S(2)}, u32[]{:S(2)}) collective-permute-start(bf16[152,128]{1,0:T(8,128)(2,1)S(1)} %get-tuple-element.38), channel_id=1, source_target_pairs={{0,24},{2,26},{4,28},{6,30},{8,16},{10,18},{12,20},{14,22},{16,8},... | collective-permute-start | bytes 116744 | tf_op jit(solution)/shard_map/ppermute | solution.py:837
  10.0 30.7 %all-to-all-start = ((bf16[16,2,8,2048]{3,2,1,0:T(8,128)(2,1)}), bf16[16,2,8,2048]{3,2,1,0:T(8,128)(2,1)S(1)}, u32[]{:S(2)}, u32[]{:S(2)}) async-start(bf16[16,2,8,2048]{3,2,1,0:T(8,128)(2,1)} %get-tuple-element.41), calls=%async_computation | async-start | bytes 2097152 | tf_op jit(solution)/shard_map/all_to_all | solution.py:40
  17.2 9.6 %collective-permute-start.3 = (bf16[4,152,128]{2,1,0:T(8,128)(2,1)S(1)}, bf16[4,152,128]{2,1,0:T(8,128)(2,1)S(1)}, u32[]{:S(2)}, u32[]{:S(2)}) collective-permute-start(bf16[4,152,128]{2,1,0:T(8,128)(2,1)S(1)} %pad_maximum_fusion), channel_id=1, source_target_pairs={{0,2},{2,0},{4,6},{6,4},{8,10},{10,8},{12,14},{14,12},{16,18},{18,... | collective-permute-start | bytes 466952 | tf_op jit(solution)/shard_map/ppermute | solution.py:837
  19.1 13.6 %collective-permute-start.4 = (bf16[4,152,128]{2,1,0:T(8,128)(2,1)S(1)}, bf16[4,152,128]{2,1,0:T(8,128)(2,1)S(1)}, u32[]{:S(2)}, u32[]{:S(2)}) collective-permute-start(bf16[4,152,128]{2,1,0:T(8,128)(2,1)S(1)} %pad_maximum_fusion), channel_id=1, source_target_pairs={{0,4},{2,6},{4,0},{6,2},{8,12},{10,14},{12,8},{14,10},{16,20},{18,... | collective-permute-start | bytes 466952 | tf_op jit(solution)/shard_map/ppermute | solution.py:837
  20.6 13.9 %collective-permute-start.5 = (bf16[4,152,128]{2,1,0:T(8,128)(2,1)S(1)}, bf16[4,152,128]{2,1,0:T(8,128)(2,1)S(1)}, u32[]{:S(2)}, u32[]{:S(2)}) collective-permute-start(bf16[4,152,128]{2,1,0:T(8,128)(2,1)S(1)} %pad_maximum_fusion), channel_id=1, source_target_pairs={{0,6},{2,4},{4,2},{6,0},{8,14},{10,12},{12,10},{14,8},{16,22},{18,... | collective-permute-start | bytes 466952 | tf_op jit(solution)/shard_map/ppermute | solution.py:837
  34.5 2.1 %collective-permute-start.6 = (bf16[16,152,128]{2,1,0:T(8,128)(2,1)S(1)}, bf16[16,152,128]{2,1,0:T(8,128)(2,1)S(1)}, u32[]{:S(2)}, u32[]{:S(2)}) collective-permute-start(bf16[16,152,128]{2,1,0:T(8,128)(2,1)S(1)} %constant_dynamic-update-slice_fusion.own_ref), channel_id=1, source_target_pairs={{0,1},{1,0},{2,3},{3,2},{4,5},{5,4},{6,7},{7,6},{8,9},{9,8},{10,11... | collective-permute-start | bytes 1867784 | tf_op jit(solution)/shard_map/ppermute | solution.py:921
  48.6 6.0 %copy-start = (bf16[1,1,128,2048]{3,2,1,0:T(8,128)(2,1)S(1)}, bf16[1,1,128,2048]{3,2,1,0:T(8,128)(2,1)}, u32[]{:S(2)}) copy-start(bf16[1,1,128,2048]{3,2,1,0:T(8,128)(2,1)} %param.10) | copy-start | bytes 1572868
  48.7 6.0 %copy-start.1 = (bf16[1,1,128,2048]{3,2,1,0:T(8,128)(2,1)S(1)}, bf16[1,1,128,2048]{3,2,1,0:T(8,128)(2,1)}, u32[]{:S(2)}) copy-start(bf16[1,1,128,2048]{3,2,1,0:T(8,128)(2,1)} %param.11) | copy-start | bytes 1572868
  48.7 37.1 %all-to-all-start.1 = ((bf16[16,2,8,2048]{3,2,1,0:T(8,128)(2,1)}), bf16[16,2,8,2048]{3,2,1,0:T(8,128)(2,1)S(1)}, u32[]{:S(2)}, u32[]{:S(2)}) async-start(bf16[16,2,8,2048]{3,2,1,0:T(8,128)(2,1)} %get-tuple-element.62), calls=%async_computation.1 | async-start | bytes 2097152 | tf_op jit(solution)/shard_map/all_to_all | solution.py:40
  60.3 1.9 %collective-permute-start.7 = (bf16[2048,128]{1,0:T(8,128)(2,1)S(1)}, bf16[2048,128]{1,0:T(8,128)(2,1)S(1)}, u32[]{:S(2)}, u32[]{:S(2)}) collective-permute-start(bf16[2048,128]{1,0:T(8,128)(2,1)S(1)} %get-tuple-element.47), channel_id=1, source_target_pairs={{0,1},{1,0},{2,3},{3,2},{4,5},{5,4},{6,7},{7,6},{8,9},{9,8},{10,11... | collective-permute-start | bytes 1572872 | tf_op jit(solution)/shard_map/ppermute | solution.py:967
  62.8 8.3 %copy-start.6 = (bf16[128,2048]{1,0:T(8,128)(2,1)S(1)}, bf16[128,2048]{1,0:T(8,128)(2,1)}, u32[]{:S(2)}) copy-start(bf16[128,2048]{1,0:T(8,128)(2,1)} %get-tuple-element.54.site_x) | copy-start | bytes 1572868
  62.9 8.3 %copy-start.7 = (f32[2,2048]{1,0:T(2,128)S(1)}, f32[2,2048]{1,0:T(2,128)}, u32[]{:S(2)}) copy-start(f32[2,2048]{1,0:T(2,128)} %get-tuple-element.57.site_gmod) | copy-start | bytes 49156
  71.1 3.6 %copy-start.2 = (f32[128,2048]{1,0:T(8,128)}, f32[128,2048]{1,0:T(8,128)S(1)}, u32[]{:S(2)}) copy-start(f32[128,2048]{1,0:T(8,128)S(1)} %get-tuple-element.60.mix_ref) | copy-start | bytes 3145732
  71.1 3.6 %copy-start.4 = (f32[128,2048]{1,0:T(8,128)}, f32[128,2048]{1,0:T(8,128)S(1)}, u32[]{:S(2)}) copy-start(f32[128,2048]{1,0:T(8,128)S(1)} %get-tuple-element.61.pre_ref) | copy-start | bytes 3145732
  72.4 2.1 %collective-permute-start.8 = (bf16[16,152,128]{2,1,0:T(8,128)(2,1)S(1)}, bf16[16,152,128]{2,1,0:T(8,128)(2,1)S(1)}, u32[]{:S(2)}, u32[]{:S(2)}) collective-permute-start(bf16[16,152,128]{2,1,0:T(8,128)(2,1)S(1)} %get-tuple-element.59), channel_id=1, source_target_pairs={{0,1},{1,0},{2,3},{3,2},{4,5},{5,4},{6,7},{7,6},{8,9},{9,8},{10,11... | collective-permute-start | bytes 1867784 | tf_op jit(solution)/shard_map/ppermute | solution.py:996
  74.7 9.5 %collective-permute-start.10 = (bf16[4,152,128]{2,1,0:T(8,128)(2,1)S(1)}, bf16[4,152,128]{2,1,0:T(8,128)(2,1)S(1)}, u32[]{:S(2)}, u32[]{:S(2)}) collective-permute-start(bf16[4,152,128]{2,1,0:T(8,128)(2,1)S(1)} %get-tuple-element.73), channel_id=1, source_target_pairs={{0,4},{2,6},{4,0},{6,2},{8,12},{10,14},{12,8},{14,10},{16,20},{18,... | collective-permute-start | bytes 466952 | tf_op jit(solution)/shard_map/ppermute | solution.py:849
  76.6 7.8 %collective-permute-start.11 = (bf16[4,152,128]{2,1,0:T(8,128)(2,1)S(1)}, bf16[4,152,128]{2,1,0:T(8,128)(2,1)S(1)}, u32[]{:S(2)}, u32[]{:S(2)}) collective-permute-start(bf16[4,152,128]{2,1,0:T(8,128)(2,1)S(1)} %get-tuple-element.72), channel_id=1, source_target_pairs={{0,6},{2,4},{4,2},{6,0},{8,14},{10,12},{12,10},{14,8},{16,22},{18,... | collective-permute-start | bytes 466952 | tf_op jit(solution)/shard_map/ppermute | solution.py:849
  78.1 7.5 %collective-permute-start.9 = (bf16[4,152,128]{2,1,0:T(8,128)(2,1)S(1)}, bf16[4,152,128]{2,1,0:T(8,128)(2,1)S(1)}, u32[]{:S(2)}, u32[]{:S(2)}) collective-permute-start(bf16[4,152,128]{2,1,0:T(8,128)(2,1)S(1)} %get-tuple-element.71), channel_id=1, source_target_pairs={{0,2},{2,0},{4,6},{6,4},{8,10},{10,8},{12,14},{14,12},{16,18},{18,... | collective-permute-start | bytes 466952 | tf_op jit(solution)/shard_map/ppermute | solution.py:849
  89.9 4.5 %collective-permute-start.12 = (bf16[152,128]{1,0:T(8,128)(2,1)S(1)}, bf16[152,128]{1,0:T(8,128)(2,1)S(1)}, u32[]{:S(2)}, u32[]{:S(2)}) collective-permute-start(bf16[152,128]{1,0:T(8,128)(2,1)S(1)} %get-tuple-element.74), channel_id=1, source_target_pairs={{0,8},{2,10},{4,12},{6,14},{8,0},{10,2},{12,4},{14,6},{16,24},{18,... | collective-permute-start | bytes 116744 | tf_op jit(solution)/shard_map/ppermute | solution.py:849
  91.6 5.2 %collective-permute-start.13 = (bf16[152,128]{1,0:T(8,128)(2,1)S(1)}, bf16[152,128]{1,0:T(8,128)(2,1)S(1)}, u32[]{:S(2)}, u32[]{:S(2)}) collective-permute-start(bf16[152,128]{1,0:T(8,128)(2,1)S(1)} %get-tuple-element.76), channel_id=1, source_target_pairs={{0,16},{2,18},{4,20},{6,22},{8,24},{10,26},{12,28},{14,30},{16,0},... | collective-permute-start | bytes 116744 | tf_op jit(solution)/shard_map/ppermute | solution.py:849
  94.0 5.8 %collective-permute-start.14 = (bf16[152,128]{1,0:T(8,128)(2,1)S(1)}, bf16[152,128]{1,0:T(8,128)(2,1)S(1)}, u32[]{:S(2)}, u32[]{:S(2)}) collective-permute-start(bf16[152,128]{1,0:T(8,128)(2,1)S(1)} %get-tuple-element.75), channel_id=1, source_target_pairs={{0,24},{2,26},{4,28},{6,30},{8,16},{10,18},{12,20},{14,22},{16,8},... | collective-permute-start | bytes 116744 | tf_op jit(solution)/shard_map/ppermute | solution.py:849
  99.8 1.3 %collective-permute-start.15 = (f32[152,128]{1,0:T(8,128)S(1)}, f32[152,128]{1,0:T(8,128)S(1)}, u32[]{:S(2)}, u32[]{:S(2)}) collective-permute-start(f32[152,128]{1,0:T(8,128)S(1)} %fusion.1.own_ref), channel_id=1, source_target_pairs={{0,1},{1,0},{2,3},{3,2},{4,5},{5,4},{6,7},{7,6},{8,9},{9,8},{10,11... | collective-permute-start | bytes 233480 | tf_op jit(solution)/shard_map/ppermute | solution.py:1001
  (6 other events, 5.1 us)

commit v6 on v5

--- a/solution.py
+++ b/solution.py
@@ -239,9 +239,10 @@
 
 
 def site_fast_kernel(sites, got_ref, *refs):
-    inputs, (sent_hbm, x_hbm, gmod_hbm, dc_ref, dl_ref) = refs[:6], refs[6:11]
-    tok_ref, grad_ref, sent_ref, x_ref, gmod_ref, sems = refs[11:17]
-    scratch = refs[17:]
+    inputs, (small_ref, sent_hbm, x_hbm, gmod_hbm, dc_ref, dl_ref) = refs[:4], refs[4:10]
+    inputs = (*inputs, small_ref[0:1, :], small_ref[1:2, :])
+    tok_ref, grad_ref, sent_ref, x_ref, gmod_ref, sems = refs[10:16]
+    scratch = refs[16:]
     frames, width = got_ref.shape[0], got_ref.shape[3]
     for _, sl in blocks(width):
         for ref, which in ((tok_ref, 0), (grad_ref, 1)):
@@ -358,8 +359,9 @@
 
 
 def band_fast_kernel(ids_ref, *refs):
-    give_ref = refs[-1]
-    band_kernel(*refs[:-1], None, give_ref, first=ids_ref[1] == 0)
+    small_ref, give_ref = refs[6], refs[-1]
+    inputs = (*refs[:6], small_ref[0:1, :], small_ref[2:3, :])
+    band_kernel(*inputs, *refs[7:-1], None, give_ref, first=ids_ref[1] == 0)
 
 
 def band_kernel(
@@ -450,7 +452,8 @@
 
 
 def space_fast_kernel(ids_ref, arrived_ref, *refs):
-    inputs, outs = refs[:11], refs[11:]
+    inputs, small_ref, outs = refs[:8], refs[8], refs[9:]
+    inputs = (*inputs, *(small_ref[n : n + 1, :] for n in (0, 2, 3)))
     first = ids_ref[1] == 0
 
     class Arrived:
@@ -843,12 +846,7 @@
 
 
 def sum_over_frames(keep, given, radix, ahead):
-    def gathered(pieces, stride):
-        frames = radix * radix
-        return [pieces[0]] + [
-            lax.ppermute(pieces[d], "frame", [(i, i ^ (d * stride)) for i in range(frames)])
-            for d in range(1, radix)
-        ]
+    frames = radix * radix
 
     def total(pieces):
         value = pieces[0].astype(f32)
@@ -856,10 +854,19 @@
             value = value + piece.astype(f32)
         return value
 
+    def partner(piece, offset):
+        return lax.ppermute(piece, "frame", [(i, i ^ offset) for i in range(frames)])
+
     parts = [slice(d * radix, (d + 1) * radix) for d in range(radix)]
     near = [total([keep[p], given[p]]).astype(bf16) for p in parts]
-    near, *ahead = lax.optimization_barrier((total(gathered(near, 1)).astype(bf16), *ahead))
-    return total(gathered([near[d] for d in range(radix)], radix)), *ahead
+    near = [near[0]] + [partner(near[d], d) for d in range(1, radix)]
+    near, ahead = lax.optimization_barrier((near, ahead))
+    value = total(near)
+    while value.shape[0] > 1:
+        half = value.shape[0] // 2
+        value = value.astype(bf16)
+        value = total([value[:half], partner(value[half:], half * radix)])
+    return value[0], *ahead
 
 
 def per_device_fast(
@@ -888,7 +895,7 @@
     tok = tokens.reshape(length, width)
     grad = cotangent.reshape(length, width)
     wide = (length, width)
-    bias = step_bias[None]
+    small = jnp.stack([step_bias, rate_time, rate_space, skip_gain])
     swap = [(0, 1), (1, 0)]
 
     packed = (frames, 2, sites, width)
@@ -926,6 +933,21 @@
         specs="svv",
     )(ids, payload, other)
 
+    normed, coeffs, logits, inverse, _, give = call(
+        band_fast_kernel,
+        [
+            (wide, bf16),
+            ((length, pair), bf16),
+            ((length, heads), bf16),
+            ((length, 1), f32),
+            ((1, heads), f32),
+            ((width, state), bf16),
+        ],
+        name="band",
+        specs="svvvvvvv",
+    )(ids, tok, grad, shift, gain, proj_full, step_full, small)
+    arrived = lax.ppermute(give, "row", swap)
+
     sent, site_x, site_gmod, site_dc, site_dl = call(
         functools.partial(site_fast_kernel, sites),
         [
@@ -945,33 +967,19 @@
         ]
         + [(wide, bf16)] * 5,
         name="site",
-        specs="vvvvvvv",
+        specs="vvvvvv",
         hbm_outs=(0, 1, 2),
-    )(got, shift, gain, proj_full, step_full, bias, rate_time[None])
-    sent, proj_full = lax.optimization_barrier((sent, proj_full))
+    )(got, shift, gain, proj_full, step_full, small)
+    sent, arrived = lax.optimization_barrier((sent, arrived))
     came = exchange(sent)
 
-    normed, coeffs, logits, inverse, _, give = call(
-        band_fast_kernel,
-        [
-            (wide, bf16),
-            ((length, pair), bf16),
-            ((length, heads), bf16),
-            ((length, 1), f32),
-            ((1, heads), f32),
-            ((width, state), bf16),
-        ],
-        name="band",
-        specs="svvvvvvvv",
-    )(ids, tok, grad, shift, gain, proj_full, step_full, bias, rate_space[None])
-    arrived = lax.ppermute(give, "row", swap)
     halves = (frames, size, LANES)
     mix, pre, own_dc, own_dl, gmod = call(
         space_fast_kernel,
         [(wide, f32), (wide, f32), ((length, pair), bf16), ((length, heads), bf16), ((2, width), f32)],
         [(wide, bf16)] * 7,
         name="space",
-        specs="s" + "v" * 12,
+        specs="s" + "v" * 10,
     )(
         ids,
         arrived,
@@ -983,9 +991,7 @@
         inverse,
         proj_full,
         step_full,
-        bias,
-        rate_space[None],
-        skip_gain[None],
+        small,
     )
     keep, give = call(
         functools.partial(terms_kernel, 4),

time: 103 us -> 102 us (level)
  waiting for transfers between devices: 36.5 us -> 28.9 us
  local copies, waits for them, and re-layouts: 4.67 us -> 7.25 us
  starting transfers between devices: 30.6 us -> 32.6 us
  other arithmetic: 0.5 us -> 1.59 us
    ppermute x6 -> x5, waiting for transfers between devices: 12.8 us -> 4.37 us  [partner(): lax.ppermute(piece, 'frame', [(i, i ^ offset) for i in range(frames)])]
    all_to_all x2, waiting for transfers between devices: 3.05 us -> 7.19 us  [exchange(): lax.all_to_all(packed, 'frame', split_axis=0, concat_axis=0, tiled=True)]
    unnamed x30 -> x50, local copies, waits for them, and re-layouts: 4.5 us -> 7.08 us
    ppermute x1, waiting for transfers between devices: 1.91 us -> 0.01 us  [per_device_fast(): arrived = lax.ppermute(give, 'row', swap)]
    ppermute x6 -> x5, starting transfers between devices: 8.01 us -> 9.75 us  [partner(): lax.ppermute(piece, 'frame', [(i, i ^ offset) for i in range(frames)])]
    concatenate x2, other arithmetic: 0.1 us -> 1.16 us  [time_embed(): jnp.concatenate([jnp.cos(angles), jnp.sin(angles)], axis=1)]
  transfers between devices with their start and end apart: 18 -> 17, of which waited for: 13 -> 9; matrix products, arithmetic and copies ran while one was open for 1% -> 0% of each run, Pallas kernels for 15% -> 25%
where the time goes in v6:
time: 102 us
  starting transfers between devices  32.6 us (32%)
  Pallas kernels  29.6 us (29%)
  waiting for transfers between devices  28.9 us (28%)
  local copies, waits for them, and re-layouts  7.25 us (7%)
  between operations  1.65 us (2%)
  other arithmetic  1.59 us (2%)
    ppermute x6, waiting for transfers between devices, others(): lax.ppermute(piece, 'frame', [(i, i ^ d * stride) for i in range(frames)])  13.7 us
    all_to_all x2, starting transfers between devices, exchange(): lax.all_to_all(packed, 'frame', split_axis=0, concat_axis=0, tiled=True)  13.2 us
    ppermute x5, starting transfers between devices, partner(): lax.ppermute(piece, 'frame', [(i, i ^ offset) for i in range(frames)])  9.75 us
    ppermute x6, starting transfers between devices, others(): lax.ppermute(piece, 'frame', [(i, i ^ d * stride) for i in range(frames)])  9.26 us
    pallas_call x1, Pallas kernels, per_device_fast(): call(space_fast_kernel, [(wide, f32), (wide, f32), ((length, pair), bf16)...  8.79 us
    all_to_all x2, waiting for transfers between devices, exchange(): lax.all_to_all(packed, 'frame', split_axis=0, concat_axis=0, tiled=True)  7.19 us
    pallas_call x1, Pallas kernels, per_device_fast(): call(functools.partial(site_fast_kernel, sites), [(packed, bf16), (wide,...  7.16 us
    unnamed x50, local copies, waits for them, and re-layouts  7.08 us
  transfers between devices with their start and end apart: 17, of which 9 were waited for; matrix products, arithmetic and copies ran while one was open for 0% of the time, Pallas kernels for 25%

profile of v6, /device:TPU:0, one launch (start us, length us, event | category | flops | bytes accessed | tf_op | source)
XLA Modules:
  0.0 101.7 jit_solution(8871693285888408026)
XLA Ops:
  2.5 2.8 %start.1 = (bf16[16,2,8,2048]{3,2,1,0:T(8,128)(2,1)}, bf16[152,128]{1,0:T(8,128)(2,1)S(1)}) custom-call(s32[2]{0:T(128)S(1)} %pad_add_fusion.ids_ref, bf16[16,8,2048]{2,1,0:T(8,128)(2,1)} %bitcast.33, bf16[16,8,2048]{2,1,0:T(8,128)(2,1)} %bitcast.37, bf16[128,256]{1,0:T(8,128)(2,1)} %proj_hbm.1, bf16[32,128]{1,0:T(8,128)(2,1)} %bitcast.44, ...), custom_call_target="tpu_custom_call" | custom-call | tf_op jit(solution)/shard_map/start/pallas_call | solution.py:904
  5.3 3.1 %collective-permute-start = (bf16[152,128]{1,0:T(8,128)(2,1)S(1)}, bf16[152,128]{1,0:T(8,128)(2,1)S(1)}, u32[]{:S(2)}, u32[]{:S(2)}) collective-permute-start(bf16[152,128]{1,0:T(8,128)(2,1)S(1)} %get-tuple-element.41), channel_id=1, source_target_pairs={{0,8},{2,10},{4,12},{6,14},{8,0},{10,2},{12,4},{14,6},{16,24},{18,... | collective-permute-start | bytes 116744 | tf_op jit(solution)/shard_map/ppermute | solution.py:840
  8.4 2.6 %collective-permute-start.1 = (bf16[152,128]{1,0:T(8,128)(2,1)S(1)}, bf16[152,128]{1,0:T(8,128)(2,1)S(1)}, u32[]{:S(2)}, u32[]{:S(2)}) collective-permute-start(bf16[152,128]{1,0:T(8,128)(2,1)S(1)} %get-tuple-element.41), channel_id=1, source_target_pairs={{0,16},{2,18},{4,20},{6,22},{8,24},{10,26},{12,28},{14,30},{16,0},... | collective-permute-start | bytes 116744 | tf_op jit(solution)/shard_map/ppermute | solution.py:840
  11.0 7.1 %all-to-all-start = ((bf16[16,2,8,2048]{3,2,1,0:T(8,128)(2,1)}), bf16[16,2,8,2048]{3,2,1,0:T(8,128)(2,1)S(1)}, u32[]{:S(2)}, u32[]{:S(2)}) async-start(bf16[16,2,8,2048]{3,2,1,0:T(8,128)(2,1)} %get-tuple-element.47), calls=%async_computation | async-start | bytes 2097152 | tf_op jit(solution)/shard_map/all_to_all | solution.py:40
  18.2 2.0 %collective-permute-start.3 = (bf16[4,152,128]{2,1,0:T(8,128)(2,1)S(1)}, bf16[4,152,128]{2,1,0:T(8,128)(2,1)S(1)}, u32[]{:S(2)}, u32[]{:S(2)}) collective-permute-start(bf16[4,152,128]{2,1,0:T(8,128)(2,1)S(1)} %pad_maximum_fusion), channel_id=1, source_target_pairs={{0,2},{2,0},{4,6},{6,4},{8,10},{10,8},{12,14},{14,12},{16,18},{18,... | collective-permute-start | bytes 466952 | tf_op jit(solution)/shard_map/ppermute | solution.py:840
  20.2 1.5 %collective-permute-start.4 = (bf16[4,152,128]{2,1,0:T(8,128)(2,1)S(1)}, bf16[4,152,128]{2,1,0:T(8,128)(2,1)S(1)}, u32[]{:S(2)}, u32[]{:S(2)}) collective-permute-start(bf16[4,152,128]{2,1,0:T(8,128)(2,1)S(1)} %pad_maximum_fusion), channel_id=1, source_target_pairs={{0,4},{2,6},{4,0},{6,2},{8,12},{10,14},{12,8},{14,10},{16,20},{18,... | collective-permute-start | bytes 466952 | tf_op jit(solution)/shard_map/ppermute | solution.py:840
  21.8 6.0 %collective-permute-done.3 = bf16[4,152,128]{2,1,0:T(8,128)(2,1)S(1)} collective-permute-done((bf16[4,152,128]{2,1,0:T(8,128)(2,1)S(1)}, bf16[4,152,128]{2,1,0:T(8,128)(2,1)S(1)}, u32[]{:S(2)}, u32[]{:S(2)}) %collective-permute-start.3) | collective-permute-done | bytes 155680 | tf_op jit(solution)/shard_map/ppermute | solution.py:840
  27.8 6.0 %collective-permute-done.4 = bf16[4,152,128]{2,1,0:T(8,128)(2,1)S(1)} collective-permute-done((bf16[4,152,128]{2,1,0:T(8,128)(2,1)S(1)}, bf16[4,152,128]{2,1,0:T(8,128)(2,1)S(1)}, u32[]{:S(2)}, u32[]{:S(2)}) %collective-permute-start.4) | collective-permute-done | bytes 155680 | tf_op jit(solution)/shard_map/ppermute | solution.py:840
  33.8 1.7 %collective-permute-done.5 = bf16[4,152,128]{2,1,0:T(8,128)(2,1)S(1)} collective-permute-done((bf16[4,152,128]{2,1,0:T(8,128)(2,1)S(1)}, bf16[4,152,128]{2,1,0:T(8,128)(2,1)S(1)}, u32[]{:S(2)}, u32[]{:S(2)}) %collective-permute-start.5) | collective-permute-done | bytes 155680 | tf_op jit(solution)/shard_map/ppermute | solution.py:840
  36.4 1.3 %collective-permute-done.6.other_ref = bf16[16,152,128]{2,1,0:T(8,128)(2,1)S(1)} collective-permute-done((bf16[16,152,128]{2,1,0:T(8,128)(2,1)S(1)}, bf16[16,152,128]{2,1,0:T(8,128)(2,1)S(1)}, u32[]{:S(2)}, u32[]{:S(2)}) %collective-permute-start.6) | collective-permute-done | bytes 622624 | tf_op jit(solution)/shard_map/ppermute | solution.py:928
  38.8 5.5 %band.1 = (bf16[128,2048]{1,0:T(8,128)(2,1)S(1)}, bf16[128,256]{1,0:T(8,128)(2,1)S(1)}, bf16[128,32]{1,0:T(8,128)(2,1)S(1)}, f32[128,1]{1,0:T(8,128)S(1)}, f32[1,32]{1,0:T(1,128)}, /*index=5*/bf16[2048,128]{1,0:T(8,128)(2,1)}) custom-call(s32[2]{0:T(128)S(1)} %pad_add_fusion.ids_ref, bf16[128,2048]{1,0:T(8,128)(2,1)S(1)} %bitcast.34, ...), custom_call_target="tpu_custom_call" | custom-call | tf_op jit(solution)/shard_map/band/pallas_call | solution.py:936
  45.9 7.2 %site.1 = (bf16[16,2,8,2048]{3,2,1,0:T(8,128)(2,1)}, bf16[128,2048]{1,0:T(8,128)(2,1)}, f32[2,2048]{1,0:T(2,128)}, bf16[128,256]{1,0:T(8,128)(2,1)S(1)}, bf16[128,32]{1,0:T(8,128)(2,1)S(1)}) custom-call(bf16[16,2,8,2048]{3,2,1,0:T(8,128)(2,1)S(1)} %all-to-all-done.got_ref, f32[1,2048]{1,0:T(1,128)S(1)} %get-tuple-element.42.refs_2_.refs_0_, ...), custom_call_target="tpu_custom_call" | custom-call | tf_op jit(solution)/shard_map/site/pallas_call | solution.py:951
  53.1 6.1 %all-to-all-start.1 = ((bf16[16,2,8,2048]{3,2,1,0:T(8,128)(2,1)}), bf16[16,2,8,2048]{3,2,1,0:T(8,128)(2,1)S(1)}, u32[]{:S(2)}, u32[]{:S(2)}) async-start(bf16[16,2,8,2048]{3,2,1,0:T(8,128)(2,1)} %get-tuple-element.65), calls=%async_computation.1 | async-start | bytes 2097152 | tf_op jit(solution)/shard_map/all_to_all | solution.py:40
  60.9 8.8 %space.1 = (f32[128,2048]{1,0:T(8,128)S(1)}, f32[128,2048]{1,0:T(8,128)S(1)}, bf16[128,256]{1,0:T(8,128)(2,1)S(1)}, bf16[128,32]{1,0:T(8,128)(2,1)S(1)}, f32[2,2048]{1,0:T(2,128)S(1)}) custom-call(s32[2]{0:T(128)S(1)} %copy-done.14, bf16[2048,128]{1,0:T(8,128)(2,1)} %collective-permute-done.7.arrived_ref, bf16[128,2048]{1,0:T(8,128)(2,1)S(1)} %bitcast.35, ...), custom_call_target="tpu_custom_call" | custom-call | tf_op jit(solution)/shard_map/space/pallas_call | solution.py:977
  71.2 2.0 %collective-permute-done.8 = bf16[16,152,128]{2,1,0:T(8,128)(2,1)S(1)} collective-permute-done((bf16[16,152,128]{2,1,0:T(8,128)(2,1)S(1)}, bf16[16,152,128]{2,1,0:T(8,128)(2,1)S(1)}, u32[]{:S(2)}, u32[]{:S(2)}) %collective-permute-start.8) | collective-permute-done | bytes 622624 | tf_op jit(solution)/shard_map/ppermute | solution.py:1002
  73.4 2.0 %collective-permute-start.10 = (bf16[4,152,128]{2,1,0:T(8,128)(2,1)S(1)}, bf16[4,152,128]{2,1,0:T(8,128)(2,1)S(1)}, u32[]{:S(2)}, u32[]{:S(2)}) collective-permute-start(bf16[4,152,128]{2,1,0:T(8,128)(2,1)S(1)} %get-tuple-element.78), channel_id=1, source_target_pairs={{0,4},{2,6},{4,0},{6,2},{8,12},{10,14},{12,8},{14,10},{16,20},{18,... | collective-permute-start | bytes 466952 | tf_op jit(solution)/shard_map/ppermute | solution.py:858
  75.4 1.5 %collective-permute-start.11 = (bf16[4,152,128]{2,1,0:T(8,128)(2,1)S(1)}, bf16[4,152,128]{2,1,0:T(8,128)(2,1)S(1)}, u32[]{:S(2)}, u32[]{:S(2)}) collective-permute-start(bf16[4,152,128]{2,1,0:T(8,128)(2,1)S(1)} %get-tuple-element.77), channel_id=1, source_target_pairs={{0,6},{2,4},{4,2},{6,0},{8,14},{10,12},{12,10},{14,8},{16,22},{18,... | collective-permute-start | bytes 466952 | tf_op jit(solution)/shard_map/ppermute | solution.py:858
  76.9 7.2 %all-to-all-done.1.came_ref = bf16[16,2,8,2048]{3,2,1,0:T(8,128)(2,1)S(1)} async-done(((bf16[16,2,8,2048]{3,2,1,0:T(8,128)(2,1)}), bf16[16,2,8,2048]{3,2,1,0:T(8,128)(2,1)S(1)}, u32[]{:S(2)}, u32[]{:S(2)}) %all-to-all-start.1) | async-done | bytes 1048608 | tf_op jit(solution)/shard_map/all_to_all | solution.py:40
  86.6 1.7 %last.1 = (bf16[128,2048]{1,0:T(8,128)(2,1)}, bf16[128,2048]{1,0:T(8,128)(2,1)}) custom-call(bf16[128,2048]{1,0:T(8,128)(2,1)S(1)} %bitcast.36, f32[128,1]{1,0:T(8,128)S(1)} %get-tuple-element.53.refs_5_.inverse_ref, f32[1,2048]{1,0:T(1,128)S(1)} %get-tuple-element.43.refs_3_.refs_1_.gain_ref, f32[128,2048]{1,0:T(8,128)S(1)} %copy-done.6, ...), custom_call_target="tpu_custom_call" | custom-call | tf_op jit(solution)/shard_map/last/pallas_call | solution.py:1003
  88.4 4.1 %collective-permute-start.12 = (bf16[2,152,128]{2,1,0:T(8,128)(2,1)S(1)}, bf16[2,152,128]{2,1,0:T(8,128)(2,1)S(1)}, u32[]{:S(2)}, u32[]{:S(2)}) collective-permute-start(bf16[2,152,128]{2,1,0:T(8,128)(2,1)S(1)} %slice.53), channel_id=1, source_target_pairs={{0,16},{2,18},{4,20},{6,22},{8,24},{10,26},{12,28},{14,30},{16,0},... | collective-permute-start | bytes 233480 | tf_op jit(solution)/shard_map/ppermute | solution.py:858
  92.5 2.4 %collective-permute-done.12 = bf16[2,152,128]{2,1,0:T(8,128)(2,1)S(1)} collective-permute-done((bf16[2,152,128]{2,1,0:T(8,128)(2,1)S(1)}, bf16[2,152,128]{2,1,0:T(8,128)(2,1)S(1)}, u32[]{:S(2)}, u32[]{:S(2)}) %collective-permute-start.12) | collective-permute-done | bytes 77856 | tf_op jit(solution)/shard_map/ppermute | solution.py:858
  94.9 2.1 %collective-permute-start.13 = (bf16[1,152,128]{2,1,0:T(8,128)(2,1)S(1)}, bf16[1,152,128]{2,1,0:T(8,128)(2,1)S(1)}, u32[]{:S(2)}, u32[]{:S(2)}) collective-permute-start(bf16[1,152,128]{2,1,0:T(8,128)(2,1)S(1)} %slice.55), channel_id=1, source_target_pairs={{0,8},{2,10},{4,12},{6,14},{8,0},{10,2},{12,4},{14,6},{16,24},{18,... | collective-permute-start | bytes 116744 | tf_op jit(solution)/shard_map/ppermute | solution.py:858
  97.0 2.0 %collective-permute-done.13 = bf16[1,152,128]{2,1,0:T(8,128)(2,1)S(1)} collective-permute-done((bf16[1,152,128]{2,1,0:T(8,128)(2,1)S(1)}, bf16[1,152,128]{2,1,0:T(8,128)(2,1)S(1)}, u32[]{:S(2)}, u32[]{:S(2)}) %collective-permute-start.13) | collective-permute-done | bytes 38944 | tf_op jit(solution)/shard_map/ppermute | solution.py:858
  100.3 1.4 %finish.1 = (f32[128,256]{1,0:T(8,128)}, f32[32,128]{1,0:T(8,128)}, f32[256,256]{1,0:T(8,128)}) custom-call(s32[2]{0:T(128)S(1)} %copy-done.14, f32[152,128]{1,0:T(8,128)S(1)} %add_bitcast_fusion.own_ref, f32[152,128]{1,0:T(8,128)S(1)} %collective-permute-done.14.other_ref, f32[256,1]{1,0:T(8,128)S(1)} %copy.20.active_ref), custom_call_target="tpu_custom_call" | custom-call | tf_op jit(solution)/shard_map/finish/pallas_call | solution.py:1008
  (83 shorter events, 12.3 us)
Async XLA Ops:
  2.5 36.2 %copy-start.13 = (s32[2]{0:T(128)}, s32[2]{0:T(128)S(1)}, u32[]{:S(2)}) copy-start(s32[2]{0:T(128)S(1)} %pad_add_fusion.ids_ref) | copy-start | bytes 28
  5.3 12.8 %collective-permute-start = (bf16[152,128]{1,0:T(8,128)(2,1)S(1)}, bf16[152,128]{1,0:T(8,128)(2,1)S(1)}, u32[]{:S(2)}, u32[]{:S(2)}) collective-permute-start(bf16[152,128]{1,0:T(8,128)(2,1)S(1)} %get-tuple-element.41), channel_id=1, source_target_pairs={{0,8},{2,10},{4,12},{6,14},{8,0},{10,2},{12,4},{14,6},{16,24},{18,... | collective-permute-start | bytes 116744 | tf_op jit(solution)/shard_map/ppermute | solution.py:840
  8.4 9.7 %collective-permute-start.1 = (bf16[152,128]{1,0:T(8,128)(2,1)S(1)}, bf16[152,128]{1,0:T(8,128)(2,1)S(1)}, u32[]{:S(2)}, u32[]{:S(2)}) collective-permute-start(bf16[152,128]{1,0:T(8,128)(2,1)S(1)} %get-tuple-element.41), channel_id=1, source_target_pairs={{0,16},{2,18},{4,20},{6,22},{8,24},{10,26},{12,28},{14,30},{16,0},... | collective-permute-start | bytes 116744 | tf_op jit(solution)/shard_map/ppermute | solution.py:840
  11.0 7.1 %collective-permute-start.2 = (bf16[152,128]{1,0:T(8,128)(2,1)S(1)}, bf16[152,128]{1,0:T(8,128)(2,1)S(1)}, u32[]{:S(2)}, u32[]{:S(2)}) collective-permute-start(bf16[152,128]{1,0:T(8,128)(2,1)S(1)} %get-tuple-element.41), channel_id=1, source_target_pairs={{0,24},{2,26},{4,28},{6,30},{8,16},{10,18},{12,20},{14,22},{16,8},... | collective-permute-start | bytes 116744 | tf_op jit(solution)/shard_map/ppermute | solution.py:840
  11.0 34.2 %all-to-all-start = ((bf16[16,2,8,2048]{3,2,1,0:T(8,128)(2,1)}), bf16[16,2,8,2048]{3,2,1,0:T(8,128)(2,1)S(1)}, u32[]{:S(2)}, u32[]{:S(2)}) async-start(bf16[16,2,8,2048]{3,2,1,0:T(8,128)(2,1)} %get-tuple-element.47), calls=%async_computation | async-start | bytes 2097152 | tf_op jit(solution)/shard_map/all_to_all | solution.py:40
  18.2 9.6 %collective-permute-start.3 = (bf16[4,152,128]{2,1,0:T(8,128)(2,1)S(1)}, bf16[4,152,128]{2,1,0:T(8,128)(2,1)S(1)}, u32[]{:S(2)}, u32[]{:S(2)}) collective-permute-start(bf16[4,152,128]{2,1,0:T(8,128)(2,1)S(1)} %pad_maximum_fusion), channel_id=1, source_target_pairs={{0,2},{2,0},{4,6},{6,4},{8,10},{10,8},{12,14},{14,12},{16,18},{18,... | collective-permute-start | bytes 466952 | tf_op jit(solution)/shard_map/ppermute | solution.py:840
  20.2 13.6 %collective-permute-start.4 = (bf16[4,152,128]{2,1,0:T(8,128)(2,1)S(1)}, bf16[4,152,128]{2,1,0:T(8,128)(2,1)S(1)}, u32[]{:S(2)}, u32[]{:S(2)}) collective-permute-start(bf16[4,152,128]{2,1,0:T(8,128)(2,1)S(1)} %pad_maximum_fusion), channel_id=1, source_target_pairs={{0,4},{2,6},{4,0},{6,2},{8,12},{10,14},{12,8},{14,10},{16,20},{18,... | collective-permute-start | bytes 466952 | tf_op jit(solution)/shard_map/ppermute | solution.py:840
  21.7 13.9 %collective-permute-start.5 = (bf16[4,152,128]{2,1,0:T(8,128)(2,1)S(1)}, bf16[4,152,128]{2,1,0:T(8,128)(2,1)S(1)}, u32[]{:S(2)}, u32[]{:S(2)}) collective-permute-start(bf16[4,152,128]{2,1,0:T(8,128)(2,1)S(1)} %pad_maximum_fusion), channel_id=1, source_target_pairs={{0,6},{2,4},{4,2},{6,0},{8,14},{10,12},{12,10},{14,8},{16,22},{18,... | collective-permute-start | bytes 466952 | tf_op jit(solution)/shard_map/ppermute | solution.py:840
  35.6 2.1 %collective-permute-start.6 = (bf16[16,152,128]{2,1,0:T(8,128)(2,1)S(1)}, bf16[16,152,128]{2,1,0:T(8,128)(2,1)S(1)}, u32[]{:S(2)}, u32[]{:S(2)}) collective-permute-start(bf16[16,152,128]{2,1,0:T(8,128)(2,1)S(1)} %constant_dynamic-update-slice_fusion.own_ref), channel_id=1, source_target_pairs={{0,1},{1,0},{2,3},{3,2},{4,5},{5,4},{6,7},{7,6},{8,9},{9,8},{10,11... | collective-permute-start | bytes 1867784 | tf_op jit(solution)/shard_map/ppermute | solution.py:928
  36.4 2.4 %copy-start.10 = (f32[4,32]{1,0:T(4,128)}, f32[4,32]{1,0:T(4,128)S(1)}, u32[]{:S(2)}) copy-start(f32[4,32]{1,0:T(4,128)S(1)} %pad_maximum_fusion.1.refs_6_.refs_4_.refs_8_) | copy-start | bytes 1540
  45.1 8.0 %collective-permute-start.7 = (bf16[2048,128]{1,0:T(8,128)(2,1)}, bf16[2048,128]{1,0:T(8,128)(2,1)}, u32[]{:S(2)}, u32[]{:S(2)}) collective-permute-start(bf16[2048,128]{1,0:T(8,128)(2,1)} %get-tuple-element.49), channel_id=1, source_target_pairs={{0,1},{1,0},{2,3},{3,2},{4,5},{5,4},{6,7},{7,6},{8,9},{9,8},{10,11... | collective-permute-start | bytes 1572872 | tf_op jit(solution)/shard_map/ppermute | solution.py:949
  53.1 31.0 %all-to-all-start.1 = ((bf16[16,2,8,2048]{3,2,1,0:T(8,128)(2,1)}), bf16[16,2,8,2048]{3,2,1,0:T(8,128)(2,1)S(1)}, u32[]{:S(2)}, u32[]{:S(2)}) async-start(bf16[16,2,8,2048]{3,2,1,0:T(8,128)(2,1)} %get-tuple-element.65), calls=%async_computation.1 | async-start | bytes 2097152 | tf_op jit(solution)/shard_map/all_to_all | solution.py:40
  60.9 8.8 %copy-start.4 = (bf16[128,2048]{1,0:T(8,128)(2,1)S(1)}, bf16[128,2048]{1,0:T(8,128)(2,1)}, u32[]{:S(2)}) copy-start(bf16[128,2048]{1,0:T(8,128)(2,1)} %copy-done.2) | copy-start | bytes 1572868
  60.9 8.8 %copy-start.9 = (bf16[128,2048]{1,0:T(8,128)(2,1)S(1)}, bf16[128,2048]{1,0:T(8,128)(2,1)}, u32[]{:S(2)}) copy-start(bf16[128,2048]{1,0:T(8,128)(2,1)} %get-tuple-element.57.site_x) | copy-start | bytes 1572868
  60.9 8.8 %copy-start.15 = (f32[2,2048]{1,0:T(2,128)S(1)}, f32[2,2048]{1,0:T(2,128)}, u32[]{:S(2)}) copy-start(f32[2,2048]{1,0:T(2,128)} %get-tuple-element.60.site_gmod) | copy-start | bytes 49156
  69.7 3.6 %copy-start.5 = (f32[128,2048]{1,0:T(8,128)}, f32[128,2048]{1,0:T(8,128)S(1)}, u32[]{:S(2)}) copy-start(f32[128,2048]{1,0:T(8,128)S(1)} %get-tuple-element.63.mix_ref) | copy-start | bytes 3145732
  69.7 3.6 %copy-start.7 = (f32[128,2048]{1,0:T(8,128)}, f32[128,2048]{1,0:T(8,128)S(1)}, u32[]{:S(2)}) copy-start(f32[128,2048]{1,0:T(8,128)S(1)} %get-tuple-element.64.pre_ref) | copy-start | bytes 3145732
  71.1 2.1 %collective-permute-start.8 = (bf16[16,152,128]{2,1,0:T(8,128)(2,1)S(1)}, bf16[16,152,128]{2,1,0:T(8,128)(2,1)S(1)}, u32[]{:S(2)}, u32[]{:S(2)}) collective-permute-start(bf16[16,152,128]{2,1,0:T(8,128)(2,1)S(1)} %get-tuple-element.62), channel_id=1, source_target_pairs={{0,1},{1,0},{2,3},{3,2},{4,5},{5,4},{6,7},{7,6},{8,9},{9,8},{10,11... | collective-permute-start | bytes 1867784 | tf_op jit(solution)/shard_map/ppermute | solution.py:1002
  73.4 14.9 %collective-permute-start.10 = (bf16[4,152,128]{2,1,0:T(8,128)(2,1)S(1)}, bf16[4,152,128]{2,1,0:T(8,128)(2,1)S(1)}, u32[]{:S(2)}, u32[]{:S(2)}) collective-permute-start(bf16[4,152,128]{2,1,0:T(8,128)(2,1)S(1)} %get-tuple-element.78), channel_id=1, source_target_pairs={{0,4},{2,6},{4,0},{6,2},{8,12},{10,14},{12,8},{14,10},{16,20},{18,... | collective-permute-start | bytes 466952 | tf_op jit(solution)/shard_map/ppermute | solution.py:858
  75.4 12.9 %collective-permute-start.11 = (bf16[4,152,128]{2,1,0:T(8,128)(2,1)S(1)}, bf16[4,152,128]{2,1,0:T(8,128)(2,1)S(1)}, u32[]{:S(2)}, u32[]{:S(2)}) collective-permute-start(bf16[4,152,128]{2,1,0:T(8,128)(2,1)S(1)} %get-tuple-element.77), channel_id=1, source_target_pairs={{0,6},{2,4},{4,2},{6,0},{8,14},{10,12},{12,10},{14,8},{16,22},{18,... | collective-permute-start | bytes 466952 | tf_op jit(solution)/shard_map/ppermute | solution.py:858
  76.8 11.5 %collective-permute-start.9 = (bf16[4,152,128]{2,1,0:T(8,128)(2,1)S(1)}, bf16[4,152,128]{2,1,0:T(8,128)(2,1)S(1)}, u32[]{:S(2)}, u32[]{:S(2)}) collective-permute-start(bf16[4,152,128]{2,1,0:T(8,128)(2,1)S(1)} %get-tuple-element.79), channel_id=1, source_target_pairs={{0,2},{2,0},{4,6},{6,4},{8,10},{10,8},{12,14},{14,12},{16,18},{18,... | collective-permute-start | bytes 466952 | tf_op jit(solution)/shard_map/ppermute | solution.py:858
  88.4 6.5 %collective-permute-start.12 = (bf16[2,152,128]{2,1,0:T(8,128)(2,1)S(1)}, bf16[2,152,128]{2,1,0:T(8,128)(2,1)S(1)}, u32[]{:S(2)}, u32[]{:S(2)}) collective-permute-start(bf16[2,152,128]{2,1,0:T(8,128)(2,1)S(1)} %slice.53), channel_id=1, source_target_pairs={{0,16},{2,18},{4,20},{6,22},{8,24},{10,26},{12,28},{14,30},{16,0},... | collective-permute-start | bytes 233480 | tf_op jit(solution)/shard_map/ppermute | solution.py:858
  94.9 4.0 %collective-permute-start.13 = (bf16[1,152,128]{2,1,0:T(8,128)(2,1)S(1)}, bf16[1,152,128]{2,1,0:T(8,128)(2,1)S(1)}, u32[]{:S(2)}, u32[]{:S(2)}) collective-permute-start(bf16[1,152,128]{2,1,0:T(8,128)(2,1)S(1)} %slice.55), channel_id=1, source_target_pairs={{0,8},{2,10},{4,12},{6,14},{8,0},{10,2},{12,4},{14,6},{16,24},{18,... | collective-permute-start | bytes 116744 | tf_op jit(solution)/shard_map/ppermute | solution.py:858
  99.0 1.3 %collective-permute-start.14 = (f32[152,128]{1,0:T(8,128)S(1)}, f32[152,128]{1,0:T(8,128)S(1)}, u32[]{:S(2)}, u32[]{:S(2)}) collective-permute-start(f32[152,128]{1,0:T(8,128)S(1)} %add_bitcast_fusion.own_ref), channel_id=1, source_target_pairs={{0,1},{1,0},{2,3},{3,2},{4,5},{5,4},{6,7},{7,6},{8,9},{9,8},{10,11... | collective-permute-start | bytes 233480 | tf_op jit(solution)/shard_map/ppermute | solution.py:1007
  (15 other events, 15.0 us)

commit v7 on v6

--- a/solution.py
+++ b/solution.py
@@ -861,12 +861,9 @@
     near = [total([keep[p], given[p]]).astype(bf16) for p in parts]
     near = [near[0]] + [partner(near[d], d) for d in range(1, radix)]
     near, ahead = lax.optimization_barrier((near, ahead))
-    value = total(near)
-    while value.shape[0] > 1:
-        half = value.shape[0] // 2
-        value = value.astype(bf16)
-        value = total([value[:half], partner(value[half:], half * radix)])
-    return value[0], *ahead
+    near = total(near).astype(bf16)
+    far = [near[0]] + [partner(near[d], d * radix) for d in range(1, radix)]
+    return total(far), *ahead
 
 
 def per_device_fast(
@@ -933,21 +930,6 @@
         specs="svv",
     )(ids, payload, other)
 
-    normed, coeffs, logits, inverse, _, give = call(
-        band_fast_kernel,
-        [
-            (wide, bf16),
-            ((length, pair), bf16),
-            ((length, heads), bf16),
-            ((length, 1), f32),
-            ((1, heads), f32),
-            ((width, state), bf16),
-        ],
-        name="band",
-        specs="svvvvvvv",
-    )(ids, tok, grad, shift, gain, proj_full, step_full, small)
-    arrived = lax.ppermute(give, "row", swap)
-
     sent, site_x, site_gmod, site_dc, site_dl = call(
         functools.partial(site_fast_kernel, sites),
         [
@@ -970,8 +952,23 @@
         specs="vvvvvv",
         hbm_outs=(0, 1, 2),
     )(got, shift, gain, proj_full, step_full, small)
-    sent, arrived = lax.optimization_barrier((sent, arrived))
+    sent, proj_full = lax.optimization_barrier((sent, proj_full))
     came = exchange(sent)
+
+    normed, coeffs, logits, inverse, _, give = call(
+        band_fast_kernel,
+        [
+            (wide, bf16),
+            ((length, pair), bf16),
+            ((length, heads), bf16),
+            ((length, 1), f32),
+            ((1, heads), f32),
+            ((width, state), bf16),
+        ],
+        name="band",
+        specs="svvvvvvv",
+    )(ids, tok, grad, shift, gain, proj_full, step_full, small)
+    arrived = lax.ppermute(give, "row", swap)
 
     halves = (frames, size, LANES)
     mix, pre, own_dc, own_dl, gmod = call(

time: 102 us -> 97 us (0.951)
  local copies, waits for them, and re-layouts: 7.25 us -> 3.39 us
  waiting for transfers between devices: 28.9 us -> 31.3 us
  starting transfers between devices: 32.6 us -> 31.2 us
  other arithmetic: 1.59 us -> 0.52 us
    unnamed x50 -> x30, local copies, waits for them, and re-layouts: 7.08 us -> 3.22 us
    all_to_all x2, waiting for transfers between devices: 7.19 us -> 3.64 us  [exchange(): lax.all_to_all(packed, 'frame', split_axis=0, concat_axis=0, tiled=True)]
    ppermute x5 -> x6, waiting for transfers between devices: 4.37 us -> 7.67 us  [partner(): lax.ppermute(piece, 'frame', [(i, i ^ offset) for i in range(frames)])]
    ppermute x1, waiting for transfers between devices: 0.01 us -> 1.91 us  [per_device_fast(): arrived = lax.ppermute(give, 'row', swap)]
    ppermute x5 -> x6, starting transfers between devices: 9.75 us -> 8.6 us  [partner(): lax.ppermute(piece, 'frame', [(i, i ^ offset) for i in range(frames)])]
    concatenate x2, other arithmetic: 1.16 us -> 0.1 us  [time_embed(): jnp.concatenate([jnp.cos(angles), jnp.sin(angles)], axis=1)]
  transfers between devices with their start and end apart: 17 -> 18, of which waited for: 9 -> 13; matrix products, arithmetic and copies ran while one was open for 0% -> 0% of each run, Pallas kernels for 25% -> 18%
where the time goes in v7:
time: 97 us; the launch traced here: 96.5 us
  waiting for transfers between devices  31.3 us (32%)
  starting transfers between devices  31.2 us (32%)
  Pallas kernels  28.6 us (29%)
  local copies, waits for them, and re-layouts  3.39 us (3%)
  between operations  1.58 us (2%)
    ppermute x6, waiting for transfers between devices, others(): lax.ppermute(piece, 'frame', [(i, i ^ d * stride) for i in range(frames)])  13.7 us
    all_to_all x2, starting transfers between devices, exchange(): lax.all_to_all(packed, 'frame', split_axis=0, concat_axis=0, tiled=True)  13 us
    ppermute x6, starting transfers between devices, others(): lax.ppermute(piece, 'frame', [(i, i ^ d * stride) for i in range(frames)])  9.26 us
    ppermute x6, starting transfers between devices, partner(): lax.ppermute(piece, 'frame', [(i, i ^ offset) for i in range(frames)])  8.6 us
    pallas_call x1, Pallas kernels, per_device_fast(): call(space_fast_kernel, [(wide, f32), (wide, f32), ((length, pair), bf16)...  8.2 us
    ppermute x6, waiting for transfers between devices, partner(): lax.ppermute(piece, 'frame', [(i, i ^ offset) for i in range(frames)])  7.67 us
    pallas_call x1, Pallas kernels, per_device_fast(): call(functools.partial(site_fast_kernel, sites), [(packed, bf16), (wide,...  7.15 us
    pallas_call x1, Pallas kernels, per_device_fast(): call(band_fast_kernel, [(wide, bf16), ((length, pair), bf16), ((length, h...  5.05 us
  transfers between devices with their start and end apart: 18, of which 13 were waited for; matrix products, arithmetic and copies ran while one was open for 0% of the time, Pallas kernels for 18%

profile of v7, /device:TPU:0, one launch (start us, length us, event | category | flops | bytes accessed | tf_op | source)
XLA Modules:
  0.0 96.5 jit_solution(797835064797533632)
XLA Ops:
  1.5 2.8 %start.1 = (bf16[16,2,8,2048]{3,2,1,0:T(8,128)(2,1)}, bf16[152,128]{1,0:T(8,128)(2,1)S(1)}) custom-call(s32[2]{0:T(128)S(1)} %pad_add_fusion.ids_ref, bf16[16,8,2048]{2,1,0:T(8,128)(2,1)} %bitcast.42, bf16[16,8,2048]{2,1,0:T(8,128)(2,1)} %bitcast.46, bf16[128,256]{1,0:T(8,128)(2,1)} %proj_hbm.1, bf16[32,128]{1,0:T(8,128)(2,1)} %bitcast.53, ...), custom_call_target="tpu_custom_call" | custom-call | tf_op jit(solution)/shard_map/start/pallas_call | solution.py:901
  4.3 3.1 %collective-permute-start = (bf16[152,128]{1,0:T(8,128)(2,1)S(1)}, bf16[152,128]{1,0:T(8,128)(2,1)S(1)}, u32[]{:S(2)}, u32[]{:S(2)}) collective-permute-start(bf16[152,128]{1,0:T(8,128)(2,1)S(1)} %get-tuple-element.41), channel_id=1, source_target_pairs={{0,8},{2,10},{4,12},{6,14},{8,0},{10,2},{12,4},{14,6},{16,24},{18,... | collective-permute-start | bytes 116744 | tf_op jit(solution)/shard_map/ppermute | solution.py:840
  7.4 2.6 %collective-permute-start.1 = (bf16[152,128]{1,0:T(8,128)(2,1)S(1)}, bf16[152,128]{1,0:T(8,128)(2,1)S(1)}, u32[]{:S(2)}, u32[]{:S(2)}) collective-permute-start(bf16[152,128]{1,0:T(8,128)(2,1)S(1)} %get-tuple-element.41), channel_id=1, source_target_pairs={{0,16},{2,18},{4,20},{6,22},{8,24},{10,26},{12,28},{14,30},{16,0},... | collective-permute-start | bytes 116744 | tf_op jit(solution)/shard_map/ppermute | solution.py:840
  10.0 7.1 %all-to-all-start = ((bf16[16,2,8,2048]{3,2,1,0:T(8,128)(2,1)}), bf16[16,2,8,2048]{3,2,1,0:T(8,128)(2,1)S(1)}, u32[]{:S(2)}, u32[]{:S(2)}) async-start(bf16[16,2,8,2048]{3,2,1,0:T(8,128)(2,1)} %get-tuple-element.44), calls=%async_computation | async-start | bytes 2097152 | tf_op jit(solution)/shard_map/all_to_all | solution.py:40
  17.2 2.0 %collective-permute-start.3 = (bf16[4,152,128]{2,1,0:T(8,128)(2,1)S(1)}, bf16[4,152,128]{2,1,0:T(8,128)(2,1)S(1)}, u32[]{:S(2)}, u32[]{:S(2)}) collective-permute-start(bf16[4,152,128]{2,1,0:T(8,128)(2,1)S(1)} %pad_maximum_fusion), channel_id=1, source_target_pairs={{0,2},{2,0},{4,6},{6,4},{8,10},{10,8},{12,14},{14,12},{16,18},{18,... | collective-permute-start | bytes 466952 | tf_op jit(solution)/shard_map/ppermute | solution.py:840
  19.1 1.5 %collective-permute-start.4 = (bf16[4,152,128]{2,1,0:T(8,128)(2,1)S(1)}, bf16[4,152,128]{2,1,0:T(8,128)(2,1)S(1)}, u32[]{:S(2)}, u32[]{:S(2)}) collective-permute-start(bf16[4,152,128]{2,1,0:T(8,128)(2,1)S(1)} %pad_maximum_fusion), channel_id=1, source_target_pairs={{0,4},{2,6},{4,0},{6,2},{8,12},{10,14},{12,8},{14,10},{16,20},{18,... | collective-permute-start | bytes 466952 | tf_op jit(solution)/shard_map/ppermute | solution.py:840
  20.7 6.0 %collective-permute-done.3 = bf16[4,152,128]{2,1,0:T(8,128)(2,1)S(1)} collective-permute-done((bf16[4,152,128]{2,1,0:T(8,128)(2,1)S(1)}, bf16[4,152,128]{2,1,0:T(8,128)(2,1)S(1)}, u32[]{:S(2)}, u32[]{:S(2)}) %collective-permute-start.3) | collective-permute-done | bytes 155680 | tf_op jit(solution)/shard_map/ppermute | solution.py:840
  26.8 6.0 %collective-permute-done.4 = bf16[4,152,128]{2,1,0:T(8,128)(2,1)S(1)} collective-permute-done((bf16[4,152,128]{2,1,0:T(8,128)(2,1)S(1)}, bf16[4,152,128]{2,1,0:T(8,128)(2,1)S(1)}, u32[]{:S(2)}, u32[]{:S(2)}) %collective-permute-start.4) | collective-permute-done | bytes 155680 | tf_op jit(solution)/shard_map/ppermute | solution.py:840
  32.8 1.7 %collective-permute-done.5 = bf16[4,152,128]{2,1,0:T(8,128)(2,1)S(1)} collective-permute-done((bf16[4,152,128]{2,1,0:T(8,128)(2,1)S(1)}, bf16[4,152,128]{2,1,0:T(8,128)(2,1)S(1)}, u32[]{:S(2)}, u32[]{:S(2)}) %collective-permute-start.5) | collective-permute-done | bytes 155680 | tf_op jit(solution)/shard_map/ppermute | solution.py:840
  37.7 3.0 %all-to-all-done.got_ref = bf16[16,2,8,2048]{3,2,1,0:T(8,128)(2,1)S(1)} async-done(((bf16[16,2,8,2048]{3,2,1,0:T(8,128)(2,1)}), bf16[16,2,8,2048]{3,2,1,0:T(8,128)(2,1)S(1)}, u32[]{:S(2)}, u32[]{:S(2)}) %all-to-all-start) | async-done | bytes 1048608 | tf_op jit(solution)/shard_map/all_to_all | solution.py:40
  40.7 7.2 %site.1 = (bf16[16,2,8,2048]{3,2,1,0:T(8,128)(2,1)}, bf16[128,2048]{1,0:T(8,128)(2,1)}, f32[2,2048]{1,0:T(2,128)}, bf16[128,256]{1,0:T(8,128)(2,1)S(1)}, bf16[128,32]{1,0:T(8,128)(2,1)S(1)}) custom-call(bf16[16,2,8,2048]{3,2,1,0:T(8,128)(2,1)S(1)} %all-to-all-done.got_ref, f32[1,2048]{1,0:T(1,128)S(1)} %get-tuple-element.42.refs_0_.refs_2_, ...), custom_call_target="tpu_custom_call" | custom-call | tf_op jit(solution)/shard_map/site/pallas_call | solution.py:933
  47.9 5.9 %all-to-all-start.1 = ((bf16[16,2,8,2048]{3,2,1,0:T(8,128)(2,1)}), bf16[16,2,8,2048]{3,2,1,0:T(8,128)(2,1)S(1)}, u32[]{:S(2)}, u32[]{:S(2)}) async-start(bf16[16,2,8,2048]{3,2,1,0:T(8,128)(2,1)} %get-tuple-element.65), calls=%async_computation.1 | async-start | bytes 2097152 | tf_op jit(solution)/shard_map/all_to_all | solution.py:40
  53.9 5.0 %band.1 = (bf16[128,2048]{1,0:T(8,128)(2,1)S(1)}, bf16[128,256]{1,0:T(8,128)(2,1)S(1)}, bf16[128,32]{1,0:T(8,128)(2,1)S(1)}, f32[128,1]{1,0:T(8,128)S(1)}, f32[1...) custom-call(s32[2]{0:T(128)S(1)} %pad_add_fusion.ids_ref, bf16[128,2048]{1,0:T(8,128)(2,1)S(1)} %bitcast.43, ...), custom_call_target="tpu_custom_call" | custom-call | tf_op jit(solution)/shard_map/band/pallas_call | solution.py:958
  58.9 1.9 %collective-permute-done.7.arrived_ref = bf16[2048,128]{1,0:T(8,128)(2,1)S(1)} collective-permute-done((bf16[2048,128]{1,0:T(8,128)(2,1)S(1)}, bf16[2048,128]{1,0:T(8,128)(2,1)S(1)}, u32[]{:S(2)}, u32[]{:S(2)}) %collective-permute-start.7) | collective-permute-done | bytes 524320 | tf_op jit(solution)/shard_map/ppermute | solution.py:971
  60.8 8.2 %space.1 = (f32[128,2048]{1,0:T(8,128)S(1)}, f32[128,2048]{1,0:T(8,128)S(1)}, bf16[128,256]{1,0:T(8,128)(2,1)S(1)}, bf16[128,32]{1,0:T(8,128)(2,1)S(1)}, f32[2,2048]{1,0:T(2,128)S(1)}) custom-call(s32[2]{0:T(128)S(1)} %pad_add_fusion.ids_ref, bf16[2048,128]{1,0:T(8,128)(2,1)S(1)} %collective-permute-done.7.arrived_ref, bf16[128,2048]{1,0:T(8,128)(2,1)S(1)} %bitcast.44, ...), custom_call_target="tpu_custom_call" | custom-call | tf_op jit(solution)/shard_map/space/pallas_call | solution.py:974
  70.6 1.9 %collective-permute-done.8 = bf16[16,152,128]{2,1,0:T(8,128)(2,1)S(1)} collective-permute-done((bf16[16,152,128]{2,1,0:T(8,128)(2,1)S(1)}, bf16[16,152,128]{2,1,0:T(8,128)(2,1)S(1)}, u32[]{:S(2)}, u32[]{:S(2)}) %collective-permute-start.8) | collective-permute-done | bytes 622624 | tf_op jit(solution)/shard_map/ppermute | solution.py:999
  72.7 2.0 %collective-permute-start.10 = (bf16[4,152,128]{2,1,0:T(8,128)(2,1)S(1)}, bf16[4,152,128]{2,1,0:T(8,128)(2,1)S(1)}, u32[]{:S(2)}, u32[]{:S(2)}) collective-permute-start(bf16[4,152,128]{2,1,0:T(8,128)(2,1)S(1)} %get-tuple-element.78), channel_id=1, source_target_pairs={{0,4},{2,6},{4,0},{6,2},{8,12},{10,14},{12,8},{14,10},{16,20},{18,... | collective-permute-start | bytes 466952 | tf_op jit(solution)/shard_map/ppermute | solution.py:858
  74.6 1.5 %collective-permute-start.11 = (bf16[4,152,128]{2,1,0:T(8,128)(2,1)S(1)}, bf16[4,152,128]{2,1,0:T(8,128)(2,1)S(1)}, u32[]{:S(2)}, u32[]{:S(2)}) collective-permute-start(bf16[4,152,128]{2,1,0:T(8,128)(2,1)S(1)} %get-tuple-element.77), channel_id=1, source_target_pairs={{0,6},{2,4},{4,2},{6,0},{8,14},{10,12},{12,10},{14,8},{16,22},{18,... | collective-permute-start | bytes 466952 | tf_op jit(solution)/shard_map/ppermute | solution.py:858
  79.3 1.7 %last.1 = (bf16[128,2048]{1,0:T(8,128)(2,1)}, bf16[128,2048]{1,0:T(8,128)(2,1)}) custom-call(bf16[128,2048]{1,0:T(8,128)(2,1)S(1)} %bitcast.45, f32[128,1]{1,0:T(8,128)S(1)} %get-tuple-element.53.refs_5_.inverse_ref, f32[1,2048]{1,0:T(1,128)S(1)} %get-tuple-element.43.refs_1_.refs_3_.gain_ref, f32[128,2048]{1,0:T(8,128)S(1)} %copy-done.3, ...), custom_call_target="tpu_custom_call" | custom-call | tf_op jit(solution)/shard_map/last/pallas_call | solution.py:1000
  81.0 1.9 %collective-permute-done.10 = bf16[4,152,128]{2,1,0:T(8,128)(2,1)S(1)} collective-permute-done((bf16[4,152,128]{2,1,0:T(8,128)(2,1)S(1)}, bf16[4,152,128]{2,1,0:T(8,128)(2,1)S(1)}, u32[]{:S(2)}, u32[]{:S(2)}) %collective-permute-start.10) | collective-permute-done | bytes 155680 | tf_op jit(solution)/shard_map/ppermute | solution.py:858
  83.9 2.6 %collective-permute-start.12 = (bf16[152,128]{1,0:T(8,128)(2,1)S(1)}, bf16[152,128]{1,0:T(8,128)(2,1)S(1)}, u32[]{:S(2)}, u32[]{:S(2)}) collective-permute-start(bf16[152,128]{1,0:T(8,128)(2,1)S(1)} %get-tuple-element.81), channel_id=1, source_target_pairs={{0,8},{2,10},{4,12},{6,14},{8,0},{10,2},{12,4},{14,6},{16,24},{18,... | collective-permute-start | bytes 116744 | tf_op jit(solution)/shard_map/ppermute | solution.py:858
  86.5 1.5 %collective-permute-start.13 = (bf16[152,128]{1,0:T(8,128)(2,1)S(1)}, bf16[152,128]{1,0:T(8,128)(2,1)S(1)}, u32[]{:S(2)}, u32[]{:S(2)}) collective-permute-start(bf16[152,128]{1,0:T(8,128)(2,1)S(1)} %get-tuple-element.83), channel_id=1, source_target_pairs={{0,16},{2,18},{4,20},{6,22},{8,24},{10,26},{12,28},{14,30},{16,0},... | collective-permute-start | bytes 116744 | tf_op jit(solution)/shard_map/ppermute | solution.py:858
  88.9 3.2 %collective-permute-done.13 = bf16[152,128]{1,0:T(8,128)(2,1)S(1)} collective-permute-done((bf16[152,128]{1,0:T(8,128)(2,1)S(1)}, bf16[152,128]{1,0:T(8,128)(2,1)S(1)}, u32[]{:S(2)}, u32[]{:S(2)}) %collective-permute-start.13) | collective-permute-done | bytes 38944 | tf_op jit(solution)/shard_map/ppermute | solution.py:858
  92.1 1.7 %collective-permute-done.14 = bf16[152,128]{1,0:T(8,128)(2,1)S(1)} collective-permute-done((bf16[152,128]{1,0:T(8,128)(2,1)S(1)}, bf16[152,128]{1,0:T(8,128)(2,1)S(1)}, u32[]{:S(2)}, u32[]{:S(2)}) %collective-permute-start.14) | collective-permute-done | bytes 38944 | tf_op jit(solution)/shard_map/ppermute | solution.py:858
  (63 shorter events, 13.0 us)
Async XLA Ops:
  4.3 12.8 %collective-permute-start = (bf16[152,128]{1,0:T(8,128)(2,1)S(1)}, bf16[152,128]{1,0:T(8,128)(2,1)S(1)}, u32[]{:S(2)}, u32[]{:S(2)}) collective-permute-start(bf16[152,128]{1,0:T(8,128)(2,1)S(1)} %get-tuple-element.41), channel_id=1, source_target_pairs={{0,8},{2,10},{4,12},{6,14},{8,0},{10,2},{12,4},{14,6},{16,24},{18,... | collective-permute-start | bytes 116744 | tf_op jit(solution)/shard_map/ppermute | solution.py:840
  7.4 9.7 %collective-permute-start.1 = (bf16[152,128]{1,0:T(8,128)(2,1)S(1)}, bf16[152,128]{1,0:T(8,128)(2,1)S(1)}, u32[]{:S(2)}, u32[]{:S(2)}) collective-permute-start(bf16[152,128]{1,0:T(8,128)(2,1)S(1)} %get-tuple-element.41), channel_id=1, source_target_pairs={{0,16},{2,18},{4,20},{6,22},{8,24},{10,26},{12,28},{14,30},{16,0},... | collective-permute-start | bytes 116744 | tf_op jit(solution)/shard_map/ppermute | solution.py:840
  10.0 7.1 %collective-permute-start.2 = (bf16[152,128]{1,0:T(8,128)(2,1)S(1)}, bf16[152,128]{1,0:T(8,128)(2,1)S(1)}, u32[]{:S(2)}, u32[]{:S(2)}) collective-permute-start(bf16[152,128]{1,0:T(8,128)(2,1)S(1)} %get-tuple-element.41), channel_id=1, source_target_pairs={{0,24},{2,26},{4,28},{6,30},{8,16},{10,18},{12,20},{14,22},{16,8},... | collective-permute-start | bytes 116744 | tf_op jit(solution)/shard_map/ppermute | solution.py:840
  10.0 30.7 %all-to-all-start = ((bf16[16,2,8,2048]{3,2,1,0:T(8,128)(2,1)}), bf16[16,2,8,2048]{3,2,1,0:T(8,128)(2,1)S(1)}, u32[]{:S(2)}, u32[]{:S(2)}) async-start(bf16[16,2,8,2048]{3,2,1,0:T(8,128)(2,1)} %get-tuple-element.44), calls=%async_computation | async-start | bytes 2097152 | tf_op jit(solution)/shard_map/all_to_all | solution.py:40
  17.2 9.6 %collective-permute-start.3 = (bf16[4,152,128]{2,1,0:T(8,128)(2,1)S(1)}, bf16[4,152,128]{2,1,0:T(8,128)(2,1)S(1)}, u32[]{:S(2)}, u32[]{:S(2)}) collective-permute-start(bf16[4,152,128]{2,1,0:T(8,128)(2,1)S(1)} %pad_maximum_fusion), channel_id=1, source_target_pairs={{0,2},{2,0},{4,6},{6,4},{8,10},{10,8},{12,14},{14,12},{16,18},{18,... | collective-permute-start | bytes 466952 | tf_op jit(solution)/shard_map/ppermute | solution.py:840
  19.1 13.6 %collective-permute-start.4 = (bf16[4,152,128]{2,1,0:T(8,128)(2,1)S(1)}, bf16[4,152,128]{2,1,0:T(8,128)(2,1)S(1)}, u32[]{:S(2)}, u32[]{:S(2)}) collective-permute-start(bf16[4,152,128]{2,1,0:T(8,128)(2,1)S(1)} %pad_maximum_fusion), channel_id=1, source_target_pairs={{0,4},{2,6},{4,0},{6,2},{8,12},{10,14},{12,8},{14,10},{16,20},{18,... | collective-permute-start | bytes 466952 | tf_op jit(solution)/shard_map/ppermute | solution.py:840
  20.6 13.9 %collective-permute-start.5 = (bf16[4,152,128]{2,1,0:T(8,128)(2,1)S(1)}, bf16[4,152,128]{2,1,0:T(8,128)(2,1)S(1)}, u32[]{:S(2)}, u32[]{:S(2)}) collective-permute-start(bf16[4,152,128]{2,1,0:T(8,128)(2,1)S(1)} %pad_maximum_fusion), channel_id=1, source_target_pairs={{0,6},{2,4},{4,2},{6,0},{8,14},{10,12},{12,10},{14,8},{16,22},{18,... | collective-permute-start | bytes 466952 | tf_op jit(solution)/shard_map/ppermute | solution.py:840
  34.5 2.1 %collective-permute-start.6 = (bf16[16,152,128]{2,1,0:T(8,128)(2,1)S(1)}, bf16[16,152,128]{2,1,0:T(8,128)(2,1)S(1)}, u32[]{:S(2)}, u32[]{:S(2)}) collective-permute-start(bf16[16,152,128]{2,1,0:T(8,128)(2,1)S(1)} %constant_dynamic-update-slice_fusion.own_ref), channel_id=1, source_target_pairs={{0,1},{1,0},{2,3},{3,2},{4,5},{5,4},{6,7},{7,6},{8,9},{9,8},{10,11... | collective-permute-start | bytes 1867784 | tf_op jit(solution)/shard_map/ppermute | solution.py:925
  47.9 6.0 %copy-start = (bf16[1,1,128,2048]{3,2,1,0:T(8,128)(2,1)S(1)}, bf16[1,1,128,2048]{3,2,1,0:T(8,128)(2,1)}, u32[]{:S(2)}) copy-start(bf16[1,1,128,2048]{3,2,1,0:T(8,128)(2,1)} %param.10) | copy-start | bytes 1572868
  47.9 6.0 %copy-start.1 = (bf16[1,1,128,2048]{3,2,1,0:T(8,128)(2,1)S(1)}, bf16[1,1,128,2048]{3,2,1,0:T(8,128)(2,1)}, u32[]{:S(2)}) copy-start(bf16[1,1,128,2048]{3,2,1,0:T(8,128)(2,1)} %param.11) | copy-start | bytes 1572868
  47.9 28.9 %all-to-all-start.1 = ((bf16[16,2,8,2048]{3,2,1,0:T(8,128)(2,1)}), bf16[16,2,8,2048]{3,2,1,0:T(8,128)(2,1)S(1)}, u32[]{:S(2)}, u32[]{:S(2)}) async-start(bf16[16,2,8,2048]{3,2,1,0:T(8,128)(2,1)} %get-tuple-element.65), calls=%async_computation.1 | async-start | bytes 2097152 | tf_op jit(solution)/shard_map/all_to_all | solution.py:40
  58.9 1.9 %collective-permute-start.7 = (bf16[2048,128]{1,0:T(8,128)(2,1)S(1)}, bf16[2048,128]{1,0:T(8,128)(2,1)S(1)}, u32[]{:S(2)}, u32[]{:S(2)}) collective-permute-start(bf16[2048,128]{1,0:T(8,128)(2,1)S(1)} %get-tuple-element.50), channel_id=1, source_target_pairs={{0,1},{1,0},{2,3},{3,2},{4,5},{5,4},{6,7},{7,6},{8,9},{9,8},{10,11... | collective-permute-start | bytes 1572872 | tf_op jit(solution)/shard_map/ppermute | solution.py:971
  60.8 8.2 %copy-start.6 = (bf16[128,2048]{1,0:T(8,128)(2,1)S(1)}, bf16[128,2048]{1,0:T(8,128)(2,1)}, u32[]{:S(2)}) copy-start(bf16[128,2048]{1,0:T(8,128)(2,1)} %get-tuple-element.57.site_x) | copy-start | bytes 1572868
  60.8 8.2 %copy-start.7 = (f32[2,2048]{1,0:T(2,128)S(1)}, f32[2,2048]{1,0:T(2,128)}, u32[]{:S(2)}) copy-start(f32[2,2048]{1,0:T(2,128)} %get-tuple-element.60.site_gmod) | copy-start | bytes 49156
  69.0 3.6 %copy-start.2 = (f32[128,2048]{1,0:T(8,128)}, f32[128,2048]{1,0:T(8,128)S(1)}, u32[]{:S(2)}) copy-start(f32[128,2048]{1,0:T(8,128)S(1)} %get-tuple-element.63.mix_ref) | copy-start | bytes 3145732
  69.0 3.6 %copy-start.4 = (f32[128,2048]{1,0:T(8,128)}, f32[128,2048]{1,0:T(8,128)S(1)}, u32[]{:S(2)}) copy-start(f32[128,2048]{1,0:T(8,128)S(1)} %get-tuple-element.64.pre_ref) | copy-start | bytes 3145732
  70.4 2.1 %collective-permute-start.8 = (bf16[16,152,128]{2,1,0:T(8,128)(2,1)S(1)}, bf16[16,152,128]{2,1,0:T(8,128)(2,1)S(1)}, u32[]{:S(2)}, u32[]{:S(2)}) collective-permute-start(bf16[16,152,128]{2,1,0:T(8,128)(2,1)S(1)} %get-tuple-element.62), channel_id=1, source_target_pairs={{0,1},{1,0},{2,3},{3,2},{4,5},{5,4},{6,7},{7,6},{8,9},{9,8},{10,11... | collective-permute-start | bytes 1867784 | tf_op jit(solution)/shard_map/ppermute | solution.py:999
  72.7 10.2 %collective-permute-start.10 = (bf16[4,152,128]{2,1,0:T(8,128)(2,1)S(1)}, bf16[4,152,128]{2,1,0:T(8,128)(2,1)S(1)}, u32[]{:S(2)}, u32[]{:S(2)}) collective-permute-start(bf16[4,152,128]{2,1,0:T(8,128)(2,1)S(1)} %get-tuple-element.78), channel_id=1, source_target_pairs={{0,4},{2,6},{4,0},{6,2},{8,12},{10,14},{12,8},{14,10},{16,20},{18,... | collective-permute-start | bytes 466952 | tf_op jit(solution)/shard_map/ppermute | solution.py:858
  74.6 8.3 %collective-permute-start.11 = (bf16[4,152,128]{2,1,0:T(8,128)(2,1)S(1)}, bf16[4,152,128]{2,1,0:T(8,128)(2,1)S(1)}, u32[]{:S(2)}, u32[]{:S(2)}) collective-permute-start(bf16[4,152,128]{2,1,0:T(8,128)(2,1)S(1)} %get-tuple-element.77), channel_id=1, source_target_pairs={{0,6},{2,4},{4,2},{6,0},{8,14},{10,12},{12,10},{14,8},{16,22},{18,... | collective-permute-start | bytes 466952 | tf_op jit(solution)/shard_map/ppermute | solution.py:858
  76.1 7.7 %collective-permute-start.9 = (bf16[4,152,128]{2,1,0:T(8,128)(2,1)S(1)}, bf16[4,152,128]{2,1,0:T(8,128)(2,1)S(1)}, u32[]{:S(2)}, u32[]{:S(2)}) collective-permute-start(bf16[4,152,128]{2,1,0:T(8,128)(2,1)S(1)} %get-tuple-element.79), channel_id=1, source_target_pairs={{0,2},{2,0},{4,6},{6,4},{8,10},{10,8},{12,14},{14,12},{16,18},{18,... | collective-permute-start | bytes 466952 | tf_op jit(solution)/shard_map/ppermute | solution.py:858
  83.9 5.0 %collective-permute-start.12 = (bf16[152,128]{1,0:T(8,128)(2,1)S(1)}, bf16[152,128]{1,0:T(8,128)(2,1)S(1)}, u32[]{:S(2)}, u32[]{:S(2)}) collective-permute-start(bf16[152,128]{1,0:T(8,128)(2,1)S(1)} %get-tuple-element.81), channel_id=1, source_target_pairs={{0,8},{2,10},{4,12},{6,14},{8,0},{10,2},{12,4},{14,6},{16,24},{18,... | collective-permute-start | bytes 116744 | tf_op jit(solution)/shard_map/ppermute | solution.py:858
  86.5 5.6 %collective-permute-start.13 = (bf16[152,128]{1,0:T(8,128)(2,1)S(1)}, bf16[152,128]{1,0:T(8,128)(2,1)S(1)}, u32[]{:S(2)}, u32[]{:S(2)}) collective-permute-start(bf16[152,128]{1,0:T(8,128)(2,1)S(1)} %get-tuple-element.83), channel_id=1, source_target_pairs={{0,16},{2,18},{4,20},{6,22},{8,24},{10,26},{12,28},{14,30},{16,0},... | collective-permute-start | bytes 116744 | tf_op jit(solution)/shard_map/ppermute | solution.py:858
  88.0 5.8 %collective-permute-start.14 = (bf16[152,128]{1,0:T(8,128)(2,1)S(1)}, bf16[152,128]{1,0:T(8,128)(2,1)S(1)}, u32[]{:S(2)}, u32[]{:S(2)}) collective-permute-start(bf16[152,128]{1,0:T(8,128)(2,1)S(1)} %get-tuple-element.82), channel_id=1, source_target_pairs={{0,24},{2,26},{4,28},{6,30},{8,16},{10,18},{12,20},{14,22},{16,8},... | collective-permute-start | bytes 116744 | tf_op jit(solution)/shard_map/ppermute | solution.py:858
  93.8 1.3 %collective-permute-start.15 = (f32[152,128]{1,0:T(8,128)S(1)}, f32[152,128]{1,0:T(8,128)S(1)}, u32[]{:S(2)}, u32[]{:S(2)}) collective-permute-start(f32[152,128]{1,0:T(8,128)S(1)} %fusion.1.own_ref), channel_id=1, source_target_pairs={{0,1},{1,0},{2,3},{3,2},{4,5},{5,4},{6,7},{7,6},{8,9},{9,8},{10,11... | collective-permute-start | bytes 233480 | tf_op jit(solution)/shard_map/ppermute | solution.py:1004
  (6 other events, 5.1 us)

commit v8 on v7

--- a/solution.py
+++ b/solution.py
@@ -17,9 +17,11 @@
 
 def time_embed(timestep, embed_dim):
     half_dim = embed_dim // 2
-    frequency = jnp.exp(-math.log(10000.0) * jnp.arange(half_dim, dtype=f32) / half_dim)
+    place = (jnp.arange(embed_dim) % half_dim).astype(f32)
+    frequency = jnp.exp(-math.log(10000.0) * place / half_dim)
     angles = timestep.astype(f32)[:, None] * frequency[None, :]
-    return jax.nn.silu(jnp.concatenate([jnp.cos(angles), jnp.sin(angles)], axis=1))
+    lower = jnp.arange(embed_dim)[None, :] < half_dim
+    return jax.nn.silu(jnp.where(lower, jnp.cos(angles), jnp.sin(angles)))
 
 
 def to_tiles(a):
@@ -108,39 +110,51 @@
     return z, step, cum, cum_rows
 
 
-def expand(parts, lanes_of):
-    return mm(parts[0], lanes_of, 1, 0) + mm(parts[1], lanes_of, 1, 0)
+def halves_of(a):
+    return jnp.concatenate(split(a), axis=1)
+
+
+def doubled(lanes_of):
+    return jnp.concatenate([lanes_of, lanes_of], axis=0)
 
 
 def scan_block(j, x, grad, step_wide, scores, cum, cum_rows, heads, width, d_scores):
     size = width // heads
     per_block = LANES // size
+    length = x.shape[0]
     stepped = (x.astype(f32) * step_wide).astype(bf16)
     lane = lax.broadcasted_iota(jnp.int32, x.shape, 1)
-    weights, steppeds, grads = [], [], []
+    inside = [lane // size == i for i in range(per_block)]
+    zero = jnp.zeros_like(x)
+    steppeds = jnp.concatenate([jnp.where(own, stepped, zero) for own in inside], axis=0)
+    grads = jnp.concatenate([jnp.where(own, grad, zero) for own in inside], axis=0)
+    d_weights = mm(grads, stepped, 1, 1)
+    weights = []
     for i in range(per_block):
         h = j * per_block + i
         decay = jnp.exp(jnp.minimum(cum[:, h : h + 1] - cum_rows[h : h + 1, :], 0.0))
-        inside = lane // size == i
-        own_grad = jnp.where(inside, grad, jnp.zeros_like(grad))
-        d_weight = mm(own_grad, stepped, 1, 1)
-        d_scores = d_scores + d_weight * decay
+        d_scores = d_scores + d_weights[i * length : (i + 1) * length] * decay
         weights.append((scores * decay).astype(bf16))
-        steppeds.append(jnp.where(inside, stepped, jnp.zeros_like(stepped)))
-        grads.append(own_grad)
-    out = mm(jnp.concatenate(weights, axis=1), jnp.concatenate(steppeds, axis=0), 1, 0)
-    d_stepped = mm(jnp.concatenate(weights, axis=0), jnp.concatenate(grads, axis=0), 0, 0)
+    out = mm(jnp.concatenate(weights, axis=1), steppeds, 1, 0)
+    d_stepped = mm(jnp.concatenate(weights, axis=0), grads, 0, 0)
     return stepped, out, d_stepped, d_scores
 
 
-def head_sums(high_ref, low_ref, lanes_of):
-    return mm(high_ref[...], lanes_of, 1, 1) + mm(low_ref[...], lanes_of, 1, 1)
-
-
-def put(refs, sl, value):
-    high, low = split(value)
-    refs[0][:, sl] = high
-    refs[1][:, sl] = low
+def put(sums_ref, which, sl, value):
+    length = value.shape[0]
+    for n, part in enumerate(split(value)):
+        at = (2 * which + n) * length
+        sums_ref[at : at + length, sl] = part
+
+
+def head_sums(sums_ref, lanes_of, length):
+    sums = mm(sums_ref[...], lanes_of, 1, 1)
+    sums = [sums[at : at + length] for at in range(0, sums.shape[0], length)]
+    return [sums[n] + sums[n + 1] for n in range(0, len(sums), 2)]
+
+
+def wide_blocks(width):
+    return [(slice(at, at + 2 * LANES)) for at in range(0, width, 2 * LANES)]
 
 
 def start_kernel(ids_ref, tok_ref, grad_ref, proj_hbm, step_hbm, mod_hbm, active_ref, sent_ref, pay_ref,
@@ -234,8 +248,11 @@
             at += part
         step_ref[pl.ds(pl.multiple_of(half * heads, heads), heads), :] = ref[at : at + heads, :] * factor
         at += heads
+    rest = jnp.zeros((7, active_ref.shape[1]), f32)
+    active = jnp.concatenate([active_ref[...].astype(f32), rest], axis=0)
     for k, sl in blocks(mod_ref.shape[1]):
-        mod_ref[:, sl] = active_ref[...] * (own_ref[at + k : at + k + 1, :] * factor)
+        own = jnp.broadcast_to(own_ref[at + k : at + k + 1, :] * factor, (8, LANES))
+        mod_ref[:, sl] = exact(active, own, 0, 0)
 
 
 def site_fast_kernel(sites, got_ref, *refs):
@@ -249,7 +266,7 @@
             value = got_ref[:, which, :, sl].astype(f32)
             ref[:, sl] = value.reshape(frames * sites, LANES).astype(bf16)
 
-    parts = 2
+    parts = 4
     share = width // parts
     copies = []
 
@@ -269,7 +286,7 @@
         def __setitem__(self, at, value):
             if not copies:
                 begin(x_ref, x_hbm)
-            value = value.astype(f32).reshape(frames, sites, LANES)
+            value = value.astype(f32).reshape(frames, sites, value.shape[1])
             sent_ref[:, self.which, :, at[1]] = value.astype(bf16)
             if at[1].stop % share == 0:
                 send(self.which, at[1].stop // share - 1)
@@ -299,10 +316,7 @@
     gmod_ref,
     x_ref,
     dn_ref,
-    a_hi,
-    a_lo,
-    b_hi,
-    b_lo,
+    sums_ref,
 ):
     length, width = tok_ref.shape
     heads = step_ref.shape[0]
@@ -317,27 +331,26 @@
     z, step, cum, cum_rows = steps_of(logits, bias_ref[...], rate, mask)
     b_part, c_part = coeffs[:, :state], coeffs[:, state:]
     scores = mm(c_part, b_part, 1, 1) * (mask / state)
-    step_parts = split(step)
+    step_parts, twice = halves_of(step), doubled(lanes_of)
     d_scores = jnp.zeros((length, length), f32)
     for j, sl in blocks(width):
         x, grad = x_ref[:, sl], grad_ref[:, sl]
-        step_wide = expand(step_parts, lanes_of[:, sl])
+        step_wide = mm(step_parts, twice[:, sl], 1, 0)
         stepped, out, d_stepped, d_scores = scan_block(
             j, x, grad, step_wide, scores, cum, cum_rows, heads, width, d_scores
         )
         out_ref[:, sl] = out.astype(bf16)
         dn_ref[:, sl] = (step_wide * d_stepped).astype(bf16)
-        put((a_hi, a_lo), sl, grad.astype(f32) * out - stepped.astype(f32) * d_stepped)
-        put((b_hi, b_lo), sl, x.astype(f32) * d_stepped)
-    d_cum = head_sums(a_hi, a_lo, lanes_of)
-    d_step = head_sums(b_hi, b_lo, lanes_of)
+        put(sums_ref, 0, sl, grad.astype(f32) * out - stepped.astype(f32) * d_stepped)
+        put(sums_ref, 1, sl, x.astype(f32) * d_stepped)
+    d_cum, d_step = head_sums(sums_ref, lanes_of, length)
     d_log = exact(mask, d_cum, 0, 0)
     d_logits = (jax.nn.sigmoid(z) * (d_step - rate * d_log)).astype(bf16)
     d_scores = (d_scores * (mask / state)).astype(bf16)
     d_coeffs = jnp.concatenate(
         [mm(d_scores, c_part, 0, 0), mm(d_scores, b_part, 1, 0)], axis=1
     ).astype(bf16)
-    for _, sl in blocks(width):
+    for sl in wide_blocks(width):
         back = (
             dn_ref[:, sl].astype(f32)
             + mm(d_coeffs, proj_ref[sl, :], 1, 1)
@@ -361,7 +374,7 @@
 def band_fast_kernel(ids_ref, *refs):
     small_ref, give_ref = refs[6], refs[-1]
     inputs = (*refs[:6], small_ref[0:1, :], small_ref[2:3, :])
-    band_kernel(*inputs, *refs[7:-1], None, give_ref, first=ids_ref[1] == 0)
+    band_kernel(*inputs, *refs[7:-1], None, None, give_ref, first=ids_ref[1] == 0)
 
 
 def band_kernel(
@@ -386,7 +399,7 @@
     heads = step_ref.shape[0]
     state = proj_ref.shape[1] // 2
     inverse_ref[...] = normalize_into(tok_ref, shift_ref, gain_ref, x_ref)
-    lanes_of = head_map(heads, width)
+    twice = doubled(head_map(heads, width))
     mask = sequence_mask(length, 1)
     coeffs = mm(x_ref[...], proj_ref[...], 1, 0).astype(bf16)
     logits = mm(x_ref[...], step_ref[...], 1, 1).astype(bf16)
@@ -394,21 +407,21 @@
     logits_ref[...] = logits
     _, step, cum, _ = steps_of(logits, bias_ref[...], rate_ref[...], mask)
     last = cum[length - 1 : length, :]
-    decay_ref[...] = jnp.exp(last)
-    lead = split(jnp.exp(last - cum) * step)
-    reach = split(jnp.exp(cum) / state)
     b_part, c_part = coeffs[:, :state], coeffs[:, state:]
     if first is not None:
-        gain = split(jnp.where(first, jnp.exp(last - cum) * step, jnp.exp(cum) / state))
+        gain = halves_of(jnp.where(first, jnp.exp(last - cum) * step, jnp.exp(cum) / state))
         other = jnp.where(first, b_part, c_part)
         for _, sl in blocks(width):
             value = jnp.where(first, x_ref[:, sl], grad_ref[:, sl]).astype(f32)
-            value = (value * expand(gain, lanes_of[:, sl])).astype(bf16)
+            value = (value * mm(gain, twice[:, sl], 1, 0)).astype(bf16)
             own_ref[sl, :] = mm(value, other, 0, 0).astype(bf16)
         return
+    decay_ref[...] = jnp.exp(last)
+    lead = halves_of(jnp.exp(last - cum) * step)
+    reach = halves_of(jnp.exp(cum) / state)
     for _, sl in blocks(width):
-        lead_wide = expand(lead, lanes_of[:, sl])
-        reach_wide = expand(reach, lanes_of[:, sl])
+        lead_wide = mm(lead, twice[:, sl], 1, 0)
+        reach_wide = mm(reach, twice[:, sl], 1, 0)
         scaled = (x_ref[:, sl].astype(f32) * lead_wide).astype(bf16)
         faded = (grad_ref[:, sl].astype(f32) * reach_wide).astype(bf16)
         end_ref[sl, :] = mm(scaled, b_part, 0, 0).astype(bf16)
@@ -436,7 +449,7 @@
 
     for j, sl in blocks(width):
         offset = jnp.bitwise_xor(me, j)
-        place = jnp.bitwise_and(offset, radix - 1) * radix + offset // radix
+        place = jnp.bitwise_and(offset, radix - 1) * radix + j // radix
         tall = jnp.concatenate([x_ref[:, sl], site_x[:, sl]], axis=0)
         at = put_halves(place, 0, mm(tall, coeffs, 0, 0))
         at = put_halves(place, at, mm(logits, tall, 0, 0))
@@ -454,17 +467,7 @@
 def space_fast_kernel(ids_ref, arrived_ref, *refs):
     inputs, small_ref, outs = refs[:8], refs[8], refs[9:]
     inputs = (*inputs, *(small_ref[n : n + 1, :] for n in (0, 2, 3)))
-    first = ids_ref[1] == 0
-
-    class Arrived:
-        def __init__(self, wanted):
-            self.wanted = wanted
-
-        def __getitem__(self, at):
-            value = arrived_ref[at]
-            return jnp.where(self.wanted, value, jnp.zeros_like(value))
-
-    space_kernel(*inputs, Arrived(jnp.logical_not(first)), Arrived(first), None, None, *outs)
+    space_kernel(*inputs, arrived_ref, None, None, None, *outs, first=ids_ref[1] == 0)
 
 
 def space_kernel(
@@ -489,64 +492,80 @@
     gstep_ref,
     gmod_ref,
     dn_ref,
-    a_hi,
-    a_lo,
-    b_hi,
-    b_lo,
-    c_hi,
-    c_lo,
+    sums_ref,
+    first=None,
 ):
     length, width = tok_ref.shape
     heads = step_ref.shape[0]
     state = proj_ref.shape[1] // 2
     lanes_of = head_map(heads, width)
+    twice = doubled(lanes_of)
     mask = sequence_mask(length, 1)
     coeffs = coeffs_ref[...]
     rate = rate_ref[...]
     z, step, cum, cum_rows = steps_of(logits_ref[...], bias_ref[...], rate, mask)
     last = cum[length - 1 : length, :]
     rest = jnp.exp(last - cum)
-    lead = rest * step
+    lead, reach = rest * step, jnp.exp(cum) / state
     b_part, c_part = coeffs[:, :state], coeffs[:, state:]
     scores = mm(c_part, b_part, 1, 1) * (mask / state)
-    step_parts, lead_parts, reach_parts = split(step), split(lead), split(jnp.exp(cum) / state)
-    skip_parts = split(jnp.broadcast_to(skip_ref[...], (8, heads)))
+    skip = jnp.broadcast_to(skip_ref[...], (8, heads))
+    if first is None:
+        parts = [step, lead, reach, skip]
+    else:
+        parts = [step, jnp.where(first, lead, reach), skip]
+        chosen = jnp.where(first, b_part, c_part)
+        is_first = jnp.where(first, 1.0, 0.0).astype(f32)
+        is_second = 1.0 - is_first
+    parts = jnp.concatenate([halves_of(part) for part in parts], axis=0)
     d_scores = jnp.zeros((length, length), f32)
     d_b = jnp.zeros((length, state), f32)
     d_c = jnp.zeros((length, state), f32)
     d_end = jnp.zeros((heads, state), f32)
     for j, sl in blocks(width):
         x, grad = x_ref[:, sl], grad_ref[:, sl]
-        wide_map = lanes_of[:, sl]
-        step_wide = expand(step_parts, wide_map)
-        lead_wide = expand(lead_parts, wide_map)
-        reach_wide = expand(reach_parts, wide_map)
+        wide_parts = mm(parts, twice[:, sl], 1, 0)
+        step_wide, lead_wide = wide_parts[:length], wide_parts[length : 2 * length]
+        skip = wide_parts[-8:-7]
         stepped, out, d_stepped, d_scores = scan_block(
             j, x, grad, step_wide, scores, cum, cum_rows, heads, width, d_scores
         )
-        x, wide = x.astype(f32), grad.astype(f32)
-        before, later = state_ref[sl, :], later_ref[sl, :]
-        carried = mm(c_part, before, 1, 1) * reach_wide
-        d_c = d_c + mm((wide * reach_wide).astype(bf16), before, 1, 0)
-        d_b = d_b + mm((x * lead_wide).astype(bf16), later, 1, 0)
-        d_scaled = mm(b_part, later, 1, 1)
-        both = split(before.astype(f32) * later.astype(f32))
-        d_end = d_end + mm(wide_map, both[0], 1, 0) + mm(wide_map, both[1], 1, 0)
-        total = out + carried
-        skip = expand(skip_parts, wide_map)[0:1, :]
+        if first is None:
+            x, wide = x.astype(f32), grad.astype(f32)
+            reach_wide = wide_parts[2 * length : 3 * length]
+            before, later = state_ref[sl, :], later_ref[sl, :]
+            total = out + mm(c_part, before, 1, 1) * reach_wide
+            d_c = d_c + mm((wide * reach_wide).astype(bf16), before, 1, 0)
+            d_b = d_b + mm((x * lead_wide).astype(bf16), later, 1, 0)
+            d_scaled = mm(b_part, later, 1, 1)
+            d_x = step_wide * d_stepped + d_scaled * lead_wide
+            both = split(before.astype(f32) * later.astype(f32))
+            d_end = d_end + mm(lanes_of[:, sl], both[0], 1, 0) + mm(lanes_of[:, sl], both[1], 1, 0)
+        else:
+            arrived = state_ref[sl, :]
+            value = jnp.where(first, x, grad).astype(f32)
+            d_b = d_b + mm((value * lead_wide).astype(bf16), arrived, 1, 0)
+            x, wide = x.astype(f32), grad.astype(f32)
+            d_scaled = mm(chosen, arrived, 1, 1)
+            carried = d_scaled * lead_wide
+            total = out + carried * is_second
+            d_x = step_wide * d_stepped + carried * is_first
+            d_scaled = d_scaled * is_first
         mix_ref[:, sl] = total + skip * x
-        d_x = (step_wide * d_stepped + d_scaled * lead_wide).astype(bf16)
-        dn_ref[:, sl] = d_x + (wide * skip).astype(bf16)
-        put((a_hi, a_lo), sl, wide * total - stepped.astype(f32) * d_stepped)
-        put((b_hi, b_lo), sl, x * d_stepped)
-        put((c_hi, c_lo), sl, x * d_scaled)
-    d_lead = head_sums(c_hi, c_lo, lanes_of)
-    d_step = head_sums(b_hi, b_lo, lanes_of) + d_lead * rest
+        dn_ref[:, sl] = d_x.astype(bf16) + (wide * skip).astype(bf16)
+        put(sums_ref, 0, sl, wide * total - stepped.astype(f32) * d_stepped)
+        put(sums_ref, 1, sl, x * d_stepped)
+        put(sums_ref, 2, sl, x * d_scaled)
+    d_cum, d_step, d_lead = head_sums(sums_ref, lanes_of, length)
+    d_step = d_step + d_lead * rest
     fall = d_lead * lead
-    d_cum = head_sums(a_hi, a_lo, lanes_of) - fall
-    ones = jnp.ones((8, state), f32)
-    end_sum = exact(ones, d_end, 1, 1)[0:1, :] * jnp.exp(last)
-    end_sum = end_sum + jnp.sum(fall, axis=0, keepdims=True)
+    d_cum = d_cum - fall
+    end_sum = jnp.sum(fall, axis=0, keepdims=True)
+    if first is None:
+        ones = jnp.ones((8, state), f32)
+        end_sum = end_sum + exact(ones, d_end, 1, 1)[0:1, :] * jnp.exp(last)
+    else:
+        d_b, d_c = d_b * is_first, d_b * is_second
     d_log = exact(mask, d_cum, 0, 0) + end_sum
     d_logits = (jax.nn.sigmoid(z) * (d_step - rate * d_log)).astype(bf16)
     d_scores = (d_scores * (mask / state)).astype(bf16)
@@ -557,7 +576,7 @@
     if gproj_in is None:
         gproj_ref[...] = d_coeffs
         gstep_ref[...] = d_logits
-    for _, sl in blocks(width):
+    for sl in wide_blocks(width):
         pre = (
             dn_ref[:, sl].astype(f32)
             + mm(d_coeffs, proj_ref[sl, :], 1, 1)
@@ -729,7 +748,7 @@
     site_out, site_back, gproj, gstep, site_gmod = call(
         functools.partial(site_kernel, sites),
         [(wide, bf16), (wide, bf16), ((width, pair), f32), ((heads, width), f32), ((2 * clips, width), f32)],
-        [(wide, bf16)] * 6,
+        [(wide, bf16)] * 2 + [((4 * length, width), bf16)],
         name="site",
     )(site_tok, site_grad, shift, gain, proj_full, step_full, bias, rate_time[None])
 
@@ -765,7 +784,7 @@
     mix, pre, gproj, gstep, gmod = call(
         space_kernel,
         [(wide, f32), (wide, f32), ((width, pair), bf16), ((heads, width), bf16), ((2, width), f32)],
-        [(wide, bf16)] * 7,
+        [(wide, bf16), ((6 * length, width), bf16)],
         name="space",
     )(
         tok,
@@ -862,8 +881,9 @@
     near = [near[0]] + [partner(near[d], d) for d in range(1, radix)]
     near, ahead = lax.optimization_barrier((near, ahead))
     near = total(near).astype(bf16)
-    far = [near[0]] + [partner(near[d], d * radix) for d in range(1, radix)]
-    return total(far), *ahead
+    planes = [[p * radix + i for p in range(radix)] for i in range(radix)]
+    far = lax.all_to_all(near, "frame", 0, 0, tiled=True, axis_index_groups=planes)
+    return jnp.sum(far.astype(f32), axis=0), *ahead
 
 
 def per_device_fast(
@@ -945,9 +965,9 @@
             (packed, bf16),
             (wide, bf16),
             ((2, width), f32),
-            pltpu.SemaphoreType.DMA((6,)),
+            pltpu.SemaphoreType.DMA((10,)),
         ]
-        + [(wide, bf16)] * 5,
+        + [(wide, bf16), ((4 * length, width), bf16)],
         name="site",
         specs="vvvvvv",
         hbm_outs=(0, 1, 2),
@@ -955,14 +975,13 @@
     sent, proj_full = lax.optimization_barrier((sent, proj_full))
     came = exchange(sent)
 
-    normed, coeffs, logits, inverse, _, give = call(
+    normed, coeffs, logits, inverse, give = call(
         band_fast_kernel,
         [
             (wide, bf16),
             ((length, pair), bf16),
             ((length, heads), bf16),
             ((length, 1), f32),
-            ((1, heads), f32),
             ((width, state), bf16),
         ],
         name="band",
@@ -974,7 +993,7 @@
     mix, pre, own_dc, own_dl, gmod = call(
         space_fast_kernel,
         [(wide, f32), (wide, f32), ((length, pair), bf16), ((length, heads), bf16), ((2, width), f32)],
-        [(wide, bf16)] * 7,
+        [(wide, bf16), ((6 * length, width), bf16)],
         name="space",
         specs="s" + "v" * 10,
     )(
@@ -1007,7 +1026,7 @@
         [((depth, pair), f32), ((heads, depth), f32), ((mod_weight.shape[0], mod_cols), f32)],
         name="finish",
         specs="svvv",
-    )(ids, terms, other, activated.astype(f32).T)
+    )(ids, terms, other, activated)
     return (mixed.reshape(tokens.shape), d_tokens.reshape(tokens.shape), grad_proj, grad_step.T, grad_mod)
 
 

time: 97 us -> 97.9 us (level)
  blocking collectives: 0 us -> 11.5 us
  starting transfers between devices: 31.2 us -> 26.3 us
  waiting for transfers between devices: 31.3 us -> 28.3 us
  Pallas kernels: 28.6 us -> 26.1 us
    all_to_all x0 -> x1, blocking collectives: none -> 11.5 us  [sum_over_frames(): lax.all_to_all(near, 'frame', 0, 0, tiled=True, axis_index_groups=planes)]
    ppermute x6 -> x3, waiting for transfers between devices: 7.67 us -> 1.61 us  [partner(): lax.ppermute(piece, 'frame', [(i, i ^ offset) for i in range(frames)])]
    ppermute x6 -> x3, starting transfers between devices: 8.6 us -> 3.55 us  [partner(): lax.ppermute(piece, 'frame', [(i, i ^ offset) for i in range(frames)])]
    all_to_all x2, waiting for transfers between devices: 3.64 us -> 6.99 us  [exchange(): lax.all_to_all(packed, 'frame', split_axis=0, concat_axis=0, tiled=True)]
    pallas_call x1, Pallas kernels: 5.05 us -> 2.42 us  [per_device_fast(): call(band_fast_kernel, [(wide, bf16), ((length, pair), bf16), ((length, h...]
  transfers between devices with their start and end apart: 18 -> 15, of which waited for: 13 -> 11; matrix products, arithmetic and copies ran while one was open for 0% -> 0% of each run, Pallas kernels for 18% -> 15%
where the time goes in v8:
time: 97.9 us; the launch traced here: 97.4 us
  waiting for transfers between devices  28.3 us (29%)
  starting transfers between devices  26.3 us (27%)
  Pallas kernels  26.1 us (27%)
  blocking collectives  11.5 us (12%)
  local copies, waits for them, and re-layouts  3.24 us (3%)
  between operations  1.56 us (2%)
    ppermute x6, waiting for transfers between devices, others(): lax.ppermute(piece, 'frame', [(i, i ^ d * stride) for i in range(frames)])  13.3 us
    all_to_all x2, starting transfers between devices, exchange(): lax.all_to_all(packed, 'frame', split_axis=0, concat_axis=0, tiled=True)  13 us
    all_to_all x1, blocking collectives, sum_over_frames(): lax.all_to_all(near, 'frame', 0, 0, tiled=True, axis_index_groups=planes)  11.5 us
    ppermute x6, starting transfers between devices, others(): lax.ppermute(piece, 'frame', [(i, i ^ d * stride) for i in range(frames)])  9.34 us
    pallas_call x1, Pallas kernels, per_device_fast(): call(space_fast_kernel, [(wide, f32), (wide, f32), ((length, pair), bf16)...  7.85 us
    pallas_call x1, Pallas kernels, per_device_fast(): call(functools.partial(site_fast_kernel, sites), [(packed, bf16), (wide,...  7.42 us
    all_to_all x2, waiting for transfers between devices, exchange(): lax.all_to_all(packed, 'frame', split_axis=0, concat_axis=0, tiled=True)  6.99 us
    ppermute x3, starting transfers between devices, partner(): lax.ppermute(piece, 'frame', [(i, i ^ offset) for i in range(frames)])  3.55 us
  transfers between devices with their start and end apart: 15, of which 11 were waited for; matrix products, arithmetic and copies ran while one was open for 0% of the time, Pallas kernels for 15%

profile of v8, /device:TPU:0, one launch (start us, length us, event | category | flops | bytes accessed | tf_op | source)
XLA Modules:
  0.0 97.4 jit_solution(2230481101172169823)
XLA Ops:
  1.4 2.7 %start.1 = (bf16[16,2,8,2048]{3,2,1,0:T(8,128)(2,1)}, bf16[152,128]{1,0:T(8,128)(2,1)S(1)}) custom-call(s32[2]{0:T(128)S(1)} %pad_add_fusion.ids_ref, bf16[16,8,2048]{2,1,0:T(8,128)(2,1)} %bitcast.23, bf16[16,8,2048]{2,1,0:T(8,128)(2,1)} %bitcast.27, bf16[128,256]{1,0:T(8,128)(2,1)} %proj_hbm.1, bf16[32,128]{1,0:T(8,128)(2,1)} %bitcast.34, ...), custom_call_target="tpu_custom_call" | custom-call | tf_op jit(solution)/shard_map/start/pallas_call | solution.py:921
  4.2 5.1 %collective-permute-start.2 = (bf16[152,128]{1,0:T(8,128)(2,1)S(1)}, bf16[152,128]{1,0:T(8,128)(2,1)S(1)}, u32[]{:S(2)}, u32[]{:S(2)}) collective-permute-start(bf16[152,128]{1,0:T(8,128)(2,1)S(1)} %get-tuple-element.41), channel_id=1, source_target_pairs={{0,24},{2,26},{4,28},{6,30},{8,16},{10,18},{12,20},{14,22},{16,8},... | collective-permute-start | bytes 116744 | tf_op jit(solution)/shard_map/ppermute | solution.py:859
  10.0 7.0 %all-to-all-start = ((bf16[16,2,8,2048]{3,2,1,0:T(8,128)(2,1)}), bf16[16,2,8,2048]{3,2,1,0:T(8,128)(2,1)S(1)}, u32[]{:S(2)}, u32[]{:S(2)}) async-start(bf16[16,2,8,2048]{3,2,1,0:T(8,128)(2,1)} %get-tuple-element.44), calls=%async_computation | async-start | bytes 2097152 | tf_op jit(solution)/shard_map/all_to_all | solution.py:42
  17.1 2.9 %collective-permute-start.5 = (bf16[4,152,128]{2,1,0:T(8,128)(2,1)S(1)}, bf16[4,152,128]{2,1,0:T(8,128)(2,1)S(1)}, u32[]{:S(2)}, u32[]{:S(2)}) collective-permute-start(bf16[4,152,128]{2,1,0:T(8,128)(2,1)S(1)} %pad_maximum_fusion), channel_id=1, source_target_pairs={{0,6},{2,4},{4,2},{6,0},{8,14},{10,12},{12,10},{14,8},{16,22},{18,... | collective-permute-start | bytes 466952 | tf_op jit(solution)/shard_map/ppermute | solution.py:859
  20.7 12.6 %collective-permute-done.3 = bf16[4,152,128]{2,1,0:T(8,128)(2,1)S(1)} collective-permute-done((bf16[4,152,128]{2,1,0:T(8,128)(2,1)S(1)}, bf16[4,152,128]{2,1,0:T(8,128)(2,1)S(1)}, u32[]{:S(2)}, u32[]{:S(2)}) %collective-permute-start.3) | collective-permute-done | bytes 155680 | tf_op jit(solution)/shard_map/ppermute | solution.py:859
  34.8 1.3 %collective-permute-done.6.other_ref = bf16[16,152,128]{2,1,0:T(8,128)(2,1)S(1)} collective-permute-done((bf16[16,152,128]{2,1,0:T(8,128)(2,1)S(1)}, bf16[16,152,128]{2,1,0:T(8,128)(2,1)S(1)}, u32[]{:S(2)}, u32[]{:S(2)}) %collective-permute-start.6) | collective-permute-done | bytes 622624 | tf_op jit(solution)/shard_map/ppermute | solution.py:945
  36.1 1.0 %unpack.1 = (bf16[2048,256]{1,0:T(8,128)(2,1)S(1)}, bf16[32,2048]{1,0:T(8,128)(2,1)S(1)}, f32[1,2048]{1,0:T(1,128)S(1)}, f32[1,2048]{1,0:T(1,128)S(1)}) custom-call(s32[2]{0:T(128)S(1)} %pad_add_fusion.ids_ref, bf16[16,152,128]{2,1,0:T(8,128)(2,1)S(1)} %constant_dynamic-update-slice_fusion.own_ref, bf16[16,152,128]{2,1,0:T(8,128)(2,1)S(1)} %collective-permute-done.6.other_ref), custom_call_target="tpu_custom_call" | custom-call | tf_op jit(solution)/shard_map/unpack/pallas_call | solution.py:946
  37.2 3.4 %all-to-all-done.got_ref = bf16[16,2,8,2048]{3,2,1,0:T(8,128)(2,1)S(1)} async-done(((bf16[16,2,8,2048]{3,2,1,0:T(8,128)(2,1)}), bf16[16,2,8,2048]{3,2,1,0:T(8,128)(2,1)S(1)}, u32[]{:S(2)}, u32[]{:S(2)}) %all-to-all-start) | async-done | bytes 1048608 | tf_op jit(solution)/shard_map/all_to_all | solution.py:42
  40.6 7.4 %site.1 = (bf16[16,2,8,2048]{3,2,1,0:T(8,128)(2,1)}, bf16[128,2048]{1,0:T(8,128)(2,1)}, f32[2,2048]{1,0:T(2,128)}, bf16[128,256]{1,0:T(8,128)(2,1)S(1)}, bf16[128,32]{1,0:T(8,128)(2,1)S(1)}) custom-call(bf16[16,2,8,2048]{3,2,1,0:T(8,128)(2,1)S(1)} %all-to-all-done.got_ref, f32[1,2048]{1,0:T(1,128)S(1)} %get-tuple-element.42.refs_0_.refs_2_, ...), custom_call_target="tpu_custom_call" | custom-call | tf_op jit(solution)/shard_map/site/pallas_call | solution.py:953
  48.0 6.0 %all-to-all-start.1 = ((bf16[16,2,8,2048]{3,2,1,0:T(8,128)(2,1)}), bf16[16,2,8,2048]{3,2,1,0:T(8,128)(2,1)S(1)}, u32[]{:S(2)}, u32[]{:S(2)}) async-start(bf16[16,2,8,2048]{3,2,1,0:T(8,128)(2,1)} %get-tuple-element.65), calls=%async_computation.1 | async-start | bytes 2097152 | tf_op jit(solution)/shard_map/all_to_all | solution.py:42
  54.0 2.4 %band.1 = (bf16[128,2048]{1,0:T(8,128)(2,1)S(1)}, bf16[128,256]{1,0:T(8,128)(2,1)S(1)}, bf16[128,32]{1,0:T(8,128)(2,1)S(1)}, f32[128,1]{1,0:T(8,128)S(1)}, bf16[2048,128]{1,0:T(8,128)(2,1)S(1)}) custom-call(s32[2]{0:T(128)S(1)} %pad_add_fusion.ids_ref, bf16[128,2048]{1,0:T(8,128)(2,1)S(1)} %bitcast.24, bf16[128,2048]{1,0:T(8,128)(2,1)S(1)} %bitcast.28, ...), custom_call_target="tpu_custom_call" | custom-call | tf_op jit(solution)/shard_map/band/pallas_call | solution.py:978
  56.5 1.9 %collective-permute-done.7.arrived_ref = bf16[2048,128]{1,0:T(8,128)(2,1)S(1)} collective-permute-done((bf16[2048,128]{1,0:T(8,128)(2,1)S(1)}, bf16[2048,128]{1,0:T(8,128)(2,1)S(1)}, u32[]{:S(2)}, u32[]{:S(2)}) %collective-permute-start.7) | collective-permute-done | bytes 524320 | tf_op jit(solution)/shard_map/ppermute | solution.py:990
  58.5 7.8 %space.1 = (f32[128,2048]{1,0:T(8,128)S(1)}, f32[128,2048]{1,0:T(8,128)S(1)}, bf16[128,256]{1,0:T(8,128)(2,1)S(1)}, bf16[128,32]{1,0:T(8,128)(2,1)S(1)}, f32[2,2048]{1,0:T(2,128)S(1)}) custom-call(s32[2]{0:T(128)S(1)} %pad_add_fusion.ids_ref, bf16[2048,128]{1,0:T(8,128)(2,1)S(1)} %collective-permute-done.7.arrived_ref, bf16[128,2048]{1,0:T(8,128)(2,1)S(1)} %bitcast.25, ...), custom_call_target="tpu_custom_call" | custom-call | tf_op jit(solution)/shard_map/space/pallas_call | solution.py:993
  66.3 1.3 %terms.1 = (bf16[16,152,128]{2,1,0:T(8,128)(2,1)S(1)}, bf16[16,152,128]{2,1,0:T(8,128)(2,1)S(1)}) custom-call(s32[2]{0:T(128)S(1)} %pad_add_fusion.ids_ref, bf16[128,2048]{1,0:T(8,128)(2,1)S(1)} %get-tuple-element.49.refs_2_.x_ref, bf16[128,256]{1,0:T(8,128)(2,1)S(1)} %get-tuple-element.54.dc_ref, bf16[128,32]{1,0:T(8,128)(2,1)S(1)} %get-tuple-element.55.dl_ref, ...), custom_call_target="tpu_custom_call" | custom-call | tf_op jit(solution)/shard_map/terms/pallas_call | solution.py:1012
  67.8 1.9 %collective-permute-done.8 = bf16[16,152,128]{2,1,0:T(8,128)(2,1)S(1)} collective-permute-done((bf16[16,152,128]{2,1,0:T(8,128)(2,1)S(1)}, bf16[16,152,128]{2,1,0:T(8,128)(2,1)S(1)}, u32[]{:S(2)}, u32[]{:S(2)}) %collective-permute-start.8) | collective-permute-done | bytes 622624 | tf_op jit(solution)/shard_map/ppermute | solution.py:1018
  69.9 2.9 %collective-permute-start.11 = (bf16[4,152,128]{2,1,0:T(8,128)(2,1)S(1)}, bf16[4,152,128]{2,1,0:T(8,128)(2,1)S(1)}, u32[]{:S(2)}, u32[]{:S(2)}) collective-permute-start(bf16[4,152,128]{2,1,0:T(8,128)(2,1)S(1)} %get-tuple-element.77), channel_id=1, source_target_pairs={{0,6},{2,4},{4,2},{6,0},{8,14},{10,12},{12,10},{14,8},{16,22},{18,... | collective-permute-start | bytes 466952 | tf_op jit(solution)/shard_map/ppermute | solution.py:877
  73.5 3.6 %all-to-all-done.1.came_ref = bf16[16,2,8,2048]{3,2,1,0:T(8,128)(2,1)S(1)} async-done(((bf16[16,2,8,2048]{3,2,1,0:T(8,128)(2,1)}), bf16[16,2,8,2048]{3,2,1,0:T(8,128)(2,1)S(1)}, u32[]{:S(2)}, u32[]{:S(2)}) %all-to-all-start.1) | async-done | bytes 1048608 | tf_op jit(solution)/shard_map/all_to_all | solution.py:42
  77.1 1.2 %copy-done.3 = f32[128,2048]{1,0:T(8,128)S(1)} copy-done((f32[128,2048]{1,0:T(8,128)S(1)}, f32[128,2048]{1,0:T(8,128)}, u32[]{:S(2)}) %copy-start.3) | copy-done | bytes 1048600
  78.3 1.2 %copy-done.5 = f32[128,2048]{1,0:T(8,128)S(1)} copy-done((f32[128,2048]{1,0:T(8,128)S(1)}, f32[128,2048]{1,0:T(8,128)}, u32[]{:S(2)}) %copy-start.5) | copy-done | bytes 1048600
  79.5 1.7 %last.1 = (bf16[128,2048]{1,0:T(8,128)(2,1)}, bf16[128,2048]{1,0:T(8,128)(2,1)}) custom-call(bf16[128,2048]{1,0:T(8,128)(2,1)S(1)} %bitcast.26, f32[128,1]{1,0:T(8,128)S(1)} %get-tuple-element.53.refs_5_.inverse_ref, f32[1,2048]{1,0:T(1,128)S(1)} %get-tuple-element.43.refs_1_.refs_3_.gain_ref, f32[128,2048]{1,0:T(8,128)S(1)} %copy-done.3, ...), custom_call_target="tpu_custom_call" | custom-call | tf_op jit(solution)/shard_map/last/pallas_call | solution.py:1019
  81.2 0.9 collective-permute-done.10
  82.9 11.5 %all_to_all.15 = bf16[4,152,128]{2,1,0:T(8,128)(2,1)S(1)} all-to-all(bf16[4,152,128]{2,1,0:T(8,128)(2,1)S(1)} %add_convert_fusion), channel_id=1, replica_groups={{0,8,16,24},{2,10,18,26},{4,12,20,28},{6,14,22,30},{1,9,17,25},{3,11,19..., dimensions={0} | all-to-all | bytes 311296 | tf_op jit(solution)/shard_map/all_to_all | solution.py:885
  94.5 1.3 %collective-permute-done.12.other_ref = f32[152,128]{1,0:T(8,128)S(1)} collective-permute-done((f32[152,128]{1,0:T(8,128)S(1)}, f32[152,128]{1,0:T(8,128)S(1)}, u32[]{:S(2)}, u32[]{:S(2)}) %collective-permute-start.12) | collective-permute-done | bytes 77856 | tf_op jit(solution)/shard_map/ppermute | solution.py:1023
  95.7 1.7 %finish.1 = (f32[128,256]{1,0:T(8,128)}, f32[32,128]{1,0:T(8,128)}, f32[256,256]{1,0:T(8,128)}) custom-call(s32[2]{0:T(128)S(1)} %pad_add_fusion.ids_ref, f32[152,128]{1,0:T(8,128)S(1)} %convert_reduce_fusion.own_ref, f32[152,128]{1,0:T(8,128)S(1)} %collective-permute-done.12.other_ref, bf16[1,256]{1,0:T(2,128)(2,1)S(1)} %fusion.4.active_ref), custom_call_target="tpu_custom_call" | custom-call | tf_op jit(solution)/shard_map/finish/pallas_call | solution.py:1024
  (53 shorter events, 5.0 us)
Async XLA Ops:
  4.2 12.8 %collective-permute-start.2 = (bf16[152,128]{1,0:T(8,128)(2,1)S(1)}, bf16[152,128]{1,0:T(8,128)(2,1)S(1)}, u32[]{:S(2)}, u32[]{:S(2)}) collective-permute-start(bf16[152,128]{1,0:T(8,128)(2,1)S(1)} %get-tuple-element.41), channel_id=1, source_target_pairs={{0,24},{2,26},{4,28},{6,30},{8,16},{10,18},{12,20},{14,22},{16,8},... | collective-permute-start | bytes 116744 | tf_op jit(solution)/shard_map/ppermute | solution.py:859
  9.3 7.7 %collective-permute-start.1 = (bf16[152,128]{1,0:T(8,128)(2,1)S(1)}, bf16[152,128]{1,0:T(8,128)(2,1)S(1)}, u32[]{:S(2)}, u32[]{:S(2)}) collective-permute-start(bf16[152,128]{1,0:T(8,128)(2,1)S(1)} %get-tuple-element.41), channel_id=1, source_target_pairs={{0,16},{2,18},{4,20},{6,22},{8,24},{10,26},{12,28},{14,30},{16,0},... | collective-permute-start | bytes 116744 | tf_op jit(solution)/shard_map/ppermute | solution.py:859
  9.3 7.7 %collective-permute-start = (bf16[152,128]{1,0:T(8,128)(2,1)S(1)}, bf16[152,128]{1,0:T(8,128)(2,1)S(1)}, u32[]{:S(2)}, u32[]{:S(2)}) collective-permute-start(bf16[152,128]{1,0:T(8,128)(2,1)S(1)} %get-tuple-element.41), channel_id=1, source_target_pairs={{0,8},{2,10},{4,12},{6,14},{8,0},{10,2},{12,4},{14,6},{16,24},{18,... | collective-permute-start | bytes 116744 | tf_op jit(solution)/shard_map/ppermute | solution.py:859
  10.0 30.6 %all-to-all-start = ((bf16[16,2,8,2048]{3,2,1,0:T(8,128)(2,1)}), bf16[16,2,8,2048]{3,2,1,0:T(8,128)(2,1)S(1)}, u32[]{:S(2)}, u32[]{:S(2)}) async-start(bf16[16,2,8,2048]{3,2,1,0:T(8,128)(2,1)} %get-tuple-element.44), calls=%async_computation | async-start | bytes 2097152 | tf_op jit(solution)/shard_map/all_to_all | solution.py:42
  17.1 16.9 %collective-permute-start.5 = (bf16[4,152,128]{2,1,0:T(8,128)(2,1)S(1)}, bf16[4,152,128]{2,1,0:T(8,128)(2,1)S(1)}, u32[]{:S(2)}, u32[]{:S(2)}) collective-permute-start(bf16[4,152,128]{2,1,0:T(8,128)(2,1)S(1)} %pad_maximum_fusion), channel_id=1, source_target_pairs={{0,6},{2,4},{4,2},{6,0},{8,14},{10,12},{12,10},{14,8},{16,22},{18,... | collective-permute-start | bytes 466952 | tf_op jit(solution)/shard_map/ppermute | solution.py:859
  20.0 13.5 %collective-permute-start.4 = (bf16[4,152,128]{2,1,0:T(8,128)(2,1)S(1)}, bf16[4,152,128]{2,1,0:T(8,128)(2,1)S(1)}, u32[]{:S(2)}, u32[]{:S(2)}) collective-permute-start(bf16[4,152,128]{2,1,0:T(8,128)(2,1)S(1)} %pad_maximum_fusion), channel_id=1, source_target_pairs={{0,4},{2,6},{4,0},{6,2},{8,12},{10,14},{12,8},{14,10},{16,20},{18,... | collective-permute-start | bytes 466952 | tf_op jit(solution)/shard_map/ppermute | solution.py:859
  20.5 12.8 %collective-permute-start.3 = (bf16[4,152,128]{2,1,0:T(8,128)(2,1)S(1)}, bf16[4,152,128]{2,1,0:T(8,128)(2,1)S(1)}, u32[]{:S(2)}, u32[]{:S(2)}) collective-permute-start(bf16[4,152,128]{2,1,0:T(8,128)(2,1)S(1)} %pad_maximum_fusion), channel_id=1, source_target_pairs={{0,2},{2,0},{4,6},{6,4},{8,10},{10,8},{12,14},{14,12},{16,18},{18,... | collective-permute-start | bytes 466952 | tf_op jit(solution)/shard_map/ppermute | solution.py:859
  34.0 2.1 %collective-permute-start.6 = (bf16[16,152,128]{2,1,0:T(8,128)(2,1)S(1)}, bf16[16,152,128]{2,1,0:T(8,128)(2,1)S(1)}, u32[]{:S(2)}, u32[]{:S(2)}) collective-permute-start(bf16[16,152,128]{2,1,0:T(8,128)(2,1)S(1)} %constant_dynamic-update-slice_fusion.own_ref), channel_id=1, source_target_pairs={{0,1},{1,0},{2,3},{3,2},{4,5},{5,4},{6,7},{7,6},{8,9},{9,8},{10,11... | collective-permute-start | bytes 1867784 | tf_op jit(solution)/shard_map/ppermute | solution.py:945
  34.1 0.7 copy-start.10
  48.0 6.0 %copy-start = (bf16[1,1,128,2048]{3,2,1,0:T(8,128)(2,1)S(1)}, bf16[1,1,128,2048]{3,2,1,0:T(8,128)(2,1)}, u32[]{:S(2)}) copy-start(bf16[1,1,128,2048]{3,2,1,0:T(8,128)(2,1)} %param.10) | copy-start | bytes 1572868
  48.0 6.0 %copy-start.1 = (bf16[1,1,128,2048]{3,2,1,0:T(8,128)(2,1)S(1)}, bf16[1,1,128,2048]{3,2,1,0:T(8,128)(2,1)}, u32[]{:S(2)}) copy-start(bf16[1,1,128,2048]{3,2,1,0:T(8,128)(2,1)} %param.11) | copy-start | bytes 1572868
  48.0 29.0 %all-to-all-start.1 = ((bf16[16,2,8,2048]{3,2,1,0:T(8,128)(2,1)}), bf16[16,2,8,2048]{3,2,1,0:T(8,128)(2,1)S(1)}, u32[]{:S(2)}, u32[]{:S(2)}) async-start(bf16[16,2,8,2048]{3,2,1,0:T(8,128)(2,1)} %get-tuple-element.65), calls=%async_computation.1 | async-start | bytes 2097152 | tf_op jit(solution)/shard_map/all_to_all | solution.py:42
  56.5 2.0 %collective-permute-start.7 = (bf16[2048,128]{1,0:T(8,128)(2,1)S(1)}, bf16[2048,128]{1,0:T(8,128)(2,1)S(1)}, u32[]{:S(2)}, u32[]{:S(2)}) collective-permute-start(bf16[2048,128]{1,0:T(8,128)(2,1)S(1)} %get-tuple-element.50), channel_id=1, source_target_pairs={{0,1},{1,0},{2,3},{3,2},{4,5},{5,4},{6,7},{7,6},{8,9},{9,8},{10,11... | collective-permute-start | bytes 1572872 | tf_op jit(solution)/shard_map/ppermute | solution.py:990
  58.4 7.9 %copy-start.6 = (bf16[128,2048]{1,0:T(8,128)(2,1)S(1)}, bf16[128,2048]{1,0:T(8,128)(2,1)}, u32[]{:S(2)}) copy-start(bf16[128,2048]{1,0:T(8,128)(2,1)} %get-tuple-element.57.site_x) | copy-start | bytes 1572868
  58.4 7.9 %copy-start.7 = (f32[2,2048]{1,0:T(2,128)S(1)}, f32[2,2048]{1,0:T(2,128)}, u32[]{:S(2)}) copy-start(f32[2,2048]{1,0:T(2,128)} %get-tuple-element.60.site_gmod) | copy-start | bytes 49156
  66.3 3.6 %copy-start.2 = (f32[128,2048]{1,0:T(8,128)}, f32[128,2048]{1,0:T(8,128)S(1)}, u32[]{:S(2)}) copy-start(f32[128,2048]{1,0:T(8,128)S(1)} %get-tuple-element.63.mix_ref) | copy-start | bytes 3145732
  66.3 3.6 %copy-start.4 = (f32[128,2048]{1,0:T(8,128)}, f32[128,2048]{1,0:T(8,128)S(1)}, u32[]{:S(2)}) copy-start(f32[128,2048]{1,0:T(8,128)S(1)} %get-tuple-element.64.pre_ref) | copy-start | bytes 3145732
  67.6 2.1 %collective-permute-start.8 = (bf16[16,152,128]{2,1,0:T(8,128)(2,1)S(1)}, bf16[16,152,128]{2,1,0:T(8,128)(2,1)S(1)}, u32[]{:S(2)}, u32[]{:S(2)}) collective-permute-start(bf16[16,152,128]{2,1,0:T(8,128)(2,1)S(1)} %get-tuple-element.62), channel_id=1, source_target_pairs={{0,1},{1,0},{2,3},{3,2},{4,5},{5,4},{6,7},{7,6},{8,9},{9,8},{10,11... | collective-permute-start | bytes 1867784 | tf_op jit(solution)/shard_map/ppermute | solution.py:1018
  69.9 11.3 %collective-permute-start.11 = (bf16[4,152,128]{2,1,0:T(8,128)(2,1)S(1)}, bf16[4,152,128]{2,1,0:T(8,128)(2,1)S(1)}, u32[]{:S(2)}, u32[]{:S(2)}) collective-permute-start(bf16[4,152,128]{2,1,0:T(8,128)(2,1)S(1)} %get-tuple-element.77), channel_id=1, source_target_pairs={{0,6},{2,4},{4,2},{6,0},{8,14},{10,12},{12,10},{14,8},{16,22},{18,... | collective-permute-start | bytes 466952 | tf_op jit(solution)/shard_map/ppermute | solution.py:877
  72.8 9.3 %collective-permute-start.10 = (bf16[4,152,128]{2,1,0:T(8,128)(2,1)S(1)}, bf16[4,152,128]{2,1,0:T(8,128)(2,1)S(1)}, u32[]{:S(2)}, u32[]{:S(2)}) collective-permute-start(bf16[4,152,128]{2,1,0:T(8,128)(2,1)S(1)} %get-tuple-element.78), channel_id=1, source_target_pairs={{0,4},{2,6},{4,0},{6,2},{8,12},{10,14},{12,8},{14,10},{16,20},{18,... | collective-permute-start | bytes 466952 | tf_op jit(solution)/shard_map/ppermute | solution.py:877
  73.4 9.4 %collective-permute-start.9 = (bf16[4,152,128]{2,1,0:T(8,128)(2,1)S(1)}, bf16[4,152,128]{2,1,0:T(8,128)(2,1)S(1)}, u32[]{:S(2)}, u32[]{:S(2)}) collective-permute-start(bf16[4,152,128]{2,1,0:T(8,128)(2,1)S(1)} %get-tuple-element.79), channel_id=1, source_target_pairs={{0,2},{2,0},{4,6},{6,4},{8,10},{10,8},{12,14},{14,12},{16,18},{18,... | collective-permute-start | bytes 466952 | tf_op jit(solution)/shard_map/ppermute | solution.py:877
  77.0 1.2 %copy-start.3 = (f32[128,2048]{1,0:T(8,128)S(1)}, f32[128,2048]{1,0:T(8,128)}, u32[]{:S(2)}) copy-start(f32[128,2048]{1,0:T(8,128)} %copy-done.2) | copy-start | bytes 3145732
  78.3 1.2 %copy-start.5 = (f32[128,2048]{1,0:T(8,128)S(1)}, f32[128,2048]{1,0:T(8,128)}, u32[]{:S(2)}) copy-start(f32[128,2048]{1,0:T(8,128)} %copy-done.4) | copy-start | bytes 3145732
  94.4 1.3 %collective-permute-start.12 = (f32[152,128]{1,0:T(8,128)S(1)}, f32[152,128]{1,0:T(8,128)S(1)}, u32[]{:S(2)}, u32[]{:S(2)}) collective-permute-start(f32[152,128]{1,0:T(8,128)S(1)} %convert_reduce_fusion.own_ref), channel_id=1, source_target_pairs={{0,1},{1,0},{2,3},{3,2},{4,5},{5,4},{6,7},{7,6},{8,9},{9,8},{10,11... | collective-permute-start | bytes 233480 | tf_op jit(solution)/shard_map/ppermute | solution.py:1023
  (3 other events, 2.0 us)

commit v9 on v8

--- a/solution.py
+++ b/solution.py
@@ -10,6 +10,7 @@
 
 norm_eps = 1e-05
 LANES = 128
+LOG2E = math.log2(math.e)
 f32 = jnp.float32
 bf16 = jnp.bfloat16
 EXACT = lax.Precision.HIGHEST
@@ -85,11 +86,15 @@
     return jnp.concatenate([jnp.broadcast_to(rows[c : c + 1], part) for c in range(count)], axis=0)
 
 
-def normalize_into(tok_ref, shift_ref, gain_ref, x_ref):
+def normalize_into(tok_ref, shift_ref, gain_ref, x_ref, read=None):
     length, width = tok_ref.shape
     total = jnp.zeros((length, LANES), f32)
     for _, sl in blocks(width):
-        v = tok_ref[:, sl].astype(f32)
+        if read is None:
+            v = tok_ref[:, sl].astype(f32)
+        else:
+            v = read(sl)
+            tok_ref[:, sl] = v.astype(bf16)
         total = total + v * v
     mean = jnp.sum(total, axis=1, keepdims=True) / width
     inverse = lax.rsqrt(mean + norm_eps)
@@ -106,8 +111,7 @@
     step = jnp.maximum(z, 0.0) + jnp.log1p(jnp.exp(-jnp.abs(z)))
     log_decay = -step * rate
     cum = exact(mask, log_decay, 1, 0)
-    cum_rows = exact(log_decay, mask, 0, 1)
-    return z, step, cum, cum_rows
+    return z, step, cum, (cum * LOG2E, exact(log_decay * LOG2E, mask, 0, 1))
 
 
 def halves_of(a):
@@ -118,7 +122,7 @@
     return jnp.concatenate([lanes_of, lanes_of], axis=0)
 
 
-def scan_block(j, x, grad, step_wide, scores, cum, cum_rows, heads, width, d_scores):
+def scan_block(j, x, grad, step_wide, scores, cums, heads, width, d_scores):
     size = width // heads
     per_block = LANES // size
     length = x.shape[0]
@@ -132,7 +136,7 @@
     weights = []
     for i in range(per_block):
         h = j * per_block + i
-        decay = jnp.exp(jnp.minimum(cum[:, h : h + 1] - cum_rows[h : h + 1, :], 0.0))
+        decay = jnp.exp2(jnp.minimum(cums[0][:, h : h + 1] - cums[1][h : h + 1, :], 0.0))
         d_scores = d_scores + d_weights[i * length : (i + 1) * length] * decay
         weights.append((scores * decay).astype(bf16))
     out = mm(jnp.concatenate(weights, axis=1), steppeds, 1, 0)
@@ -142,15 +146,12 @@
 
 def put(sums_ref, which, sl, value):
     length = value.shape[0]
-    for n, part in enumerate(split(value)):
-        at = (2 * which + n) * length
-        sums_ref[at : at + length, sl] = part
+    sums_ref[which * length : (which + 1) * length, sl] = value.astype(bf16)
 
 
 def head_sums(sums_ref, lanes_of, length):
     sums = mm(sums_ref[...], lanes_of, 1, 1)
-    sums = [sums[at : at + length] for at in range(0, sums.shape[0], length)]
-    return [sums[n] + sums[n + 1] for n in range(0, len(sums), 2)]
+    return [sums[at : at + length] for at in range(0, sums.shape[0], length)]
 
 
 def wide_blocks(width):
@@ -248,23 +249,22 @@
             at += part
         step_ref[pl.ds(pl.multiple_of(half * heads, heads), heads), :] = ref[at : at + heads, :] * factor
         at += heads
-    rest = jnp.zeros((7, active_ref.shape[1]), f32)
-    active = jnp.concatenate([active_ref[...].astype(f32), rest], axis=0)
     for k, sl in blocks(mod_ref.shape[1]):
-        own = jnp.broadcast_to(own_ref[at + k : at + k + 1, :] * factor, (8, LANES))
-        mod_ref[:, sl] = exact(active, own, 0, 0)
+        mod_ref[:, sl] = active_ref[...] * (own_ref[at + k : at + k + 1, :] * factor)
 
 
 def site_fast_kernel(sites, got_ref, *refs):
     inputs, (small_ref, sent_hbm, x_hbm, gmod_hbm, dc_ref, dl_ref) = refs[:4], refs[4:10]
     inputs = (*inputs, small_ref[0:1, :], small_ref[1:2, :])
-    tok_ref, grad_ref, sent_ref, x_ref, gmod_ref, sems = refs[10:16]
-    scratch = refs[16:]
+    tok_ref, sent_ref, x_ref, gmod_ref, sems = refs[10:15]
+    scratch = refs[15:]
     frames, width = got_ref.shape[0], got_ref.shape[3]
-    for _, sl in blocks(width):
-        for ref, which in ((tok_ref, 0), (grad_ref, 1)):
-            value = got_ref[:, which, :, sl].astype(f32)
-            ref[:, sl] = value.reshape(frames * sites, LANES).astype(bf16)
+    def read(which):
+        return lambda sl: got_ref[:, which, :, sl].astype(f32).reshape(frames * sites, LANES)
+
+    class Grad:
+        def __getitem__(self, at):
+            return read(1)(at[1]).astype(bf16)
 
     parts = 4
     share = width // parts
@@ -292,7 +292,18 @@
                 send(self.which, at[1].stop // share - 1)
 
     site_kernel(
-        sites, tok_ref, grad_ref, *inputs, Packed(0), Packed(1), dc_ref, dl_ref, gmod_ref, x_ref, *scratch
+        sites,
+        tok_ref,
+        Grad(),
+        *inputs,
+        Packed(0),
+        Packed(1),
+        dc_ref,
+        dl_ref,
+        gmod_ref,
+        x_ref,
+        *scratch,
+        read=read(0),
     )
     begin(gmod_ref, gmod_hbm)
     for copy in copies:
@@ -317,18 +328,19 @@
     x_ref,
     dn_ref,
     sums_ref,
+    read=None,
 ):
     length, width = tok_ref.shape
     heads = step_ref.shape[0]
     state = proj_ref.shape[1] // 2
     clips = shift_ref.shape[0]
-    inverse = normalize_into(tok_ref, shift_ref, gain_ref, x_ref)
+    inverse = normalize_into(tok_ref, shift_ref, gain_ref, x_ref, read)
     lanes_of = head_map(heads, width)
     mask = sequence_mask(length, sites)
     coeffs = mm(x_ref[...], proj_ref[...], 1, 0).astype(bf16)
     logits = mm(x_ref[...], step_ref[...], 1, 1).astype(bf16)
     rate = rate_ref[...]
-    z, step, cum, cum_rows = steps_of(logits, bias_ref[...], rate, mask)
+    z, step, cum, cums = steps_of(logits, bias_ref[...], rate, mask)
     b_part, c_part = coeffs[:, :state], coeffs[:, state:]
     scores = mm(c_part, b_part, 1, 1) * (mask / state)
     step_parts, twice = halves_of(step), doubled(lanes_of)
@@ -337,7 +349,7 @@
         x, grad = x_ref[:, sl], grad_ref[:, sl]
         step_wide = mm(step_parts, twice[:, sl], 1, 0)
         stepped, out, d_stepped, d_scores = scan_block(
-            j, x, grad, step_wide, scores, cum, cum_rows, heads, width, d_scores
+            j, x, grad, step_wide, scores, cums, heads, width, d_scores
         )
         out_ref[:, sl] = out.astype(bf16)
         dn_ref[:, sl] = (step_wide * d_stepped).astype(bf16)
@@ -355,9 +367,8 @@
             dn_ref[:, sl].astype(f32)
             + mm(d_coeffs, proj_ref[sl, :], 1, 1)
             + mm(d_logits, step_ref[:, sl], 1, 0)
-        ).astype(bf16)
-        back_ref[:, sl] = back
-        back = back.astype(f32)
+        )
+        back_ref[:, sl] = back.astype(bf16)
         scaled = back * (tok_ref[:, sl].astype(f32) * inverse)
         for c in range(clips):
             rows = slice(c * (length // clips), (c + 1) * (length // clips))
@@ -449,7 +460,7 @@
 
     for j, sl in blocks(width):
         offset = jnp.bitwise_xor(me, j)
-        place = jnp.bitwise_and(offset, radix - 1) * radix + j // radix
+        place = jnp.bitwise_and(offset, radix - 1) * radix + offset // radix
         tall = jnp.concatenate([x_ref[:, sl], site_x[:, sl]], axis=0)
         at = put_halves(place, 0, mm(tall, coeffs, 0, 0))
         at = put_halves(place, at, mm(logits, tall, 0, 0))
@@ -503,7 +514,7 @@
     mask = sequence_mask(length, 1)
     coeffs = coeffs_ref[...]
     rate = rate_ref[...]
-    z, step, cum, cum_rows = steps_of(logits_ref[...], bias_ref[...], rate, mask)
+    z, step, cum, cums = steps_of(logits_ref[...], bias_ref[...], rate, mask)
     last = cum[length - 1 : length, :]
     rest = jnp.exp(last - cum)
     lead, reach = rest * step, jnp.exp(cum) / state
@@ -528,7 +539,7 @@
         step_wide, lead_wide = wide_parts[:length], wide_parts[length : 2 * length]
         skip = wide_parts[-8:-7]
         stepped, out, d_stepped, d_scores = scan_block(
-            j, x, grad, step_wide, scores, cum, cum_rows, heads, width, d_scores
+            j, x, grad, step_wide, scores, cums, heads, width, d_scores
         )
         if first is None:
             x, wide = x.astype(f32), grad.astype(f32)
@@ -748,7 +759,7 @@
     site_out, site_back, gproj, gstep, site_gmod = call(
         functools.partial(site_kernel, sites),
         [(wide, bf16), (wide, bf16), ((width, pair), f32), ((heads, width), f32), ((2 * clips, width), f32)],
-        [(wide, bf16)] * 2 + [((4 * length, width), bf16)],
+        [(wide, bf16)] * 2 + [((2 * length, width), bf16)],
         name="site",
     )(site_tok, site_grad, shift, gain, proj_full, step_full, bias, rate_time[None])
 
@@ -784,7 +795,7 @@
     mix, pre, gproj, gstep, gmod = call(
         space_kernel,
         [(wide, f32), (wide, f32), ((width, pair), bf16), ((heads, width), bf16), ((2, width), f32)],
-        [(wide, bf16), ((6 * length, width), bf16)],
+        [(wide, bf16), ((3 * length, width), bf16)],
         name="space",
     )(
         tok,
@@ -881,9 +892,8 @@
     near = [near[0]] + [partner(near[d], d) for d in range(1, radix)]
     near, ahead = lax.optimization_barrier((near, ahead))
     near = total(near).astype(bf16)
-    planes = [[p * radix + i for p in range(radix)] for i in range(radix)]
-    far = lax.all_to_all(near, "frame", 0, 0, tiled=True, axis_index_groups=planes)
-    return jnp.sum(far.astype(f32), axis=0), *ahead
+    far = [near[0]] + [partner(near[d], d * radix) for d in range(1, radix)]
+    return total(far), *ahead
 
 
 def per_device_fast(
@@ -961,13 +971,12 @@
         ],
         [
             (wide, bf16),
-            (wide, bf16),
             (packed, bf16),
             (wide, bf16),
             ((2, width), f32),
             pltpu.SemaphoreType.DMA((10,)),
         ]
-        + [(wide, bf16), ((4 * length, width), bf16)],
+        + [(wide, bf16), ((2 * length, width), bf16)],
         name="site",
         specs="vvvvvv",
         hbm_outs=(0, 1, 2),
@@ -993,7 +1002,7 @@
     mix, pre, own_dc, own_dl, gmod = call(
         space_fast_kernel,
         [(wide, f32), (wide, f32), ((length, pair), bf16), ((length, heads), bf16), ((2, width), f32)],
-        [(wide, bf16), ((6 * length, width), bf16)],
+        [(wide, bf16), ((3 * length, width), bf16)],
         name="space",
         specs="s" + "v" * 10,
     )(
@@ -1026,7 +1035,7 @@
         [((depth, pair), f32), ((heads, depth), f32), ((mod_weight.shape[0], mod_cols), f32)],
         name="finish",
         specs="svvv",
-    )(ids, terms, other, activated)
+    )(ids, terms, other, activated.astype(f32).T)
     return (mixed.reshape(tokens.shape), d_tokens.reshape(tokens.shape), grad_proj, grad_step.T, grad_mod)
 
 

time: 97.9 us -> 94 us (0.960)
  blocking collectives: 11.5 us -> 0 us
  waiting for transfers between devices: 28.3 us -> 33.9 us
  starting transfers between devices: 26.3 us -> 29.9 us
  Pallas kernels: 26.1 us -> 24.1 us
    all_to_all x1 -> x0, blocking collectives: 11.5 us -> none  [sum_over_frames(): lax.all_to_all(near, 'frame', 0, 0, tiled=True, axis_index_groups=planes)]
    ppermute x3 -> x6, waiting for transfers between devices: 1.61 us -> 6.88 us  [partner(): lax.ppermute(piece, 'frame', [(i, i ^ offset) for i in range(frames)])]
    ppermute x3 -> x6, starting transfers between devices: 3.55 us -> 8.11 us  [partner(): lax.ppermute(piece, 'frame', [(i, i ^ offset) for i in range(frames)])]
  transfers between devices with their start and end apart: 15 -> 18, of which waited for: 11 -> 12; matrix products, arithmetic and copies ran while one was open for 0% -> 1% of each run, Pallas kernels for 15% -> 14%
where the time goes in v9:
time: 94 us; the launch traced here: 93.6 us
  waiting for transfers between devices  33.9 us (36%)
  starting transfers between devices  29.9 us (32%)
  Pallas kernels  24.1 us (26%)
  local copies, waits for them, and re-layouts  3.25 us (3%)
  between operations  1.57 us (2%)
  other arithmetic  0.96 us (1%)
    ppermute x6, waiting for transfers between devices, others(): lax.ppermute(piece, 'frame', [(i, i ^ d * stride) for i in range(frames)])  13.7 us
    all_to_all x2, starting transfers between devices, exchange(): lax.all_to_all(packed, 'frame', split_axis=0, concat_axis=0, tiled=True)  12.1 us
    ppermute x6, starting transfers between devices, others(): lax.ppermute(piece, 'frame', [(i, i ^ d * stride) for i in range(frames)])  9.26 us
    ppermute x6, starting transfers between devices, partner(): lax.ppermute(piece, 'frame', [(i, i ^ offset) for i in range(frames)])  8.11 us
    all_to_all x2, waiting for transfers between devices, exchange(): lax.all_to_all(packed, 'frame', split_axis=0, concat_axis=0, tiled=True)  7.39 us
    pallas_call x1, Pallas kernels, per_device_fast(): call(space_fast_kernel, [(wide, f32), (wide, f32), ((length, pair), bf16)...  7 us
    ppermute x6, waiting for transfers between devices, partner(): lax.ppermute(piece, 'frame', [(i, i ^ offset) for i in range(frames)])  6.88 us
    pallas_call x1, Pallas kernels, per_device_fast(): call(functools.partial(site_fast_kernel, sites), [(packed, bf16), (wide,...  6.5 us
  transfers between devices with their start and end apart: 18, of which 12 were waited for; matrix products, arithmetic and copies ran while one was open for 1% of the time, Pallas kernels for 14%

profile of v9, /device:TPU:0, one launch (start us, length us, event | category | flops | bytes accessed | tf_op | source)
XLA Modules:
  0.0 93.6 jit_solution(15411540184445406196)
XLA Ops:
  1.4 2.7 %start.1 = (bf16[16,2,8,2048]{3,2,1,0:T(8,128)(2,1)}, bf16[152,128]{1,0:T(8,128)(2,1)S(1)}) custom-call(s32[2]{0:T(128)S(1)} %pad_add_fusion.ids_ref, bf16[16,8,2048]{2,1,0:T(8,128)(2,1)} %bitcast.34, bf16[16,8,2048]{2,1,0:T(8,128)(2,1)} %bitcast.38, bf16[128,256]{1,0:T(8,128)(2,1)} %proj_hbm.1, bf16[32,128]{1,0:T(8,128)(2,1)} %bitcast.45, ...), custom_call_target="tpu_custom_call" | custom-call | tf_op jit(solution)/shard_map/start/pallas_call | solution.py:931
  4.2 4.1 %collective-permute-start.1 = (bf16[152,128]{1,0:T(8,128)(2,1)S(1)}, bf16[152,128]{1,0:T(8,128)(2,1)S(1)}, u32[]{:S(2)}, u32[]{:S(2)}) collective-permute-start(bf16[152,128]{1,0:T(8,128)(2,1)S(1)} %get-tuple-element.41), channel_id=1, source_target_pairs={{0,16},{2,18},{4,20},{6,22},{8,24},{10,26},{12,28},{14,30},{16,0},... | collective-permute-start | bytes 116744 | tf_op jit(solution)/shard_map/ppermute | solution.py:870
  9.9 6.2 %all-to-all-start = ((bf16[16,2,8,2048]{3,2,1,0:T(8,128)(2,1)}), bf16[16,2,8,2048]{3,2,1,0:T(8,128)(2,1)S(1)}, u32[]{:S(2)}, u32[]{:S(2)}) async-start(bf16[16,2,8,2048]{3,2,1,0:T(8,128)(2,1)} %get-tuple-element.44), calls=%async_computation | async-start | bytes 2097152 | tf_op jit(solution)/shard_map/all_to_all | solution.py:43
  16.2 2.0 %collective-permute-start.3 = (bf16[4,152,128]{2,1,0:T(8,128)(2,1)S(1)}, bf16[4,152,128]{2,1,0:T(8,128)(2,1)S(1)}, u32[]{:S(2)}, u32[]{:S(2)}) collective-permute-start(bf16[4,152,128]{2,1,0:T(8,128)(2,1)S(1)} %pad_maximum_fusion), channel_id=1, source_target_pairs={{0,2},{2,0},{4,6},{6,4},{8,10},{10,8},{12,14},{14,12},{16,18},{18,... | collective-permute-start | bytes 466952 | tf_op jit(solution)/shard_map/ppermute | solution.py:870
  18.2 1.5 %collective-permute-start.4 = (bf16[4,152,128]{2,1,0:T(8,128)(2,1)S(1)}, bf16[4,152,128]{2,1,0:T(8,128)(2,1)S(1)}, u32[]{:S(2)}, u32[]{:S(2)}) collective-permute-start(bf16[4,152,128]{2,1,0:T(8,128)(2,1)S(1)} %pad_maximum_fusion), channel_id=1, source_target_pairs={{0,4},{2,6},{4,0},{6,2},{8,12},{10,14},{12,8},{14,10},{16,20},{18,... | collective-permute-start | bytes 466952 | tf_op jit(solution)/shard_map/ppermute | solution.py:870
  19.8 6.0 %collective-permute-done.3 = bf16[4,152,128]{2,1,0:T(8,128)(2,1)S(1)} collective-permute-done((bf16[4,152,128]{2,1,0:T(8,128)(2,1)S(1)}, bf16[4,152,128]{2,1,0:T(8,128)(2,1)S(1)}, u32[]{:S(2)}, u32[]{:S(2)}) %collective-permute-start.3) | collective-permute-done | bytes 155680 | tf_op jit(solution)/shard_map/ppermute | solution.py:870
  25.8 6.0 %collective-permute-done.4 = bf16[4,152,128]{2,1,0:T(8,128)(2,1)S(1)} collective-permute-done((bf16[4,152,128]{2,1,0:T(8,128)(2,1)S(1)}, bf16[4,152,128]{2,1,0:T(8,128)(2,1)S(1)}, u32[]{:S(2)}, u32[]{:S(2)}) %collective-permute-start.4) | collective-permute-done | bytes 155680 | tf_op jit(solution)/shard_map/ppermute | solution.py:870
  31.8 1.7 %collective-permute-done.5 = bf16[4,152,128]{2,1,0:T(8,128)(2,1)S(1)} collective-permute-done((bf16[4,152,128]{2,1,0:T(8,128)(2,1)S(1)}, bf16[4,152,128]{2,1,0:T(8,128)(2,1)S(1)}, u32[]{:S(2)}, u32[]{:S(2)}) %collective-permute-start.5) | collective-permute-done | bytes 155680 | tf_op jit(solution)/shard_map/ppermute | solution.py:870
  36.7 3.0 %all-to-all-done.got_ref = bf16[16,2,8,2048]{3,2,1,0:T(8,128)(2,1)S(1)} async-done(((bf16[16,2,8,2048]{3,2,1,0:T(8,128)(2,1)}), bf16[16,2,8,2048]{3,2,1,0:T(8,128)(2,1)S(1)}, u32[]{:S(2)}, u32[]{:S(2)}) %all-to-all-start) | async-done | bytes 1048608 | tf_op jit(solution)/shard_map/all_to_all | solution.py:43
  39.7 6.5 %site.1 = (bf16[16,2,8,2048]{3,2,1,0:T(8,128)(2,1)}, bf16[128,2048]{1,0:T(8,128)(2,1)}, f32[2,2048]{1,0:T(2,128)}, bf16[128,256]{1,0:T(8,128)(2,1)S(1)}, bf16[128,32]{1,0:T(8,128)(2,1)S(1)}) custom-call(bf16[16,2,8,2048]{3,2,1,0:T(8,128)(2,1)S(1)} %all-to-all-done.got_ref, f32[1,2048]{1,0:T(1,128)S(1)} %get-tuple-element.42.refs_0_.refs_2_, ...), custom_call_target="tpu_custom_call" | custom-call | tf_op jit(solution)/shard_map/site/pallas_call | solution.py:963
  46.3 5.9 %all-to-all-start.1 = ((bf16[16,2,8,2048]{3,2,1,0:T(8,128)(2,1)}), bf16[16,2,8,2048]{3,2,1,0:T(8,128)(2,1)S(1)}, u32[]{:S(2)}, u32[]{:S(2)}) async-start(bf16[16,2,8,2048]{3,2,1,0:T(8,128)(2,1)} %get-tuple-element.65), calls=%async_computation.1 | async-start | bytes 2097152 | tf_op jit(solution)/shard_map/all_to_all | solution.py:43
  52.2 2.4 %band.1 = (bf16[128,2048]{1,0:T(8,128)(2,1)S(1)}, bf16[128,256]{1,0:T(8,128)(2,1)S(1)}, bf16[128,32]{1,0:T(8,128)(2,1)S(1)}, f32[128,1]{1,0:T(8,128)S(1)}, bf16[2048,128]{1,0:T(8,128)(2,1)S(1)}) custom-call(s32[2]{0:T(128)S(1)} %pad_add_fusion.ids_ref, bf16[128,2048]{1,0:T(8,128)(2,1)S(1)} %bitcast.35, bf16[128,2048]{1,0:T(8,128)(2,1)S(1)} %bitcast.39, ...), custom_call_target="tpu_custom_call" | custom-call | tf_op jit(solution)/shard_map/band/pallas_call | solution.py:987
  54.7 1.9 %collective-permute-done.7.arrived_ref = bf16[2048,128]{1,0:T(8,128)(2,1)S(1)} collective-permute-done((bf16[2048,128]{1,0:T(8,128)(2,1)S(1)}, bf16[2048,128]{1,0:T(8,128)(2,1)S(1)}, u32[]{:S(2)}, u32[]{:S(2)}) %collective-permute-start.7) | collective-permute-done | bytes 524320 | tf_op jit(solution)/shard_map/ppermute | solution.py:999
  56.6 7.0 %space.1 = (f32[128,2048]{1,0:T(8,128)S(1)}, f32[128,2048]{1,0:T(8,128)S(1)}, bf16[128,256]{1,0:T(8,128)(2,1)S(1)}, bf16[128,32]{1,0:T(8,128)(2,1)S(1)}, f32[2,2048]{1,0:T(2,128)S(1)}) custom-call(s32[2]{0:T(128)S(1)} %pad_add_fusion.ids_ref, bf16[2048,128]{1,0:T(8,128)(2,1)S(1)} %collective-permute-done.7.arrived_ref, bf16[128,2048]{1,0:T(8,128)(2,1)S(1)} %bitcast.36, ...), custom_call_target="tpu_custom_call" | custom-call | tf_op jit(solution)/shard_map/space/pallas_call | solution.py:1002
  65.2 1.9 %collective-permute-done.8 = bf16[16,152,128]{2,1,0:T(8,128)(2,1)S(1)} collective-permute-done((bf16[16,152,128]{2,1,0:T(8,128)(2,1)S(1)}, bf16[16,152,128]{2,1,0:T(8,128)(2,1)S(1)}, u32[]{:S(2)}, u32[]{:S(2)}) %collective-permute-start.8) | collective-permute-done | bytes 622624 | tf_op jit(solution)/shard_map/ppermute | solution.py:1027
  67.3 2.0 %collective-permute-start.10 = (bf16[4,152,128]{2,1,0:T(8,128)(2,1)S(1)}, bf16[4,152,128]{2,1,0:T(8,128)(2,1)S(1)}, u32[]{:S(2)}, u32[]{:S(2)}) collective-permute-start(bf16[4,152,128]{2,1,0:T(8,128)(2,1)S(1)} %get-tuple-element.78), channel_id=1, source_target_pairs={{0,4},{2,6},{4,0},{6,2},{8,12},{10,14},{12,8},{14,10},{16,20},{18,... | collective-permute-start | bytes 466952 | tf_op jit(solution)/shard_map/ppermute | solution.py:888
  69.3 1.5 %collective-permute-start.11 = (bf16[4,152,128]{2,1,0:T(8,128)(2,1)S(1)}, bf16[4,152,128]{2,1,0:T(8,128)(2,1)S(1)}, u32[]{:S(2)}, u32[]{:S(2)}) collective-permute-start(bf16[4,152,128]{2,1,0:T(8,128)(2,1)S(1)} %get-tuple-element.77), channel_id=1, source_target_pairs={{0,6},{2,4},{4,2},{6,0},{8,14},{10,12},{12,10},{14,8},{16,22},{18,... | collective-permute-start | bytes 466952 | tf_op jit(solution)/shard_map/ppermute | solution.py:888
  70.8 4.3 %all-to-all-done.1.came_ref = bf16[16,2,8,2048]{3,2,1,0:T(8,128)(2,1)S(1)} async-done(((bf16[16,2,8,2048]{3,2,1,0:T(8,128)(2,1)}), bf16[16,2,8,2048]{3,2,1,0:T(8,128)(2,1)S(1)}, u32[]{:S(2)}, u32[]{:S(2)}) %all-to-all-start.1) | async-done | bytes 1048608 | tf_op jit(solution)/shard_map/all_to_all | solution.py:43
  77.6 1.7 %last.1 = (bf16[128,2048]{1,0:T(8,128)(2,1)}, bf16[128,2048]{1,0:T(8,128)(2,1)}) custom-call(bf16[128,2048]{1,0:T(8,128)(2,1)S(1)} %bitcast.37, f32[128,1]{1,0:T(8,128)S(1)} %get-tuple-element.53.refs_5_.inverse_ref, f32[1,2048]{1,0:T(1,128)S(1)} %get-tuple-element.43.refs_1_.refs_3_.gain_ref, f32[128,2048]{1,0:T(8,128)S(1)} %copy-done.3, ...), custom_call_target="tpu_custom_call" | custom-call | tf_op jit(solution)/shard_map/last/pallas_call | solution.py:1028
  80.7 2.1 %collective-permute-start.12 = (bf16[152,128]{1,0:T(8,128)(2,1)S(1)}, bf16[152,128]{1,0:T(8,128)(2,1)S(1)}, u32[]{:S(2)}, u32[]{:S(2)}) collective-permute-start(bf16[152,128]{1,0:T(8,128)(2,1)S(1)} %get-tuple-element.81), channel_id=1, source_target_pairs={{0,8},{2,10},{4,12},{6,14},{8,0},{10,2},{12,4},{14,6},{16,24},{18,... | collective-permute-start | bytes 116744 | tf_op jit(solution)/shard_map/ppermute | solution.py:888
  82.9 2.3 %collective-permute-start.13 = (bf16[152,128]{1,0:T(8,128)(2,1)S(1)}, bf16[152,128]{1,0:T(8,128)(2,1)S(1)}, u32[]{:S(2)}, u32[]{:S(2)}) collective-permute-start(bf16[152,128]{1,0:T(8,128)(2,1)S(1)} %get-tuple-element.83), channel_id=1, source_target_pairs={{0,16},{2,18},{4,20},{6,22},{8,24},{10,26},{12,28},{14,30},{16,0},... | collective-permute-start | bytes 116744 | tf_op jit(solution)/shard_map/ppermute | solution.py:888
  85.3 2.6 %collective-permute-done.13 = bf16[152,128]{1,0:T(8,128)(2,1)S(1)} collective-permute-done((bf16[152,128]{1,0:T(8,128)(2,1)S(1)}, bf16[152,128]{1,0:T(8,128)(2,1)S(1)}, u32[]{:S(2)}, u32[]{:S(2)}) %collective-permute-start.13) | collective-permute-done | bytes 38944 | tf_op jit(solution)/shard_map/ppermute | solution.py:888
  87.9 3.0 %collective-permute-done.14 = bf16[152,128]{1,0:T(8,128)(2,1)S(1)} collective-permute-done((bf16[152,128]{1,0:T(8,128)(2,1)S(1)}, bf16[152,128]{1,0:T(8,128)(2,1)S(1)}, u32[]{:S(2)}, u32[]{:S(2)}) %collective-permute-start.14) | collective-permute-done | bytes 38944 | tf_op jit(solution)/shard_map/ppermute | solution.py:888
  92.2 1.4 %finish.1 = (f32[128,256]{1,0:T(8,128)}, f32[32,128]{1,0:T(8,128)}, f32[256,256]{1,0:T(8,128)}) custom-call(s32[2]{0:T(128)S(1)} %pad_add_fusion.ids_ref, f32[152,128]{1,0:T(8,128)S(1)} %fusion.8.own_ref, f32[152,128]{1,0:T(8,128)S(1)} %collective-permute-done.15.other_ref, f32[256,1]{1,0:T(8,128)S(1)} %fusion.9.active_ref), custom_call_target="tpu_custom_call" | custom-call | tf_op jit(solution)/shard_map/finish/pallas_call | solution.py:1033
  (60 shorter events, 12.3 us)
Async XLA Ops:
  4.2 11.9 %collective-permute-start.1 = (bf16[152,128]{1,0:T(8,128)(2,1)S(1)}, bf16[152,128]{1,0:T(8,128)(2,1)S(1)}, u32[]{:S(2)}, u32[]{:S(2)}) collective-permute-start(bf16[152,128]{1,0:T(8,128)(2,1)S(1)} %get-tuple-element.41), channel_id=1, source_target_pairs={{0,16},{2,18},{4,20},{6,22},{8,24},{10,26},{12,28},{14,30},{16,0},... | collective-permute-start | bytes 116744 | tf_op jit(solution)/shard_map/ppermute | solution.py:870
  8.3 7.8 %collective-permute-start.2 = (bf16[152,128]{1,0:T(8,128)(2,1)S(1)}, bf16[152,128]{1,0:T(8,128)(2,1)S(1)}, u32[]{:S(2)}, u32[]{:S(2)}) collective-permute-start(bf16[152,128]{1,0:T(8,128)(2,1)S(1)} %get-tuple-element.41), channel_id=1, source_target_pairs={{0,24},{2,26},{4,28},{6,30},{8,16},{10,18},{12,20},{14,22},{16,8},... | collective-permute-start | bytes 116744 | tf_op jit(solution)/shard_map/ppermute | solution.py:870
  9.7 6.5 %collective-permute-start = (bf16[152,128]{1,0:T(8,128)(2,1)S(1)}, bf16[152,128]{1,0:T(8,128)(2,1)S(1)}, u32[]{:S(2)}, u32[]{:S(2)}) collective-permute-start(bf16[152,128]{1,0:T(8,128)(2,1)S(1)} %get-tuple-element.41), channel_id=1, source_target_pairs={{0,8},{2,10},{4,12},{6,14},{8,0},{10,2},{12,4},{14,6},{16,24},{18,... | collective-permute-start | bytes 116744 | tf_op jit(solution)/shard_map/ppermute | solution.py:870
  9.9 29.8 %all-to-all-start = ((bf16[16,2,8,2048]{3,2,1,0:T(8,128)(2,1)}), bf16[16,2,8,2048]{3,2,1,0:T(8,128)(2,1)S(1)}, u32[]{:S(2)}, u32[]{:S(2)}) async-start(bf16[16,2,8,2048]{3,2,1,0:T(8,128)(2,1)} %get-tuple-element.44), calls=%async_computation | async-start | bytes 2097152 | tf_op jit(solution)/shard_map/all_to_all | solution.py:43
  16.2 9.6 %collective-permute-start.3 = (bf16[4,152,128]{2,1,0:T(8,128)(2,1)S(1)}, bf16[4,152,128]{2,1,0:T(8,128)(2,1)S(1)}, u32[]{:S(2)}, u32[]{:S(2)}) collective-permute-start(bf16[4,152,128]{2,1,0:T(8,128)(2,1)S(1)} %pad_maximum_fusion), channel_id=1, source_target_pairs={{0,2},{2,0},{4,6},{6,4},{8,10},{10,8},{12,14},{14,12},{16,18},{18,... | collective-permute-start | bytes 466952 | tf_op jit(solution)/shard_map/ppermute | solution.py:870
  18.2 13.6 %collective-permute-start.4 = (bf16[4,152,128]{2,1,0:T(8,128)(2,1)S(1)}, bf16[4,152,128]{2,1,0:T(8,128)(2,1)S(1)}, u32[]{:S(2)}, u32[]{:S(2)}) collective-permute-start(bf16[4,152,128]{2,1,0:T(8,128)(2,1)S(1)} %pad_maximum_fusion), channel_id=1, source_target_pairs={{0,4},{2,6},{4,0},{6,2},{8,12},{10,14},{12,8},{14,10},{16,20},{18,... | collective-permute-start | bytes 466952 | tf_op jit(solution)/shard_map/ppermute | solution.py:870
  19.6 13.9 %collective-permute-start.5 = (bf16[4,152,128]{2,1,0:T(8,128)(2,1)S(1)}, bf16[4,152,128]{2,1,0:T(8,128)(2,1)S(1)}, u32[]{:S(2)}, u32[]{:S(2)}) collective-permute-start(bf16[4,152,128]{2,1,0:T(8,128)(2,1)S(1)} %pad_maximum_fusion), channel_id=1, source_target_pairs={{0,6},{2,4},{4,2},{6,0},{8,14},{10,12},{12,10},{14,8},{16,22},{18,... | collective-permute-start | bytes 466952 | tf_op jit(solution)/shard_map/ppermute | solution.py:870
  33.5 2.1 %collective-permute-start.6 = (bf16[16,152,128]{2,1,0:T(8,128)(2,1)S(1)}, bf16[16,152,128]{2,1,0:T(8,128)(2,1)S(1)}, u32[]{:S(2)}, u32[]{:S(2)}) collective-permute-start(bf16[16,152,128]{2,1,0:T(8,128)(2,1)S(1)} %constant_dynamic-update-slice_fusion.own_ref), channel_id=1, source_target_pairs={{0,1},{1,0},{2,3},{3,2},{4,5},{5,4},{6,7},{7,6},{8,9},{9,8},{10,11... | collective-permute-start | bytes 1867784 | tf_op jit(solution)/shard_map/ppermute | solution.py:955
  46.3 6.0 %copy-start = (bf16[1,1,128,2048]{3,2,1,0:T(8,128)(2,1)S(1)}, bf16[1,1,128,2048]{3,2,1,0:T(8,128)(2,1)}, u32[]{:S(2)}) copy-start(bf16[1,1,128,2048]{3,2,1,0:T(8,128)(2,1)} %param.10) | copy-start | bytes 1572868
  46.3 6.0 %copy-start.1 = (bf16[1,1,128,2048]{3,2,1,0:T(8,128)(2,1)S(1)}, bf16[1,1,128,2048]{3,2,1,0:T(8,128)(2,1)}, u32[]{:S(2)}) copy-start(bf16[1,1,128,2048]{3,2,1,0:T(8,128)(2,1)} %param.11) | copy-start | bytes 1572868
  46.3 28.9 %all-to-all-start.1 = ((bf16[16,2,8,2048]{3,2,1,0:T(8,128)(2,1)}), bf16[16,2,8,2048]{3,2,1,0:T(8,128)(2,1)S(1)}, u32[]{:S(2)}, u32[]{:S(2)}) async-start(bf16[16,2,8,2048]{3,2,1,0:T(8,128)(2,1)} %get-tuple-element.65), calls=%async_computation.1 | async-start | bytes 2097152 | tf_op jit(solution)/shard_map/all_to_all | solution.py:43
  54.7 2.0 %collective-permute-start.7 = (bf16[2048,128]{1,0:T(8,128)(2,1)S(1)}, bf16[2048,128]{1,0:T(8,128)(2,1)S(1)}, u32[]{:S(2)}, u32[]{:S(2)}) collective-permute-start(bf16[2048,128]{1,0:T(8,128)(2,1)S(1)} %get-tuple-element.50), channel_id=1, source_target_pairs={{0,1},{1,0},{2,3},{3,2},{4,5},{5,4},{6,7},{7,6},{8,9},{9,8},{10,11... | collective-permute-start | bytes 1572872 | tf_op jit(solution)/shard_map/ppermute | solution.py:999
  56.6 7.0 %copy-start.6 = (bf16[128,2048]{1,0:T(8,128)(2,1)S(1)}, bf16[128,2048]{1,0:T(8,128)(2,1)}, u32[]{:S(2)}) copy-start(bf16[128,2048]{1,0:T(8,128)(2,1)} %get-tuple-element.57.site_x) | copy-start | bytes 1572868
  56.6 7.0 %copy-start.7 = (f32[2,2048]{1,0:T(2,128)S(1)}, f32[2,2048]{1,0:T(2,128)}, u32[]{:S(2)}) copy-start(f32[2,2048]{1,0:T(2,128)} %get-tuple-element.60.site_gmod) | copy-start | bytes 49156
  63.6 3.6 %copy-start.2 = (f32[128,2048]{1,0:T(8,128)}, f32[128,2048]{1,0:T(8,128)S(1)}, u32[]{:S(2)}) copy-start(f32[128,2048]{1,0:T(8,128)S(1)} %get-tuple-element.63.mix_ref) | copy-start | bytes 3145732
  63.7 3.6 %copy-start.4 = (f32[128,2048]{1,0:T(8,128)}, f32[128,2048]{1,0:T(8,128)S(1)}, u32[]{:S(2)}) copy-start(f32[128,2048]{1,0:T(8,128)S(1)} %get-tuple-element.64.pre_ref) | copy-start | bytes 3145732
  65.0 2.1 %collective-permute-start.8 = (bf16[16,152,128]{2,1,0:T(8,128)(2,1)S(1)}, bf16[16,152,128]{2,1,0:T(8,128)(2,1)S(1)}, u32[]{:S(2)}, u32[]{:S(2)}) collective-permute-start(bf16[16,152,128]{2,1,0:T(8,128)(2,1)S(1)} %get-tuple-element.62), channel_id=1, source_target_pairs={{0,1},{1,0},{2,3},{3,2},{4,5},{5,4},{6,7},{7,6},{8,9},{9,8},{10,11... | collective-permute-start | bytes 1867784 | tf_op jit(solution)/shard_map/ppermute | solution.py:1027
  67.3 12.1 %collective-permute-start.10 = (bf16[4,152,128]{2,1,0:T(8,128)(2,1)S(1)}, bf16[4,152,128]{2,1,0:T(8,128)(2,1)S(1)}, u32[]{:S(2)}, u32[]{:S(2)}) collective-permute-start(bf16[4,152,128]{2,1,0:T(8,128)(2,1)S(1)} %get-tuple-element.78), channel_id=1, source_target_pairs={{0,4},{2,6},{4,0},{6,2},{8,12},{10,14},{12,8},{14,10},{16,20},{18,... | collective-permute-start | bytes 466952 | tf_op jit(solution)/shard_map/ppermute | solution.py:888
  69.3 10.1 %collective-permute-start.11 = (bf16[4,152,128]{2,1,0:T(8,128)(2,1)S(1)}, bf16[4,152,128]{2,1,0:T(8,128)(2,1)S(1)}, u32[]{:S(2)}, u32[]{:S(2)}) collective-permute-start(bf16[4,152,128]{2,1,0:T(8,128)(2,1)S(1)} %get-tuple-element.77), channel_id=1, source_target_pairs={{0,6},{2,4},{4,2},{6,0},{8,14},{10,12},{12,10},{14,8},{16,22},{18,... | collective-permute-start | bytes 466952 | tf_op jit(solution)/shard_map/ppermute | solution.py:888
  70.7 9.9 %collective-permute-start.9 = (bf16[4,152,128]{2,1,0:T(8,128)(2,1)S(1)}, bf16[4,152,128]{2,1,0:T(8,128)(2,1)S(1)}, u32[]{:S(2)}, u32[]{:S(2)}) collective-permute-start(bf16[4,152,128]{2,1,0:T(8,128)(2,1)S(1)} %get-tuple-element.79), channel_id=1, source_target_pairs={{0,2},{2,0},{4,6},{6,4},{8,10},{10,8},{12,14},{14,12},{16,18},{18,... | collective-permute-start | bytes 466952 | tf_op jit(solution)/shard_map/ppermute | solution.py:888
  80.7 4.6 %collective-permute-start.12 = (bf16[152,128]{1,0:T(8,128)(2,1)S(1)}, bf16[152,128]{1,0:T(8,128)(2,1)S(1)}, u32[]{:S(2)}, u32[]{:S(2)}) collective-permute-start(bf16[152,128]{1,0:T(8,128)(2,1)S(1)} %get-tuple-element.81), channel_id=1, source_target_pairs={{0,8},{2,10},{4,12},{6,14},{8,0},{10,2},{12,4},{14,6},{16,24},{18,... | collective-permute-start | bytes 116744 | tf_op jit(solution)/shard_map/ppermute | solution.py:888
  82.9 5.0 %collective-permute-start.13 = (bf16[152,128]{1,0:T(8,128)(2,1)S(1)}, bf16[152,128]{1,0:T(8,128)(2,1)S(1)}, u32[]{:S(2)}, u32[]{:S(2)}) collective-permute-start(bf16[152,128]{1,0:T(8,128)(2,1)S(1)} %get-tuple-element.83), channel_id=1, source_target_pairs={{0,16},{2,18},{4,20},{6,22},{8,24},{10,26},{12,28},{14,30},{16,0},... | collective-permute-start | bytes 116744 | tf_op jit(solution)/shard_map/ppermute | solution.py:888
  85.1 5.8 %collective-permute-start.14 = (bf16[152,128]{1,0:T(8,128)(2,1)S(1)}, bf16[152,128]{1,0:T(8,128)(2,1)S(1)}, u32[]{:S(2)}, u32[]{:S(2)}) collective-permute-start(bf16[152,128]{1,0:T(8,128)(2,1)S(1)} %get-tuple-element.82), channel_id=1, source_target_pairs={{0,24},{2,26},{4,28},{6,30},{8,16},{10,18},{12,20},{14,22},{16,8},... | collective-permute-start | bytes 116744 | tf_op jit(solution)/shard_map/ppermute | solution.py:888
  90.9 1.3 %collective-permute-start.15 = (f32[152,128]{1,0:T(8,128)S(1)}, f32[152,128]{1,0:T(8,128)S(1)}, u32[]{:S(2)}, u32[]{:S(2)}) collective-permute-start(f32[152,128]{1,0:T(8,128)S(1)} %fusion.8.own_ref), channel_id=1, source_target_pairs={{0,1},{1,0},{2,3},{3,2},{4,5},{5,4},{6,7},{7,6},{8,9},{9,8},{10,11... | collective-permute-start | bytes 233480 | tf_op jit(solution)/shard_map/ppermute | solution.py:1032
  (6 other events, 5.1 us)

commit v10 on v9

--- a/solution.py
+++ b/solution.py
@@ -160,26 +160,25 @@
 
 def start_kernel(ids_ref, tok_ref, grad_ref, proj_hbm, step_hbm, mod_hbm, active_ref, sent_ref, pay_ref,
                  proj_ref, step_ref, mod_ref, both_ref, sems):
+    parts = 4
+    share = tok_ref.shape[0] // parts
+    pairs = [(proj_hbm, proj_ref), (step_hbm, step_ref), (mod_hbm, mod_ref)]
+    for p in range(parts):
+        at = slice(p * share, (p + 1) * share)
+        pairs += [(tok_ref.at[at], both_ref.at[at, 0]), (grad_ref.at[at], both_ref.at[at, 1])]
+    for p in range(parts):
+        at = slice(p * share, (p + 1) * share)
+        pairs.append((both_ref.at[at], sent_ref.at[at]))
     copies = [
-        pltpu.make_async_copy(src, dst, sems.at[n])
-        for n, (src, dst) in enumerate(
-            [
-                (proj_hbm, proj_ref),
-                (step_hbm, step_ref),
-                (mod_hbm, mod_ref),
-                (tok_ref, both_ref.at[:, 0]),
-                (grad_ref, both_ref.at[:, 1]),
-                (both_ref.at[:, 0], sent_ref.at[:, 0]),
-                (both_ref.at[:, 1], sent_ref.at[:, 1]),
-            ]
-        )
+        pltpu.make_async_copy(src, dst, sems.at[n]) for n, (src, dst) in enumerate(pairs)
     ]
-    for copy in copies[:5]:
+    inward, outward = copies[: 3 + 2 * parts], copies[3 + 2 * parts :]
+    for copy in inward:
         copy.start()
-    copies[3].wait()
-    copies[5].start()
-    copies[4].wait()
-    copies[6].start()
+    for p, copy in enumerate(outward):
+        inward[3 + 2 * p].wait()
+        inward[4 + 2 * p].wait()
+        copy.start()
     row = ids_ref[1]
     part, pair = proj_ref.shape[0] // 2, proj_ref.shape[1]
     copies[0].wait()
@@ -198,8 +197,8 @@
     pieces = [piece[:, sl] for piece in (high, own - high) for _, sl in blocks(own.shape[1])]
     pieces.append(jnp.zeros((8 - len(pieces), LANES), f32))
     pay_ref[at : at + 8, :] = jnp.concatenate(pieces, axis=0).astype(bf16)
-    copies[5].wait()
-    copies[6].wait()
+    for copy in outward:
+        copy.wait()
 
 
 def unpack_kernel(radix, ids_ref, own_ref, other_ref, proj_ref, step_ref, shift_ref, gain_ref):
@@ -237,7 +236,15 @@
                 gain_ref[:, lanes] = value
 
 
-def finish_kernel(factor, ids_ref, own_ref, other_ref, active_ref, proj_ref, step_ref, mod_ref):
+def finish_mod_kernel(factor, at, sums_ref, active_ref, mod_ref):
+    rest = jnp.zeros((7, active_ref.shape[1]), f32)
+    active = jnp.concatenate([active_ref[...].astype(f32), rest], axis=0)
+    for k, sl in blocks(mod_ref.shape[1]):
+        own = jnp.broadcast_to(sums_ref[at + k : at + k + 1, :] * factor, (8, LANES))
+        mod_ref[:, sl] = exact(active, own, 0, 0)
+
+
+def finish_kernel(factor, ids_ref, own_ref, other_ref, proj_ref, step_ref):
     row = ids_ref[1]
     pair = proj_ref.shape[1]
     part, heads = proj_ref.shape[0] // 2, step_ref.shape[0] // 2
@@ -248,9 +255,6 @@
             proj_ref[rows, sl] = ref[at : at + part, :] * factor
             at += part
         step_ref[pl.ds(pl.multiple_of(half * heads, heads), heads), :] = ref[at : at + heads, :] * factor
-        at += heads
-    for k, sl in blocks(mod_ref.shape[1]):
-        mod_ref[:, sl] = active_ref[...] * (own_ref[at + k : at + k + 1, :] * factor)
 
 
 def site_fast_kernel(sites, got_ref, *refs):
@@ -266,7 +270,7 @@
         def __getitem__(self, at):
             return read(1)(at[1]).astype(bf16)
 
-    parts = 4
+    parts = 8
     share = width // parts
     copies = []
 
@@ -936,7 +940,7 @@
             ((heads, depth), bf16),
             (mod_weight.shape, bf16),
             (packed, bf16),
-            pltpu.SemaphoreType.DMA((7,)),
+            pltpu.SemaphoreType.DMA((15,)),
         ],
         name="start",
         specs="shhhhhv",
@@ -974,7 +978,7 @@
             (packed, bf16),
             (wide, bf16),
             ((2, width), f32),
-            pltpu.SemaphoreType.DMA((10,)),
+            pltpu.SemaphoreType.DMA((18,)),
         ]
         + [(wide, bf16), ((2 * length, width), bf16)],
         name="site",
@@ -1030,12 +1034,19 @@
     )
     terms, mixed, d_tokens = sum_over_frames(keep, given, 4, (mixed, d_tokens))
     other = lax.ppermute(terms, "row", swap)
-    grad_proj, grad_step, grad_mod = call(
+    (grad_mod,) = call(
+        functools.partial(finish_mod_kernel, factor, size - 8),
+        [((mod_weight.shape[0], mod_cols), f32)],
+        name="finish_mod",
+        specs="vv",
+    )(terms, activated)
+    other, grad_mod = lax.optimization_barrier((other, grad_mod))
+    grad_proj, grad_step = call(
         functools.partial(finish_kernel, factor),
-        [((depth, pair), f32), ((heads, depth), f32), ((mod_weight.shape[0], mod_cols), f32)],
+        [((depth, pair), f32), ((heads, depth), f32)],
         name="finish",
-        specs="svvv",
-    )(ids, terms, other, activated.astype(f32).T)
+        specs="svv",
+    )(ids, terms, other)
     return (mixed.reshape(tokens.shape), d_tokens.reshape(tokens.shape), grad_proj, grad_step.T, grad_mod)
 
 

time: 94 us -> 94.3 us (level)
  waiting for transfers between devices: 33.9 us -> 32.7 us
  Pallas kernels: 24.1 us -> 25.1 us
    pallas_call x0 -> x1, Pallas kernels: none -> 1.13 us  [per_device_fast(): call(functools.partial(finish_mod_kernel, factor, size - 8), [((mod_weigh...]
  transfers between devices with their start and end apart: 18 -> 18, of which waited for: 12 -> 13; matrix products, arithmetic and copies ran while one was open for 1% -> 0% of each run, Pallas kernels for 14% -> 16%
where the time goes in v10:
time: 94.3 us; the launch traced here: 93.8 us
  waiting for transfers between devices  32.7 us (35%)
  starting transfers between devices  30.7 us (33%)
  Pallas kernels  25.1 us (27%)
  local copies, waits for them, and re-layouts  3.25 us (3%)
  between operations  1.57 us (2%)
    ppermute x6, waiting for transfers between devices, others(): lax.ppermute(piece, 'frame', [(i, i ^ d * stride) for i in range(frames)])  13.3 us
    all_to_all x2, starting transfers between devices, exchange(): lax.all_to_all(packed, 'frame', split_axis=0, concat_axis=0, tiled=True)  13 us
    ppermute x6, starting transfers between devices, others(): lax.ppermute(piece, 'frame', [(i, i ^ d * stride) for i in range(frames)])  9.34 us
    ppermute x6, starting transfers between devices, partner(): lax.ppermute(piece, 'frame', [(i, i ^ offset) for i in range(frames)])  7.97 us
    all_to_all x2, waiting for transfers between devices, exchange(): lax.all_to_all(packed, 'frame', split_axis=0, concat_axis=0, tiled=True)  7.87 us
    pallas_call x1, Pallas kernels, per_device_fast(): call(space_fast_kernel, [(wide, f32), (wide, f32), ((length, pair), bf16)...  7.02 us
    pallas_call x1, Pallas kernels, per_device_fast(): call(functools.partial(site_fast_kernel, sites), [(packed, bf16), (wide,...  6.56 us
    ppermute x6, waiting for transfers between devices, partner(): lax.ppermute(piece, 'frame', [(i, i ^ offset) for i in range(frames)])  6.29 us
  transfers between devices with their start and end apart: 18, of which 13 were waited for; matrix products, arithmetic and copies ran while one was open for 0% of the time, Pallas kernels for 16%

profile of v10, /device:TPU:0, one launch (start us, length us, event | category | flops | bytes accessed | tf_op | source)
XLA Modules:
  0.0 93.8 jit_solution(10232554534484214926)
XLA Ops:
  1.4 2.8 %start.1 = (bf16[16,2,8,2048]{3,2,1,0:T(8,128)(2,1)}, bf16[152,128]{1,0:T(8,128)(2,1)S(1)}) custom-call(s32[2]{0:T(128)S(1)} %pad_add_fusion.ids_ref, bf16[16,8,2048]{2,1,0:T(8,128)(2,1)} %bitcast.34, bf16[16,8,2048]{2,1,0:T(8,128)(2,1)} %bitcast.38, bf16[128,256]{1,0:T(8,128)(2,1)} %proj_hbm.1, bf16[32,128]{1,0:T(8,128)(2,1)} %bitcast.45, ...), custom_call_target="tpu_custom_call" | custom-call | tf_op jit(solution)/shard_map/start/pallas_call | solution.py:935
  4.2 5.1 %collective-permute-start.2 = (bf16[152,128]{1,0:T(8,128)(2,1)S(1)}, bf16[152,128]{1,0:T(8,128)(2,1)S(1)}, u32[]{:S(2)}, u32[]{:S(2)}) collective-permute-start(bf16[152,128]{1,0:T(8,128)(2,1)S(1)} %get-tuple-element.42), channel_id=1, source_target_pairs={{0,24},{2,26},{4,28},{6,30},{8,16},{10,18},{12,20},{14,22},{16,8},... | collective-permute-start | bytes 116744 | tf_op jit(solution)/shard_map/ppermute | solution.py:874
  10.0 7.0 %all-to-all-start = ((bf16[16,2,8,2048]{3,2,1,0:T(8,128)(2,1)}), bf16[16,2,8,2048]{3,2,1,0:T(8,128)(2,1)S(1)}, u32[]{:S(2)}, u32[]{:S(2)}) async-start(bf16[16,2,8,2048]{3,2,1,0:T(8,128)(2,1)} %get-tuple-element.45), calls=%async_computation | async-start | bytes 2097152 | tf_op jit(solution)/shard_map/all_to_all | solution.py:43
  17.1 2.9 %collective-permute-start.5 = (bf16[4,152,128]{2,1,0:T(8,128)(2,1)S(1)}, bf16[4,152,128]{2,1,0:T(8,128)(2,1)S(1)}, u32[]{:S(2)}, u32[]{:S(2)}) collective-permute-start(bf16[4,152,128]{2,1,0:T(8,128)(2,1)S(1)} %pad_maximum_fusion), channel_id=1, source_target_pairs={{0,6},{2,4},{4,2},{6,0},{8,14},{10,12},{12,10},{14,8},{16,22},{18,... | collective-permute-start | bytes 466952 | tf_op jit(solution)/shard_map/ppermute | solution.py:874
  20.7 12.6 %collective-permute-done.3 = bf16[4,152,128]{2,1,0:T(8,128)(2,1)S(1)} collective-permute-done((bf16[4,152,128]{2,1,0:T(8,128)(2,1)S(1)}, bf16[4,152,128]{2,1,0:T(8,128)(2,1)S(1)}, u32[]{:S(2)}, u32[]{:S(2)}) %collective-permute-start.3) | collective-permute-done | bytes 155680 | tf_op jit(solution)/shard_map/ppermute | solution.py:874
  34.8 1.3 %collective-permute-done.6.other_ref = bf16[16,152,128]{2,1,0:T(8,128)(2,1)S(1)} collective-permute-done((bf16[16,152,128]{2,1,0:T(8,128)(2,1)S(1)}, bf16[16,152,128]{2,1,0:T(8,128)(2,1)S(1)}, u32[]{:S(2)}, u32[]{:S(2)}) %collective-permute-start.6) | collective-permute-done | bytes 622624 | tf_op jit(solution)/shard_map/ppermute | solution.py:959
  37.2 3.4 %all-to-all-done.got_ref = bf16[16,2,8,2048]{3,2,1,0:T(8,128)(2,1)S(1)} async-done(((bf16[16,2,8,2048]{3,2,1,0:T(8,128)(2,1)}), bf16[16,2,8,2048]{3,2,1,0:T(8,128)(2,1)S(1)}, u32[]{:S(2)}, u32[]{:S(2)}) %all-to-all-start) | async-done | bytes 1048608 | tf_op jit(solution)/shard_map/all_to_all | solution.py:43
  40.6 6.6 %site.1 = (bf16[16,2,8,2048]{3,2,1,0:T(8,128)(2,1)}, bf16[128,2048]{1,0:T(8,128)(2,1)}, f32[2,2048]{1,0:T(2,128)}, bf16[128,256]{1,0:T(8,128)(2,1)S(1)}, bf16[128,32]{1,0:T(8,128)(2,1)S(1)}) custom-call(bf16[16,2,8,2048]{3,2,1,0:T(8,128)(2,1)S(1)} %all-to-all-done.got_ref, f32[1,2048]{1,0:T(1,128)S(1)} %get-tuple-element.43.refs_0_.refs_2_, ...), custom_call_target="tpu_custom_call" | custom-call | tf_op jit(solution)/shard_map/site/pallas_call | solution.py:967
  47.2 6.0 %all-to-all-start.1 = ((bf16[16,2,8,2048]{3,2,1,0:T(8,128)(2,1)}), bf16[16,2,8,2048]{3,2,1,0:T(8,128)(2,1)S(1)}, u32[]{:S(2)}, u32[]{:S(2)}) async-start(bf16[16,2,8,2048]{3,2,1,0:T(8,128)(2,1)} %get-tuple-element.66), calls=%async_computation.1 | async-start | bytes 2097152 | tf_op jit(solution)/shard_map/all_to_all | solution.py:43
  53.2 2.4 %band.1 = (bf16[128,2048]{1,0:T(8,128)(2,1)S(1)}, bf16[128,256]{1,0:T(8,128)(2,1)S(1)}, bf16[128,32]{1,0:T(8,128)(2,1)S(1)}, f32[128,1]{1,0:T(8,128)S(1)}, bf16[2048,128]{1,0:T(8,128)(2,1)S(1)}) custom-call(s32[2]{0:T(128)S(1)} %pad_add_fusion.ids_ref, bf16[128,2048]{1,0:T(8,128)(2,1)S(1)} %bitcast.35, bf16[128,2048]{1,0:T(8,128)(2,1)S(1)} %bitcast.39, ...), custom_call_target="tpu_custom_call" | custom-call | tf_op jit(solution)/shard_map/band/pallas_call | solution.py:991
  55.7 1.9 %collective-permute-done.7.arrived_ref = bf16[2048,128]{1,0:T(8,128)(2,1)S(1)} collective-permute-done((bf16[2048,128]{1,0:T(8,128)(2,1)S(1)}, bf16[2048,128]{1,0:T(8,128)(2,1)S(1)}, u32[]{:S(2)}, u32[]{:S(2)}) %collective-permute-start.7) | collective-permute-done | bytes 524320 | tf_op jit(solution)/shard_map/ppermute | solution.py:1003
  57.6 7.0 %space.1 = (f32[128,2048]{1,0:T(8,128)S(1)}, f32[128,2048]{1,0:T(8,128)S(1)}, bf16[128,256]{1,0:T(8,128)(2,1)S(1)}, bf16[128,32]{1,0:T(8,128)(2,1)S(1)}, f32[2,2048]{1,0:T(2,128)S(1)}) custom-call(s32[2]{0:T(128)S(1)} %pad_add_fusion.ids_ref, bf16[2048,128]{1,0:T(8,128)(2,1)S(1)} %collective-permute-done.7.arrived_ref, bf16[128,2048]{1,0:T(8,128)(2,1)S(1)} %bitcast.36, ...), custom_call_target="tpu_custom_call" | custom-call | tf_op jit(solution)/shard_map/space/pallas_call | solution.py:1006
  64.7 1.3 %terms.1 = (bf16[16,152,128]{2,1,0:T(8,128)(2,1)S(1)}, bf16[16,152,128]{2,1,0:T(8,128)(2,1)S(1)}) custom-call(s32[2]{0:T(128)S(1)} %pad_add_fusion.ids_ref, bf16[128,2048]{1,0:T(8,128)(2,1)S(1)} %get-tuple-element.50.refs_2_.x_ref, bf16[128,256]{1,0:T(8,128)(2,1)S(1)} %get-tuple-element.55.dc_ref, bf16[128,32]{1,0:T(8,128)(2,1)S(1)} %get-tuple-element.56.dl_ref, ...), custom_call_target="tpu_custom_call" | custom-call | tf_op jit(solution)/shard_map/terms/pallas_call | solution.py:1025
  66.2 1.9 %collective-permute-done.8 = bf16[16,152,128]{2,1,0:T(8,128)(2,1)S(1)} collective-permute-done((bf16[16,152,128]{2,1,0:T(8,128)(2,1)S(1)}, bf16[16,152,128]{2,1,0:T(8,128)(2,1)S(1)}, u32[]{:S(2)}, u32[]{:S(2)}) %collective-permute-start.8) | collective-permute-done | bytes 622624 | tf_op jit(solution)/shard_map/ppermute | solution.py:1031
  68.3 2.9 %collective-permute-start.11 = (bf16[4,152,128]{2,1,0:T(8,128)(2,1)S(1)}, bf16[4,152,128]{2,1,0:T(8,128)(2,1)S(1)}, u32[]{:S(2)}, u32[]{:S(2)}) collective-permute-start(bf16[4,152,128]{2,1,0:T(8,128)(2,1)S(1)} %get-tuple-element.79), channel_id=1, source_target_pairs={{0,6},{2,4},{4,2},{6,0},{8,14},{10,12},{12,10},{14,8},{16,22},{18,... | collective-permute-start | bytes 466952 | tf_op jit(solution)/shard_map/ppermute | solution.py:892
  71.8 4.5 %all-to-all-done.1.came_ref = bf16[16,2,8,2048]{3,2,1,0:T(8,128)(2,1)S(1)} async-done(((bf16[16,2,8,2048]{3,2,1,0:T(8,128)(2,1)}), bf16[16,2,8,2048]{3,2,1,0:T(8,128)(2,1)S(1)}, u32[]{:S(2)}, u32[]{:S(2)}) %all-to-all-start.1) | async-done | bytes 1048608 | tf_op jit(solution)/shard_map/all_to_all | solution.py:43
  76.3 1.2 %copy-done.3 = f32[128,2048]{1,0:T(8,128)S(1)} copy-done((f32[128,2048]{1,0:T(8,128)S(1)}, f32[128,2048]{1,0:T(8,128)}, u32[]{:S(2)}) %copy-start.3) | copy-done | bytes 1048600
  77.5 1.2 %copy-done.5 = f32[128,2048]{1,0:T(8,128)S(1)} copy-done((f32[128,2048]{1,0:T(8,128)S(1)}, f32[128,2048]{1,0:T(8,128)}, u32[]{:S(2)}) %copy-start.5) | copy-done | bytes 1048600
  78.7 1.7 %last.1 = (bf16[128,2048]{1,0:T(8,128)(2,1)}, bf16[128,2048]{1,0:T(8,128)(2,1)}) custom-call(bf16[128,2048]{1,0:T(8,128)(2,1)S(1)} %bitcast.37, f32[128,1]{1,0:T(8,128)S(1)} %get-tuple-element.54.refs_5_.inverse_ref, f32[1,2048]{1,0:T(1,128)S(1)} %get-tuple-element.44.refs_1_.refs_3_.gain_ref, f32[128,2048]{1,0:T(8,128)S(1)} %copy-done.3, ...), custom_call_target="tpu_custom_call" | custom-call | tf_op jit(solution)/shard_map/last/pallas_call | solution.py:1032
  81.7 1.9 %collective-permute-start.12 = (bf16[152,128]{1,0:T(8,128)(2,1)S(1)}, bf16[152,128]{1,0:T(8,128)(2,1)S(1)}, u32[]{:S(2)}, u32[]{:S(2)}) collective-permute-start(bf16[152,128]{1,0:T(8,128)(2,1)S(1)} %get-tuple-element.83), channel_id=1, source_target_pairs={{0,8},{2,10},{4,12},{6,14},{8,0},{10,2},{12,4},{14,6},{16,24},{18,... | collective-permute-start | bytes 116744 | tf_op jit(solution)/shard_map/ppermute | solution.py:892
  83.6 2.5 %collective-permute-start.14 = (bf16[152,128]{1,0:T(8,128)(2,1)S(1)}, bf16[152,128]{1,0:T(8,128)(2,1)S(1)}, u32[]{:S(2)}, u32[]{:S(2)}) collective-permute-start(bf16[152,128]{1,0:T(8,128)(2,1)S(1)} %get-tuple-element.84), channel_id=1, source_target_pairs={{0,24},{2,26},{4,28},{6,30},{8,16},{10,18},{12,20},{14,22},{16,8},... | collective-permute-start | bytes 116744 | tf_op jit(solution)/shard_map/ppermute | solution.py:892
  86.1 3.4 %collective-permute-done.14 = bf16[152,128]{1,0:T(8,128)(2,1)S(1)} collective-permute-done((bf16[152,128]{1,0:T(8,128)(2,1)S(1)}, bf16[152,128]{1,0:T(8,128)(2,1)S(1)}, u32[]{:S(2)}, u32[]{:S(2)}) %collective-permute-start.14) | collective-permute-done | bytes 38944 | tf_op jit(solution)/shard_map/ppermute | solution.py:892
  89.5 1.7 %collective-permute-done.13 = bf16[152,128]{1,0:T(8,128)(2,1)S(1)} collective-permute-done((bf16[152,128]{1,0:T(8,128)(2,1)S(1)}, bf16[152,128]{1,0:T(8,128)(2,1)S(1)}, u32[]{:S(2)}, u32[]{:S(2)}) %collective-permute-start.13) | collective-permute-done | bytes 38944 | tf_op jit(solution)/shard_map/ppermute | solution.py:892
  92.6 1.2 %finish.1 = (f32[128,256]{1,0:T(8,128)}, f32[32,128]{1,0:T(8,128)}) custom-call(s32[2]{0:T(128)S(1)} %pad_add_fusion.ids_ref, f32[152,128]{1,0:T(8,128)S(1)} %fusion.1.sums_ref.own_ref, f32[152,128]{1,0:T(8,128)S(1)} %collective-permute-done.15.other_ref), custom_call_target="tpu_custom_call" | custom-call | tf_op jit(solution)/shard_map/finish/pallas_call | solution.py:1044
  (60 shorter events, 7.7 us)
Async XLA Ops:
  4.2 12.8 %collective-permute-start.2 = (bf16[152,128]{1,0:T(8,128)(2,1)S(1)}, bf16[152,128]{1,0:T(8,128)(2,1)S(1)}, u32[]{:S(2)}, u32[]{:S(2)}) collective-permute-start(bf16[152,128]{1,0:T(8,128)(2,1)S(1)} %get-tuple-element.42), channel_id=1, source_target_pairs={{0,24},{2,26},{4,28},{6,30},{8,16},{10,18},{12,20},{14,22},{16,8},... | collective-permute-start | bytes 116744 | tf_op jit(solution)/shard_map/ppermute | solution.py:874
  9.4 7.7 %collective-permute-start.1 = (bf16[152,128]{1,0:T(8,128)(2,1)S(1)}, bf16[152,128]{1,0:T(8,128)(2,1)S(1)}, u32[]{:S(2)}, u32[]{:S(2)}) collective-permute-start(bf16[152,128]{1,0:T(8,128)(2,1)S(1)} %get-tuple-element.42), channel_id=1, source_target_pairs={{0,16},{2,18},{4,20},{6,22},{8,24},{10,26},{12,28},{14,30},{16,0},... | collective-permute-start | bytes 116744 | tf_op jit(solution)/shard_map/ppermute | solution.py:874
  9.4 7.7 %collective-permute-start = (bf16[152,128]{1,0:T(8,128)(2,1)S(1)}, bf16[152,128]{1,0:T(8,128)(2,1)S(1)}, u32[]{:S(2)}, u32[]{:S(2)}) collective-permute-start(bf16[152,128]{1,0:T(8,128)(2,1)S(1)} %get-tuple-element.42), channel_id=1, source_target_pairs={{0,8},{2,10},{4,12},{6,14},{8,0},{10,2},{12,4},{14,6},{16,24},{18,... | collective-permute-start | bytes 116744 | tf_op jit(solution)/shard_map/ppermute | solution.py:874
  10.0 30.6 %all-to-all-start = ((bf16[16,2,8,2048]{3,2,1,0:T(8,128)(2,1)}), bf16[16,2,8,2048]{3,2,1,0:T(8,128)(2,1)S(1)}, u32[]{:S(2)}, u32[]{:S(2)}) async-start(bf16[16,2,8,2048]{3,2,1,0:T(8,128)(2,1)} %get-tuple-element.45), calls=%async_computation | async-start | bytes 2097152 | tf_op jit(solution)/shard_map/all_to_all | solution.py:43
  17.1 16.9 %collective-permute-start.5 = (bf16[4,152,128]{2,1,0:T(8,128)(2,1)S(1)}, bf16[4,152,128]{2,1,0:T(8,128)(2,1)S(1)}, u32[]{:S(2)}, u32[]{:S(2)}) collective-permute-start(bf16[4,152,128]{2,1,0:T(8,128)(2,1)S(1)} %pad_maximum_fusion), channel_id=1, source_target_pairs={{0,6},{2,4},{4,2},{6,0},{8,14},{10,12},{12,10},{14,8},{16,22},{18,... | collective-permute-start | bytes 466952 | tf_op jit(solution)/shard_map/ppermute | solution.py:874
  20.0 13.5 %collective-permute-start.4 = (bf16[4,152,128]{2,1,0:T(8,128)(2,1)S(1)}, bf16[4,152,128]{2,1,0:T(8,128)(2,1)S(1)}, u32[]{:S(2)}, u32[]{:S(2)}) collective-permute-start(bf16[4,152,128]{2,1,0:T(8,128)(2,1)S(1)} %pad_maximum_fusion), channel_id=1, source_target_pairs={{0,4},{2,6},{4,0},{6,2},{8,12},{10,14},{12,8},{14,10},{16,20},{18,... | collective-permute-start | bytes 466952 | tf_op jit(solution)/shard_map/ppermute | solution.py:874
  20.6 12.8 %collective-permute-start.3 = (bf16[4,152,128]{2,1,0:T(8,128)(2,1)S(1)}, bf16[4,152,128]{2,1,0:T(8,128)(2,1)S(1)}, u32[]{:S(2)}, u32[]{:S(2)}) collective-permute-start(bf16[4,152,128]{2,1,0:T(8,128)(2,1)S(1)} %pad_maximum_fusion), channel_id=1, source_target_pairs={{0,2},{2,0},{4,6},{6,4},{8,10},{10,8},{12,14},{14,12},{16,18},{18,... | collective-permute-start | bytes 466952 | tf_op jit(solution)/shard_map/ppermute | solution.py:874
  34.0 2.1 %collective-permute-start.6 = (bf16[16,152,128]{2,1,0:T(8,128)(2,1)S(1)}, bf16[16,152,128]{2,1,0:T(8,128)(2,1)S(1)}, u32[]{:S(2)}, u32[]{:S(2)}) collective-permute-start(bf16[16,152,128]{2,1,0:T(8,128)(2,1)S(1)} %constant_dynamic-update-slice_fusion.own_ref), channel_id=1, source_target_pairs={{0,1},{1,0},{2,3},{3,2},{4,5},{5,4},{6,7},{7,6},{8,9},{9,8},{10,11... | collective-permute-start | bytes 1867784 | tf_op jit(solution)/shard_map/ppermute | solution.py:959
  47.2 6.0 %copy-start = (bf16[1,1,128,2048]{3,2,1,0:T(8,128)(2,1)S(1)}, bf16[1,1,128,2048]{3,2,1,0:T(8,128)(2,1)}, u32[]{:S(2)}) copy-start(bf16[1,1,128,2048]{3,2,1,0:T(8,128)(2,1)} %param.10) | copy-start | bytes 1572868
  47.2 6.0 %copy-start.1 = (bf16[1,1,128,2048]{3,2,1,0:T(8,128)(2,1)S(1)}, bf16[1,1,128,2048]{3,2,1,0:T(8,128)(2,1)}, u32[]{:S(2)}) copy-start(bf16[1,1,128,2048]{3,2,1,0:T(8,128)(2,1)} %param.11) | copy-start | bytes 1572868
  47.2 29.1 %all-to-all-start.1 = ((bf16[16,2,8,2048]{3,2,1,0:T(8,128)(2,1)}), bf16[16,2,8,2048]{3,2,1,0:T(8,128)(2,1)S(1)}, u32[]{:S(2)}, u32[]{:S(2)}) async-start(bf16[16,2,8,2048]{3,2,1,0:T(8,128)(2,1)} %get-tuple-element.66), calls=%async_computation.1 | async-start | bytes 2097152 | tf_op jit(solution)/shard_map/all_to_all | solution.py:43
  55.7 2.0 %collective-permute-start.7 = (bf16[2048,128]{1,0:T(8,128)(2,1)S(1)}, bf16[2048,128]{1,0:T(8,128)(2,1)S(1)}, u32[]{:S(2)}, u32[]{:S(2)}) collective-permute-start(bf16[2048,128]{1,0:T(8,128)(2,1)S(1)} %get-tuple-element.51), channel_id=1, source_target_pairs={{0,1},{1,0},{2,3},{3,2},{4,5},{5,4},{6,7},{7,6},{8,9},{9,8},{10,11... | collective-permute-start | bytes 1572872 | tf_op jit(solution)/shard_map/ppermute | solution.py:1003
  57.6 7.1 %copy-start.6 = (bf16[128,2048]{1,0:T(8,128)(2,1)S(1)}, bf16[128,2048]{1,0:T(8,128)(2,1)}, u32[]{:S(2)}) copy-start(bf16[128,2048]{1,0:T(8,128)(2,1)} %get-tuple-element.58.site_x) | copy-start | bytes 1572868
  57.6 7.1 %copy-start.7 = (f32[2,2048]{1,0:T(2,128)S(1)}, f32[2,2048]{1,0:T(2,128)}, u32[]{:S(2)}) copy-start(f32[2,2048]{1,0:T(2,128)} %get-tuple-element.61.site_gmod) | copy-start | bytes 49156
  64.7 3.6 %copy-start.2 = (f32[128,2048]{1,0:T(8,128)}, f32[128,2048]{1,0:T(8,128)S(1)}, u32[]{:S(2)}) copy-start(f32[128,2048]{1,0:T(8,128)S(1)} %get-tuple-element.64.mix_ref) | copy-start | bytes 3145732
  64.7 3.6 %copy-start.4 = (f32[128,2048]{1,0:T(8,128)}, f32[128,2048]{1,0:T(8,128)S(1)}, u32[]{:S(2)}) copy-start(f32[128,2048]{1,0:T(8,128)S(1)} %get-tuple-element.65.pre_ref) | copy-start | bytes 3145732
  66.0 2.1 %collective-permute-start.8 = (bf16[16,152,128]{2,1,0:T(8,128)(2,1)S(1)}, bf16[16,152,128]{2,1,0:T(8,128)(2,1)S(1)}, u32[]{:S(2)}, u32[]{:S(2)}) collective-permute-start(bf16[16,152,128]{2,1,0:T(8,128)(2,1)S(1)} %get-tuple-element.63), channel_id=1, source_target_pairs={{0,1},{1,0},{2,3},{3,2},{4,5},{5,4},{6,7},{7,6},{8,9},{9,8},{10,11... | collective-permute-start | bytes 1867784 | tf_op jit(solution)/shard_map/ppermute | solution.py:1031
  68.3 12.2 %collective-permute-start.11 = (bf16[4,152,128]{2,1,0:T(8,128)(2,1)S(1)}, bf16[4,152,128]{2,1,0:T(8,128)(2,1)S(1)}, u32[]{:S(2)}, u32[]{:S(2)}) collective-permute-start(bf16[4,152,128]{2,1,0:T(8,128)(2,1)S(1)} %get-tuple-element.79), channel_id=1, source_target_pairs={{0,6},{2,4},{4,2},{6,0},{8,14},{10,12},{12,10},{14,8},{16,22},{18,... | collective-permute-start | bytes 466952 | tf_op jit(solution)/shard_map/ppermute | solution.py:892
  71.2 9.5 %collective-permute-start.10 = (bf16[4,152,128]{2,1,0:T(8,128)(2,1)S(1)}, bf16[4,152,128]{2,1,0:T(8,128)(2,1)S(1)}, u32[]{:S(2)}, u32[]{:S(2)}) collective-permute-start(bf16[4,152,128]{2,1,0:T(8,128)(2,1)S(1)} %get-tuple-element.80), channel_id=1, source_target_pairs={{0,4},{2,6},{4,0},{6,2},{8,12},{10,14},{12,8},{14,10},{16,20},{18,... | collective-permute-start | bytes 466952 | tf_op jit(solution)/shard_map/ppermute | solution.py:892
  71.7 9.9 %collective-permute-start.9 = (bf16[4,152,128]{2,1,0:T(8,128)(2,1)S(1)}, bf16[4,152,128]{2,1,0:T(8,128)(2,1)S(1)}, u32[]{:S(2)}, u32[]{:S(2)}) collective-permute-start(bf16[4,152,128]{2,1,0:T(8,128)(2,1)S(1)} %get-tuple-element.81), channel_id=1, source_target_pairs={{0,2},{2,0},{4,6},{6,4},{8,10},{10,8},{12,14},{14,12},{16,18},{18,... | collective-permute-start | bytes 466952 | tf_op jit(solution)/shard_map/ppermute | solution.py:892
  81.7 4.4 %collective-permute-start.12 = (bf16[152,128]{1,0:T(8,128)(2,1)S(1)}, bf16[152,128]{1,0:T(8,128)(2,1)S(1)}, u32[]{:S(2)}, u32[]{:S(2)}) collective-permute-start(bf16[152,128]{1,0:T(8,128)(2,1)S(1)} %get-tuple-element.83), channel_id=1, source_target_pairs={{0,8},{2,10},{4,12},{6,14},{8,0},{10,2},{12,4},{14,6},{16,24},{18,... | collective-permute-start | bytes 116744 | tf_op jit(solution)/shard_map/ppermute | solution.py:892
  83.6 5.9 %collective-permute-start.14 = (bf16[152,128]{1,0:T(8,128)(2,1)S(1)}, bf16[152,128]{1,0:T(8,128)(2,1)S(1)}, u32[]{:S(2)}, u32[]{:S(2)}) collective-permute-start(bf16[152,128]{1,0:T(8,128)(2,1)S(1)} %get-tuple-element.84), channel_id=1, source_target_pairs={{0,24},{2,26},{4,28},{6,30},{8,16},{10,18},{12,20},{14,22},{16,8},... | collective-permute-start | bytes 116744 | tf_op jit(solution)/shard_map/ppermute | solution.py:892
  86.1 5.2 %collective-permute-start.13 = (bf16[152,128]{1,0:T(8,128)(2,1)S(1)}, bf16[152,128]{1,0:T(8,128)(2,1)S(1)}, u32[]{:S(2)}, u32[]{:S(2)}) collective-permute-start(bf16[152,128]{1,0:T(8,128)(2,1)S(1)} %get-tuple-element.85), channel_id=1, source_target_pairs={{0,16},{2,18},{4,20},{6,22},{8,24},{10,26},{12,28},{14,30},{16,0},... | collective-permute-start | bytes 116744 | tf_op jit(solution)/shard_map/ppermute | solution.py:892
  91.3 1.3 %collective-permute-start.15 = (f32[152,128]{1,0:T(8,128)S(1)}, f32[152,128]{1,0:T(8,128)S(1)}, u32[]{:S(2)}, u32[]{:S(2)}) collective-permute-start(f32[152,128]{1,0:T(8,128)S(1)} %fusion.1.sums_ref.own_ref), channel_id=1, source_target_pairs={{0,1},{1,0},{2,3},{3,2},{4,5},{5,4},{6,7},{7,6},{8,9},{9,8},{10,11... | collective-permute-start | bytes 233480 | tf_op jit(solution)/shard_map/ppermute | solution.py:1036
  (6 other events, 5.1 us)

commit v11 on v10

--- a/solution.py
+++ b/solution.py
@@ -7,6 +7,7 @@
 from jax.experimental import pallas as pl
 from jax.experimental.pallas import tpu as pltpu
 from jax.sharding import PartitionSpec as P
+
 
 norm_eps = 1e-05
 LANES = 128
@@ -201,26 +202,29 @@
         copy.wait()
 
 
-def unpack_kernel(radix, ids_ref, own_ref, other_ref, proj_ref, step_ref, shift_ref, gain_ref):
+def unpack_kernel(radix, ids_ref, *refs):
+    own_refs, other_refs = refs[:radix], refs[radix : 2 * radix]
+    proj_ref, step_ref, shift_ref, gain_ref = refs[2 * radix :]
     me, row = ids_ref[0], ids_ref[1]
     width, pair = proj_ref.shape
-    frames = own_ref.shape[0]
+    frames = radix * radix
     depth = width // frames
     part, heads = depth // 2, step_ref.shape[0] // 2
     cols = 2 * width // frames
     for i in range(frames):
         source = jnp.bitwise_xor(me, (i % radix) * radix + i // radix)
-        for ref, half in ((own_ref, row), (other_ref, 1 - row)):
+        near, far = i // radix, i % radix
+        for ref, half in ((own_refs[near], row), (other_refs[near], 1 - row)):
             rows = pl.ds(pl.multiple_of(source * depth + half * part, part), part)
             at = 0
             for _, sl in blocks(pair):
-                proj_ref[rows, sl] = ref[i, at : at + part, :]
+                proj_ref[rows, sl] = ref[far, at : at + part, :]
                 at += part
             rows = pl.ds(pl.multiple_of(half * heads, heads), heads)
             lanes = pl.ds(pl.multiple_of(source * depth, depth), depth)
-            step_ref[rows, lanes] = ref[i, at : at + heads, :]
+            step_ref[rows, lanes] = ref[far, at : at + heads, :]
             at += heads
-        own = own_ref[i, at : at + 8, :].astype(f32)
+        own = own_refs[near][far, at : at + 8, :].astype(f32)
         count = cols // LANES
         lanes_at = jnp.bitwise_and(source, frames // 2 - 1) * cols
         for k in range(count):
@@ -263,6 +267,7 @@
     tok_ref, sent_ref, x_ref, gmod_ref, sems = refs[10:15]
     scratch = refs[15:]
     frames, width = got_ref.shape[0], got_ref.shape[3]
+
     def read(which):
         return lambda sl: got_ref[:, which, :, sl].astype(f32).reshape(frames * sites, LANES)
 
@@ -344,7 +349,7 @@
     coeffs = mm(x_ref[...], proj_ref[...], 1, 0).astype(bf16)
     logits = mm(x_ref[...], step_ref[...], 1, 1).astype(bf16)
     rate = rate_ref[...]
-    z, step, cum, cums = steps_of(logits, bias_ref[...], rate, mask)
+    z, step, _, cums = steps_of(logits, bias_ref[...], rate, mask)
     b_part, c_part = coeffs[:, :state], coeffs[:, state:]
     scores = mm(c_part, b_part, 1, 1) * (mask / state)
     step_parts, twice = halves_of(step), doubled(lanes_of)
@@ -443,40 +448,42 @@
         own_ref[sl, :] = mm(faded, c_part, 0, 0).astype(bf16)
 
 
-def terms_kernel(radix, ids_ref, x_ref, dc_ref, dl_ref, gmod_ref, site_x, site_dc, site_dl, site_gmod,
-                 keep_ref, give_ref):
+def terms_kernel(radix, ids_ref, x_ref, dc_ref, dl_ref, gmod_ref, site_x, site_dc, site_dl, site_gmod, *refs):
     me, first = ids_ref[0], ids_ref[1] == 0
     width = x_ref.shape[1]
     coeffs = jnp.concatenate([dc_ref[...], site_dc[...]], axis=0)
     logits = jnp.concatenate([dl_ref[...], site_dl[...]], axis=0)
-    frames = keep_ref.shape[0]
-    share = 2 * width // LANES // frames
-
-    def put_halves(j, at, value):
+    share = 2 * width // LANES // (radix * radix)
+    half = radix * radix // 2
+
+    def put_halves(keep_ref, give_ref, e, at, value):
         part = value.shape[0] // 2
         own = jnp.where(first, value[:part], value[part:]).astype(bf16)
         other = jnp.where(first, value[part:], value[:part]).astype(bf16)
         for _, sl in blocks(value.shape[1]):
-            keep_ref[j, at : at + part, :] = own[:, sl]
-            give_ref[j, at : at + part, :] = other[:, sl]
+            keep_ref[e, at : at + part, :] = own[:, sl]
+            give_ref[e, at : at + part, :] = other[:, sl]
             at += part
         return at
 
-    for j, sl in blocks(width):
-        offset = jnp.bitwise_xor(me, j)
-        place = jnp.bitwise_and(offset, radix - 1) * radix + offset // radix
-        tall = jnp.concatenate([x_ref[:, sl], site_x[:, sl]], axis=0)
-        at = put_halves(place, 0, mm(tall, coeffs, 0, 0))
-        at = put_halves(place, at, mm(logits, tall, 0, 0))
-        rows = []
-        for n in range(j * share, (j + 1) * share):
-            which, at_lane = n // (width // LANES), n % (width // LANES) * LANES
-            lanes = slice(at_lane, at_lane + LANES)
-            rows.append(gmod_ref[which : which + 1, lanes] + site_gmod[which : which + 1, lanes])
-        rows.append(jnp.zeros((8 - len(rows), LANES), f32))
-        rows = jnp.concatenate(rows, axis=0).astype(bf16)
-        keep_ref[place, at : at + 8, :] = rows
-        give_ref[place, at : at + 8, :] = rows
+    for d in (*range(1, radix), 0):
+        keep_ref, give_ref = refs[d], refs[radix + d]
+        for e in range(radix):
+            frame = jnp.bitwise_xor(me, e * radix + d)
+            sl = pl.ds(pl.multiple_of(frame * LANES, LANES), LANES)
+            tall = jnp.concatenate([x_ref[:, sl], site_x[:, sl]], axis=0)
+            at = put_halves(keep_ref, give_ref, e, 0, mm(tall, coeffs, 0, 0))
+            at = put_halves(keep_ref, give_ref, e, at, mm(logits, tall, 0, 0))
+            start = jnp.bitwise_and(frame, half - 1) * share * LANES
+            rows = []
+            for k in range(share):
+                lanes = pl.ds(pl.multiple_of(start + k * LANES, LANES), LANES)
+                both = gmod_ref[:, lanes] + site_gmod[:, lanes]
+                rows.append(jnp.where(frame < half, both[0:1], both[1:2]))
+            rows.append(jnp.zeros((8 - len(rows), LANES), f32))
+            rows = jnp.concatenate(rows, axis=0).astype(bf16)
+            keep_ref[e, at : at + 8, :] = rows
+            give_ref[e, at : at + 8, :] = rows
 
 
 def space_fast_kernel(ids_ref, arrived_ref, *refs):
@@ -637,7 +644,7 @@
     return pltpu.with_memory_space_constraint(array, pltpu.MemorySpace.HBM)
 
 
-def call(kernel, outs, scratch=(), name=None, specs=None, hbm_outs=()):
+def call(kernel, outs, scratch=(), specs=None, hbm_outs=()):
     shapes = [
         pltpu.MemorySpace.HBM(s, d) if n in hbm_outs else jax.ShapeDtypeStruct(s, d)
         for n, (s, d) in enumerate(outs)
@@ -655,7 +662,6 @@
         **spaces,
         scratch_shapes=[pltpu.VMEM(*s) if isinstance(s, tuple) else s for s in scratch],
         compiler_params=pltpu.CompilerParams(vmem_limit_bytes=24 << 20),
-        name=name,
     )
 
 
@@ -764,7 +770,6 @@
         functools.partial(site_kernel, sites),
         [(wide, bf16), (wide, bf16), ((width, pair), f32), ((heads, width), f32), ((2 * clips, width), f32)],
         [(wide, bf16)] * 2 + [((2 * length, width), bf16)],
-        name="site",
     )(site_tok, site_grad, shift, gain, proj_full, step_full, bias, rate_time[None])
 
     came = exchange(
@@ -792,7 +797,6 @@
             ((width, state), bf16),
             ((width, state), bf16),
         ],
-        name="band",
     )(tok, grad, own_shift, own_gain, proj_full, step_full, bias, rate_space[None])
     state_in = chain(end_own, decay, True)
     later_grad = chain(start_grad, decay, False)
@@ -800,7 +804,6 @@
         space_kernel,
         [(wide, f32), (wide, f32), ((width, pair), bf16), ((heads, width), bf16), ((2, width), f32)],
         [(wide, bf16), ((3 * length, width), bf16)],
-        name="space",
     )(
         tok,
         grad,
@@ -845,7 +848,7 @@
     mod_sum = sums[0, at : at + size].reshape(clips, mod_cols)
     grad_mod = jnp.dot(activated.astype(f32).T, mod_sum, precision=EXACT)
 
-    mixed, d_tokens = call(last_kernel, [(wide, bf16), (wide, bf16)], name="last")(
+    mixed, d_tokens = call(last_kernel, [(wide, bf16), (wide, bf16)])(
         tok, inverse, own_gain, mix, pre, time_out, time_back
     )
     return (mixed.reshape(tokens.shape), d_tokens.reshape(tokens.shape), grad_proj, grad_step, grad_mod)
@@ -876,7 +879,7 @@
         ]
 
     far = jnp.stack(others(own, radix))
-    return jnp.concatenate(others(far, 1))
+    return others(far, 1)
 
 
 def sum_over_frames(keep, given, radix, ahead):
@@ -891,8 +894,7 @@
     def partner(piece, offset):
         return lax.ppermute(piece, "frame", [(i, i ^ offset) for i in range(frames)])
 
-    parts = [slice(d * radix, (d + 1) * radix) for d in range(radix)]
-    near = [total([keep[p], given[p]]).astype(bf16) for p in parts]
+    near = [total([keep[d], given[d]]).astype(bf16) for d in range(radix)]
     near = [near[0]] + [partner(near[d], d) for d in range(1, radix)]
     near, ahead = lax.optimization_barrier((near, ahead))
     near = total(near).astype(bf16)
@@ -942,7 +944,6 @@
             (packed, bf16),
             pltpu.SemaphoreType.DMA((15,)),
         ],
-        name="start",
         specs="shhhhhv",
         hbm_outs=(0,),
     )(
@@ -956,13 +957,12 @@
     )
     got = exchange(sent)
     payload = spread_over_frames(payload)
-    other = lax.ppermute(payload, "row", swap)
+    other = [lax.ppermute(piece, "row", swap) for piece in payload]
     proj_full, step_full, shift, gain = call(
         functools.partial(unpack_kernel, 4),
         [((width, pair), bf16), ((heads, width), bf16), ((1, width), f32), ((1, width), f32)],
-        name="unpack",
-        specs="svv",
-    )(ids, payload, other)
+        specs="s" + "v" * 8,
+    )(ids, *payload, *other)
 
     sent, site_x, site_gmod, site_dc, site_dl = call(
         functools.partial(site_fast_kernel, sites),
@@ -981,7 +981,6 @@
             pltpu.SemaphoreType.DMA((18,)),
         ]
         + [(wide, bf16), ((2 * length, width), bf16)],
-        name="site",
         specs="vvvvvv",
         hbm_outs=(0, 1, 2),
     )(got, shift, gain, proj_full, step_full, small)
@@ -997,17 +996,14 @@
             ((length, 1), f32),
             ((width, state), bf16),
         ],
-        name="band",
         specs="svvvvvvv",
     )(ids, tok, grad, shift, gain, proj_full, step_full, small)
     arrived = lax.ppermute(give, "row", swap)
 
-    halves = (frames, size, LANES)
     mix, pre, own_dc, own_dl, gmod = call(
         space_fast_kernel,
         [(wide, f32), (wide, f32), ((length, pair), bf16), ((length, heads), bf16), ((2, width), f32)],
         [(wide, bf16), ((3 * length, width), bf16)],
-        name="space",
         specs="s" + "v" * 10,
     )(
         ids,
@@ -1022,14 +1018,11 @@
         step_full,
         small,
     )
-    keep, give = call(
-        functools.partial(terms_kernel, 4),
-        [(halves, bf16), (halves, bf16)],
-        name="terms",
-        specs="svvvvvvvv",
+    pieces = call(
+        functools.partial(terms_kernel, 4), [((4, size, LANES), bf16)] * 8, specs="svvvvvvvv"
     )(ids, normed, own_dc, own_dl, gmod, site_x, site_dc, site_dl, site_gmod)
-    given = lax.ppermute(give, "row", swap)
-    mixed, d_tokens = call(last_fast_kernel, [(wide, bf16), (wide, bf16)], name="last")(
+    keep, given = pieces[:4], [lax.ppermute(piece, "row", swap) for piece in pieces[4:]]
+    mixed, d_tokens = call(last_fast_kernel, [(wide, bf16), (wide, bf16)])(
         tok, inverse, gain, mix, pre, came
     )
     terms, mixed, d_tokens = sum_over_frames(keep, given, 4, (mixed, d_tokens))
@@ -1037,14 +1030,12 @@
     (grad_mod,) = call(
         functools.partial(finish_mod_kernel, factor, size - 8),
         [((mod_weight.shape[0], mod_cols), f32)],
-        name="finish_mod",
         specs="vv",
     )(terms, activated)
     other, grad_mod = lax.optimization_barrier((other, grad_mod))
     grad_proj, grad_step = call(
         functools.partial(finish_kernel, factor),
         [((depth, pair), f32), ((heads, depth), f32)],
-        name="finish",
         specs="svv",
     )(ids, terms, other)
     return (mixed.reshape(tokens.shape), d_tokens.reshape(tokens.shape), grad_proj, grad_step.T, grad_mod)

time: 94.3 us -> 106 us (1.12)
  waiting for transfers between devices: 32.7 us -> 44.3 us
    ppermute x6, waiting for transfers between devices: 13.3 us -> 30.2 us  [others(): lax.ppermute(piece, 'frame', [(i, i ^ d * stride) for i in range(frames)])]
    ppermute x2 -> x8, waiting for transfers between devices: 3.26 us -> 0.74 us  [the longest x4 0.38 us: per_device_fast(): other = [lax.ppermute(piece, 'row', swap) for piece in payload]]
    all_to_all x2, waiting for transfers between devices: 7.87 us -> 6.24 us  [exchange(): lax.all_to_all(packed, 'frame', split_axis=0, concat_axis=0, tiled=True)]
    ppermute x6, starting transfers between devices: 9.34 us -> 8.01 us  [others(): lax.ppermute(piece, 'frame', [(i, i ^ d * stride) for i in range(frames)])]
    ppermute x2 -> x8, starting transfers between devices: 0.27 us -> 1.48 us  [the longest x4 1.09 us: per_device_fast(): lax.ppermute(piece, 'row', swap)]
    ppermute x6, waiting for transfers between devices: 6.29 us -> 5.08 us  [partner(): lax.ppermute(piece, 'frame', [(i, i ^ offset) for i in range(frames)])]
    unnamed x30 -> x24, local copies, waits for them, and re-layouts: 3.22 us -> 3.16 us
  transfers between devices with their start and end apart: 18 -> 24, of which waited for: 13 -> 14; matrix products, arithmetic and copies ran while one was open for 0% -> 0% of each run, Pallas kernels for 16% -> 14%
where the time goes in v11:
time: 106 us
  waiting for transfers between devices  44.3 us (42%)
  starting transfers between devices  31.1 us (29%)
  Pallas kernels  25.2 us (24%)
  local copies, waits for them, and re-layouts  3.17 us (3%)
  between operations  1.53 us (1%)
    ppermute x6, waiting for transfers between devices, others(): lax.ppermute(piece, 'frame', [(i, i ^ d * stride) for i in range(frames)])  30.2 us
    all_to_all x2, starting transfers between devices, exchange(): lax.all_to_all(packed, 'frame', split_axis=0, concat_axis=0, tiled=True)  12.7 us
    ppermute x6, starting transfers between devices, partner(): lax.ppermute(piece, 'frame', [(i, i ^ offset) for i in range(frames)])  8.71 us
    ppermute x6, starting transfers between devices, others(): lax.ppermute(piece, 'frame', [(i, i ^ d * stride) for i in range(frames)])  8.01 us
    pallas_call x1, Pallas kernels, per_device_fast(): call(space_fast_kernel, [(wide, f32), (wide, f32), ((length, pair), bf16)...  7.01 us
    pallas_call x1, Pallas kernels, per_device_fast(): call(functools.partial(site_fast_kernel, sites), [(packed, bf16), (wide,...  6.56 us
    all_to_all x2, waiting for transfers between devices, exchange(): lax.all_to_all(packed, 'frame', split_axis=0, concat_axis=0, tiled=True)  6.24 us
    ppermute x6, waiting for transfers between devices, partner(): lax.ppermute(piece, 'frame', [(i, i ^ offset) for i in range(frames)])  5.08 us
  transfers between devices with their start and end apart: 24, of which 14 were waited for; matrix products, arithmetic and copies ran while one was open for 0% of the time, Pallas kernels for 14%

profile of v11, /device:TPU:0, one launch (start us, length us, event | category | flops | bytes accessed | tf_op | source)
XLA Modules:
  0.0 105.7 jit_solution(17283706604306586375)
XLA Ops:
  1.4 2.8 %shard_map.137 = (bf16[16,2,8,2048]{3,2,1,0:T(8,128)(2,1)}, bf16[152,128]{1,0:T(8,128)(2,1)S(1)}) custom-call(s32[2]{0:T(128)S(1)} %pad_add_fusion.ids_ref, bf16[16,8,2048]{2,1,0:T(8,128)(2,1)} %bitcast.30, bf16[16,8,2048]{2,1,0:T(8,128)(2,1)} %bitcast.34, bf16[128,256]{1,0:T(8,128)(2,1)} %proj_hbm.1, bf16[32,128]{1,0:T(8,128)(2,1)} %bitcast.41, ...), custom_call_target="tpu_custom_call" | custom-call | tf_op jit(solution)/shard_map/pallas_call | solution.py:937
  4.3 8.4 %all-to-all-start = ((bf16[16,2,8,2048]{3,2,1,0:T(8,128)(2,1)}), bf16[16,2,8,2048]{3,2,1,0:T(8,128)(2,1)S(1)}, u32[]{:S(2)}, u32[]{:S(2)}) async-start(bf16[16,2,8,2048]{3,2,1,0:T(8,128)(2,1)} %get-tuple-element.51), calls=%async_computation | async-start | bytes 2097152 | tf_op jit(solution)/shard_map/all_to_all | solution.py:44
  12.6 3.7 %collective-permute-start.2 = (bf16[152,128]{1,0:T(8,128)(2,1)S(1)}, bf16[152,128]{1,0:T(8,128)(2,1)S(1)}, u32[]{:S(2)}, u32[]{:S(2)}) collective-permute-start(bf16[152,128]{1,0:T(8,128)(2,1)S(1)} %get-tuple-element.48), channel_id=1, source_target_pairs={{0,24},{2,26},{4,28},{6,30},{8,16},{10,18},{12,20},{14,22},{16,8},... | collective-permute-start | bytes 116744 | tf_op jit(solution)/shard_map/ppermute | solution.py:877
  17.1 18.3 %collective-permute-done.2 = bf16[152,128]{1,0:T(8,128)(2,1)S(1)} collective-permute-done((bf16[152,128]{1,0:T(8,128)(2,1)S(1)}, bf16[152,128]{1,0:T(8,128)(2,1)S(1)}, u32[]{:S(2)}, u32[]{:S(2)}) %collective-permute-start.2) | collective-permute-done | bytes 38944 | tf_op jit(solution)/shard_map/ppermute | solution.py:877
  35.4 6.2 %collective-permute-done.1 = bf16[152,128]{1,0:T(8,128)(2,1)S(1)} collective-permute-done((bf16[152,128]{1,0:T(8,128)(2,1)S(1)}, bf16[152,128]{1,0:T(8,128)(2,1)S(1)}, u32[]{:S(2)}, u32[]{:S(2)}) %collective-permute-start.1) | collective-permute-done | bytes 38944 | tf_op jit(solution)/shard_map/ppermute | solution.py:877
  41.7 2.6 %collective-permute-start.5 = (bf16[4,152,128]{2,1,0:T(8,128)(2,1)S(1)}, bf16[4,152,128]{2,1,0:T(8,128)(2,1)S(1)}, u32[]{:S(2)}, u32[]{:S(2)}) collective-permute-start(bf16[4,152,128]{2,1,0:T(8,128)(2,1)S(1)} %pad_maximum_fusion.refs_0_), channel_id=1, source_target_pairs={{0,6},{2,4},{4,2},{6,0},{8,14},{10,12},{12,10},{14,8},{16,22},{18,... | collective-permute-start | bytes 466952 | tf_op jit(solution)/shard_map/ppermute | solution.py:877
  45.2 4.0 %collective-permute-done.5.refs_3_ = bf16[4,152,128]{2,1,0:T(8,128)(2,1)S(1)} collective-permute-done((bf16[4,152,128]{2,1,0:T(8,128)(2,1)S(1)}, bf16[4,152,128]{2,1,0:T(8,128)(2,1)S(1)}, u32[]{:S(2)}, u32[]{:S(2)}) %collective-permute-start.5) | collective-permute-done | bytes 155680 | tf_op jit(solution)/shard_map/ppermute | solution.py:877
  49.2 1.5 %collective-permute-done.4.refs_2_ = bf16[4,152,128]{2,1,0:T(8,128)(2,1)S(1)} collective-permute-done((bf16[4,152,128]{2,1,0:T(8,128)(2,1)S(1)}, bf16[4,152,128]{2,1,0:T(8,128)(2,1)S(1)}, u32[]{:S(2)}, u32[]{:S(2)}) %collective-permute-start.4) | collective-permute-done | bytes 155680 | tf_op jit(solution)/shard_map/ppermute | solution.py:877
  53.4 6.6 %shard_map.139 = (bf16[16,2,8,2048]{3,2,1,0:T(8,128)(2,1)}, bf16[128,2048]{1,0:T(8,128)(2,1)}, f32[2,2048]{1,0:T(2,128)}, bf16[128,256]{1,0:T(8,128)(2,1)S(1)}, bf16[128,32]{1,0:T(8,128)(2,1)S(1)}) custom-call(bf16[16,2,8,2048]{3,2,1,0:T(8,128)(2,1)S(1)} %all-to-all-done.got_ref, f32[1,2048]{1,0:T(1,128)S(1)} %get-tuple-element.49.refs_0_.refs_2_, ...), custom_call_target="tpu_custom_call" | custom-call | tf_op jit(solution)/shard_map/pallas_call | solution.py:967
  60.0 4.4 %all-to-all-start.1 = ((bf16[16,2,8,2048]{3,2,1,0:T(8,128)(2,1)}), bf16[16,2,8,2048]{3,2,1,0:T(8,128)(2,1)S(1)}, u32[]{:S(2)}, u32[]{:S(2)}) async-start(bf16[16,2,8,2048]{3,2,1,0:T(8,128)(2,1)} %get-tuple-element.78), calls=%async_computation.1 | async-start | bytes 2097152 | tf_op jit(solution)/shard_map/all_to_all | solution.py:44
  64.4 2.4 %shard_map.140 = (bf16[128,2048]{1,0:T(8,128)(2,1)S(1)}, bf16[128,256]{1,0:T(8,128)(2,1)S(1)}, bf16[128,32]{1,0:T(8,128)(2,1)S(1)}, f32[128,1]{1,0:T(8,128)S(1)}, bf16[2048,128]{1,0:T(8,128)(2,1)S(1)}) custom-call(s32[2]{0:T(128)S(1)} %pad_add_fusion.ids_ref, bf16[128,2048]{1,0:T(8,128)(2,1)S(1)} %bitcast.31, bf16[128,2048]{1,0:T(8,128)(2,1)S(1)} %bitcast.35, ...), custom_call_target="tpu_custom_call" | custom-call | tf_op jit(solution)/shard_map/pallas_call | solution.py:990
  66.9 1.9 %collective-permute-done.10.arrived_ref = bf16[2048,128]{1,0:T(8,128)(2,1)S(1)} collective-permute-done((bf16[2048,128]{1,0:T(8,128)(2,1)S(1)}, bf16[2048,128]{1,0:T(8,128)(2,1)S(1)}, u32[]{:S(2)}, u32[]{:S(2)}) %collective-permute-start.10) | collective-permute-done | bytes 524320 | tf_op jit(solution)/shard_map/ppermute | solution.py:1001
  68.8 7.0 %shard_map.141 = (f32[128,2048]{1,0:T(8,128)S(1)}, f32[128,2048]{1,0:T(8,128)S(1)}, bf16[128,256]{1,0:T(8,128)(2,1)S(1)}, bf16[128,32]{1,0:T(8,128)(2,1)S(1)}, f32[2,2048]{1,0:T(2,128)S(1)}) custom-call(s32[2]{0:T(128)S(1)} %pad_add_fusion.ids_ref, bf16[2048,128]{1,0:T(8,128)(2,1)S(1)} %collective-permute-done.10.arrived_ref, ...), custom_call_target="tpu_custom_call" | custom-call | tf_op jit(solution)/shard_map/pallas_call | solution.py:1003
  75.8 1.3 %shard_map.142 = (bf16[4,152,128]{2,1,0:T(8,128)(2,1)S(1)}, bf16[4,152,128]{2,1,0:T(8,128)(2,1)S(1)}, bf16[4,152,128]{2,1,0:T(8,128)(2,1)S(1)}, bf16[4,152,128]{...) custom-call(s32[2]{0:T(128)S(1)} %pad_add_fusion.ids_ref, ...), custom_call_target="tpu_custom_call" | custom-call | tf_op jit(solution)/shard_map/pallas_call | solution.py:1021
  78.6 2.0 %collective-permute-start.13 = (bf16[4,152,128]{2,1,0:T(8,128)(2,1)S(1)}, bf16[4,152,128]{2,1,0:T(8,128)(2,1)S(1)}, u32[]{:S(2)}, u32[]{:S(2)}) collective-permute-start(bf16[4,152,128]{2,1,0:T(8,128)(2,1)S(1)} %add_convert_fusion.3), channel_id=1, source_target_pairs={{0,2},{2,0},{4,6},{6,4},{8,10},{10,8},{12,14},{14,12},{16,18},{18,... | collective-permute-start | bytes 466952 | tf_op jit(solution)/shard_map/ppermute | solution.py:895
  80.7 1.5 %collective-permute-start.15 = (bf16[4,152,128]{2,1,0:T(8,128)(2,1)S(1)}, bf16[4,152,128]{2,1,0:T(8,128)(2,1)S(1)}, u32[]{:S(2)}, u32[]{:S(2)}) collective-permute-start(bf16[4,152,128]{2,1,0:T(8,128)(2,1)S(1)} %add_convert_fusion.2), channel_id=1, source_target_pairs={{0,4},{2,6},{4,0},{6,2},{8,12},{10,14},{12,8},{14,10},{16,20},{18,... | collective-permute-start | bytes 466952 | tf_op jit(solution)/shard_map/ppermute | solution.py:895
  82.8 6.2 %all-to-all-done.1.came_ref = bf16[16,2,8,2048]{3,2,1,0:T(8,128)(2,1)S(1)} async-done(((bf16[16,2,8,2048]{3,2,1,0:T(8,128)(2,1)}), bf16[16,2,8,2048]{3,2,1,0:T(8,128)(2,1)S(1)}, u32[]{:S(2)}, u32[]{:S(2)}) %all-to-all-start.1) | async-done | bytes 1048608 | tf_op jit(solution)/shard_map/all_to_all | solution.py:44
  89.0 1.2 %copy-done.3 = f32[128,2048]{1,0:T(8,128)S(1)} copy-done((f32[128,2048]{1,0:T(8,128)S(1)}, f32[128,2048]{1,0:T(8,128)}, u32[]{:S(2)}) %copy-start.3) | copy-done | bytes 1048600
  90.3 1.2 %copy-done.5 = f32[128,2048]{1,0:T(8,128)S(1)} copy-done((f32[128,2048]{1,0:T(8,128)S(1)}, f32[128,2048]{1,0:T(8,128)}, u32[]{:S(2)}) %copy-start.5) | copy-done | bytes 1048600
  91.5 1.7 %shard_map.143 = (bf16[128,2048]{1,0:T(8,128)(2,1)}, bf16[128,2048]{1,0:T(8,128)(2,1)}) custom-call(bf16[128,2048]{1,0:T(8,128)(2,1)S(1)} %bitcast.33, f32[128,1]{1,0:T(8,128)S(1)} %get-tuple-element.60.refs_5_.inverse_ref, f32[1,2048]{1,0:T(1,128)S(1)} %get-tuple-element.50.refs_1_.refs_3_.gain_ref, f32[128,2048]{1,0:T(8,128)S(1)} %copy-done.3, ...), custom_call_target="tpu_custom_call" | custom-call | tf_op jit(solution)/shard_map/pallas_call | solution.py:1025
  93.3 3.2 %collective-permute-start.18 = (bf16[152,128]{1,0:T(8,128)(2,1)S(1)}, bf16[152,128]{1,0:T(8,128)(2,1)S(1)}, u32[]{:S(2)}, u32[]{:S(2)}) collective-permute-start(bf16[152,128]{1,0:T(8,128)(2,1)S(1)} %get-tuple-element.91), channel_id=1, source_target_pairs={{0,8},{2,10},{4,12},{6,14},{8,0},{10,2},{12,4},{14,6},{16,24},{18,... | collective-permute-start | bytes 116744 | tf_op jit(solution)/shard_map/ppermute | solution.py:895
  96.5 1.4 %collective-permute-start.20 = (bf16[152,128]{1,0:T(8,128)(2,1)S(1)}, bf16[152,128]{1,0:T(8,128)(2,1)S(1)}, u32[]{:S(2)}, u32[]{:S(2)}) collective-permute-start(bf16[152,128]{1,0:T(8,128)(2,1)S(1)} %get-tuple-element.92), channel_id=1, source_target_pairs={{0,24},{2,26},{4,28},{6,30},{8,16},{10,18},{12,20},{14,22},{16,8},... | collective-permute-start | bytes 116744 | tf_op jit(solution)/shard_map/ppermute | solution.py:895
  98.5 3.8 %collective-permute-done.20 = bf16[152,128]{1,0:T(8,128)(2,1)S(1)} collective-permute-done((bf16[152,128]{1,0:T(8,128)(2,1)S(1)}, bf16[152,128]{1,0:T(8,128)(2,1)S(1)}, u32[]{:S(2)}, u32[]{:S(2)}) %collective-permute-start.20) | collective-permute-done | bytes 38944 | tf_op jit(solution)/shard_map/ppermute | solution.py:895
  104.5 1.2 %shard_map.145 = (f32[128,256]{1,0:T(8,128)}, f32[32,128]{1,0:T(8,128)}) custom-call(s32[2]{0:T(128)S(1)} %pad_add_fusion.ids_ref, f32[152,128]{1,0:T(8,128)S(1)} %fusion.1.sums_ref.own_ref, f32[152,128]{1,0:T(8,128)S(1)} %collective-permute-done.21.other_ref), custom_call_target="tpu_custom_call" | custom-call | tf_op jit(solution)/shard_map/pallas_call | solution.py:1036
  (68 shorter events, 9.6 us)
Async XLA Ops:
  4.3 49.1 %all-to-all-start = ((bf16[16,2,8,2048]{3,2,1,0:T(8,128)(2,1)}), bf16[16,2,8,2048]{3,2,1,0:T(8,128)(2,1)S(1)}, u32[]{:S(2)}, u32[]{:S(2)}) async-start(bf16[16,2,8,2048]{3,2,1,0:T(8,128)(2,1)} %get-tuple-element.51), calls=%async_computation | async-start | bytes 2097152 | tf_op jit(solution)/shard_map/all_to_all | solution.py:44
  12.6 22.8 %collective-permute-start.2 = (bf16[152,128]{1,0:T(8,128)(2,1)S(1)}, bf16[152,128]{1,0:T(8,128)(2,1)S(1)}, u32[]{:S(2)}, u32[]{:S(2)}) collective-permute-start(bf16[152,128]{1,0:T(8,128)(2,1)S(1)} %get-tuple-element.48), channel_id=1, source_target_pairs={{0,24},{2,26},{4,28},{6,30},{8,16},{10,18},{12,20},{14,22},{16,8},... | collective-permute-start | bytes 116744 | tf_op jit(solution)/shard_map/ppermute | solution.py:877
  16.3 25.3 %collective-permute-start.1 = (bf16[152,128]{1,0:T(8,128)(2,1)S(1)}, bf16[152,128]{1,0:T(8,128)(2,1)S(1)}, u32[]{:S(2)}, u32[]{:S(2)}) collective-permute-start(bf16[152,128]{1,0:T(8,128)(2,1)S(1)} %get-tuple-element.48), channel_id=1, source_target_pairs={{0,16},{2,18},{4,20},{6,22},{8,24},{10,26},{12,28},{14,30},{16,0},... | collective-permute-start | bytes 116744 | tf_op jit(solution)/shard_map/ppermute | solution.py:877
  16.3 25.3 %collective-permute-start = (bf16[152,128]{1,0:T(8,128)(2,1)S(1)}, bf16[152,128]{1,0:T(8,128)(2,1)S(1)}, u32[]{:S(2)}, u32[]{:S(2)}) collective-permute-start(bf16[152,128]{1,0:T(8,128)(2,1)S(1)} %get-tuple-element.48), channel_id=1, source_target_pairs={{0,8},{2,10},{4,12},{6,14},{8,0},{10,2},{12,4},{14,6},{16,24},{18,... | collective-permute-start | bytes 116744 | tf_op jit(solution)/shard_map/ppermute | solution.py:877
  41.7 7.5 %collective-permute-start.5 = (bf16[4,152,128]{2,1,0:T(8,128)(2,1)S(1)}, bf16[4,152,128]{2,1,0:T(8,128)(2,1)S(1)}, u32[]{:S(2)}, u32[]{:S(2)}) collective-permute-start(bf16[4,152,128]{2,1,0:T(8,128)(2,1)S(1)} %pad_maximum_fusion.refs_0_), channel_id=1, source_target_pairs={{0,6},{2,4},{4,2},{6,0},{8,14},{10,12},{12,10},{14,8},{16,22},{18,... | collective-permute-start | bytes 466952 | tf_op jit(solution)/shard_map/ppermute | solution.py:877
  44.2 6.5 %collective-permute-start.4 = (bf16[4,152,128]{2,1,0:T(8,128)(2,1)S(1)}, bf16[4,152,128]{2,1,0:T(8,128)(2,1)S(1)}, u32[]{:S(2)}, u32[]{:S(2)}) collective-permute-start(bf16[4,152,128]{2,1,0:T(8,128)(2,1)S(1)} %pad_maximum_fusion.refs_0_), channel_id=1, source_target_pairs={{0,4},{2,6},{4,0},{6,2},{8,12},{10,14},{12,8},{14,10},{16,20},{18,... | collective-permute-start | bytes 466952 | tf_op jit(solution)/shard_map/ppermute | solution.py:877
  44.6 6.2 %collective-permute-start.3 = (bf16[4,152,128]{2,1,0:T(8,128)(2,1)S(1)}, bf16[4,152,128]{2,1,0:T(8,128)(2,1)S(1)}, u32[]{:S(2)}, u32[]{:S(2)}) collective-permute-start(bf16[4,152,128]{2,1,0:T(8,128)(2,1)S(1)} %pad_maximum_fusion.refs_0_), channel_id=1, source_target_pairs={{0,2},{2,0},{4,6},{6,4},{8,10},{10,8},{12,14},{14,12},{16,18},{18,... | collective-permute-start | bytes 466952 | tf_op jit(solution)/shard_map/ppermute | solution.py:877
  45.2 6.7 %collective-permute-start.6 = (bf16[4,152,128]{2,1,0:T(8,128)(2,1)S(1)}, bf16[4,152,128]{2,1,0:T(8,128)(2,1)S(1)}, u32[]{:S(2)}, u32[]{:S(2)}) collective-permute-start(bf16[4,152,128]{2,1,0:T(8,128)(2,1)S(1)} %pad_maximum_fusion.refs_0_), channel_id=1, source_target_pairs={{0,1},{1,0},{2,3},{3,2},{4,5},{5,4},{6,7},{7,6},{8,9},{9,8},{10,11... | collective-permute-start | bytes 466952 | tf_op jit(solution)/shard_map/ppermute | solution.py:960
  49.2 2.8 %collective-permute-start.9 = (bf16[4,152,128]{2,1,0:T(8,128)(2,1)S(1)}, bf16[4,152,128]{2,1,0:T(8,128)(2,1)S(1)}, u32[]{:S(2)}, u32[]{:S(2)}) collective-permute-start(bf16[4,152,128]{2,1,0:T(8,128)(2,1)S(1)} %collective-permute-done.5.refs_3_), channel_id=1, source_target_pairs={{0,1},{1,0},{2,3},{3,2},{4,5},{5,4},{6,7},{7,6},{8,9},{9,8},{10,11... | collective-permute-start | bytes 466952 | tf_op jit(solution)/shard_map/ppermute | solution.py:960
  50.7 1.4 %collective-permute-start.8 = (bf16[4,152,128]{2,1,0:T(8,128)(2,1)S(1)}, bf16[4,152,128]{2,1,0:T(8,128)(2,1)S(1)}, u32[]{:S(2)}, u32[]{:S(2)}) collective-permute-start(bf16[4,152,128]{2,1,0:T(8,128)(2,1)S(1)} %collective-permute-done.4.refs_2_), channel_id=1, source_target_pairs={{0,1},{1,0},{2,3},{3,2},{4,5},{5,4},{6,7},{7,6},{8,9},{9,8},{10,11... | collective-permute-start | bytes 466952 | tf_op jit(solution)/shard_map/ppermute | solution.py:960
  50.8 1.5 %collective-permute-start.7 = (bf16[4,152,128]{2,1,0:T(8,128)(2,1)S(1)}, bf16[4,152,128]{2,1,0:T(8,128)(2,1)S(1)}, u32[]{:S(2)}, u32[]{:S(2)}) collective-permute-start(bf16[4,152,128]{2,1,0:T(8,128)(2,1)S(1)} %collective-permute-done.3.refs_1_), channel_id=1, source_target_pairs={{0,1},{1,0},{2,3},{3,2},{4,5},{5,4},{6,7},{7,6},{8,9},{9,8},{10,11... | collective-permute-start | bytes 466952 | tf_op jit(solution)/shard_map/ppermute | solution.py:960
  60.0 29.1 %all-to-all-start.1 = ((bf16[16,2,8,2048]{3,2,1,0:T(8,128)(2,1)}), bf16[16,2,8,2048]{3,2,1,0:T(8,128)(2,1)S(1)}, u32[]{:S(2)}, u32[]{:S(2)}) async-start(bf16[16,2,8,2048]{3,2,1,0:T(8,128)(2,1)} %get-tuple-element.78), calls=%async_computation.1 | async-start | bytes 2097152 | tf_op jit(solution)/shard_map/all_to_all | solution.py:44
  66.8 2.0 %collective-permute-start.10 = (bf16[2048,128]{1,0:T(8,128)(2,1)S(1)}, bf16[2048,128]{1,0:T(8,128)(2,1)S(1)}, u32[]{:S(2)}, u32[]{:S(2)}) collective-permute-start(bf16[2048,128]{1,0:T(8,128)(2,1)S(1)} %get-tuple-element.57), channel_id=1, source_target_pairs={{0,1},{1,0},{2,3},{3,2},{4,5},{5,4},{6,7},{7,6},{8,9},{9,8},{10,11... | collective-permute-start | bytes 1572872 | tf_op jit(solution)/shard_map/ppermute | solution.py:1001
  77.1 1.4 %collective-permute-start.12 = (bf16[4,152,128]{2,1,0:T(8,128)(2,1)S(1)}, bf16[4,152,128]{2,1,0:T(8,128)(2,1)S(1)}, u32[]{:S(2)}, u32[]{:S(2)}) collective-permute-start(bf16[4,152,128]{2,1,0:T(8,128)(2,1)S(1)} %get-tuple-element.71), channel_id=1, source_target_pairs={{0,1},{1,0},{2,3},{3,2},{4,5},{5,4},{6,7},{7,6},{8,9},{9,8},{10,11... | collective-permute-start | bytes 466952 | tf_op jit(solution)/shard_map/ppermute | solution.py:1024
  77.3 5.4 %collective-permute-start.11 = (bf16[4,152,128]{2,1,0:T(8,128)(2,1)S(1)}, bf16[4,152,128]{2,1,0:T(8,128)(2,1)S(1)}, u32[]{:S(2)}, u32[]{:S(2)}) collective-permute-start(bf16[4,152,128]{2,1,0:T(8,128)(2,1)S(1)} %get-tuple-element.69), channel_id=1, source_target_pairs={{0,1},{1,0},{2,3},{3,2},{4,5},{5,4},{6,7},{7,6},{8,9},{9,8},{10,11... | collective-permute-start | bytes 466952 | tf_op jit(solution)/shard_map/ppermute | solution.py:1024
  77.7 2.9 %collective-permute-start.14 = (bf16[4,152,128]{2,1,0:T(8,128)(2,1)S(1)}, bf16[4,152,128]{2,1,0:T(8,128)(2,1)S(1)}, u32[]{:S(2)}, u32[]{:S(2)}) collective-permute-start(bf16[4,152,128]{2,1,0:T(8,128)(2,1)S(1)} %get-tuple-element.73), channel_id=1, source_target_pairs={{0,1},{1,0},{2,3},{3,2},{4,5},{5,4},{6,7},{7,6},{8,9},{9,8},{10,11... | collective-permute-start | bytes 466952 | tf_op jit(solution)/shard_map/ppermute | solution.py:1024
  77.9 4.4 %collective-permute-start.16 = (bf16[4,152,128]{2,1,0:T(8,128)(2,1)S(1)}, bf16[4,152,128]{2,1,0:T(8,128)(2,1)S(1)}, u32[]{:S(2)}, u32[]{:S(2)}) collective-permute-start(bf16[4,152,128]{2,1,0:T(8,128)(2,1)S(1)} %get-tuple-element.75), channel_id=1, source_target_pairs={{0,1},{1,0},{2,3},{3,2},{4,5},{5,4},{6,7},{7,6},{8,9},{9,8},{10,11... | collective-permute-start | bytes 466952 | tf_op jit(solution)/shard_map/ppermute | solution.py:1024
  78.6 14.5 %collective-permute-start.13 = (bf16[4,152,128]{2,1,0:T(8,128)(2,1)S(1)}, bf16[4,152,128]{2,1,0:T(8,128)(2,1)S(1)}, u32[]{:S(2)}, u32[]{:S(2)}) collective-permute-start(bf16[4,152,128]{2,1,0:T(8,128)(2,1)S(1)} %add_convert_fusion.3), channel_id=1, source_target_pairs={{0,2},{2,0},{4,6},{6,4},{8,10},{10,8},{12,14},{14,12},{16,18},{18,... | collective-permute-start | bytes 466952 | tf_op jit(solution)/shard_map/ppermute | solution.py:895
  80.7 12.5 %collective-permute-start.15 = (bf16[4,152,128]{2,1,0:T(8,128)(2,1)S(1)}, bf16[4,152,128]{2,1,0:T(8,128)(2,1)S(1)}, u32[]{:S(2)}, u32[]{:S(2)}) collective-permute-start(bf16[4,152,128]{2,1,0:T(8,128)(2,1)S(1)} %add_convert_fusion.2), channel_id=1, source_target_pairs={{0,4},{2,6},{4,0},{6,2},{8,12},{10,14},{12,8},{14,10},{16,20},{18,... | collective-permute-start | bytes 466952 | tf_op jit(solution)/shard_map/ppermute | solution.py:895
  82.3 10.9 %collective-permute-start.17 = (bf16[4,152,128]{2,1,0:T(8,128)(2,1)S(1)}, bf16[4,152,128]{2,1,0:T(8,128)(2,1)S(1)}, u32[]{:S(2)}, u32[]{:S(2)}) collective-permute-start(bf16[4,152,128]{2,1,0:T(8,128)(2,1)S(1)} %add_convert_fusion.1), channel_id=1, source_target_pairs={{0,6},{2,4},{4,2},{6,0},{8,14},{10,12},{12,10},{14,8},{16,22},{18,... | collective-permute-start | bytes 466952 | tf_op jit(solution)/shard_map/ppermute | solution.py:895
  93.3 5.2 %collective-permute-start.18 = (bf16[152,128]{1,0:T(8,128)(2,1)S(1)}, bf16[152,128]{1,0:T(8,128)(2,1)S(1)}, u32[]{:S(2)}, u32[]{:S(2)}) collective-permute-start(bf16[152,128]{1,0:T(8,128)(2,1)S(1)} %get-tuple-element.91), channel_id=1, source_target_pairs={{0,8},{2,10},{4,12},{6,14},{8,0},{10,2},{12,4},{14,6},{16,24},{18,... | collective-permute-start | bytes 116744 | tf_op jit(solution)/shard_map/ppermute | solution.py:895
  96.5 5.8 %collective-permute-start.20 = (bf16[152,128]{1,0:T(8,128)(2,1)S(1)}, bf16[152,128]{1,0:T(8,128)(2,1)S(1)}, u32[]{:S(2)}, u32[]{:S(2)}) collective-permute-start(bf16[152,128]{1,0:T(8,128)(2,1)S(1)} %get-tuple-element.92), channel_id=1, source_target_pairs={{0,24},{2,26},{4,28},{6,30},{8,16},{10,18},{12,20},{14,22},{16,8},... | collective-permute-start | bytes 116744 | tf_op jit(solution)/shard_map/ppermute | solution.py:895
  97.9 5.2 %collective-permute-start.19 = (bf16[152,128]{1,0:T(8,128)(2,1)S(1)}, bf16[152,128]{1,0:T(8,128)(2,1)S(1)}, u32[]{:S(2)}, u32[]{:S(2)}) collective-permute-start(bf16[152,128]{1,0:T(8,128)(2,1)S(1)} %get-tuple-element.93), channel_id=1, source_target_pairs={{0,16},{2,18},{4,20},{6,22},{8,24},{10,26},{12,28},{14,30},{16,0},... | collective-permute-start | bytes 116744 | tf_op jit(solution)/shard_map/ppermute | solution.py:895
  103.1 1.3 %collective-permute-start.21 = (f32[152,128]{1,0:T(8,128)S(1)}, f32[152,128]{1,0:T(8,128)S(1)}, u32[]{:S(2)}, u32[]{:S(2)}) collective-permute-start(f32[152,128]{1,0:T(8,128)S(1)} %fusion.1.sums_ref.own_ref), channel_id=1, source_target_pairs={{0,1},{1,0},{2,3},{3,2},{4,5},{5,4},{6,7},{7,6},{8,9},{9,8},{10,11... | collective-permute-start | bytes 233480 | tf_op jit(solution)/shard_map/ppermute | solution.py:1029
  (12 other events, 46.7 us)
